TPU v7x, 32 devices: a whole 2x2x4 slice. The times are simulated.
32 devices in a mesh: img: 8 (over z, y), patch: 4 (over x, core).
Axes of the slice: x: 2, y: 2, z: 4, core: 2. Of those that a mesh axis runs over, the one named last changes fastest.
Arguments:
- media: bfloat16 [80, 256, 1024], P('img', 'patch'), may hold values from -6 to 6
- latents: bfloat16 [80, 64, 1024], P('img', 'patch'), may hold values from -6 to 6
- counts: int32 [16], P('img'), may hold values from 1 to 5
- gains: float32 [3, 1024], replicated, may hold values from 0.1 to 1.9
- biases: float32 [3, 1024], replicated, may hold values from -3 to 3
- w_query: bfloat16 [1024, 512], replicated, may hold values from -0.1875 to 0.1875
- w_keyval: bfloat16 [1024, 1024], replicated, may hold values from -0.1875 to 0.1875
- w_out: bfloat16 [512, 1024], replicated, may hold values from -2 to 2
- w_up: bfloat16 [1024, 4096], replicated, may hold values from -0.1875 to 0.1875
- w_down: bfloat16 [4096, 1024], replicated, may hold values from -0.09375 to 0.09375
- out_grad: bfloat16 [80, 64, 1024], P('img', 'patch'), may hold values from -6 to 6
Outputs:
- latents_out: bfloat16 [80, 64, 1024], P('img', 'patch')
- media_grad: bfloat16 [80, 256, 1024], P('img', 'patch')
- latent_grad: bfloat16 [80, 64, 1024], P('img', 'patch')
- query_wgrad: float32 [1024, 512], P(None, ('img', 'patch'))
- keyval_wgrad: float32 [1024, 1024], P(None, ('img', 'patch'))
- out_wgrad: float32 [512, 1024], P(None, ('img', 'patch'))
- up_wgrad: float32 [1024, 4096], P(None, ('img', 'patch'))
- down_wgrad: float32 [4096, 1024], P(None, ('img', 'patch'))
- gain_grad: float32 [3, 1024], P(None, ('img', 'patch'))
- bias_grad: float32 [3, 1024], P(None, ('img', 'patch'))
All inputs are finite; a program needn't handle non-finite values.
Results may differ from a plain program's by a relative error of at most 0.015.
Values may be sent and summed in bfloat16 or wider, within the bound.
No kernel may reach another device: no remote copies, remote signals or barrier semaphores. Data moves between devices by JAX's collectives and lax.ppermute only.
A program may use at most 192 MiB of HBM per device.

v0:
```python
import functools
import math

import jax
import jax.numpy as jnp
from jax import lax
from jax.experimental import pallas as pl
from jax.experimental.pallas import tpu as pltpu
from jax.sharding import PartitionSpec as P

HEADS = 8
SLOTS_PER = 5
EPS = 1e-05
LANES = 128
F32 = jnp.float32
BF16 = jnp.bfloat16
MIB = 1024 * 1024


def swap(values, axis, bit):
    n = lax.axis_size(axis)
    return lax.ppermute(values, axis, [(k, k ^ bit) for k in range(n)])


def log2(n):
    return n.bit_length() - 1


def gather(values, axis):
    n = lax.axis_size(axis)
    blocks = {0: values}
    bit = n // 2
    while bit:
        for j in list(blocks):
            blocks[j ^ bit] = swap(blocks[j], axis, bit)
        bit //= 2
    return [blocks[j] for j in range(n)]


class Piece:
    def __init__(self, values, digits):
        self.digits = list(digits)
        count = math.prod(size for _, size in digits)
        self.values = values.reshape((count, -1) + values.shape[-1:])

    def step(self, axis, bit):
        at = [name for name, _ in self.digits].index((axis, bit))
        before = math.prod(s for _, s in self.digits[:at])
        after = math.prod(s for _, s in self.digits[at + 1 :])
        inner = self.values.shape[1:]
        split = self.values.reshape((before, 2, after * inner[0]) + inner[1:])
        mine = (lax.axis_index(axis) // bit) % 2 == 1
        low, high = split[:, 0], split[:, 1]
        kept = jnp.where(mine, high, low)
        sent = jnp.where(mine, low, high)
        del self.digits[at]
        shape = (before * after,) + inner
        return kept.reshape(shape), sent.reshape(shape)


def scatter_sum(pieces, order):
    for axis, bit in order:
        both = [piece.step(axis, bit) for piece in pieces]
        got = [swap(sent, axis, bit) for _, sent in both]
        for piece, (kept, _), other in zip(pieces, both, got):
            piece.values = (kept.astype(F32) + other.astype(F32)).astype(kept.dtype)
    return [piece.values[0] for piece in pieces]


def digits_of(axis):
    n = lax.axis_size(axis)
    return [((axis, 1 << k), 2) for k in reversed(range(log2(n)))]


def stats(values):
    average = jnp.mean(values, axis=-1, keepdims=True)
    centred = values - average
    spread = jnp.mean(centred * centred, axis=-1, keepdims=True)
    inverse = lax.rsqrt(spread + EPS)
    return centred * inverse, inverse


def pull(hat, inverse, grad, gain):
    scaled = grad * gain
    first = jnp.mean(scaled, axis=-1, keepdims=True)
    second = jnp.mean(scaled * hat, axis=-1, keepdims=True)
    return inverse * (scaled - first - hat * second)


def gelu_parts(values):
    cdf = 0.5 + 0.5 * lax.erf(values * (1.0 / math.sqrt(2.0)))
    density = jnp.exp(-0.5 * values * values) * (1.0 / math.sqrt(2.0 * math.pi))
    return values * cdf, cdf + values * density


def dot(a, b, dims=((1,), (0,))):
    return lax.dot_general(a, b, (dims, ((), ())), preferred_element_type=F32)


NT = ((1,), (1,))
TN = ((0,), (0,))


def low_lanes(shape):
    return lax.broadcasted_iota(jnp.int32, shape, len(shape) - 1) < LANES // 2


def live_rows(counts_ref, rows, per_slot):
    row = lax.broadcasted_iota(jnp.int32, (rows, 1), 0)
    live = jnp.zeros((rows, 1), F32)
    for sample in range(rows // (per_slot * SLOTS_PER)):
        start = sample * SLOTS_PER * per_slot
        inside = jnp.logical_and(row >= start, row < start + counts_ref[sample] * per_slot)
        live = jnp.where(inside, 1.0, live)
    return live


def paired(block):
    low = low_lanes(block.shape)
    zero = jnp.zeros_like(block)
    return jnp.concatenate([jnp.where(low, block, zero), jnp.where(low, zero, block)], axis=0)


def unpaired(block):
    half = block.shape[0] // 2
    return jnp.where(low_lanes((half, block.shape[1])), block[:half], block[half:])


def flipped(values):
    a, b = values.shape
    tall, wide = -a % LANES, -b % LANES
    if wide:
        values = jnp.concatenate([values, jnp.zeros((a, wide), F32)], axis=1)
    if tall:
        values = jnp.concatenate([values, jnp.zeros((tall, b + wide), F32)], axis=0)
    return values.T[:b, :a]


def call(kernel, grid, ins, outs, scratch=(), vmem=40, flops=0, moved=0, prefetch=0, name=None):
    return pl.pallas_call(
        kernel,
        grid_spec=pltpu.PrefetchScalarGridSpec(
            num_scalar_prefetch=prefetch,
            grid=grid,
            in_specs=ins,
            out_specs=[spec for spec, _ in outs],
            scratch_shapes=list(scratch),
        ),
        out_shape=[shape for _, shape in outs],
        compiler_params=pltpu.CompilerParams(
            vmem_limit_bytes=vmem * MIB, dimension_semantics=("arbitrary",) * len(grid)
        ),
        cost_estimate=pl.CostEstimate(flops=int(flops), bytes_accessed=int(moved), transcendentals=0),
        name=name,
    )


def whole(shape):
    zeros = (0,) * len(shape)
    return pl.BlockSpec(tuple(shape), lambda *_: zeros)


def leading(shape):
    zeros = (0,) * (len(shape) - 1)
    return pl.BlockSpec(tuple(shape), lambda g, *_: (g,) + zeros)


def out(shape, dtype):
    return jax.ShapeDtypeStruct(tuple(shape), dtype)


SMEM = pl.BlockSpec(memory_space=pltpu.SMEM)


def latent_kernel(per_slot, counts, lat, grad, gain, bias, w_query, lat_low, q_low, dy):
    hat, _ = stats(lat[...].astype(F32))
    low = (hat * gain[1:2] + bias[1:2]).astype(BF16)
    lat_low[...] = low
    q_low[...] = dot(low, w_query[...]).astype(BF16)
    live = live_rows(counts, lat.shape[0], per_slot)
    dy[...] = (live * grad[...].astype(F32)).astype(BF16)


def media_kernel(media, lat_low, gain, bias, w_keyval, key_input, keyval):
    n, rows, width = media.shape
    hat, _ = stats(media[...].reshape(n * rows, width).astype(F32))
    low = (hat * gain[0:1] + bias[0:1]).astype(BF16)
    key_input[:, :rows, :] = low.reshape(n, rows, width)
    key_input[:, rows:, :] = lat_low[...].reshape(n, -1, width)
    every = key_input[...].reshape(-1, width)
    keyval[...] = dot(every, w_keyval[...]).astype(BF16).reshape(keyval.shape)


def attend_kernel(peers, scale, *refs):
    qs, (kv,), parts, lses, (held,) = (
        refs[:peers], refs[peers : peers + 1], refs[peers + 1 : 2 * peers + 1],
        refs[2 * peers + 1 : 3 * peers + 1], refs[3 * peers + 1 :],
    )
    n, per_slot, inner = qs[0].shape
    step = pl.program_id(0)
    for s in range(n):
        lane = lax.broadcasted_iota(jnp.int32, (peers * per_slot, LANES), 1)
        logs = jnp.zeros((peers * per_slot, LANES), F32)
        for t in range(inner // LANES):
            cut = slice(t * LANES, (t + 1) * LANES)
            q = paired(jnp.concatenate([ref[s, :, cut] for ref in qs], axis=0))
            k = kv[s, :, cut]
            v = kv[s, :, inner + t * LANES : inner + (t + 1) * LANES]
            scores = dot(q, k, NT) * scale
            top = jnp.max(scores, axis=-1, keepdims=True)
            expd = jnp.exp(scores - top)
            total = jnp.sum(expd, axis=-1, keepdims=True)
            probs = (expd * (1.0 / total)).astype(BF16)
            o = unpaired(dot(probs, v)).astype(BF16)
            lse = top + jnp.log(total)
            half = lse.shape[0] // 2
            logs = jnp.where(lane == 2 * t, lse[:half], logs)
            logs = jnp.where(lane == 2 * t + 1, lse[half:], logs)
            for i in range(peers):
                parts[i][s, :, cut] = o[i * per_slot : (i + 1) * per_slot]
        row = pl.multiple_of((step * n + s) * per_slot, per_slot)
        for i in range(peers):
            held[i, pl.ds(row, per_slot), :] = logs[i * per_slot : (i + 1) * per_slot]

    @pl.when(step == pl.num_programs(0) - 1)
    def _():
        for i in range(peers):
            lses[i][...] = held[i].T[: lses[i].shape[0], : lses[i].shape[1]]


def mix_kernel(peers, *refs):
    parts, lses = refs[:peers], refs[peers : 2 * peers]
    lat, w_out, gain, bias, attended, att_low, hidden, ff_low, lse_out = refs[2 * peers :]
    rows, inner = attended.shape
    logs = [ref[...] for ref in lses]
    top = functools.reduce(jnp.maximum, logs)
    lse = top + jnp.log(sum(jnp.exp(v - top) for v in logs))
    lse_out[...] = lse
    weights = flipped(jnp.concatenate([jnp.exp(v - lse) for v in logs], axis=0))
    low = low_lanes((rows, LANES))
    for t in range(inner // LANES):
        cut = slice(t * LANES, (t + 1) * LANES)
        total = jnp.zeros((rows, LANES), F32)
        for j in range(peers):
            at = j * HEADS + 2 * t
            weight = jnp.where(low, weights[:, at : at + 1], weights[:, at + 1 : at + 2])
            total = total + weight * parts[j][:, cut].astype(F32)
        attended[:, cut] = total
        att_low[:, cut] = total.astype(BF16)
    state = lat[...].astype(F32) + dot(att_low[...], w_out[...])
    hidden[...] = state
    hat, _ = stats(state)
    ff_low[...] = (hat * gain[2:3] + bias[2:3]).astype(BF16)


def feed_kernel(per_slot, halves, blocks, own, counts, *refs):
    count = halves * blocks
    ff_low, dy, hidden, attended, lse, w_out, gain = refs[:7]
    ups, downs = refs[7 : 7 + count], refs[7 + count : 7 + 2 * count]
    act, dpre, result, dhidden, dhid_low, datt_low, stat, sums, res, dff = refs[7 + 2 * count :]
    step = pl.program_id(0)

    @pl.when(step == 0)
    def _():
        res[...] = jnp.zeros_like(res)
        dff[...] = jnp.zeros_like(dff)

    for a in range(halves):
        up = jnp.concatenate([ref[...] for ref in ups[a * blocks : (a + 1) * blocks]], axis=1)
        down = jnp.concatenate([ref[...] for ref in downs[a * blocks : (a + 1) * blocks]], axis=0)
        value, slope = gelu_parts(dot(ff_low[...], up))
        value = value.astype(BF16)
        act[0, a] = value
        back = (slope * dot(dy[...], down, NT)).astype(BF16)
        dpre[0, a] = back
        res[...] += dot(value, down)
        dff[...] += dot(back, up, NT)

    @pl.when(step == pl.num_programs(0) - 1)
    def _():
        rows, inner = attended.shape
        live = live_rows(counts, rows, per_slot)
        state = hidden[...]
        result[...] = (live * (state + res[...])).astype(BF16)
        hat, inverse = stats(state)
        grad = dff[...]
        sums[0:1] = jnp.sum(grad * hat, axis=0, keepdims=True)
        sums[1:2] = jnp.sum(grad, axis=0, keepdims=True)
        back = dy[...].astype(F32) + pull(hat, inverse, grad, gain[2:3])
        dhidden[...] = back
        dhid_low[...] = back.astype(BF16)
        datt = dot(dhid_low[...], w_out[...], NT).astype(BF16)
        datt_low[...] = datt
        product = datt.astype(F32) * attended[...]
        low = low_lanes((rows, LANES))
        lane = lax.broadcasted_iota(jnp.int32, (rows, LANES), 1)
        delta = jnp.zeros((rows, LANES), F32)
        for t in range(inner // LANES):
            both = product[:, t * LANES : (t + 1) * LANES]
            first = jnp.sum(jnp.where(low, both, 0.0), axis=-1, keepdims=True)
            second = jnp.sum(jnp.where(low, 0.0, both), axis=-1, keepdims=True)
            delta = jnp.where(lane == 2 * t, first, delta)
            delta = jnp.where(lane == 2 * t + 1, second, delta)
        stat[:HEADS] = lse[...]
        stat[HEADS:] = flipped(delta)[:HEADS]


def attend_back_kernel(peers, scale, *refs):
    qs, das, sts = refs[:peers], refs[peers : 2 * peers], refs[2 * peers : 3 * peers]
    kv, dkv = refs[3 * peers], refs[3 * peers + 1]
    dqs, held = refs[3 * peers + 2 : 4 * peers + 2], refs[4 * peers + 2]
    n, per_slot, inner = qs[0].shape
    step = pl.program_id(0)

    @pl.when(step == 0)
    def _():
        for i in range(peers):
            rows = sts[i].shape[1]
            held[i, :rows, : 2 * HEADS] = flipped(sts[i][...])

    for s in range(n):
        row = pl.multiple_of((step * n + s) * per_slot, per_slot)
        st = jnp.concatenate([held[i, pl.ds(row, per_slot), :] for i in range(peers)], axis=0)
        for t in range(inner // LANES):
            cut = slice(t * LANES, (t + 1) * LANES)
            after = slice(inner + t * LANES, inner + (t + 1) * LANES)
            q = paired(jnp.concatenate([ref[s, :, cut] for ref in qs], axis=0))
            da = paired(jnp.concatenate([ref[s, :, cut] for ref in das], axis=0))
            k, v = kv[s, :, cut], kv[s, :, after]
            h = 2 * t
            lse = jnp.concatenate([st[:, h : h + 1], st[:, h + 1 : h + 2]], axis=0)
            h = HEADS + 2 * t
            delta = jnp.concatenate([st[:, h : h + 1], st[:, h + 1 : h + 2]], axis=0)
            probs = jnp.exp(dot(q, k, NT) * scale - lse)
            dprobs = dot(da, v, NT)
            dscores = (probs * (dprobs - delta)).astype(BF16)
            dq = (unpaired(dot(dscores, k)) * scale).astype(BF16)
            for i in range(peers):
                dqs[i][s, :, cut] = dq[i * per_slot : (i + 1) * per_slot]
            dkv[s, :, cut] = (dot(dscores, q, TN) * scale).astype(BF16)
            dkv[s, :, after] = dot(probs.astype(BF16), da, TN).astype(BF16)


def keyval_back_kernel(media, dkv, w_keyval, gain, media_grad, dlat, sums):
    n, rows, width = media.shape
    grad = dot(dkv[...].reshape(-1, dkv.shape[2]), w_keyval[...], NT).reshape(n, -1, width)
    dlat[...] = grad[:, rows:].reshape(dlat.shape)
    grad = grad[:, :rows].reshape(n * rows, width)
    hat, inverse = stats(media[...].reshape(n * rows, width).astype(F32))
    media_grad[...] = pull(hat, inverse, grad, gain[0:1]).astype(BF16).reshape(media_grad.shape)

    @pl.when(pl.program_id(0) == 0)
    def _():
        sums[...] = jnp.zeros_like(sums)

    sums[0:1] += jnp.sum(grad * hat, axis=0, keepdims=True)
    sums[1:2] += jnp.sum(grad, axis=0, keepdims=True)


def latent_back_kernel(peers, *refs):
    dqs = refs[:peers]
    dlat, lat, dhidden, w_query, gain, sums_media, sums_ff, dq_low, latent_grad, sums = refs[peers:]
    dq = sum(ref[...].astype(F32) for ref in dqs).astype(BF16)
    dq_low[...] = dq
    grad = dlat[...] + dot(dq, w_query[...], NT)
    hat, inverse = stats(lat[...].astype(F32))
    latent_grad[...] = (dhidden[...] + pull(hat, inverse, grad, gain[1:2])).astype(BF16)
    sums[0:1] = sums_media[0:1]
    sums[1:2] = jnp.sum(grad * hat, axis=0, keepdims=True)
    sums[2:3] = sums_ff[0:1]
    sums[3:4] = sums_media[1:2]
    sums[4:5] = jnp.sum(grad, axis=0, keepdims=True)
    sums[5:6] = sums_ff[1:2]


def outer_kernel(count, *refs):
    lefts, rights, result = refs[:count], refs[count : 2 * count], refs[2 * count]
    left = jnp.concatenate([ref[...] for ref in lefts], axis=0)
    right = jnp.concatenate([ref[...] for ref in rights], axis=0)
    result[...] = dot(left, right, TN).astype(BF16)


def outer(lefts, rights, tile, name):
    count = len(lefts)
    rows, a = lefts[0].shape
    b = rights[0].shape[1]
    return call(
        functools.partial(outer_kernel, count),
        (a // tile,),
        [pl.BlockSpec((rows, tile), lambda g: (0, g))] * count + [whole((rows, b))] * count,
        [(pl.BlockSpec((tile, b), lambda g: (g, 0)), out((a, b), BF16))],
        flops=2 * count * rows * a * b,
        moved=count * rows * (a + b) * 2 + a * b * 2,
        name=name,
    )(*lefts, *rights)[0]


def on_device(
    media, latents, counts, gains, biases, w_query, w_keyval, w_out, w_up, w_down, out_grad
):
    slots, patch_rows, width = media.shape
    per_slot = latents.shape[1]
    inner = w_query.shape[1]
    ff = w_up.shape[1]
    n_img, peers = lax.axis_size("img"), lax.axis_size("patch")
    shards = n_img * peers
    scale = 1.0 / math.sqrt(inner // HEADS)
    rows = slots * per_slot
    keys = patch_rows + per_slot
    padded = -(-rows // LANES) * LANES
    gain_spec = whole(gains.shape)
    lat = latents.reshape(rows, width)

    lat_low, q_low, dy = call(
        functools.partial(latent_kernel, per_slot),
        (1,),
        [SMEM, whole((rows, width)), whole((rows, width)), gain_spec, gain_spec, whole(w_query.shape)],
        [
            (whole((rows, width)), out((rows, width), BF16)),
            (whole((rows, inner)), out((rows, inner), BF16)),
            (whole((rows, width)), out((rows, width), BF16)),
        ],
        flops=2 * rows * width * inner, moved=2 * width * inner + 8 * rows * width, name="latent",
    )(counts, lat, out_grad.reshape(rows, width), gains, biases, w_query)
    qs = gather(q_low, "patch")
    qs = [q.reshape(slots, per_slot, inner) for q in qs]

    group = slots // 2
    key_input, keyval = call(
        media_kernel,
        (slots // group,),
        [
            leading((group, patch_rows, width)), leading((group * per_slot, width)),
            gain_spec, gain_spec, whole(w_keyval.shape),
        ],
        [
            (leading((group, keys, width)), out((slots, keys, width), BF16)),
            (leading((group, keys, 2 * inner)), out((slots, keys, 2 * inner), BF16)),
        ],
        flops=4 * slots * keys * width * inner, moved=8 * slots * keys * width, name="media",
    )(media, lat_low, gains, biases, w_keyval)

    pair = 2
    row_block = leading((pair, per_slot, inner))
    kv_block = leading((pair, keys, 2 * inner))
    row_out = (row_block, out((slots, per_slot, inner), BF16))
    stat_out = (whole((HEADS, rows)), out((HEADS, rows), F32))
    attention = 4 * slots * keys * peers * per_slot * inner
    got = call(
        functools.partial(attend_kernel, peers, scale),
        (slots // pair,),
        [row_block] * peers + [kv_block],
        [row_out] * peers + [stat_out] * peers,
        scratch=[pltpu.VMEM((peers, padded, LANES), F32)],
        flops=attention, moved=4 * slots * keys * inner + 4 * peers * rows * inner, name="attend",
    )(*qs, keyval)
    parts, lses = got[:peers], got[peers:]
    parts = [part.reshape(rows, inner) for part in parts]
    parts = [parts[0]] + [swap(parts[j], "patch", j) for j in range(1, peers)]
    lses = [lses[0]] + [swap(lses[j], "patch", j) for j in range(1, peers)]

    attended, att_low, hidden, ff_low, lse = call(
        functools.partial(mix_kernel, peers),
        (1,),
        [whole((rows, inner))] * peers + [whole((HEADS, rows))] * peers
        + [whole((rows, width)), whole(w_out.shape), gain_spec, gain_spec],
        [
            (whole((rows, inner)), out((rows, inner), F32)),
            (whole((rows, inner)), out((rows, inner), BF16)),
            (whole((rows, width)), out((rows, width), F32)),
            (whole((rows, width)), out((rows, width), BF16)),
            stat_out,
        ],
        flops=2 * rows * width * inner, moved=2 * width * inner + 8 * rows * width, name="mix",
    )(*parts, *lses, lat, w_out, gains, biases)

    halves = 2
    blocks = ff // (peers * halves * LANES)
    chunk = ff // shards
    strided = chunk % LANES == 0

    def column(own, j, a, k):
        p, y = own[0] ^ j, own[1] ^ a
        if strided:
            return (((k // (chunk // LANES)) * halves + y) * peers + p) * (chunk // LANES) + k % (chunk // LANES)
        return (p * halves + y) * blocks + k

    places = [(a, k) for a in range(halves) for k in range(blocks)]
    ups = [pl.BlockSpec((width, LANES), lambda j, own, a=a, k=k: (0, column(own, j, a, k))) for a, k in places]
    downs = [pl.BlockSpec((LANES, width), lambda j, own, a=a, k=k: (column(own, j, a, k), 0)) for a, k in places]
    own = jnp.stack([lax.axis_index("patch"), lax.axis_index("img") % halves]).astype(jnp.int32)
    part = ff // (peers * halves)
    tall = pl.BlockSpec((1, halves, rows, part), lambda j, *_: (j, 0, 0, 0))
    act, dpre, result, dhidden, dhid_low, datt_low, stat, sums_ff = call(
        functools.partial(feed_kernel, per_slot, halves, blocks),
        (peers,),
        [SMEM, whole((rows, width)), whole((rows, width)), whole((rows, width)), whole((rows, inner)),
         whole((HEADS, rows)), whole(w_out.shape), gain_spec] + ups + downs,
        [
            (tall, out((peers, halves, rows, part), BF16)),
            (tall, out((peers, halves, rows, part), BF16)),
            (whole((rows, width)), out((rows, width), BF16)),
            (whole((rows, width)), out((rows, width), F32)),
            (whole((rows, width)), out((rows, width), BF16)),
            (whole((rows, inner)), out((rows, inner), BF16)),
            (whole((2 * HEADS, rows)), out((2 * HEADS, rows), F32)),
            (whole((2, width)), out((2, width), F32)),
        ],
        scratch=[pltpu.VMEM((rows, width), F32), pltpu.VMEM((rows, width), F32)],
        vmem=48, flops=8 * rows * width * ff, moved=4 * width * ff, prefetch=1, name="feed",
    )(own, counts, ff_low, dy, hidden, attended, lse, w_out, gains, *([w_up] * len(ups)), *([w_down] * len(downs)))

    das = [a.reshape(slots, per_slot, inner) for a in gather(datt_low, "patch")]
    sts = gather(stat, "patch")
    got = call(
        functools.partial(attend_back_kernel, peers, scale),
        (slots // pair,),
        [row_block] * (2 * peers) + [whole((2 * HEADS, rows))] * peers + [kv_block],
        [(kv_block, out(keyval.shape, BF16))] + [row_out] * peers,
        scratch=[pltpu.VMEM((peers, padded, LANES), F32)],
        flops=2.5 * attention, moved=8 * slots * keys * inner + 8 * peers * rows * inner, name="attend_back",
    )(*qs, *das, *sts, keyval)
    dkv, dqs = got[0], [a.reshape(rows, inner) for a in got[1:]]
    dqs = [dqs[0]] + [swap(dqs[j], "patch", j) for j in range(1, peers)]

    media_grad, dlat, sums_media = call(
        keyval_back_kernel,
        (slots // group,),
        [
            leading((group, patch_rows, width)), leading((group, keys, 2 * inner)),
            whole(w_keyval.shape), gain_spec,
        ],
        [
            (leading((group, patch_rows, width)), out(media.shape, BF16)),
            (leading((group * per_slot, width)), out((rows, width), F32)),
            (whole((2, width)), out((2, width), F32)),
        ],
        flops=4 * slots * keys * width * inner, moved=8 * slots * keys * width, name="keyval_back",
    )(media, dkv, w_keyval, gains)

    dq_low, latent_grad, sums = call(
        functools.partial(latent_back_kernel, peers),
        (1,),
        [whole((rows, inner))] * peers
        + [whole((rows, width))] * 3 + [whole(w_query.shape), gain_spec, whole((2, width)), whole((2, width))],
        [
            (whole((rows, inner)), out((rows, inner), BF16)),
            (whole((rows, width)), out((rows, width), BF16)),
            (whole((6, width)), out((6, width), F32)),
        ],
        flops=2 * rows * width * inner, moved=2 * width * inner + 12 * rows * width, name="latent_back",
    )(*dqs, dlat, lat, dhidden, w_query, gains, sums_media, sums_ff)

    near = [swap_rows for swap_rows in gather(ff_low, "patch")]
    ff_rows = near + [swap(r, "img", 1) for r in near]
    near = [swap_rows for swap_rows in gather(dy, "patch")]
    dy_rows = near + [swap(r, "img", 1) for r in near]

    def exchanged(values):
        got = [values[0]] + [swap(values[j], "patch", j) for j in range(1, peers)]
        return [g[0] for g in got] + [swap(g[1], "img", 1) for g in got]

    rest = [("img", 1 << k) for k in range(1, log2(n_img))]
    rest_digits = [(name, 2) for name in reversed(rest)]
    down_part = outer(dy_rows, exchanged(act), width // 4, "down_grad")
    down_sum = scatter_sum([Piece(down_part, rest_digits)], rest)[0]
    up_part = outer(exchanged(dpre), ff_rows, part // 2, "up_grad")
    up_sum = scatter_sum([Piece(up_part, rest_digits)], rest)[0]
    if not strided:
        have = lambda i, p: (p * halves + i % 2) * (n_img // 2) + i // 2
        up_sum = lax.ppermute(
            up_sum, ("img", "patch"), [(i * peers + p, have(i, p)) for i in range(n_img) for p in range(peers)]
        )
    up_grad = up_sum.astype(F32).T

    piece = down_sum.reshape(2, peers, -1, part)
    odd = lax.axis_index("img") % 2 == 1
    sent = jnp.where(odd, piece[0], piece[1])
    kept = jnp.where(odd, piece[1], piece[0])
    other = swap(sent, "img", 1)
    both = jnp.stack([jnp.where(odd, other, kept), jnp.where(odd, kept, other)], axis=1)
    both = lax.all_to_all(both, "patch", 0, 0, tiled=True)
    if strided:
        both = both.reshape(peers, 2, -1, n_img // 2, chunk).transpose(3, 1, 0, 4, 2)
    else:
        both = both.transpose(0, 1, 3, 2)
    down_grad = both.reshape(ff, width // shards).astype(F32)

    every = digits_of("img") + digits_of("patch")
    kv_t = outer([dkv.reshape(-1, 2 * inner)], [key_input.reshape(-1, width)], 2 * inner // 4, "keyval_grad")
    q_t = outer([dq_low], [lat_low], inner // 2, "query_grad")
    out_t = outer([dhid_low], [att_low], width // 4, "out_grad")
    small = sums.reshape(6, shards, width // shards).transpose(1, 0, 2)
    order = [(("patch", 1 << k) if which else ("img", 1 << k)) for k in range(log2(max(n_img, peers)))
             for which in (1, 0) if (1 << k) < (peers if which else n_img)]
    kv_sum, q_sum, out_sum, small = scatter_sum([Piece(a, every) for a in (kv_t, q_t, out_t, small)], order)
    return (
        result.reshape(slots, per_slot, width),
        media_grad,
        latent_grad.reshape(slots, per_slot, width),
        q_sum.astype(F32).T,
        kv_sum.astype(F32).T,
        out_sum.astype(F32).T,
        up_grad,
        down_grad,
        small[:3],
        small[3:],
    )


def solution(mesh):
    rows = P("img", "patch", None)
    shard = P(None, ("img", "patch"))
    return jax.shard_map(
        on_device,
        mesh=mesh,
        in_specs=(rows, rows, P("img"), P(), P(), P(), P(), P(), P(), P(), rows),
        out_specs=(rows, rows, rows) + (shard,) * 7,
        check_vma=False,
    )
```

profile of v0, /device:TPU:0, one launch (start us, length us, event | category | flops | bytes accessed | tf_op | source)
XLA Modules:
  0.0 299.7 jit_solution(7696276912359255382)
XLA Ops:
  7.1 3.0 %collective-permute-start.1 = (bf16[160,512]{1,0:T(8,128)(2,1)S(1)}, bf16[160,512]{1,0:T(8,128)(2,1)S(1)}, u32[]{:S(2)}, u32[]{:S(2)}) collective-permute-start(bf16[160,512]{1,0:T(8,128)(2,1)S(1)} %get-tuple-element.47), channel_id=1, source_target_pairs={{0,2},{1,3},{2,0},{3,1},{4,6},{5,7},{6,4},{7,5},{8,10},{9,11},{10,... | collective-permute-start | bytes 491528 | tf_op jit(solution)/shard_map/ppermute | solution.py:22
  10.1 4.2 %collective-permute-done.1 = bf16[160,512]{1,0:T(8,128)(2,1)S(1)} collective-permute-done((bf16[160,512]{1,0:T(8,128)(2,1)S(1)}, bf16[160,512]{1,0:T(8,128)(2,1)S(1)}, u32[]{:S(2)}, u32[]{:S(2)}) %collective-permute-start.1) | collective-permute-done | bytes 163872 | tf_op jit(solution)/shard_map/ppermute | solution.py:22
  16.0 2.7 media.3
  19.5 11.1 %attend.1 = (bf16[10,16,512]{2,1,0:T(8,128)(2,1)S(1)}, bf16[10,16,512]{2,1,0:T(8,128)(2,1)}, bf16[10,16,512]{2,1,0:T(8,128)(2,1)}, bf16[10,16,512]{2,1,0:T(8,128...) custom-call(bf16[10,16,512]{2,1,0:T(8,128)(2,1)S(1)} %bitcast.477, ...), custom_call_target="tpu_custom_call" | custom-call | flops 104857600 | bytes 2949120 | tf_op jit(solution)/shard_map/attend/pallas_call | solution.py:449
  36.4 5.4 %collective-permute-done.7.refs_6_ = f32[8,160]{1,0:T(8,128)S(1)} collective-permute-done((f32[8,160]{1,0:T(8,128)S(1)}, f32[8,160]{1,0:T(8,128)S(1)}, u32[]{:S(2)}, u32[]{:S(2)}) %collective-permute-start.7) | collective-permute-done | bytes 5152 | tf_op jit(solution)/shard_map/ppermute | solution.py:22
  44.5 3.3 %mix.1 = (f32[160,512]{1,0:T(8,128)S(1)}, bf16[160,512]{1,0:T(8,128)(2,1)S(1)}, f32[160,1024]{1,0:T(8,128)S(1)}, bf16[160,1024]{1,0:T(8,128)(2,1)}, f32[8,160]{1,0:T(8,128)S(1)}) custom-call(bf16[160,512]{1,0:T(8,128)(2,1)S(1)} %bitcast.486, bf16[160,512]{1,0:T(8,128)(2,1)} %collective-permute-done.3.refs_1_, ...), custom_call_target="tpu_custom_call" | custom-call | flops 167772160 | bytes 2359296 | tf_op jit(solution)/shard_map/mix/pallas_call | solution.py:462
  47.9 15.5 %feed.1 = (bf16[4,2,160,512]{3,2,1,0:T(8,128)(2,1)S(1)}, bf16[4,2,160,512]{3,2,1,0:T(8,128)(2,1)}, bf16[160,1024]{1,0:T(8,128)(2,1)}, f32[160,1024]{1,0:T(8,128)...) custom-call(s32[2]{0:T(128)S(1)} %pad_add_fusion.own, ...), custom_call_target="tpu_custom_call" | custom-call | flops 5368709120 | bytes 16777216 | tf_op jit(solution)/shard_map/feed/pallas_call | solution.py:494
  74.1 3.5 %collective-permute-done.34 = bf16[2,160,512]{2,1,0:T(8,128)(2,1)S(1)} collective-permute-done((bf16[2,160,512]{2,1,0:T(8,128)(2,1)S(1)}, bf16[2,160,512]{2,1,0:T(8,128)(2,1)S(1)}, u32[]{:S(2)}, u32[]{:S(2)}) %collective-permute-start.34) | collective-permute-done | bytes 327712 | tf_op jit(solution)/shard_map/ppermute | solution.py:22
  80.7 7.5 %collective-permute-done.10 = bf16[160,512]{1,0:T(8,128)(2,1)S(1)} collective-permute-done((bf16[160,512]{1,0:T(8,128)(2,1)S(1)}, bf16[160,512]{1,0:T(8,128)(2,1)S(1)}, u32[]{:S(2)}, u32[]{:S(2)}) %collective-permute-start.10) | collective-permute-done | bytes 163872 | tf_op jit(solution)/shard_map/ppermute | solution.py:22
  91.5 9.7 %attend_back.1 = (bf16[10,80,1024]{2,1,0:T(8,128)(2,1)S(1)}, bf16[10,16,512]{2,1,0:T(8,128)(2,1)S(1)}, bf16[10,16,512]{2,1,0:T(8,128)(2,1)S(1)}, bf16[10,16,512]...) custom-call(bf16[10,16,512]{2,1,0:T(8,128)(2,1)S(1)} %bitcast.478, bf16[10,16,512]{2,1,0:T(8,128)(2,1)S(1)} %bitcast.482, ...), custom_call_target="tpu_custom_call" | custom-call | flops 262144000 | bytes 5898240 | tf_op jit(solution)/shard_map/attend_back/pallas_call | solution.py:515
  103.5 3.3 %keyval_grad.1 = bf16[1024,1024]{1,0:T(8,128)(2,1)S(1)} custom-call(bf16[800,1024]{1,0:T(8,128)(2,1)S(1)} %bitcast.492, bf16[800,1024]{1,0:T(8,128)(2,1)S(1)} %bitcast.496), custom_call_target="tpu_custom_call" | custom-call | flops 1677721600 | bytes 5373952 | tf_op jit(solution)/shard_map/keyval_grad/pallas_call | solution.py:387
  111.1 4.2 %keyval_back.1 = (bf16[10,64,1024]{2,1,0:T(8,128)(2,1)}, f32[160,1024]{1,0:T(8,128)S(1)}, f32[2,1024]{1,0:T(2,128)S(1)}) custom-call(bf16[10,64,1024]{2,1,0:T(8,128)(2,1)S(1)} %copy-done.41, bf16[10,80,1024]{2,1,0:T(8,128)(2,1)S(1)} %get-tuple-element.66.dkv, bf16[1024,1024]{1,0:T(8,128)(2,1)S(1)} %copy-done.39, f32[3,1024]{1,0:T(4,128)S(1)} %copy-done.29), custom_call_target="tpu_custom_call" | custom-call | flops 1677721600 | bytes 6553600 | tf_op jit(solution)/shard_map/keyval_back/pallas_call | solution.py:526
  126.9 20.5 %collective-permute-done.67 = f32[8,6,32]{2,1,0:T(8,128)S(1)} collective-permute-done((f32[8,6,32]{2,1,0:T(8,128)S(1)}, f32[8,6,32]{2,1,0:T(8,128)S(1)}, u32[]{:S(2)}, u32[]{:S(2)}) %collective-permute-start.67) | collective-permute-done | bytes 6176 | tf_op jit(solution)/shard_map/ppermute | solution.py:22
  152.3 2.2 collective-permute-done.59.refs_12_
  154.5 3.5 %collective-permute-done.60.refs_13_ = bf16[160,512]{1,0:T(8,128)(2,1)S(1)} collective-permute-done((bf16[160,512]{1,0:T(8,128)(2,1)S(1)}, bf16[160,512]{1,0:T(8,128)(2,1)S(1)}, u32[]{:S(2)}, u32[]{:S(2)}) %collective-permute-start.60) | collective-permute-done | bytes 163872 | tf_op jit(solution)/shard_map/ppermute | solution.py:22
  158.2 3.3 %collective-permute-done.61.refs_14_ = bf16[160,512]{1,0:T(8,128)(2,1)S(1)} collective-permute-done((bf16[160,512]{1,0:T(8,128)(2,1)}, bf16[160,512]{1,0:T(8,128)(2,1)S(1)}, u32[]{:S(2)}, u32[]{:S(2)}) %collective-permute-start.61) | collective-permute-done | bytes 163872 | tf_op jit(solution)/shard_map/ppermute | solution.py:22
  169.9 3.9 %down_grad.1 = bf16[1024,512]{1,0:T(8,128)(2,1)S(1)} custom-call(bf16[160,1024]{1,0:T(8,128)(2,1)S(1)} %get-tuple-element.59.refs_1_.refs_0_, bf16[160,1024]{1,0:T(8,128)(2,1)} %collective-permute-done.49.refs_1_, bf16[160,1024]{1,0:T(8,128)(2,1)} %collective-permute-done.50.refs_2_, bf16[160,1024]{1,0:T(8,128)(2,1)} %collective-permute-done.51.refs_3_, ...), custom_call_target="tpu_custom_call" | custom-call | flops 1342177280 | bytes 4980736 | tf_op jit(solution)/shard_map/down_grad/pallas_call | solution.py:387
  178.3 2.6 collective-permute-start.70
  184.0 6.4 %collective-permute-done.29 = bf16[8,32,512]{2,1,0:T(8,128)(2,1)S(1)} collective-permute-done((bf16[8,32,512]{2,1,0:T(8,128)(2,1)S(1)}, bf16[8,32,512]{2,1,0:T(8,128)(2,1)S(1)}, u32[]{:S(2)}, u32[]{:S(2)}) %collective-permute-start.29) | collective-permute-done | bytes 262176 | tf_op jit(solution)/shard_map/ppermute | solution.py:22
  200.9 22.4 %collective-permute-done.38.refs_6_ = bf16[160,512]{1,0:T(8,128)(2,1)S(1)} collective-permute-done((bf16[160,512]{1,0:T(8,128)(2,1)S(1)}, bf16[160,512]{1,0:T(8,128)(2,1)S(1)}, u32[]{:S(2)}, u32[]{:S(2)}) %collective-permute-start.38) | collective-permute-done | bytes 163872 | tf_op jit(solution)/shard_map/ppermute | solution.py:22
  227.1 2.9 up_grad.1
  234.7 6.8 %collective-permute-done.31 = bf16[2,32,512]{2,1,0:T(8,128)(2,1)S(1)} collective-permute-done((bf16[2,32,512]{2,1,0:T(8,128)(2,1)S(1)}, bf16[2,32,512]{2,1,0:T(8,128)(2,1)S(1)}, u32[]{:S(2)}, u32[]{:S(2)}) %collective-permute-start.31) | collective-permute-done | bytes 65568 | tf_op jit(solution)/shard_map/ppermute | solution.py:22
  241.5 2.7 collective-permute-start.32
  248.5 3.7 %collective-permute-done.32 = bf16[1,32,512]{2,1,0:T(8,128)(2,1)S(1)} collective-permute-done((bf16[1,32,512]{2,1,0:T(8,128)(2,1)S(1)}, bf16[1,32,512]{2,1,0:T(8,128)(2,1)S(1)}, u32[]{:S(2)}, u32[]{:S(2)}) %collective-permute-start.32) | collective-permute-done | bytes 32800 | tf_op jit(solution)/shard_map/ppermute | solution.py:22
  253.5 8.8 %collective-permute-done.64 = bf16[1,256,512]{2,1,0:T(8,128)(2,1)S(1)} collective-permute-done((bf16[1,256,512]{2,1,0:T(8,128)(2,1)S(1)}, bf16[1,256,512]{2,1,0:T(8,128)(2,1)S(1)}, u32[]{:S(2)}, u32[]{:S(2)}) %collective-permute-start.64) | collective-permute-done | bytes 262176 | tf_op jit(solution)/shard_map/ppermute | solution.py:22
  266.6 2.2 collective-permute-done.65
  269.6 3.5 %all-to-all-start = ((bf16[4,2,32,512]{3,2,1,0:T(8,128)(2,1)}), bf16[4,2,32,512]{3,2,1,0:T(8,128)(2,1)S(1)}, u32[]{:S(2)}, u32[]{:S(2)}) async-start(bf16[4,2,32,512]{3,2,1,0:T(8,128)(2,1)} %pad_maximum_fusion), calls=%async_computation | async-start | bytes 524288 | tf_op jit(solution)/shard_map/all_to_all | solution.py:582
  273.3 2.4 collective-permute-done.24
  277.8 2.5 collective-permute-start.48
  280.4 4.3 %collective-permute-done.25 = bf16[4,32,1024]{2,1,0:T(8,128)(2,1)S(1)} collective-permute-done((bf16[4,32,1024]{2,1,0:T(8,128)(2,1)S(1)}, bf16[4,32,1024]{2,1,0:T(8,128)(2,1)S(1)}, u32[]{:S(2)}, u32[]{:S(2)}) %collective-permute-start.25) | collective-permute-done | bytes 262176 | tf_op jit(solution)/shard_map/ppermute | solution.py:22
  287.1 6.5 %collective-permute-done.26 = bf16[2,32,1024]{2,1,0:T(8,128)(2,1)S(1)} collective-permute-done((bf16[2,32,1024]{2,1,0:T(8,128)(2,1)S(1)}, bf16[2,32,1024]{2,1,0:T(8,128)(2,1)S(1)}, u32[]{:S(2)}, u32[]{:S(2)}) %collective-permute-start.26) | collective-permute-done | bytes 131104 | tf_op jit(solution)/shard_map/ppermute | solution.py:22
  294.7 4.3 %collective-permute-done.27 = bf16[1,32,1024]{2,1,0:T(8,128)(2,1)S(1)} collective-permute-done((bf16[1,32,1024]{2,1,0:T(8,128)(2,1)S(1)}, bf16[1,32,1024]{2,1,0:T(8,128)(2,1)S(1)}, u32[]{:S(2)}, u32[]{:S(2)}) %collective-permute-start.27) | collective-permute-done | bytes 65568 | tf_op jit(solution)/shard_map/ppermute | solution.py:22
  (305 shorter events, 109.3 us)
Async XLA Ops:
  41.8 30.6 %collective-permute-start.50 = (bf16[160,1024]{1,0:T(8,128)(2,1)S(1)}, bf16[160,1024]{1,0:T(8,128)(2,1)}, u32[]{:S(2)}, u32[]{:S(2)}) collective-permute-start(bf16[160,1024]{1,0:T(8,128)(2,1)S(1)} %get-tuple-element.59.refs_1_.refs_0_), channel_id=1, source_target_pairs={{0,2},{1,3},{2,0},{3,1},{4,6},{5,7},{6,4},{7,5},{8,10},{9,11},{10,... | collective-permute-start | bytes 983048 | tf_op jit(solution)/shard_map/ppermute | solution.py:22
  63.5 15.5 %collective-permute-start.13 = (f32[16,160]{1,0:T(8,128)S(1)}, f32[16,160]{1,0:T(8,128)S(1)}, u32[]{:S(2)}, u32[]{:S(2)}) collective-permute-start(f32[16,160]{1,0:T(8,128)S(1)} %get-tuple-element.65.refs_8_), channel_id=1, source_target_pairs={{0,2},{1,3},{2,0},{3,1},{4,6},{5,7},{6,4},{7,5},{8,10},{9,11},{10,... | collective-permute-start | bytes 30728 | tf_op jit(solution)/shard_map/ppermute | solution.py:22
  71.6 16.5 %collective-permute-start.35 = (bf16[2,160,512]{2,1,0:T(8,128)(2,1)S(1)}, bf16[2,160,512]{2,1,0:T(8,128)(2,1)S(1)}, u32[]{:S(2)}, u32[]{:S(2)}) collective-permute-start(bf16[2,160,512]{2,1,0:T(8,128)(2,1)S(1)} %get-tuple-element.91), channel_id=1, source_target_pairs={{0,3},{1,2},{2,1},{3,0},{4,7},{5,6},{6,5},{7,4},{8,11},{9,10},{10,... | collective-permute-start | bytes 983048 | tf_op jit(solution)/shard_map/ppermute | solution.py:22
  72.4 15.8 %collective-permute-start.10 = (bf16[160,512]{1,0:T(8,128)(2,1)S(1)}, bf16[160,512]{1,0:T(8,128)(2,1)S(1)}, u32[]{:S(2)}, u32[]{:S(2)}) collective-permute-start(bf16[160,512]{1,0:T(8,128)(2,1)S(1)} %get-tuple-element.64), channel_id=1, source_target_pairs={{0,2},{1,3},{2,0},{3,1},{4,6},{5,7},{6,4},{7,5},{8,10},{9,11},{10,... | collective-permute-start | bytes 491528 | tf_op jit(solution)/shard_map/ppermute | solution.py:22
  77.6 23.6 %collective-permute-start.56 = (bf16[2,160,512]{2,1,0:T(8,128)(2,1)S(1)}, bf16[2,160,512]{2,1,0:T(8,128)(2,1)S(1)}, u32[]{:S(2)}, u32[]{:S(2)}) collective-permute-start(bf16[2,160,512]{2,1,0:T(8,128)(2,1)S(1)} %get-tuple-element.88), channel_id=1, source_target_pairs={{0,1},{1,0},{2,3},{3,2},{4,5},{5,4},{6,7},{7,6},{8,9},{9,8},{10,11... | collective-permute-start | bytes 983048 | tf_op jit(solution)/shard_map/ppermute | solution.py:22
  78.9 23.5 %collective-permute-start.57 = (bf16[2,160,512]{2,1,0:T(8,128)(2,1)S(1)}, bf16[2,160,512]{2,1,0:T(8,128)(2,1)S(1)}, u32[]{:S(2)}, u32[]{:S(2)}) collective-permute-start(bf16[2,160,512]{2,1,0:T(8,128)(2,1)S(1)} %get-tuple-element.87), channel_id=1, source_target_pairs={{0,2},{1,3},{2,0},{3,1},{4,6},{5,7},{6,4},{7,5},{8,10},{9,11},{10,... | collective-permute-start | bytes 983048 | tf_op jit(solution)/shard_map/ppermute | solution.py:22
  89.5 25.9 %collective-permute-start.49 = (bf16[160,1024]{1,0:T(8,128)(2,1)S(1)}, bf16[160,1024]{1,0:T(8,128)(2,1)}, u32[]{:S(2)}, u32[]{:S(2)}) collective-permute-start(bf16[160,1024]{1,0:T(8,128)(2,1)S(1)} %get-tuple-element.59.refs_1_.refs_0_), channel_id=1, source_target_pairs={{0,1},{1,0},{2,3},{3,2},{4,5},{5,4},{6,7},{7,6},{8,9},{9,8},{10,11... | collective-permute-start | bytes 983048 | tf_op jit(solution)/shard_map/ppermute | solution.py:22
  89.5 27.3 %collective-permute-start.51 = (bf16[160,1024]{1,0:T(8,128)(2,1)}, bf16[160,1024]{1,0:T(8,128)(2,1)}, u32[]{:S(2)}, u32[]{:S(2)}) collective-permute-start(bf16[160,1024]{1,0:T(8,128)(2,1)} %collective-permute-done.50.refs_2_), channel_id=1, source_target_pairs={{0,1},{1,0},{2,3},{3,2},{4,5},{5,4},{6,7},{7,6},{8,9},{9,8},{10,11... | collective-permute-start | bytes 983048 | tf_op jit(solution)/shard_map/ppermute | solution.py:22
  90.0 19.2 %collective-permute-start.58 = (bf16[2,160,512]{2,1,0:T(8,128)(2,1)S(1)}, bf16[2,160,512]{2,1,0:T(8,128)(2,1)S(1)}, u32[]{:S(2)}, u32[]{:S(2)}) collective-permute-start(bf16[2,160,512]{2,1,0:T(8,128)(2,1)S(1)} %get-tuple-element.86), channel_id=1, source_target_pairs={{0,3},{1,2},{2,1},{3,0},{4,7},{5,6},{6,5},{7,4},{8,11},{9,10},{10,... | collective-permute-start | bytes 983048 | tf_op jit(solution)/shard_map/ppermute | solution.py:22
  101.2 16.2 %collective-permute-start.15 = (bf16[160,512]{1,0:T(8,128)(2,1)S(1)}, bf16[160,512]{1,0:T(8,128)(2,1)S(1)}, u32[]{:S(2)}, u32[]{:S(2)}) collective-permute-start(bf16[160,512]{1,0:T(8,128)(2,1)S(1)} %bitcast.495), channel_id=1, source_target_pairs={{0,1},{1,0},{2,3},{3,2},{4,5},{5,4},{6,7},{7,6},{8,9},{9,8},{10,11... | collective-permute-start | bytes 491528 | tf_op jit(solution)/shard_map/ppermute | solution.py:22
  102.4 16.5 %collective-permute-start.16 = (bf16[160,512]{1,0:T(8,128)(2,1)S(1)}, bf16[160,512]{1,0:T(8,128)(2,1)S(1)}, u32[]{:S(2)}, u32[]{:S(2)}) collective-permute-start(bf16[160,512]{1,0:T(8,128)(2,1)S(1)} %bitcast.494), channel_id=1, source_target_pairs={{0,2},{1,3},{2,0},{3,1},{4,6},{5,7},{6,4},{7,5},{8,10},{9,11},{10,... | collective-permute-start | bytes 491528 | tf_op jit(solution)/shard_map/ppermute | solution.py:22
  115.3 33.6 %collective-permute-start.52 = (bf16[160,1024]{1,0:T(8,128)(2,1)S(1)}, bf16[160,1024]{1,0:T(8,128)(2,1)S(1)}, u32[]{:S(2)}, u32[]{:S(2)}) collective-permute-start(bf16[160,1024]{1,0:T(8,128)(2,1)S(1)} %get-tuple-element.59.refs_1_.refs_0_), channel_id=1, source_target_pairs={{0,4},{4,0},{8,12},{12,8},{16,20},{20,16},{24,28},{28,24},{1,5},{5... | collective-permute-start | bytes 983048 | tf_op jit(solution)/shard_map/ppermute | solution.py:22
  116.9 34.9 %collective-permute-start.54 = (bf16[160,1024]{1,0:T(8,128)(2,1)}, bf16[160,1024]{1,0:T(8,128)(2,1)}, u32[]{:S(2)}, u32[]{:S(2)}) collective-permute-start(bf16[160,1024]{1,0:T(8,128)(2,1)} %collective-permute-done.50.refs_2_), channel_id=1, source_target_pairs={{0,4},{4,0},{8,12},{12,8},{16,20},{20,16},{24,28},{28,24},{1,5},{5... | collective-permute-start | bytes 983048 | tf_op jit(solution)/shard_map/ppermute | solution.py:22
  117.4 32.8 %collective-permute-start.53 = (bf16[160,1024]{1,0:T(8,128)(2,1)}, bf16[160,1024]{1,0:T(8,128)(2,1)}, u32[]{:S(2)}, u32[]{:S(2)}) collective-permute-start(bf16[160,1024]{1,0:T(8,128)(2,1)} %collective-permute-done.49.refs_1_), channel_id=1, source_target_pairs={{0,4},{4,0},{8,12},{12,8},{16,20},{20,16},{24,28},{28,24},{1,5},{5... | collective-permute-start | bytes 983048 | tf_op jit(solution)/shard_map/ppermute | solution.py:22
  118.9 46.1 %collective-permute-start.55 = (bf16[160,1024]{1,0:T(8,128)(2,1)}, bf16[160,1024]{1,0:T(8,128)(2,1)}, u32[]{:S(2)}, u32[]{:S(2)}) collective-permute-start(bf16[160,1024]{1,0:T(8,128)(2,1)} %collective-permute-done.51.refs_3_), channel_id=1, source_target_pairs={{0,4},{4,0},{8,12},{12,8},{16,20},{20,16},{24,28},{28,24},{1,5},{5... | collective-permute-start | bytes 983048 | tf_op jit(solution)/shard_map/ppermute | solution.py:22
  124.5 22.9 %collective-permute-start.67 = (f32[8,6,32]{2,1,0:T(8,128)S(1)}, f32[8,6,32]{2,1,0:T(8,128)S(1)}, u32[]{:S(2)}, u32[]{:S(2)}) collective-permute-start(f32[8,6,32]{2,1,0:T(8,128)S(1)} %select_n.722), channel_id=1, source_target_pairs={{0,4},{4,0},{8,12},{12,8},{16,20},{20,16},{24,28},{28,24},{1,5},{5... | collective-permute-start | bytes 18440 | tf_op jit(solution)/shard_map/ppermute | solution.py:22
  154.5 39.3 %collective-permute-start.40 = (bf16[160,1024]{1,0:T(8,128)(2,1)}, bf16[160,1024]{1,0:T(8,128)(2,1)S(1)}, u32[]{:S(2)}, u32[]{:S(2)}) collective-permute-start(bf16[160,1024]{1,0:T(8,128)(2,1)} %get-tuple-element.58.refs_0_.refs_8_), channel_id=1, source_target_pairs={{0,1},{1,0},{2,3},{3,2},{4,5},{5,4},{6,7},{7,6},{8,9},{9,8},{10,11... | collective-permute-start | bytes 983048 | tf_op jit(solution)/shard_map/ppermute | solution.py:22
  158.0 18.7 %collective-permute-start.41 = (bf16[160,1024]{1,0:T(8,128)(2,1)}, bf16[160,1024]{1,0:T(8,128)(2,1)S(1)}, u32[]{:S(2)}, u32[]{:S(2)}) collective-permute-start(bf16[160,1024]{1,0:T(8,128)(2,1)} %get-tuple-element.58.refs_0_.refs_8_), channel_id=1, source_target_pairs={{0,2},{1,3},{2,0},{3,1},{4,6},{5,7},{6,4},{7,5},{8,10},{9,11},{10,... | collective-permute-start | bytes 983048 | tf_op jit(solution)/shard_map/ppermute | solution.py:22
  161.5 35.2 %collective-permute-start.43 = (bf16[160,1024]{1,0:T(8,128)(2,1)}, bf16[160,1024]{1,0:T(8,128)(2,1)S(1)}, u32[]{:S(2)}, u32[]{:S(2)}) collective-permute-start(bf16[160,1024]{1,0:T(8,128)(2,1)} %get-tuple-element.58.refs_0_.refs_8_), channel_id=1, source_target_pairs={{0,4},{4,0},{8,12},{12,8},{16,20},{20,16},{24,28},{28,24},{1,5},{5... | collective-permute-start | bytes 983048 | tf_op jit(solution)/shard_map/ppermute | solution.py:22
  176.7 15.9 %collective-permute-start.36 = (bf16[160,512]{1,0:T(8,128)(2,1)S(1)}, bf16[160,512]{1,0:T(8,128)(2,1)S(1)}, u32[]{:S(2)}, u32[]{:S(2)}) collective-permute-start(bf16[160,512]{1,0:T(8,128)(2,1)S(1)} %copy-done.47), channel_id=1, source_target_pairs={{0,4},{4,0},{8,12},{12,8},{16,20},{20,16},{24,28},{28,24},{1,5},{5... | collective-permute-start | bytes 491528 | tf_op jit(solution)/shard_map/ppermute | solution.py:22
  178.2 16.4 %collective-permute-start.42 = (bf16[160,1024]{1,0:T(8,128)(2,1)S(1)}, bf16[160,1024]{1,0:T(8,128)(2,1)S(1)}, u32[]{:S(2)}, u32[]{:S(2)}) collective-permute-start(bf16[160,1024]{1,0:T(8,128)(2,1)S(1)} %collective-permute-done.41.refs_10_), channel_id=1, source_target_pairs={{0,1},{1,0},{2,3},{3,2},{4,5},{5,4},{6,7},{7,6},{8,9},{9,8},{10,11... | collective-permute-start | bytes 983048 | tf_op jit(solution)/shard_map/ppermute | solution.py:22
  193.8 32.5 %collective-permute-start.45 = (bf16[160,1024]{1,0:T(8,128)(2,1)S(1)}, bf16[160,1024]{1,0:T(8,128)(2,1)S(1)}, u32[]{:S(2)}, u32[]{:S(2)}) collective-permute-start(bf16[160,1024]{1,0:T(8,128)(2,1)S(1)} %collective-permute-done.41.refs_10_), channel_id=1, source_target_pairs={{0,4},{4,0},{8,12},{12,8},{16,20},{20,16},{24,28},{28,24},{1,5},{5... | collective-permute-start | bytes 983048 | tf_op jit(solution)/shard_map/ppermute | solution.py:22
  194.7 30.4 %collective-permute-start.44 = (bf16[160,1024]{1,0:T(8,128)(2,1)S(1)}, bf16[160,1024]{1,0:T(8,128)(2,1)S(1)}, u32[]{:S(2)}, u32[]{:S(2)}) collective-permute-start(bf16[160,1024]{1,0:T(8,128)(2,1)S(1)} %collective-permute-done.40.refs_9_), channel_id=1, source_target_pairs={{0,4},{4,0},{8,12},{12,8},{16,20},{20,16},{24,28},{28,24},{1,5},{5... | collective-permute-start | bytes 983048 | tf_op jit(solution)/shard_map/ppermute | solution.py:22
  195.8 31.2 %collective-permute-start.46 = (bf16[160,1024]{1,0:T(8,128)(2,1)S(1)}, bf16[160,1024]{1,0:T(8,128)(2,1)S(1)}, u32[]{:S(2)}, u32[]{:S(2)}) collective-permute-start(bf16[160,1024]{1,0:T(8,128)(2,1)S(1)} %collective-permute-done.42.refs_11_), channel_id=1, source_target_pairs={{0,4},{4,0},{8,12},{12,8},{16,20},{20,16},{24,28},{28,24},{1,5},{5... | collective-permute-start | bytes 983048 | tf_op jit(solution)/shard_map/ppermute | solution.py:22
  196.8 26.5 %collective-permute-start.38 = (bf16[160,512]{1,0:T(8,128)(2,1)S(1)}, bf16[160,512]{1,0:T(8,128)(2,1)S(1)}, u32[]{:S(2)}, u32[]{:S(2)}) collective-permute-start(bf16[160,512]{1,0:T(8,128)(2,1)S(1)} %copy-done.48), channel_id=1, source_target_pairs={{0,4},{4,0},{8,12},{12,8},{16,20},{20,16},{24,28},{28,24},{1,5},{5... | collective-permute-start | bytes 491528 | tf_op jit(solution)/shard_map/ppermute | solution.py:22
  199.7 25.3 %collective-permute-start.39 = (bf16[160,512]{1,0:T(8,128)(2,1)S(1)}, bf16[160,512]{1,0:T(8,128)(2,1)S(1)}, u32[]{:S(2)}, u32[]{:S(2)}) collective-permute-start(bf16[160,512]{1,0:T(8,128)(2,1)S(1)} %copy-done.49), channel_id=1, source_target_pairs={{0,4},{4,0},{8,12},{12,8},{16,20},{20,16},{24,28},{28,24},{1,5},{5... | collective-permute-start | bytes 491528 | tf_op jit(solution)/shard_map/ppermute | solution.py:22
  223.3 40.0 %collective-permute-start.23 = (bf16[16,32,1024]{2,1,0:T(8,128)(2,1)}, bf16[16,32,1024]{2,1,0:T(8,128)(2,1)}, u32[]{:S(2)}, u32[]{:S(2)}) collective-permute-start(bf16[16,32,1024]{2,1,0:T(8,128)(2,1)} %fusion.1), channel_id=1, source_target_pairs={{0,1},{1,0},{2,3},{3,2},{4,5},{5,4},{6,7},{7,6},{8,9},{9,8},{10,11... | collective-permute-start | bytes 3145736 | tf_op jit(solution)/shard_map/ppermute | solution.py:22
  225.0 19.1 %collective-permute-start.18 = (bf16[16,16,1024]{2,1,0:T(8,128)(2,1)}, bf16[16,16,1024]{2,1,0:T(8,128)(2,1)}, u32[]{:S(2)}, u32[]{:S(2)}) collective-permute-start(bf16[16,16,1024]{2,1,0:T(8,128)(2,1)} %fusion.8), channel_id=1, source_target_pairs={{0,1},{1,0},{2,3},{3,2},{4,5},{5,4},{6,7},{7,6},{8,9},{9,8},{10,11... | collective-permute-start | bytes 1572872 | tf_op jit(solution)/shard_map/ppermute | solution.py:22
  225.0 21.7 %collective-permute-start.63 = (bf16[2,256,512]{2,1,0:T(8,128)(2,1)}, bf16[2,256,512]{2,1,0:T(8,128)(2,1)}, u32[]{:S(2)}, u32[]{:S(2)}) collective-permute-start(bf16[2,256,512]{2,1,0:T(8,128)(2,1)} %fusion.10), channel_id=1, source_target_pairs={{0,8},{4,12},{8,0},{12,4},{16,24},{20,28},{24,16},{28,20},{1,9},{5... | collective-permute-start | bytes 1572872 | tf_op jit(solution)/shard_map/ppermute | solution.py:22
  233.4 43.1 %collective-permute-start.47 = (bf16[2,128,1024]{1,2,0:T(8,128)(2,1)}, bf16[2,128,1024]{1,2,0:T(8,128)(2,1)}, u32[]{:S(2)}, u32[]{:S(2)}) collective-permute-start(bf16[2,128,1024]{1,2,0:T(8,128)(2,1)} %select_bitcast_fusion), channel_id=1, source_target_pairs={{0,8},{4,12},{8,0},{12,4},{16,24},{20,28},{24,16},{28,20},{1,9},{5... | collective-permute-start | bytes 1572872 | tf_op jit(solution)/shard_map/ppermute | solution.py:22
  269.6 16.0 %all-to-all-start = ((bf16[4,2,32,512]{3,2,1,0:T(8,128)(2,1)}), bf16[4,2,32,512]{3,2,1,0:T(8,128)(2,1)S(1)}, u32[]{:S(2)}, u32[]{:S(2)}) async-start(bf16[4,2,32,512]{3,2,1,0:T(8,128)(2,1)} %pad_maximum_fusion), calls=%async_computation | async-start | bytes 524288 | tf_op jit(solution)/shard_map/all_to_all | solution.py:582
  277.8 16.0 %collective-permute-start.48 = (bf16[1,128,1024]{1,2,0:T(8,128)(2,1)S(1)}, bf16[1,128,1024]{1,2,0:T(8,128)(2,1)S(1)}, u32[]{:S(2)}, u32[]{:S(2)}) collective-permute-start(bf16[1,128,1024]{1,2,0:T(8,128)(2,1)S(1)} %select_bitcast_fusion.2), channel_id=1, source_target_pairs={{0,16},{4,20},{8,24},{12,28},{16,0},{20,4},{24,8},{28,12},{1,17},{... | collective-permute-start | bytes 786440 | tf_op jit(solution)/shard_map/ppermute | solution.py:22
  (92 other events, 930.9 us)
where the time goes:
time: 301 us; the launch traced here: 300 us
  waiting for transfers between devices  125 us (42%)
  starting transfers between devices  65 us (22%)
  Pallas kernels  61 us (20%)
  local copies, waits for them, and re-layouts  31.7 us (11%)
  other arithmetic  15.5 us (5%)
    ppermute x71, waiting for transfers between devices, swap(): return lax.ppermute(values, axis, [(k, k ^ bit) for k in range(n)])  125 us
    ppermute x71, starting transfers between devices, swap(): return lax.ppermute(values, axis, [(k, k ^ bit) for k in range(n)])  61.4 us
    unnamed x107, local copies, waits for them, and re-layouts  20.7 us
    pallas_call x1, Pallas kernels, on_device(): call(functools.partial(feed_kernel, per_slot, halves, blocks), (peers,),...  15.5 us
    pallas_call x5, Pallas kernels, outer(): call(functools.partial(outer_kernel, count), (a // tile,), [pl.BlockSpec(...  11.8 us
    pallas_call x1, Pallas kernels, on_device(): call(functools.partial(attend_kernel, peers, scale), (slots // pair,), [r...  11.1 us
    pallas_call x1, Pallas kernels, on_device(): call(functools.partial(attend_back_kernel, peers, scale), (slots // pair,...  9.73 us
    squeeze x8, local copies, waits for them, and re-layouts, exchanged(): return [g[0] for g in got] + [swap(g[1], 'img', 1) for g in got]  7.11 us
  transfers between devices with their start and end apart: 72, of which 22 were waited for; matrix products, arithmetic and copies ran while one was open for 9% of the time, Pallas kernels for 16%

commit v1 on v0

v1 whole, which is shorter than its diff:
```python
import functools
import math

import jax
import jax.numpy as jnp
from jax import lax
from jax.experimental import pallas as pl
from jax.experimental.pallas import tpu as pltpu
from jax.sharding import PartitionSpec as P

HEADS = 8
SLOTS_PER = 5
EPS = 1e-05
LANES = 128
F32 = jnp.float32
BF16 = jnp.bfloat16
MIB = 1024 * 1024


def swap(values, axis, bit):
    n = lax.axis_size(axis)
    return lax.ppermute(values, axis, [(k, k ^ bit) for k in range(n)])


def log2(n):
    return n.bit_length() - 1


def after(values, *others):
    return lax.optimization_barrier((values,) + others)[0]


def spread(blocks):
    n = lax.axis_size("patch")
    blocks = dict(blocks)
    bit = n // 4
    while bit:
        for j in list(blocks):
            blocks[j ^ bit] = swap(blocks[j], "patch", bit)
        bit //= 2
    return [blocks[j] for j in range(n)]


def digits_of(axis):
    n = lax.axis_size(axis)
    return [(axis, 1 << k) for k in reversed(range(log2(n)))]


def chosen(own, bit):
    axis, weight = bit
    return (own[("patch", "img").index(axis)] // weight) % 2


def plan_of(rows, digits, order):
    digits, plan = list(digits), []
    for bit in order:
        at = digits.index(bit)
        plan.append(rows // 2 ** (at + 1))
        del digits[at]
        rows //= 2
    return plan


def parted(values, inner, which):
    width = values.shape[-1]
    split = values.reshape(-1, 2, inner, width)
    low, high = split[:, 0].reshape(-1, width), split[:, 1].reshape(-1, width)
    return jnp.where(which == 1, high, low), jnp.where(which == 1, low, high)


class Scatter:
    def __init__(self, own, both, order, plan, end, extra=None, name=None):
        self.own, self.both, self.order, self.plan, self.end = own, both, order, plan, end
        self.extra, self.name, self.at, self.open = extra, name, 0, False

    def begin(self, *others):
        kept, sent = self.both
        bit = self.order[self.at]
        sent = after(sent, *others)
        self.got = [swap(sent, *bit)]
        if self.extra is not None:
            self.got.append(swap(self.extra, *bit))
        self.at, self.open = self.at + 1, True

    def finish(self, *others):
        kept, self.open = self.both[0], False
        if others:
            kept = after(kept, *others)
        nxt = None
        if self.at < len(self.order):
            nxt = (self.order[self.at], self.plan[self.at])
        values = fold(self.own, kept, self.got, self.extra, nxt, self.end, self.name)
        if self.extra is not None:
            self.extra = values[-1]
            values = values[:-1]
        if nxt is not None:
            self.both = values
        else:
            self.values = values
        return values[0]

    def run(self):
        while self.open or self.at < len(self.order):
            if not self.open:
                self.begin()
            self.finish()
        return self.values


def stats(values):
    average = jnp.mean(values, axis=-1, keepdims=True)
    centred = values - average
    spread = jnp.mean(centred * centred, axis=-1, keepdims=True)
    inverse = lax.rsqrt(spread + EPS)
    return centred * inverse, inverse


def pull(hat, inverse, grad, gain):
    scaled = grad * gain
    first = jnp.mean(scaled, axis=-1, keepdims=True)
    second = jnp.mean(scaled * hat, axis=-1, keepdims=True)
    return inverse * (scaled - first - hat * second)


def gelu_parts(values):
    cdf = 0.5 + 0.5 * lax.erf(values * (1.0 / math.sqrt(2.0)))
    density = jnp.exp(-0.5 * values * values) * (1.0 / math.sqrt(2.0 * math.pi))
    return values * cdf, cdf + values * density


def dot(a, b, dims=((1,), (0,))):
    return lax.dot_general(a, b, (dims, ((), ())), preferred_element_type=F32)


NT = ((1,), (1,))
TN = ((0,), (0,))


def low_lanes(shape):
    return lax.broadcasted_iota(jnp.int32, shape, len(shape) - 1) < LANES // 2


def live_rows(counts_ref, rows, per_slot):
    row = lax.broadcasted_iota(jnp.int32, (rows, 1), 0)
    live = jnp.zeros((rows, 1), F32)
    for sample in range(rows // (per_slot * SLOTS_PER)):
        start = sample * SLOTS_PER * per_slot
        inside = jnp.logical_and(row >= start, row < start + counts_ref[sample] * per_slot)
        live = jnp.where(inside, 1.0, live)
    return live


def paired(block):
    low = low_lanes(block.shape)
    zero = jnp.zeros_like(block)
    return jnp.concatenate([jnp.where(low, block, zero), jnp.where(low, zero, block)], axis=0)


def unpaired(block):
    half = block.shape[0] // 2
    return jnp.where(low_lanes((half, block.shape[1])), block[:half], block[half:])


def flipped(values):
    a, b = values.shape
    tall, wide = -a % LANES, -b % LANES
    if wide:
        values = jnp.concatenate([values, jnp.zeros((a, wide), F32)], axis=1)
    if tall:
        values = jnp.concatenate([values, jnp.zeros((tall, b + wide), F32)], axis=0)
    return values.T[:b, :a]


def call(kernel, grid, ins, outs, scratch=(), vmem=40, us=2, prefetch=0, name=None):
    return pl.pallas_call(
        kernel,
        grid_spec=pltpu.PrefetchScalarGridSpec(
            num_scalar_prefetch=prefetch,
            grid=grid,
            in_specs=ins,
            out_specs=[spec for spec, _ in outs],
            scratch_shapes=list(scratch),
        ),
        out_shape=[shape for _, shape in outs],
        compiler_params=pltpu.CompilerParams(
            vmem_limit_bytes=vmem * MIB, dimension_semantics=("arbitrary",) * len(grid)
        ),
        cost_estimate=pl.CostEstimate(flops=0, bytes_accessed=int(us * 1e5), transcendentals=0),
        name=name,
    )


def whole(shape):
    zeros = (0,) * len(shape)
    return pl.BlockSpec(tuple(shape), lambda *_: zeros)


def leading(shape):
    zeros = (0,) * (len(shape) - 1)
    return pl.BlockSpec(tuple(shape), lambda g, *_: (g,) + zeros)


def out(shape, dtype):
    return jax.ShapeDtypeStruct(tuple(shape), dtype)


SMEM = pl.BlockSpec(memory_space=pltpu.SMEM)


def packed(values):
    high = values.astype(BF16)
    left = values - high.astype(F32)
    middle = left.astype(BF16)
    small = left - middle.astype(F32)
    top = jnp.concatenate([high.astype(F32), middle.astype(F32)], axis=1)
    bottom = jnp.concatenate([small, jnp.zeros_like(small)], axis=1)
    return jnp.concatenate([top, bottom], axis=0).astype(BF16)


def unpacked(values):
    values = values.astype(F32)
    n, m = values.shape[0] // 2, values.shape[1] // 2
    return values[:n, :m] + values[:n, m:] + values[n:, :m]


def latent_kernel(per_slot, counts, lat, grad, gain, bias, w_query, lat_low, q_low, dy):
    hat, _ = stats(lat[...].astype(F32))
    low = (hat * gain[1:2] + bias[1:2]).astype(BF16)
    lat_low[...] = low
    q_low[...] = dot(low, w_query[...]).astype(BF16)
    live = live_rows(counts, lat.shape[0], per_slot)
    dy[...] = (live * grad[...].astype(F32)).astype(BF16)


def media_kernel(media, lat_low, gain, bias, w_keyval, key_input, keyval):
    n, rows, width = media.shape
    hat, _ = stats(media[...].reshape(n * rows, width).astype(F32))
    low = (hat * gain[0:1] + bias[0:1]).astype(BF16)
    key_input[:, :rows, :] = low.reshape(n, rows, width)
    key_input[:, rows:, :] = lat_low[...].reshape(n, -1, width)
    every = key_input[...].reshape(-1, width)
    keyval[...] = dot(every, w_keyval[...]).astype(BF16).reshape(keyval.shape)


def attend_kernel(peers, per_slot, scale, *refs):
    qs, kv, parts, held = refs[:peers], refs[peers], refs[peers + 1 : 2 * peers + 1], refs[2 * peers + 1]
    n, keys, inner = kv.shape[0], kv.shape[1], kv.shape[2] // 2
    step = pl.program_id(0)
    items = [(s, t) for s in range(n) for t in range(inner // LANES)]
    cuts = [slice(t * LANES, (t + 1) * LANES) for t in range(2 * inner // LANES)]
    rows = [pl.multiple_of((step * n + s) * per_slot, per_slot) for s in range(n)]
    ones = jnp.ones((keys, LANES), BF16)

    @pl.when(step == 0)
    def _():
        held[...] = jnp.zeros_like(held)

    scores = []
    for s, t in items:
        q = paired(jnp.concatenate([ref[pl.ds(rows[s], per_slot), cuts[t]] for ref in qs], axis=0))
        scores.append(dot(q, kv[s, :, cuts[t]], NT) * scale)
    tops = [jnp.max(score, axis=-1, keepdims=True) for score in scores]
    probs = [jnp.exp(score - top).astype(BF16) for score, top in zip(scores, tops)]
    sums = [
        dot(prob, jnp.concatenate([kv[s, :, cuts[inner // LANES + t]], ones], axis=1))
        for prob, (s, t) in zip(probs, items)
    ]
    lane = lax.broadcasted_iota(jnp.int32, (peers * per_slot, LANES), 1)
    logs = [jnp.zeros((peers * per_slot, LANES), F32) for _ in range(n)]
    for (s, t), both, top in zip(items, sums, tops):
        total = unpaired(both[:, LANES:])
        o = (unpaired(both[:, :LANES]) / total).astype(BF16)
        lse = unpaired(jnp.broadcast_to(top, (top.shape[0], LANES))) + jnp.log(total)
        here = jnp.logical_or(lane == t, lane == LANES // 2 + HEADS // 2 + t)
        logs[s] = jnp.where(here, lse, logs[s])
        for i in range(peers):
            parts[i][pl.ds(rows[s], per_slot), cuts[t]] = o[i * per_slot : (i + 1) * per_slot]
    for s in range(n):
        for i in range(peers):
            held[i, pl.ds(rows[s], per_slot), :] = logs[s][i * per_slot : (i + 1) * per_slot]

    @pl.when(step == pl.num_programs(0) - 1)
    def _():
        for i in range(peers):
            turned = held[i].T
            turned = turned[:HEADS] + turned[LANES // 2 : LANES // 2 + HEADS]
            parts[i][-2 * HEADS :, :] = packed(turned)


def mix_kernel(peers, *refs):
    parts = refs[:peers]
    lat, w_out, gain, bias, attended, att_low, hidden, ff_low, lse_out = refs[peers:]
    rows, inner = attended.shape
    logs = [unpacked(ref[rows:, :]) for ref in parts]
    top = functools.reduce(jnp.maximum, logs)
    lse = top + jnp.log(sum(jnp.exp(v - top) for v in logs))
    lse_out[...] = lse
    weights = flipped(jnp.concatenate([jnp.exp(v - lse) for v in logs], axis=0))[:rows]
    low = low_lanes((rows, LANES))
    for t in range(inner // LANES):
        cut = slice(t * LANES, (t + 1) * LANES)
        total = jnp.zeros((rows, LANES), F32)
        for j in range(peers):
            at = j * HEADS + t
            other = at + HEADS // 2
            weight = jnp.where(low, weights[:, at : at + 1], weights[:, other : other + 1])
            total = total + weight * parts[j][:rows, cut].astype(F32)
        attended[:, cut] = total
        att_low[:, cut] = total.astype(BF16)
    state = lat[...].astype(F32) + dot(att_low[...], w_out[...])
    hidden[...] = state
    hat, _ = stats(state)
    ff_low[...] = (hat * gain[2:3] + bias[2:3]).astype(BF16)


def feed_columns(ff_low, dy, ups, downs, acts, dpres, res, dff):
    half = len(ups) // 2
    a = pl.program_id(1)
    parts = []
    for at in (slice(0, half), slice(half, 2 * half)):
        up = jnp.concatenate([ref[...] for ref in ups[at]], axis=1)
        down = jnp.concatenate([ref[...] for ref in downs[at]], axis=0)
        parts.append((up, down, dot(ff_low[...], up), dot(dy[...], down, NT)))
    done = []
    for up, down, pre, dact in parts:
        value, slope = gelu_parts(pre)
        value = value.astype(BF16)
        back = (slope * dact).astype(BF16)
        res[...] += dot(value, down)
        dff[...] += dot(back, up, NT)
        done.append((value, back))
    for at, (act, dpre) in enumerate(zip(acts, dpres)):

        @pl.when(pl.program_id(0) == at)
        def _():
            width = done[0][0].shape[1]
            for k, (value, back) in enumerate(done):
                act[a, :, k * width : (k + 1) * width] = value
                dpre[a, :, k * width : (k + 1) * width] = back


def first_step():
    return jnp.logical_and(pl.program_id(0) == 0, pl.program_id(1) == 0)


def last_step():
    ends = [pl.program_id(k) == pl.num_programs(k) - 1 for k in range(2)]
    return jnp.logical_and(*ends)


def feed_kernel(count, here, own, ff_low, dy, *refs):
    ups, downs, refs = refs[:count], refs[count : 2 * count], refs[2 * count :]
    acts, dpres, (res, dff) = refs[:here], refs[here : 2 * here], refs[2 * here :]

    @pl.when(first_step())
    def _():
        res[...] = jnp.zeros_like(res)
        dff[...] = jnp.zeros_like(dff)

    feed_columns(ff_low, dy, ups, downs, acts, dpres, res, dff)


def feed_end_kernel(per_slot, count, here, own, counts, ff_low, dy, *refs):
    ups, downs, refs = refs[:count], refs[count : 2 * count], refs[2 * count :]
    res_in, dff_in, hidden, attended, lse, w_out, gain = refs[:7]
    acts, dpres, refs = refs[7 : 7 + here], refs[7 + here : 7 + 2 * here], refs[7 + 2 * here :]
    result, dhidden, dhid_low, datt_low, sums, res, dff = refs

    @pl.when(first_step())
    def _():
        res[...] = res_in[...]
        dff[...] = dff_in[...]

    feed_columns(ff_low, dy, ups, downs, acts, dpres, res, dff)

    @pl.when(last_step())
    def _():
        rows, inner = attended.shape
        live = live_rows(counts, rows, per_slot)
        state = hidden[...]
        result[...] = (live * (state + res[...])).astype(BF16)
        hat, inverse = stats(state)
        grad = dff[...]
        sums[0:1] = jnp.sum(grad * hat, axis=0, keepdims=True)
        sums[1:2] = jnp.sum(grad, axis=0, keepdims=True)
        back = dy[...].astype(F32) + pull(hat, inverse, grad, gain[2:3])
        dhidden[...] = back
        dhid_low[...] = back.astype(BF16)
        datt = dot(dhid_low[...], w_out[...], NT).astype(BF16)
        datt_low[:rows, :] = datt
        product = datt.astype(F32) * attended[...]
        low = low_lanes((rows, LANES))
        lane = lax.broadcasted_iota(jnp.int32, (rows, LANES), 1)
        delta = jnp.zeros((rows, LANES), F32)
        for t in range(inner // LANES):
            both = product[:, t * LANES : (t + 1) * LANES]
            first = jnp.sum(jnp.where(low, both, 0.0), axis=-1, keepdims=True)
            second = jnp.sum(jnp.where(low, 0.0, both), axis=-1, keepdims=True)
            delta = jnp.where(lane == t, first, delta)
            delta = jnp.where(lane == HEADS // 2 + t, second, delta)
        turned = flipped(jnp.concatenate([delta, jnp.zeros((-rows % LANES, LANES), F32)], axis=0))
        datt_low[rows:, :] = packed(jnp.concatenate([lse[...], turned[:HEADS]], axis=0))


def attend_back_kernel(peers, per_slot, scale, *refs):
    qs, das, kv, dkv = refs[:peers], refs[peers : 2 * peers], refs[2 * peers], refs[2 * peers + 1]
    dqs, held = refs[2 * peers + 2 : 3 * peers + 2], refs[3 * peers + 2]
    n, inner = kv.shape[0], kv.shape[2] // 2
    step = pl.program_id(0)
    items = [(s, t) for s in range(n) for t in range(inner // LANES)]
    cuts = [slice(t * LANES, (t + 1) * LANES) for t in range(2 * inner // LANES)]
    rows = [pl.multiple_of((step * n + s) * per_slot, per_slot) for s in range(n)]
    later = inner // LANES

    @pl.when(step == 0)
    def _():
        for i in range(peers):
            turned = unpacked(das[i][-4 * HEADS :, :])
            held[i, :, : 2 * HEADS] = flipped(turned)

    def column(block, h):
        other = h + HEADS // 2
        return jnp.concatenate([block[:, h : h + 1], block[:, other : other + 1]], axis=0)

    sts = [
        jnp.concatenate([held[i, pl.ds(row, per_slot), :] for i in range(peers)], axis=0) for row in rows
    ]
    qp = [paired(jnp.concatenate([ref[pl.ds(rows[s], per_slot), cuts[t]] for ref in qs], axis=0)) for s, t in items]
    dp = [paired(jnp.concatenate([ref[pl.ds(rows[s], per_slot), cuts[t]] for ref in das], axis=0)) for s, t in items]
    scores = [dot(q, kv[s, :, cuts[t]], NT) for q, (s, t) in zip(qp, items)]
    dprobs = [dot(d, kv[s, :, cuts[later + t]], NT) for d, (s, t) in zip(dp, items)]
    probs = [jnp.exp(score * scale - column(sts[s], t)) for score, (s, t) in zip(scores, items)]
    dscores = [
        (prob * (dprob - column(sts[s], HEADS + t))).astype(BF16)
        for prob, dprob, (s, t) in zip(probs, dprobs, items)
    ]
    for (s, t), prob, d in zip(items, probs, dp):
        dkv[s, :, cuts[later + t]] = dot(prob.astype(BF16), d, TN).astype(BF16)
    for (s, t), ds, q in zip(items, dscores, qp):
        dkv[s, :, cuts[t]] = (dot(ds, q, TN) * scale).astype(BF16)
    for (s, t), ds in zip(items, dscores):
        dq = (unpaired(dot(ds, kv[s, :, cuts[t]])) * scale).astype(BF16)
        for i in range(peers):
            dqs[i][pl.ds(rows[s], per_slot), cuts[t]] = dq[i * per_slot : (i + 1) * per_slot]


def keyval_back_kernel(media, dkv, w_keyval, gain, media_grad, dlat, sums):
    n, rows, width = media.shape
    grad = dot(dkv[...].reshape(-1, dkv.shape[2]), w_keyval[...], NT).reshape(n, -1, width)
    dlat[...] = grad[:, rows:].reshape(dlat.shape)
    grad = grad[:, :rows].reshape(n * rows, width)
    hat, inverse = stats(media[...].reshape(n * rows, width).astype(F32))
    media_grad[...] = pull(hat, inverse, grad, gain[0:1]).astype(BF16).reshape(media_grad.shape)

    @pl.when(pl.program_id(0) == 0)
    def _():
        sums[...] = jnp.zeros_like(sums)

    sums[0:1] += jnp.sum(grad * hat, axis=0, keepdims=True)
    sums[1:2] += jnp.sum(grad, axis=0, keepdims=True)


def latent_back_kernel(peers, *refs):
    dqs = refs[:peers]
    dlat, lat, dhidden, w_query, gain, sums_media, sums_ff, dq_low, latent_grad, sums = refs[peers:]
    dq = sum(ref[...].astype(F32) for ref in dqs).astype(BF16)
    dq_low[...] = dq
    grad = dlat[...] + dot(dq, w_query[...], NT)
    hat, inverse = stats(lat[...].astype(F32))
    latent_grad[...] = (dhidden[...] + pull(hat, inverse, grad, gain[1:2])).astype(BF16)
    sums[0:1] = sums_media[0:1]
    sums[1:2] = jnp.sum(grad * hat, axis=0, keepdims=True)
    sums[2:3] = sums_ff[0:1]
    sums[3:4] = sums_media[1:2]
    sums[4:5] = jnp.sum(grad, axis=0, keepdims=True)
    sums[5:6] = sums_ff[1:2]


def stack_kernel(*refs):
    for k, ref in enumerate(refs[:-1]):
        refs[-1][k] = ref[...].reshape(refs[-1].shape[1:])


def stacked(blocks, second=False):
    inner = blocks[0].shape[-2:]
    specs = [
        pl.BlockSpec((1,) + inner, lambda *_: (1, 0, 0)) if second and b.ndim == 3 else whole(b.shape) for b in blocks
    ]
    shape = (len(blocks),) + inner
    return call(stack_kernel, (1,), specs, [(whole(shape), out(shape, BF16))], vmem=62, name="stack")(*blocks)[0]


def outer_kernel(count, bit, inner, extra, own, *refs):
    lefts, rights, refs = refs[:count], refs[count : 2 * count], refs[2 * count :]
    more, results, held = refs[:extra], refs[extra:-1], refs[-1]
    width = held.shape[1]

    @pl.when(pl.program_id(0) == 0)
    def _():
        at = 0
        for ref in rights:
            block = ref[...].reshape(-1, width)
            held[at : at + block.shape[0], :] = block
            at += block.shape[0]

    left = jnp.concatenate([ref[...].reshape(-1, ref.shape[-1]) for ref in lefts], axis=0)
    product = dot(left, held[...], TN)
    if bit is None:
        results[0][...] = product.astype(BF16)
        return
    kept, sent = parted(product, inner, chosen(own, bit))
    if extra:
        rows = more[0].shape[1]
        other = more[0][...].astype(F32).reshape(-1, more[0].shape[2])
        kept_more, sent_more = parted(other, rows, chosen(own, bit))
        join = lambda a, b: jnp.concatenate(
            [a.reshape(-1, inner, width), b.reshape(-1, rows, width)], axis=1
        ).reshape(-1, width)
        kept, sent = join(kept, kept_more), join(sent, sent_more)
    results[0][...] = kept.astype(BF16)
    results[1][...] = sent.astype(BF16)


def outer(own, lefts, rights, tile, name, bit=None, inner=0, more=None):
    count = len(lefts)
    a, b = lefts[0].shape[-1], rights[0].shape[-1]

    def block(values, width, moving):
        lead = values.shape[:-1]
        if len(lead) == 2 and lead[0] == 2:
            lead = (1,) + lead[1:]
        zeros = (0,) * len(lead)
        return pl.BlockSpec(lead + (width,), lambda g, *_: zeros + (g if moving else 0,))

    total = sum(math.prod(block(v, b, False).block_shape[:-1]) for v in rights)
    steps = a // tile
    rows, outs = a, 1
    if bit is not None:
        rows, outs = a // 2, 2
    extra = []
    if more is not None:
        extra = [pl.BlockSpec((more.shape[0] // steps,) + more.shape[1:], lambda g, *_: (g, 0, 0))]
        rows += more.shape[0] * more.shape[1] // 2
    got = call(
        functools.partial(outer_kernel, count, bit, inner, len(extra)),
        (steps,),
        [block(v, tile, True) for v in lefts] + [block(v, b, False) for v in rights] + extra,
        [(pl.BlockSpec((rows // steps, b), lambda g, *_: (g, 0)), out((rows, b), BF16))] * outs,
        scratch=[pltpu.VMEM((total, b), BF16)],
        prefetch=1,
        name=name,
    )(own, *lefts, *rights, *([more] if more is not None else []))
    return got if bit is not None else got[0]


def side_by_side_kernel(rows, left, right, result):
    product = dot(left[...], right[...], TN).astype(BF16)
    split = product.reshape(-1, 2, rows, product.shape[1])
    result[...] = jnp.concatenate([split[:, 0], split[:, 1]], axis=-1)


def fold_kernel(nxt, end, extra, own, kept, got, *refs):
    total = kept[...].astype(F32) + got[...].astype(F32)
    if extra:
        refs[-1][...] = refs[0][...] + refs[1][...]
        refs = refs[2:-1]
    if nxt is not None:
        bit, inner = nxt
        keep, send = parted(total, inner, chosen(own, bit))
        refs[0][...] = keep.astype(BF16)
        refs[1][...] = send.astype(BF16)
        return
    for ref, values in zip(refs, end(total)):
        ref[...] = values.astype(ref.dtype)


def fold(own, kept, got, extra, nxt, end, name):
    rows, width = kept.shape
    ins = [kept, got[0]]
    if nxt is not None:
        shapes = [out((rows // 2, width), BF16)] * 2
    else:
        shapes = jax.eval_shape(end, out(kept.shape, F32))
        shapes = [out(s.shape, F32 if s.dtype == F32 else BF16) for s in shapes]
    if extra is not None:
        ins += [extra, got[1]]
        shapes = shapes + [out(extra.shape, F32)]
    return call(
        functools.partial(fold_kernel, nxt, end, extra is not None),
        (1,),
        [whole(v.shape) for v in ins],
        [(whole(s.shape), s) for s in shapes],
        prefetch=1,
        name=name,
    )(own, *ins)


def on_device(
    media, latents, counts, gains, biases, w_query, w_keyval, w_out, w_up, w_down, out_grad
):
    slots, patch_rows, width = media.shape
    per_slot = latents.shape[1]
    inner = w_query.shape[1]
    ff = w_up.shape[1]
    n_img, peers = lax.axis_size("img"), lax.axis_size("patch")
    shards = n_img * peers
    scale = 1.0 / math.sqrt(inner // HEADS)
    rows = slots * per_slot
    keys = patch_rows + per_slot
    padded = -(-rows // LANES) * LANES
    gain_spec = whole(gains.shape)
    lat = latents.reshape(rows, width)

    own = jnp.stack([lax.axis_index("patch"), lax.axis_index("img")]).astype(jnp.int32)
    fine = width // shards % 16 == 0 and inner // shards % 16 == 0
    lat_low, q_low, dy = call(
        functools.partial(latent_kernel, per_slot),
        (1,),
        [SMEM, whole((rows, width)), whole((rows, width)), gain_spec, gain_spec, whole(w_query.shape)],
        [
            (whole((rows, width)), out((rows, width), BF16)),
            (whole((rows, inner)), out((rows, inner), BF16)),
            (whole((rows, width)), out((rows, width), BF16)),
        ],
        vmem=62, name="latent",
    )(counts, lat, out_grad.reshape(rows, width), gains, biases, w_query)
    q_near = q_low
    qs = {0: q_low}
    bit = peers // 2
    qs[bit] = swap(q_low, "patch", bit)
    dys = {0: dy}

    group = slots // 2
    key_input, keyval = call(
        media_kernel,
        (slots // group,),
        [
            leading((group, patch_rows, width)), leading((group * per_slot, width)),
            gain_spec, gain_spec, whole(w_keyval.shape),
        ],
        [
            (leading((group, keys, width)), out((slots, keys, width), BF16)),
            (leading((group, keys, 2 * inner)), out((slots, keys, 2 * inner), BF16)),
        ],
        name="media",
    )(media, lat_low, gains, biases, w_keyval)
    first = after(qs[bit], keyval)
    qs[bit] = first
    while bit > 1:
        bit //= 2
        for j in list(qs):
            qs[j ^ bit] = swap(qs[j], "patch", bit)
    qs = [qs[j] for j in range(peers)]

    pair = 2
    kv_block = leading((pair, keys, 2 * inner))
    part_rows = rows + 2 * HEADS
    stat_out = (whole((HEADS, padded)), out((HEADS, padded), F32))
    parts = call(
        functools.partial(attend_kernel, peers, per_slot, scale),
        (slots // pair,),
        [whole((rows, inner))] * peers + [kv_block],
        [(whole((part_rows, inner)), out((part_rows, inner), BF16))] * peers,
        scratch=[pltpu.VMEM((peers, padded, LANES), F32)],
        name="attend",
    )(*qs, keyval)
    parts = [parts[0]] + [swap(parts[j], "patch", j) for j in range(1, peers)]

    attended, att_low, hidden, ff_low, lse = call(
        functools.partial(mix_kernel, peers),
        (1,),
        [whole((part_rows, inner))] * peers
        + [whole((rows, width)), whole(w_out.shape), gain_spec, gain_spec],
        [
            (whole((rows, inner)), out((rows, inner), F32)),
            (whole((rows, inner)), out((rows, inner), BF16)),
            (whole((rows, width)), out((rows, width), F32)),
            (whole((rows, width)), out((rows, width), BF16)),
            stat_out,
        ],
        vmem=62, name="mix",
    )(*parts, lat, w_out, gains, biases)
    bit = peers // 2
    ffs = {0: ff_low, bit: swap(ff_low, "patch", bit)}
    dys[bit] = swap(after(dy, ff_low), "patch", bit)

    halves = 2
    blocks = ff // (peers * halves * LANES)
    chunk = ff // shards
    strided = chunk % LANES == 0

    def column(own, j, a, k):
        p, y = own[0] ^ j, (own[1] % halves) ^ a
        if strided:
            return (((k // (chunk // LANES)) * halves + y) * peers + p) * (chunk // LANES) + k % (chunk // LANES)
        return (p * halves + y) * blocks + k

    def weights(first, stride):
        ups = [
            pl.BlockSpec((width, LANES), lambda g, a, own, k=k: (0, column(own, first + stride * g, a, k)))
            for k in range(blocks)
        ]
        downs = [
            pl.BlockSpec((LANES, width), lambda g, a, own, k=k: (column(own, first + stride * g, a, k), 0))
            for k in range(blocks)
        ]
        return ups + downs

    part = ff // (peers * halves)
    here = peers // 2
    columns = (whole((halves, rows, part)), out((halves, rows, part), BF16))
    wide_low = (whole((rows, width)), out((rows, width), BF16))
    wide = (whole((rows, width)), out((rows, width), F32))
    count = blocks
    far = call(
        functools.partial(feed_kernel, count, here),
        (here, halves),
        [whole((rows, width))] * 2 + weights(here, 1),
        [columns] * (2 * here) + [wide, wide],
        vmem=62, prefetch=1, name="feed",
    )(own, ff_low, dy, *([w_up] * count), *([w_down] * count))
    ffs[peers // 2] = after(ffs[peers // 2], far[-1])
    ffs = spread(ffs)
    ff_all = stacked(ffs)
    ff_far = swap(ff_all, "img", 1)
    dys[peers // 2] = after(dys[peers // 2], far[-1])
    dys = spread(dys)
    dy_all = stacked(dys)
    dy_far = swap(dy_all, "img", 1)

    def cross(values, *others):
        values = after(tuple(values), *others)
        return [swap(v, "patch", here + k) for k, v in enumerate(values)]

    act_cross = cross(far[:1])
    near = call(
        functools.partial(feed_end_kernel, per_slot, count, here),
        (here, halves),
        [SMEM] + [whole((rows, width))] * 2 + weights(here - 1, -1)
        + [whole((rows, width))] * 3 + [whole((rows, inner)), whole((HEADS, padded)), whole(w_out.shape), gain_spec],
        [columns] * (2 * here)
        + [wide_low, wide, wide_low]
        + [(whole((rows + 4 * HEADS, inner)), out((rows + 4 * HEADS, inner), BF16)), (whole((2, width)), out((2, width), F32))],
        scratch=[pltpu.VMEM((rows, width), F32), pltpu.VMEM((rows, width), F32)],
        vmem=62, prefetch=1, name="feed_end",
    )(own, counts, after(ff_low, ff_all, dy_all), dy, *([w_up] * count), *([w_down] * count),
      far[2 * here], far[2 * here + 1], hidden, attended, lse, w_out, gains)
    result, dhidden, dhid_low, datt_low, sums_ff = near[2 * here :]
    act_near, dpre_near = list(reversed(near[:here])), list(reversed(near[here : 2 * here]))

    datt_low = after(datt_low, act_cross[0])
    das = {0: datt_low, peers // 2: swap(datt_low, "patch", peers // 2)}
    out_rows = width // shards // 2
    out_t = call(
        functools.partial(side_by_side_kernel, out_rows),
        (2,),
        [pl.BlockSpec((rows, width // 2), lambda g: (0, g)), whole((rows, inner))],
        [(leading((shards // 2, out_rows, 2 * inner)), out((shards, out_rows, 2 * inner), BF16))],
        name="out_grad",
    )(after(dhid_low, datt_low), att_low)[0]
    das[peers // 2] = after(das[peers // 2], out_t)
    acts = act_near + act_cross
    acts = [acts[0]] + [swap(acts[j], "patch", j) for j in range(1, here)] + list(acts[here:])
    acts += [swap(after(far[k], das[peers // 2]), "patch", here + k) for k in range(1, here)]
    das = spread(das)

    got = call(
        functools.partial(attend_back_kernel, peers, per_slot, scale),
        (slots // pair,),
        [whole((rows, inner))] * peers + [whole((rows + 4 * HEADS, inner))] * peers + [kv_block],
        [(kv_block, out(keyval.shape, BF16))] + [(whole((rows, inner)), out((rows, inner), BF16))] * peers,
        scratch=[pltpu.VMEM((peers, padded, LANES), F32)],
        name="attend_back",
    )(*qs, *das[:-1], after(das[-1], ff_far), keyval)
    dkv, dqs = got[0], got[1:]
    dkv = after(dkv, dy_far, *acts)
    act_all = stacked(acts, True)
    act_far = swap(act_all, "img", 1)
    dpres = dpre_near + [swap(after(far[here + k], dkv), "patch", here + k) for k in range(here)]
    dpres = [dpres[0]] + [swap(dpres[j], "patch", j) for j in range(1, here)] + dpres[here:]

    every = digits_of("img") + digits_of("patch")
    low_bit, both = [("patch", 1)], [("patch", 2), ("img", 1)]
    last = [bit for bit in reversed(every) if bit not in low_bit + both]
    kv_order, qo_order = low_bit + both + last, low_bit + both[::-1] + last
    kv_plan = plan_of(2 * inner, every, kv_order)
    q_plan, qo_plan = plan_of(inner, every, qo_order), plan_of(2 * inner, every, qo_order)
    kv_sum = Scatter(
        own,
        outer(
            own, [after(dkv, act_all).reshape(-1, 2 * inner)], [key_input.reshape(-1, width)], 2 * inner // 4,
            "keyval_grad", kv_order[0], kv_plan[0],
        ),
        kv_order, kv_plan, lambda t: [flipped(t)], name="keyval_fold",
    )
    kv_sum.begin()

    media_grad, dlat, sums_media = call(
        keyval_back_kernel,
        (slots // group,),
        [
            leading((group, patch_rows, width)), leading((group, keys, 2 * inner)),
            whole(w_keyval.shape), gain_spec,
        ],
        [
            (leading((group, patch_rows, width)), out(media.shape, BF16)),
            (leading((group * per_slot, width)), out((rows, width), F32)),
            (whole((2, width)), out((2, width), F32)),
        ],
        name="keyval_back",
    )(media, after(dkv, *kv_sum.both), w_keyval, gains)
    dpres = list(after(tuple(dpres), kv_sum.finish(media_grad)))
    dqs = [dqs[0]] + [swap(v, "patch", j + 1) for j, v in enumerate(after(tuple(dqs[1:]), *dpres))]
    dpre_all = stacked(after(tuple(dpres), act_far), True)
    dpre_far = swap(dpre_all, "img", 1)

    rest = [("img", 1 << k) for k in range(1, log2(n_img))]
    rest_digits = rest[::-1]
    down_order, down_plan = rest + [("img", 1)], plan_of(width, rest_digits + [("img", 1)], rest + [("img", 1)])
    down_sum = Scatter(
        own,
        outer(own, dys + [dy_far], acts + [after(act_far, dpre_all)], width // 2, "down_grad", down_order[0], down_plan[0]),
        down_order, down_plan, None, name="down_fold",
    )
    down_sum.begin()
    dqs = [dqs[0]] + list(after(tuple(dqs[1:]), *down_sum.both))
    kv_sum.begin(*dqs)

    dq_low, latent_grad, sums = call(
        functools.partial(latent_back_kernel, peers),
        (1,),
        [whole((rows, inner))] * peers
        + [whole((rows, width))] * 3 + [whole(w_query.shape), gain_spec, whole((2, width)), whole((2, width))],
        [
            (whole((rows, inner)), out((rows, inner), BF16)),
            (whole((rows, width)), out((rows, width), BF16)),
            (whole((HEADS, width)), out((HEADS, width), F32)),
        ],
        name="latent_back",
    )(*dqs, dlat, lat, dhidden, w_query, gains, sums_media, sums_ff)

    q_rows = inner // shards

    def open_rows(total):
        other = total[q_rows:]
        other = jnp.concatenate([other[:, :inner], other[:, inner:]], axis=0)
        return [flipped(total[:q_rows]), flipped(other)]

    qo_sum = Scatter(
        own,
        outer(own, [dq_low], [lat_low], inner // 2, "query_grad", qo_order[0], q_plan[0], more=out_t),
        qo_order, qo_plan, open_rows, extra=sums, name="query_fold",
    )
    qo_sum.begin()
    mark = qo_sum.finish()
    qo_sum.begin(dpre_far)
    up_plan = plan_of(part, rest_digits, rest)
    up_sum = Scatter(
        own,
        outer(own, dpres + [after(dpre_far, mark)], ffs + [ff_far], part // 2, "up_grad", rest[0], up_plan[0]),
        rest, up_plan, lambda t: [flipped(t)] if strided else [t.astype(BF16)], name="up_fold",
    )
    up_sum.begin()
    mark = up_sum.both[0]
    for one in (down_sum, kv_sum, kv_sum, qo_sum, down_sum, up_sum, kv_sum, qo_sum):
        mark = one.finish(mark)
        one.begin()
    (kv_sum,) = kv_sum.run()
    (up_sum,) = up_sum.run()
    q_sum, out_sum = qo_sum.run()
    small = lax.dynamic_slice_in_dim(
        qo_sum.extra, (own[1] * peers + own[0]) * (width // shards), width // shards, axis=1
    )
    if not strided:
        have = lambda i, p: (p * halves + i % 2) * (n_img // 2) + i // 2
        up_sum = lax.ppermute(
            up_sum, ("img", "patch"), [(i * peers + p, have(i, p)) for i in range(n_img) for p in range(peers)]
        )
        up_sum = up_sum.astype(F32).T
    up_grad = up_sum

    while down_sum.at < len(down_sum.order):
        down_sum.finish()
        down_sum.begin()

    kept, other = down_sum.both[0], down_sum.got[0]
    kept, other = (v.reshape(peers, -1, part) for v in (kept, other))
    odd = own[1] % 2 == 1
    both = jnp.stack([jnp.where(odd, other, kept), jnp.where(odd, kept, other)], axis=1)
    both = lax.all_to_all(both, "patch", 0, 0, tiled=True)
    if strided:
        both = both.reshape(peers, 2, -1, n_img // 2, chunk).transpose(3, 1, 0, 4, 2)
    else:
        both = both.transpose(0, 1, 3, 2)
    down_grad = both.reshape(ff, width // shards).astype(F32)

    return (
        result.reshape(slots, per_slot, width),
        media_grad,
        latent_grad.reshape(slots, per_slot, width),
        q_sum,
        kv_sum,
        out_sum,
        up_grad,
        down_grad,
        small[:3],
        small[3:6],
    )


def solution(mesh):
    rows = P("img", "patch", None)
    shard = P(None, ("img", "patch"))
    return jax.shard_map(
        on_device,
        mesh=mesh,
        in_specs=(rows, rows, P("img"), P(), P(), P(), P(), P(), P(), P(), rows),
        out_specs=(rows, rows, rows) + (shard,) * 7,
        check_vma=False,
    )
```

time: 301 us -> 227 us (0.75)
  waiting for transfers between devices: 125 us -> 70.3 us
  Pallas kernels: 61 us -> 83.2 us
  starting transfers between devices: 65 us -> 47.8 us
  other arithmetic: 15.5 us -> 1.33 us
  local copies, waits for them, and re-layouts: 31.7 us -> 22.3 us
    ppermute x71 -> x48, waiting for transfers between devices: 125 us -> 70.3 us  [swap(): return lax.ppermute(values, axis, [(k, k ^ bit) for k in range(n)])]
    pallas_call x9 -> x28, Pallas kernels: 51.5 us -> 70.8 us  [the longest x4 14.6 us: outer(): call(functools.partial(outer_kernel, count, bit, inner, len(extra)), (ste...]
    ppermute x71 -> x48, starting transfers between devices: 61.4 us -> 44.4 us  [swap(): return lax.ppermute(values, axis, [(k, k ^ bit) for k in range(n)])]
    squeeze x10 -> x0, local copies, waits for them, and re-layouts: 8.44 us -> none  [the longest x8 7.11 us: exchanged(): return [g[0] for g in got] + [swap(g[1], 'img', 1) for g in got]]
    select_n x22 -> x1, other arithmetic: 5.03 us -> 0.02 us  [on_device(): jnp.where(odd, other, kept)]
    convert_element_type x10 -> x0, other arithmetic: 4.06 us -> none  [scatter_sum(): piece.values = (kept.astype(F32) + other.astype(F32)).astype(kept.dtype)]
    unnamed x107 -> x117, local copies, waits for them, and re-layouts: 20.7 us -> 20.1 us
  transfers between devices with their start and end apart: 72 -> 49, of which waited for: 22 -> 14; matrix products, arithmetic and copies ran while one was open for 9% -> 2% of each run, Pallas kernels for 16% -> 29%
where the time goes in v1:
time: 227 us; the launch traced here: 226 us
  Pallas kernels  83.2 us (37%)
  waiting for transfers between devices  70.3 us (31%)
  starting transfers between devices  47.8 us (21%)
  local copies, waits for them, and re-layouts  22.3 us (10%)
    ppermute x48, waiting for transfers between devices, swap(): return lax.ppermute(values, axis, [(k, k ^ bit) for k in range(n)])  70.3 us
    ppermute x48, starting transfers between devices, swap(): return lax.ppermute(values, axis, [(k, k ^ bit) for k in range(n)])  44.4 us
    unnamed x117, local copies, waits for them, and re-layouts  20.1 us
    pallas_call x4, Pallas kernels, outer(): call(functools.partial(outer_kernel, count, bit, inner, len(extra)), (ste...  14.6 us
    pallas_call x1, Pallas kernels, on_device(): call(functools.partial(feed_end_kernel, per_slot, count, here), (here, ha...  11.8 us
    pallas_call x14, Pallas kernels, fold(): call(functools.partial(fold_kernel, nxt, end, extra is not None), (1,), [...  10.7 us
    pallas_call x1, Pallas kernels, on_device(): call(functools.partial(feed_kernel, count, here), (here, halves), [whole(...  9.4 us
    pallas_call x4, Pallas kernels, stacked(): call(stack_kernel, (1,), specs, [(whole(shape), out(shape, BF16))], vmem=...  8.91 us
  transfers between devices with their start and end apart: 49, of which 14 were waited for; matrix products, arithmetic and copies ran while one was open for 2% of the time, Pallas kernels for 29%

profile of v1, /device:TPU:0, one launch (start us, length us, event | category | flops | bytes accessed | tf_op | source)
XLA Modules:
  0.0 226.1 jit_solution(10768155512822843058)
XLA Ops:
  0.7 2.8 %latent.1 = (bf16[160,1024]{1,0:T(8,128)(2,1)}, bf16[160,512]{1,0:T(8,128)(2,1)}, bf16[160,1024]{1,0:T(8,128)(2,1)}) custom-call(s32[2]{0:T(128)} %counts.3, bf16[160,1024]{1,0:T(8,128)(2,1)} %bitcast.20, bf16[160,1024]{1,0:T(8,128)(2,1)} %bitcast.27, f32[3,1024]{1,0:T(4,128)} %refs_8_.1, f32[3,1024]{1,0:T(4,128)} %refs_7_.4, bf16[1024,512]{1,0:T(8,128)(2,1)} %refs_7_.7), custom_call_target="tpu_custom_call" | custom-call | bytes 200000 | tf_op jit(solution)/shard_map/latent/pallas_call | solution.py:616
  3.5 3.0 %collective-permute-start.1 = (bf16[160,512]{1,0:T(8,128)(2,1)}, bf16[160,512]{1,0:T(8,128)(2,1)S(1)}, u32[]{:S(2)}, u32[]{:S(2)}) collective-permute-start(bf16[160,512]{1,0:T(8,128)(2,1)} %get-tuple-element.128.refs_0_), channel_id=1, source_target_pairs={{0,2},{1,3},{2,0},{3,1},{4,6},{5,7},{6,4},{7,5},{8,10},{9,11},{10,... | collective-permute-start | bytes 491528 | tf_op jit(solution)/shard_map/ppermute | solution.py:22
  10.4 2.7 %media.3 = (bf16[10,80,1024]{2,1,0:T(8,128)(2,1)S(1)}, bf16[10,80,1024]{2,1,0:T(8,128)(2,1)S(1)}) custom-call(bf16[10,64,1024]{2,1,0:T(8,128)(2,1)S(1)} %copy-done.3, bf16[160,1024]{1,0:T(8,128)(2,1)S(1)} %copy-done.13, f32[3,1024]{1,0:T(4,128)S(1)} %copy-done.38, f32[3,1024]{1,0:T(4,128)S(1)} %copy-done.47, bf16[1024,1024]{1,0:T(8,128)(2,1)S(1)} %copy-done), custom_call_target="tpu_custom_call" | custom-call | bytes 200000 | tf_op jit(solution)/shard_map/media/pallas_call | solution.py:634
  15.8 3.1 %attend.1 = (bf16[176,512]{1,0:T(8,128)(2,1)S(1)}, bf16[176,512]{1,0:T(8,128)(2,1)S(1)}, bf16[176,512]{1,0:T(8,128)(2,1)S(1)}, bf16[176,512]{1,0:T(8,128)(2,1)S(1)}) custom-call(bf16[160,512]{1,0:T(8,128)(2,1)S(1)} %copy-done.25, bf16[160,512]{1,0:T(8,128)(2,1)S(1)} %collective-permute-done.refs_1_, bf16[160,512]{1,0:T(8,128)(2,1)S(1)} %collective-permute-done.1.refs_2_, ...), custom_call_target="tpu_custom_call" | custom-call | bytes 200000 | tf_op jit(solution)/shard_map/attend/pallas_call | solution.py:659
  21.4 5.9 %collective-permute-done.4.refs_2_ = bf16[176,512]{1,0:T(8,128)(2,1)S(1)} collective-permute-done((bf16[176,512]{1,0:T(8,128)(2,1)S(1)}, bf16[176,512]{1,0:T(8,128)(2,1)S(1)}, u32[]{:S(2)}, u32[]{:S(2)}) %collective-permute-start.4) | collective-permute-done | bytes 180256 | tf_op jit(solution)/shard_map/ppermute | solution.py:22
  27.3 2.2 collective-permute-done.5.refs_3_
  30.2 3.8 %mix.1 = (f32[160,512]{1,0:T(8,128)}, bf16[160,512]{1,0:T(8,128)(2,1)}, f32[160,1024]{1,0:T(8,128)}, bf16[160,1024]{1,0:T(8,128)(2,1)}, f32[8,256]{1,0:T(8,128)}) custom-call(bf16[176,512]{1,0:T(8,128)(2,1)} %copy-done.45, bf16[176,512]{1,0:T(8,128)(2,1)} %copy-done.53, bf16[176,512]{1,0:T(8,128)(2,1)} %copy-done.54, bf16[176,512]{1,0:T(8,128)(2,1)} %copy-done.55, ...), custom_call_target="tpu_custom_call" | custom-call | bytes 200000 | tf_op jit(solution)/shard_map/mix/pallas_call | solution.py:669
  36.8 9.4 %feed.1 = (bf16[2,160,512]{2,1,0:T(8,128)(2,1)}, bf16[2,160,512]{2,1,0:T(8,128)(2,1)}, bf16[2,160,512]{2,1,0:T(8,128)(2,1)}, bf16[2,160,512]{2,1,0:T(8,128)(2,1)...) custom-call(s32[2]{0:T(128)} %pad_add_fusion.own, bf16[160,1024]{1,0:T(8,128)(2,1)} %get-tuple-element.142.ff_low.refs_0_.refs_5_, ...), custom_call_target="tpu_custom_call" | custom-call | bytes 200000 | tf_op jit(solution)/shard_map/feed/pallas_call | solution.py:715
  46.8 4.9 %collective-permute-done.10.refs_2_ = bf16[160,1024]{1,0:T(8,128)(2,1)} collective-permute-done((bf16[160,1024]{1,0:T(8,128)(2,1)}, bf16[160,1024]{1,0:T(8,128)(2,1)}, u32[]{:S(2)}, u32[]{:S(2)}) %collective-permute-start.10) | collective-permute-done | bytes 327712 | tf_op jit(solution)/shard_map/ppermute | solution.py:22
  51.7 2.4 %stack.22 = bf16[4,160,1024]{2,1,0:T(8,128)(2,1)} custom-call(bf16[160,1024]{1,0:T(8,128)(2,1)} %get-tuple-element.142.ff_low.refs_0_.refs_5_, bf16[160,1024]{1,0:T(8,128)(2,1)} %collective-permute-done.6.refs_1_.refs_6_, bf16[160,1024]{1,0:T(8,128)(2,1)} %copy-done.11, bf16[160,1024]{1,0:T(8,128)(2,1)} %collective-permute-done.8.refs_3_.refs_8_), custom_call_target="tpu_custom_call" | custom-call | bytes 200000 | tf_op jit(solution)/shard_map/stack/pallas_call | solution.py:490
  55.6 2.4 %stack.23 = bf16[4,160,1024]{2,1,0:T(8,128)(2,1)} custom-call(bf16[160,1024]{1,0:T(8,128)(2,1)} %get-tuple-element.140.dy.refs_0_, bf16[160,1024]{1,0:T(8,128)(2,1)} %collective-permute-done.9.refs_1_, bf16[160,1024]{1,0:T(8,128)(2,1)} %collective-permute-done.10.refs_2_, bf16[160,1024]{1,0:T(8,128)(2,1)} %collective-permute-done.11.refs_3_), custom_call_target="tpu_custom_call" | custom-call | bytes 200000 | tf_op jit(solution)/shard_map/stack/pallas_call | solution.py:490
  58.8 11.8 %feed_end.1 = (bf16[2,160,512]{2,1,0:T(8,128)(2,1)}, bf16[2,160,512]{2,1,0:T(8,128)(2,1)}, bf16[2,160,512]{2,1,0:T(8,128)(2,1)}, bf16[2,160,512]{2,1,0:T(8,128)(...) custom-call(s32[2]{0:T(128)} %pad_add_fusion.own, ...), custom_call_target="tpu_custom_call" | custom-call | bytes 200000 | tf_op jit(solution)/shard_map/feed_end/pallas_call | solution.py:736
  70.7 1.8 collective-permute-start.14
  79.4 8.2 %collective-permute-done.19.refs_3_.refs_8_ = bf16[2,160,512]{2,1,0:T(8,128)(2,1)} collective-permute-done((bf16[2,160,512]{2,1,0:T(8,128)(2,1)}, bf16[2,160,512]{2,1,0:T(8,128)(2,1)}, u32[]{:S(2)}, u32[]{:S(2)}) %collective-permute-start.19) | collective-permute-done | bytes 327712 | tf_op jit(solution)/shard_map/ppermute | solution.py:22
  87.7 2.0 stack.24
  94.4 7.7 %attend_back.1 = (bf16[10,80,1024]{2,1,0:T(8,128)(2,1)S(1)}, bf16[160,512]{1,0:T(8,128)(2,1)S(1)}, bf16[160,512]{1,0:T(8,128)(2,1)}, bf16[160,512]{1,0:T(8,128)(2,1)}, bf16[160,512]{1,0:T(8,128)(2,1)}) custom-call(bf16[160,512]{1,0:T(8,128)(2,1)S(1)} %copy-done.26, bf16[160,512]{1,0:T(8,128)(2,1)S(1)} %copy-done.30, bf16[160,512]{1,0:T(8,128)(2,1)S(1)} %copy-done.28, ...), custom_call_target="tpu_custom_call" | custom-call | bytes 200000 | tf_op jit(solution)/shard_map/attend_back/pallas_call | solution.py:767
  102.1 11.6 %collective-permute-done.17.refs_4_ = bf16[4,160,1024]{2,1,0:T(8,128)(2,1)} collective-permute-done((bf16[4,160,1024]{2,1,0:T(8,128)(2,1)}, bf16[4,160,1024]{2,1,0:T(8,128)(2,1)}, u32[]{:S(2)}, u32[]{:S(2)}) %collective-permute-start.17) | collective-permute-done | bytes 1310752 | tf_op jit(solution)/shard_map/ppermute | solution.py:22
  113.7 3.9 %keyval_grad.1 = (bf16[512,1024]{1,0:T(8,128)(2,1)S(1)}, bf16[512,1024]{1,0:T(8,128)(2,1)S(1)}) custom-call(s32[2]{0:T(128)S(1)} %copy-done.43, bf16[800,1024]{1,0:T(8,128)(2,1)S(1)} %bitcast.19, bf16[800,1024]{1,0:T(8,128)(2,1)S(1)} %bitcast.23), custom_call_target="tpu_custom_call" | custom-call | bytes 200000 | tf_op jit(solution)/shard_map/keyval_grad/pallas_call | solution.py:544
  121.2 4.2 %keyval_back.1 = (bf16[10,64,1024]{2,1,0:T(8,128)(2,1)}, f32[160,1024]{1,0:T(8,128)S(1)}, f32[2,1024]{1,0:T(2,128)S(1)}) custom-call(bf16[10,64,1024]{2,1,0:T(8,128)(2,1)S(1)} %copy-done.4, bf16[10,80,1024]{2,1,0:T(8,128)(2,1)S(1)} %get-tuple-element.166.dkv, bf16[1024,1024]{1,0:T(8,128)(2,1)S(1)} %copy-done.1, f32[3,1024]{1,0:T(4,128)S(1)} %copy-done.39), custom_call_target="tpu_custom_call" | custom-call | bytes 200000 | tf_op jit(solution)/shard_map/keyval_back/pallas_call | solution.py:798
  127.8 2.4 %collective-permute-done.21.refs_2_ = bf16[2,160,512]{2,1,0:T(8,128)(2,1)S(1)} collective-permute-done((bf16[2,160,512]{2,1,0:T(8,128)(2,1)}, bf16[2,160,512]{2,1,0:T(8,128)(2,1)S(1)}, u32[]{:S(2)}, u32[]{:S(2)}) %collective-permute-start.21) | collective-permute-done | bytes 327712 | tf_op jit(solution)/shard_map/ppermute | solution.py:22
  130.2 5.8 %collective-permute-done.22.refs_3_ = bf16[2,160,512]{2,1,0:T(8,128)(2,1)S(1)} collective-permute-done((bf16[2,160,512]{2,1,0:T(8,128)(2,1)S(1)}, bf16[2,160,512]{2,1,0:T(8,128)(2,1)S(1)}, u32[]{:S(2)}, u32[]{:S(2)}) %collective-permute-start.22) | collective-permute-done | bytes 327712 | tf_op jit(solution)/shard_map/ppermute | solution.py:22
  138.8 2.0 stack.25
  141.9 4.3 %down_grad.1 = (bf16[512,512]{1,0:T(8,128)(2,1)S(1)}, bf16[512,512]{1,0:T(8,128)(2,1)S(1)}) custom-call(s32[2]{0:T(128)S(1)} %copy-done.43, bf16[160,1024]{1,0:T(8,128)(2,1)} %get-tuple-element.140.dy.refs_0_, bf16[160,1024]{1,0:T(8,128)(2,1)} %collective-permute-done.9.refs_1_, bf16[160,1024]{1,0:T(8,128)(2,1)} %collective-permute-done.10.refs_2_, ...), custom_call_target="tpu_custom_call" | custom-call | bytes 200000 | tf_op jit(solution)/shard_map/down_grad/pallas_call | solution.py:544
  146.4 2.6 %latent_back.1 = (bf16[160,512]{1,0:T(8,128)(2,1)S(1)}, bf16[160,1024]{1,0:T(8,128)(2,1)}, f32[8,1024]{1,0:T(8,128)S(1)}) custom-call(bf16[160,512]{1,0:T(8,128)(2,1)S(1)} %get-tuple-element.168.refs_0_, bf16[160,512]{1,0:T(8,128)(2,1)S(1)} %collective-permute-done.24.refs_1_, bf16[160,512]{1,0:T(8,128)(2,1)} %collective-permute-done.25.refs_2_, ...), custom_call_target="tpu_custom_call" | custom-call | bytes 200000 | tf_op jit(solution)/shard_map/latent_back/pallas_call | solution.py:829
  156.2 12.0 %collective-permute-done.30.refs_4_ = bf16[4,160,512]{2,1,0:T(8,128)(2,1)S(1)} collective-permute-done((bf16[4,160,512]{2,1,0:T(8,128)(2,1)S(1)}, bf16[4,160,512]{2,1,0:T(8,128)(2,1)S(1)}, u32[]{:S(2)}, u32[]{:S(2)}) %collective-permute-start.30) | collective-permute-done | bytes 655392 | tf_op jit(solution)/shard_map/ppermute | solution.py:22
  168.7 4.8 %up_grad.1 = (bf16[256,1024]{1,0:T(8,128)(2,1)S(1)}, bf16[256,1024]{1,0:T(8,128)(2,1)}) custom-call(s32[2]{0:T(128)S(1)} %copy-done.43, bf16[2,160,512]{2,1,0:T(8,128)(2,1)S(1)} %copy-done.15, bf16[2,160,512]{2,1,0:T(8,128)(2,1)S(1)} %copy-done.20, bf16[2,160,512]{2,1,0:T(8,128)(2,1)S(1)} %copy-done.22, bf16[2,160,512]{2,1,0:T(8,128)(2,1)S(1)} %copy-done.24, ...), custom_call_target="tpu_custom_call" | custom-call | bytes 200000 | tf_op jit(solution)/shard_map/up_grad/pallas_call | solution.py:544
  178.2 2.6 %collective-permute-start.36 = (bf16[256,512]{1,0:T(8,128)(2,1)S(1)}, bf16[256,512]{1,0:T(8,128)(2,1)S(1)}, u32[]{:S(2)}, u32[]{:S(2)}) collective-permute-start(bf16[256,512]{1,0:T(8,128)(2,1)S(1)} %get-tuple-element.223), channel_id=1, source_target_pairs={{0,16},{4,20},{8,24},{12,28},{16,0},{20,4},{24,8},{28,12},{1,17},{... | collective-permute-start | bytes 786440 | tf_op jit(solution)/shard_map/ppermute | solution.py:22
  181.3 5.9 %collective-permute-done.33.got = bf16[128,1024]{1,0:T(8,128)(2,1)S(1)} collective-permute-done((bf16[128,1024]{1,0:T(8,128)(2,1)S(1)}, bf16[128,1024]{1,0:T(8,128)(2,1)S(1)}, u32[]{:S(2)}, u32[]{:S(2)}) %collective-permute-start.33) | collective-permute-done | bytes 262176 | tf_op jit(solution)/shard_map/ppermute | solution.py:22
  190.2 2.5 %collective-permute-done.36.got = bf16[256,512]{1,0:T(8,128)(2,1)S(1)} collective-permute-done((bf16[256,512]{1,0:T(8,128)(2,1)S(1)}, bf16[256,512]{1,0:T(8,128)(2,1)S(1)}, u32[]{:S(2)}, u32[]{:S(2)}) %collective-permute-start.36) | collective-permute-done | bytes 262176 | tf_op jit(solution)/shard_map/ppermute | solution.py:22
  198.3 3.4 %collective-permute-start.46 = (bf16[128,1024]{1,0:T(8,128)(2,1)S(1)}, bf16[128,1024]{1,0:T(8,128)(2,1)S(1)}, u32[]{:S(2)}, u32[]{:S(2)}) collective-permute-start(bf16[128,1024]{1,0:T(8,128)(2,1)S(1)} %get-tuple-element.243), channel_id=1, source_target_pairs={{0,16},{4,20},{8,24},{12,28},{16,0},{20,4},{24,8},{28,12},{1,17},{... | collective-permute-start | bytes 786440 | tf_op jit(solution)/shard_map/ppermute | solution.py:22
  202.4 3.4 %all-to-all-start = ((bf16[4,2,32,512]{3,2,1,0:T(8,128)(2,1)}), bf16[4,2,32,512]{3,2,1,0:T(8,128)(2,1)S(1)}, u32[]{:S(2)}, u32[]{:S(2)}) async-start(bf16[4,2,32,512]{3,2,1,0:T(8,128)(2,1)} %pad_maximum_fusion), calls=%async_computation | async-start | bytes 524288 | tf_op jit(solution)/shard_map/all_to_all | solution.py:890
  209.7 5.1 %collective-permute-done.42.refs_1_ = f32[8,1024]{1,0:T(8,128)S(1)} collective-permute-done((f32[8,1024]{1,0:T(8,128)S(1)}, f32[8,1024]{1,0:T(8,128)S(1)}, u32[]{:S(2)}, u32[]{:S(2)}) %collective-permute-start.42) | collective-permute-done | bytes 32800 | tf_op jit(solution)/shard_map/ppermute | solution.py:22
  (223 shorter events, 73.9 us)
Async XLA Ops:
  3.5 10.7 %collective-permute-start.1 = (bf16[160,512]{1,0:T(8,128)(2,1)}, bf16[160,512]{1,0:T(8,128)(2,1)S(1)}, u32[]{:S(2)}, u32[]{:S(2)}) collective-permute-start(bf16[160,512]{1,0:T(8,128)(2,1)} %get-tuple-element.128.refs_0_), channel_id=1, source_target_pairs={{0,2},{1,3},{2,0},{3,1},{4,6},{5,7},{6,4},{7,5},{8,10},{9,11},{10,... | collective-permute-start | bytes 491528 | tf_op jit(solution)/shard_map/ppermute | solution.py:22
  19.9 9.6 %collective-permute-start.5 = (bf16[176,512]{1,0:T(8,128)(2,1)S(1)}, bf16[176,512]{1,0:T(8,128)(2,1)S(1)}, u32[]{:S(2)}, u32[]{:S(2)}) collective-permute-start(bf16[176,512]{1,0:T(8,128)(2,1)S(1)} %get-tuple-element.135), channel_id=1, source_target_pairs={{0,3},{1,2},{2,1},{3,0},{4,7},{5,6},{6,5},{7,4},{8,11},{9,10},{10,... | collective-permute-start | bytes 540680 | tf_op jit(solution)/shard_map/ppermute | solution.py:22
  34.1 12.1 %collective-permute-start.7 = (bf16[160,1024]{1,0:T(8,128)(2,1)}, bf16[160,1024]{1,0:T(8,128)(2,1)S(1)}, u32[]{:S(2)}, u32[]{:S(2)}) collective-permute-start(bf16[160,1024]{1,0:T(8,128)(2,1)} %get-tuple-element.142.ff_low.refs_0_.refs_5_), channel_id=1, source_target_pairs={{0,2},{1,3},{2,0},{3,1},{4,6},{5,7},{6,4},{7,5},{8,10},{9,11},{10,... | collective-permute-start | bytes 983048 | tf_op jit(solution)/shard_map/ppermute | solution.py:22
  34.6 17.0 %collective-permute-start.10 = (bf16[160,1024]{1,0:T(8,128)(2,1)}, bf16[160,1024]{1,0:T(8,128)(2,1)}, u32[]{:S(2)}, u32[]{:S(2)}) collective-permute-start(bf16[160,1024]{1,0:T(8,128)(2,1)} %get-tuple-element.140.dy.refs_0_), channel_id=1, source_target_pairs={{0,2},{1,3},{2,0},{3,1},{4,6},{5,7},{6,4},{7,5},{8,10},{9,11},{10,... | collective-permute-start | bytes 983048 | tf_op jit(solution)/shard_map/ppermute | solution.py:22
  36.7 15.0 %collective-permute-start.6 = (bf16[160,1024]{1,0:T(8,128)(2,1)}, bf16[160,1024]{1,0:T(8,128)(2,1)}, u32[]{:S(2)}, u32[]{:S(2)}) collective-permute-start(bf16[160,1024]{1,0:T(8,128)(2,1)} %get-tuple-element.142.ff_low.refs_0_.refs_5_), channel_id=1, source_target_pairs={{0,1},{1,0},{2,3},{3,2},{4,5},{5,4},{6,7},{7,6},{8,9},{9,8},{10,11... | collective-permute-start | bytes 983048 | tf_op jit(solution)/shard_map/ppermute | solution.py:22
  46.7 9.0 %collective-permute-start.9 = (bf16[160,1024]{1,0:T(8,128)(2,1)}, bf16[160,1024]{1,0:T(8,128)(2,1)}, u32[]{:S(2)}, u32[]{:S(2)}) collective-permute-start(bf16[160,1024]{1,0:T(8,128)(2,1)} %get-tuple-element.140.dy.refs_0_), channel_id=1, source_target_pairs={{0,1},{1,0},{2,3},{3,2},{4,5},{5,4},{6,7},{7,6},{8,9},{9,8},{10,11... | collective-permute-start | bytes 983048 | tf_op jit(solution)/shard_map/ppermute | solution.py:22
  54.1 35.6 %collective-permute-start.16 = (bf16[4,160,1024]{2,1,0:T(8,128)(2,1)}, bf16[4,160,1024]{2,1,0:T(8,128)(2,1)}, u32[]{:S(2)}, u32[]{:S(2)}) collective-permute-start(bf16[4,160,1024]{2,1,0:T(8,128)(2,1)} %stack.22), channel_id=1, source_target_pairs={{0,4},{4,0},{8,12},{12,8},{16,20},{20,16},{24,28},{28,24},{1,5},{5... | collective-permute-start | bytes 3932168 | tf_op jit(solution)/shard_map/ppermute | solution.py:22
  58.0 55.6 %collective-permute-start.17 = (bf16[4,160,1024]{2,1,0:T(8,128)(2,1)}, bf16[4,160,1024]{2,1,0:T(8,128)(2,1)}, u32[]{:S(2)}, u32[]{:S(2)}) collective-permute-start(bf16[4,160,1024]{2,1,0:T(8,128)(2,1)} %stack.23), channel_id=1, source_target_pairs={{0,4},{4,0},{8,12},{12,8},{16,20},{20,16},{24,28},{28,24},{1,5},{5... | collective-permute-start | bytes 3932168 | tf_op jit(solution)/shard_map/ppermute | solution.py:22
  58.6 12.1 %collective-permute-start.12 = (bf16[2,160,512]{2,1,0:T(8,128)(2,1)}, bf16[2,160,512]{2,1,0:T(8,128)(2,1)S(1)}, u32[]{:S(2)}, u32[]{:S(2)}) collective-permute-start(bf16[2,160,512]{2,1,0:T(8,128)(2,1)} %get-tuple-element.149), channel_id=1, source_target_pairs={{0,2},{1,3},{2,0},{3,1},{4,6},{5,7},{6,4},{7,5},{8,10},{9,11},{10,... | collective-permute-start | bytes 983048 | tf_op jit(solution)/shard_map/ppermute | solution.py:22
  77.6 10.1 %collective-permute-start.19 = (bf16[2,160,512]{2,1,0:T(8,128)(2,1)}, bf16[2,160,512]{2,1,0:T(8,128)(2,1)}, u32[]{:S(2)}, u32[]{:S(2)}) collective-permute-start(bf16[2,160,512]{2,1,0:T(8,128)(2,1)} %get-tuple-element.160), channel_id=1, source_target_pairs={{0,3},{1,2},{2,1},{3,0},{4,7},{5,6},{6,5},{7,4},{8,11},{9,10},{10,... | collective-permute-start | bytes 983048 | tf_op jit(solution)/shard_map/ppermute | solution.py:22
  77.7 12.0 %collective-permute-start.15 = (bf16[192,512]{1,0:T(8,128)(2,1)}, bf16[192,512]{1,0:T(8,128)(2,1)}, u32[]{:S(2)}, u32[]{:S(2)}) collective-permute-start(bf16[192,512]{1,0:T(8,128)(2,1)} %collective-permute-done.14.refs_6_), channel_id=1, source_target_pairs={{0,1},{1,0},{2,3},{3,2},{4,5},{5,4},{6,7},{7,6},{8,9},{9,8},{10,11... | collective-permute-start | bytes 589832 | tf_op jit(solution)/shard_map/ppermute | solution.py:22
  79.4 10.3 %collective-permute-start.13 = (bf16[192,512]{1,0:T(8,128)(2,1)}, bf16[192,512]{1,0:T(8,128)(2,1)}, u32[]{:S(2)}, u32[]{:S(2)}) collective-permute-start(bf16[192,512]{1,0:T(8,128)(2,1)} %get-tuple-element.150.refs_4_), channel_id=1, source_target_pairs={{0,1},{1,0},{2,3},{3,2},{4,5},{5,4},{6,7},{7,6},{8,9},{9,8},{10,11... | collective-permute-start | bytes 589832 | tf_op jit(solution)/shard_map/ppermute | solution.py:22
  117.7 20.2 %collective-permute-start.27 = (bf16[4,160,512]{2,1,0:T(8,128)(2,1)S(1)}, bf16[4,160,512]{2,1,0:T(8,128)(2,1)S(1)}, u32[]{:S(2)}, u32[]{:S(2)}) collective-permute-start(bf16[4,160,512]{2,1,0:T(8,128)(2,1)S(1)} %copy-done.51), channel_id=1, source_target_pairs={{0,4},{4,0},{8,12},{12,8},{16,20},{20,16},{24,28},{28,24},{1,5},{5... | collective-permute-start | bytes 1966088 | tf_op jit(solution)/shard_map/ppermute | solution.py:22
  119.3 8.5 %collective-permute-start.20 = (bf16[2,160,512]{2,1,0:T(8,128)(2,1)}, bf16[2,160,512]{2,1,0:T(8,128)(2,1)S(1)}, u32[]{:S(2)}, u32[]{:S(2)}) collective-permute-start(bf16[2,160,512]{2,1,0:T(8,128)(2,1)} %get-tuple-element.173), channel_id=1, source_target_pairs={{0,1},{1,0},{2,3},{3,2},{4,5},{5,4},{6,7},{7,6},{8,9},{9,8},{10,11... | collective-permute-start | bytes 983048 | tf_op jit(solution)/shard_map/ppermute | solution.py:22
  119.4 10.8 %collective-permute-start.21 = (bf16[2,160,512]{2,1,0:T(8,128)(2,1)}, bf16[2,160,512]{2,1,0:T(8,128)(2,1)S(1)}, u32[]{:S(2)}, u32[]{:S(2)}) collective-permute-start(bf16[2,160,512]{2,1,0:T(8,128)(2,1)} %get-tuple-element.175), channel_id=1, source_target_pairs={{0,2},{1,3},{2,0},{3,1},{4,6},{5,7},{6,4},{7,5},{8,10},{9,11},{10,... | collective-permute-start | bytes 983048 | tf_op jit(solution)/shard_map/ppermute | solution.py:22
  120.0 16.1 %collective-permute-start.22 = (bf16[2,160,512]{2,1,0:T(8,128)(2,1)S(1)}, bf16[2,160,512]{2,1,0:T(8,128)(2,1)S(1)}, u32[]{:S(2)}, u32[]{:S(2)}) collective-permute-start(bf16[2,160,512]{2,1,0:T(8,128)(2,1)S(1)} %copy-done.56), channel_id=1, source_target_pairs={{0,3},{1,2},{2,1},{3,0},{4,7},{5,6},{6,5},{7,4},{8,11},{9,10},{10,... | collective-permute-start | bytes 983048 | tf_op jit(solution)/shard_map/ppermute | solution.py:22
  136.1 10.2 %collective-permute-start.24 = (bf16[160,512]{1,0:T(8,128)(2,1)}, bf16[160,512]{1,0:T(8,128)(2,1)S(1)}, u32[]{:S(2)}, u32[]{:S(2)}) collective-permute-start(bf16[160,512]{1,0:T(8,128)(2,1)} %get-tuple-element.184), channel_id=1, source_target_pairs={{0,1},{1,0},{2,3},{3,2},{4,5},{5,4},{6,7},{7,6},{8,9},{9,8},{10,11... | collective-permute-start | bytes 491528 | tf_op jit(solution)/shard_map/ppermute | solution.py:22
  136.5 9.8 %collective-permute-start.25 = (bf16[160,512]{1,0:T(8,128)(2,1)}, bf16[160,512]{1,0:T(8,128)(2,1)}, u32[]{:S(2)}, u32[]{:S(2)}) collective-permute-start(bf16[160,512]{1,0:T(8,128)(2,1)} %get-tuple-element.185), channel_id=1, source_target_pairs={{0,2},{1,3},{2,0},{3,1},{4,6},{5,7},{6,4},{7,5},{8,10},{9,11},{10,... | collective-permute-start | bytes 491528 | tf_op jit(solution)/shard_map/ppermute | solution.py:22
  137.0 9.3 %collective-permute-start.26 = (bf16[160,512]{1,0:T(8,128)(2,1)}, bf16[160,512]{1,0:T(8,128)(2,1)}, u32[]{:S(2)}, u32[]{:S(2)}) collective-permute-start(bf16[160,512]{1,0:T(8,128)(2,1)} %get-tuple-element.186), channel_id=1, source_target_pairs={{0,3},{1,2},{2,1},{3,0},{4,7},{5,6},{6,5},{7,4},{8,11},{9,10},{10,... | collective-permute-start | bytes 491528 | tf_op jit(solution)/shard_map/ppermute | solution.py:22
  151.5 16.7 %collective-permute-start.30 = (bf16[4,160,512]{2,1,0:T(8,128)(2,1)S(1)}, bf16[4,160,512]{2,1,0:T(8,128)(2,1)S(1)}, u32[]{:S(2)}, u32[]{:S(2)}) collective-permute-start(bf16[4,160,512]{2,1,0:T(8,128)(2,1)S(1)} %copy-done.52), channel_id=1, source_target_pairs={{0,4},{4,0},{8,12},{12,8},{16,20},{20,16},{24,28},{28,24},{1,5},{5... | collective-permute-start | bytes 1966088 | tf_op jit(solution)/shard_map/ppermute | solution.py:22
  152.0 23.2 %collective-permute-start.31 = (bf16[512,512]{1,0:T(8,128)(2,1)S(1)}, bf16[512,512]{1,0:T(8,128)(2,1)S(1)}, u32[]{:S(2)}, u32[]{:S(2)}) collective-permute-start(bf16[512,512]{1,0:T(8,128)(2,1)S(1)} %get-tuple-element.193), channel_id=1, source_target_pairs={{0,8},{4,12},{8,0},{12,4},{16,24},{20,28},{24,16},{28,20},{1,9},{5... | collective-permute-start | bytes 1572872 | tf_op jit(solution)/shard_map/ppermute | solution.py:22
  153.5 22.3 %collective-permute-start.32 = (bf16[256,1024]{1,0:T(8,128)(2,1)S(1)}, bf16[256,1024]{1,0:T(8,128)(2,1)S(1)}, u32[]{:S(2)}, u32[]{:S(2)}) collective-permute-start(bf16[256,1024]{1,0:T(8,128)(2,1)S(1)} %copy-done.50), channel_id=1, source_target_pairs={{0,2},{1,3},{2,0},{3,1},{4,6},{5,7},{6,4},{7,5},{8,10},{9,11},{10,... | collective-permute-start | bytes 1572872 | tf_op jit(solution)/shard_map/ppermute | solution.py:22
  168.2 21.3 %collective-permute-start.34 = (bf16[256,1024]{1,0:T(8,128)(2,1)S(1)}, bf16[256,1024]{1,0:T(8,128)(2,1)S(1)}, u32[]{:S(2)}, u32[]{:S(2)}) collective-permute-start(bf16[256,1024]{1,0:T(8,128)(2,1)S(1)} %get-tuple-element.219), channel_id=1, source_target_pairs={{0,4},{4,0},{8,12},{12,8},{16,20},{20,16},{24,28},{28,24},{1,5},{5... | collective-permute-start | bytes 1572872 | tf_op jit(solution)/shard_map/ppermute | solution.py:22
  173.6 21.3 %collective-permute-start.37 = (bf16[256,1024]{1,0:T(8,128)(2,1)}, bf16[256,1024]{1,0:T(8,128)(2,1)S(1)}, u32[]{:S(2)}, u32[]{:S(2)}) collective-permute-start(bf16[256,1024]{1,0:T(8,128)(2,1)} %get-tuple-element.226), channel_id=1, source_target_pairs={{0,8},{4,12},{8,0},{12,4},{16,24},{20,28},{24,16},{28,20},{1,9},{5... | collective-permute-start | bytes 1572872 | tf_op jit(solution)/shard_map/ppermute | solution.py:22
  176.6 10.6 %collective-permute-start.33 = (bf16[128,1024]{1,0:T(8,128)(2,1)S(1)}, bf16[128,1024]{1,0:T(8,128)(2,1)S(1)}, u32[]{:S(2)}, u32[]{:S(2)}) collective-permute-start(bf16[128,1024]{1,0:T(8,128)(2,1)S(1)} %get-tuple-element.215), channel_id=1, source_target_pairs={{0,4},{4,0},{8,12},{12,8},{16,20},{20,16},{24,28},{28,24},{1,5},{5... | collective-permute-start | bytes 786440 | tf_op jit(solution)/shard_map/ppermute | solution.py:22
  178.2 14.5 %collective-permute-start.36 = (bf16[256,512]{1,0:T(8,128)(2,1)S(1)}, bf16[256,512]{1,0:T(8,128)(2,1)S(1)}, u32[]{:S(2)}, u32[]{:S(2)}) collective-permute-start(bf16[256,512]{1,0:T(8,128)(2,1)S(1)} %get-tuple-element.223), channel_id=1, source_target_pairs={{0,16},{4,20},{8,24},{12,28},{16,0},{20,4},{24,8},{28,12},{1,17},{... | collective-permute-start | bytes 786440 | tf_op jit(solution)/shard_map/ppermute | solution.py:22
  180.8 8.7 %collective-permute-start.35 = (f32[8,1024]{1,0:T(8,128)S(1)}, f32[8,1024]{1,0:T(8,128)S(1)}, u32[]{:S(2)}, u32[]{:S(2)}) collective-permute-start(f32[8,1024]{1,0:T(8,128)S(1)} %get-tuple-element.220.refs_0_), channel_id=1, source_target_pairs={{0,4},{4,0},{8,12},{12,8},{16,20},{20,16},{24,28},{28,24},{1,5},{5... | collective-permute-start | bytes 98312 | tf_op jit(solution)/shard_map/ppermute | solution.py:22
  196.2 9.7 %collective-permute-start.39 = (bf16[128,1024]{1,0:T(8,128)(2,1)S(1)}, bf16[128,1024]{1,0:T(8,128)(2,1)S(1)}, u32[]{:S(2)}, u32[]{:S(2)}) collective-permute-start(bf16[128,1024]{1,0:T(8,128)(2,1)S(1)} %get-tuple-element.232), channel_id=1, source_target_pairs={{0,2},{1,3},{2,0},{3,1},{4,6},{5,7},{6,4},{7,5},{8,10},{9,11},{10,... | collective-permute-start | bytes 786440 | tf_op jit(solution)/shard_map/ppermute | solution.py:22
  196.8 9.0 %collective-permute-start.40 = (f32[8,1024]{1,0:T(8,128)S(1)}, f32[8,1024]{1,0:T(8,128)S(1)}, u32[]{:S(2)}, u32[]{:S(2)}) collective-permute-start(f32[8,1024]{1,0:T(8,128)S(1)} %get-tuple-element.233.refs_0_), channel_id=1, source_target_pairs={{0,2},{1,3},{2,0},{3,1},{4,6},{5,7},{6,4},{7,5},{8,10},{9,11},{10,... | collective-permute-start | bytes 98312 | tf_op jit(solution)/shard_map/ppermute | solution.py:22
  198.3 21.7 %collective-permute-start.46 = (bf16[128,1024]{1,0:T(8,128)(2,1)S(1)}, bf16[128,1024]{1,0:T(8,128)(2,1)S(1)}, u32[]{:S(2)}, u32[]{:S(2)}) collective-permute-start(bf16[128,1024]{1,0:T(8,128)(2,1)S(1)} %get-tuple-element.243), channel_id=1, source_target_pairs={{0,16},{4,20},{8,24},{12,28},{16,0},{20,4},{24,8},{28,12},{1,17},{... | collective-permute-start | bytes 786440 | tf_op jit(solution)/shard_map/ppermute | solution.py:22
  202.4 19.1 %all-to-all-start = ((bf16[4,2,32,512]{3,2,1,0:T(8,128)(2,1)}), bf16[4,2,32,512]{3,2,1,0:T(8,128)(2,1)S(1)}, u32[]{:S(2)}, u32[]{:S(2)}) async-start(bf16[4,2,32,512]{3,2,1,0:T(8,128)(2,1)} %pad_maximum_fusion), calls=%async_computation | async-start | bytes 524288 | tf_op jit(solution)/shard_map/all_to_all | solution.py:890
  208.6 9.8 %collective-permute-start.45 = (bf16[32,1024]{1,0:T(8,128)(2,1)S(1)}, bf16[32,1024]{1,0:T(8,128)(2,1)S(1)}, u32[]{:S(2)}, u32[]{:S(2)}) collective-permute-start(bf16[32,1024]{1,0:T(8,128)(2,1)S(1)} %get-tuple-element.241), channel_id=1, source_target_pairs={{0,16},{4,20},{8,24},{12,28},{16,0},{20,4},{24,8},{28,12},{1,17},{... | collective-permute-start | bytes 196616 | tf_op jit(solution)/shard_map/ppermute | solution.py:22
  (74 other events, 511.9 us)

commit v2 on v1

--- a/solution.py
+++ b/solution.py
@@ -69,26 +69,23 @@
 
 
 class Scatter:
-    def __init__(self, own, both, order, plan, end, extra=None, name=None):
-        self.own, self.both, self.order, self.plan, self.end = own, both, order, plan, end
+    def __init__(self, own, both, lanes, end, extra=None, name=None):
+        self.own, self.both, self.lanes, self.end = own, both, lanes, end
         self.extra, self.name, self.at, self.open = extra, name, 0, False
+        self.steps = len(lanes[0][0])
 
     def begin(self, *others):
-        kept, sent = self.both
-        bit = self.order[self.at]
-        sent = after(sent, *others)
-        self.got = [swap(sent, *bit)]
-        if self.extra is not None:
-            self.got.append(swap(self.extra, *bit))
+        sent = after(tuple(self.both[1::2]), *others)
+        self.got = [swap(v, *order[self.at]) for v, (order, _) in zip(sent, self.lanes)]
         self.at, self.open = self.at + 1, True
 
     def finish(self, *others):
-        kept, self.open = self.both[0], False
+        kept, self.open = tuple(self.both[::2]), False
         if others:
             kept = after(kept, *others)
         nxt = None
-        if self.at < len(self.order):
-            nxt = (self.order[self.at], self.plan[self.at])
+        if self.at < self.steps:
+            nxt = [(order[self.at], plan[self.at]) for order, plan in self.lanes]
         values = fold(self.own, kept, self.got, self.extra, nxt, self.end, self.name)
         if self.extra is not None:
             self.extra = values[-1]
@@ -100,7 +97,7 @@
         return values[0]
 
     def run(self):
-        while self.open or self.at < len(self.order):
+        while self.open or self.at < self.steps:
             if not self.open:
                 self.begin()
             self.finish()
@@ -476,81 +473,77 @@
     sums[5:6] = sums_ff[1:2]
 
 
-def stack_kernel(*refs):
-    for k, ref in enumerate(refs[:-1]):
-        refs[-1][k] = ref[...].reshape(refs[-1].shape[1:])
-
-
-def stacked(blocks, second=False):
-    inner = blocks[0].shape[-2:]
-    specs = [
-        pl.BlockSpec((1,) + inner, lambda *_: (1, 0, 0)) if second and b.ndim == 3 else whole(b.shape) for b in blocks
-    ]
-    shape = (len(blocks),) + inner
-    return call(stack_kernel, (1,), specs, [(whole(shape), out(shape, BF16))], vmem=62, name="stack")(*blocks)[0]
-
-
-def outer_kernel(count, bit, inner, extra, own, *refs):
+def halved(values):
+    high = values.astype(BF16).astype(F32)
+    return jnp.concatenate([high, values - high], axis=0).astype(BF16)
+
+
+def joined(values):
+    values = values.astype(F32)
+    half = values.shape[0] // 2
+    return values[:half] + values[half:]
+
+
+def outer_kernel(count, lanes, own, *refs):
     lefts, rights, refs = refs[:count], refs[count : 2 * count], refs[2 * count :]
-    more, results, held = refs[:extra], refs[extra:-1], refs[-1]
-    width = held.shape[1]
+    results, held = refs[:-1], refs[-1]
 
     @pl.when(pl.program_id(0) == 0)
     def _():
         at = 0
         for ref in rights:
-            block = ref[...].reshape(-1, width)
-            held[at : at + block.shape[0], :] = block
-            at += block.shape[0]
+            rows, width = ref.shape[-2:]
+            for k in range(held.shape[1] // width):
+                held[at : at + rows, k * width : (k + 1) * width] = ref[k] if len(ref.shape) == 3 else ref[...]
+            at += rows
 
     left = jnp.concatenate([ref[...].reshape(-1, ref.shape[-1]) for ref in lefts], axis=0)
     product = dot(left, held[...], TN)
-    if bit is None:
-        results[0][...] = product.astype(BF16)
-        return
-    kept, sent = parted(product, inner, chosen(own, bit))
-    if extra:
-        rows = more[0].shape[1]
-        other = more[0][...].astype(F32).reshape(-1, more[0].shape[2])
-        kept_more, sent_more = parted(other, rows, chosen(own, bit))
-        join = lambda a, b: jnp.concatenate(
-            [a.reshape(-1, inner, width), b.reshape(-1, rows, width)], axis=1
-        ).reshape(-1, width)
-        kept, sent = join(kept, kept_more), join(sent, sent_more)
-    results[0][...] = kept.astype(BF16)
-    results[1][...] = sent.astype(BF16)
-
-
-def outer(own, lefts, rights, tile, name, bit=None, inner=0, more=None):
+    width = product.shape[1] // len(lanes)
+    for k, (bit, inner) in enumerate(lanes):
+        kept, sent = parted(product[:, k * width : (k + 1) * width], inner, chosen(own, bit))
+        results[2 * k][...] = kept.astype(BF16)
+        results[2 * k + 1][...] = sent.astype(BF16)
+
+
+def outer(own, lefts, rights, tile, lanes, name):
     count = len(lefts)
-    a, b = lefts[0].shape[-1], rights[0].shape[-1]
-
-    def block(values, width, moving):
-        lead = values.shape[:-1]
-        if len(lead) == 2 and lead[0] == 2:
-            lead = (1,) + lead[1:]
-        zeros = (0,) * len(lead)
-        return pl.BlockSpec(lead + (width,), lambda g, *_: zeros + (g if moving else 0,))
-
-    total = sum(math.prod(block(v, b, False).block_shape[:-1]) for v in rights)
-    steps = a // tile
-    rows, outs = a, 1
-    if bit is not None:
-        rows, outs = a // 2, 2
-    extra = []
-    if more is not None:
-        extra = [pl.BlockSpec((more.shape[0] // steps,) + more.shape[1:], lambda g, *_: (g, 0, 0))]
-        rows += more.shape[0] * more.shape[1] // 2
-    got = call(
-        functools.partial(outer_kernel, count, bit, inner, len(extra)),
+    wide = lambda v: v.shape[-1] * (v.shape[0] if v.ndim == 3 else 1)
+    a, b = wide(lefts[0]), wide(rights[0])
+
+    def left_spec(v):
+        if v.ndim == 3:
+            return pl.BlockSpec((1, v.shape[1], tile), lambda g, *_: (g, 0, 0))
+        return pl.BlockSpec((v.shape[0], tile), lambda g, *_: (0, g))
+
+    total = sum(v.shape[-2] for v in rights)
+    steps, part = a // tile, b // len(lanes)
+    spec = pl.BlockSpec((tile // 2, part), lambda g, *_: (g, 0))
+    return call(
+        functools.partial(outer_kernel, count, [(order[0], plan[0]) for order, plan in lanes]),
         (steps,),
-        [block(v, tile, True) for v in lefts] + [block(v, b, False) for v in rights] + extra,
-        [(pl.BlockSpec((rows // steps, b), lambda g, *_: (g, 0)), out((rows, b), BF16))] * outs,
+        [left_spec(v) for v in lefts] + [whole(v.shape) for v in rights],
+        [(spec, out((a // 2, part), BF16))] * (2 * len(lanes)),
         scratch=[pltpu.VMEM((total, b), BF16)],
-        prefetch=1,
-        name=name,
-    )(own, *lefts, *rights, *([more] if more is not None else []))
-    return got if bit is not None else got[0]
+        us=4, prefetch=1, name=name,
+    )(own, *lefts, *rights)
+
+
+def query_kernel(bit, rows, own, dq, lat_low, out_t, sums, kept, sent):
+    width = lat_low.shape[1]
+    which = chosen(own, bit)
+    other_rows = out_t.shape[1]
+    product = dot(dq[...], lat_low[...], TN)
+    first = parted(product, rows, which)
+    second = parted(out_t[...].astype(F32).reshape(-1, width), other_rows, which)
+    both = [
+        jnp.concatenate([a.reshape(-1, rows, width), b.reshape(-1, other_rows, width)], axis=1).reshape(-1, width)
+        for a, b in zip(first, second)
+    ]
+    head = 2 * sums.shape[0]
+    kept[...] = both[0].astype(BF16)
+    sent[:head, :] = halved(sums[...])
+    sent[head:, :] = both[1].astype(BF16)
 
 
 def side_by_side_kernel(rows, left, right, result):
@@ -559,40 +552,55 @@
     result[...] = jnp.concatenate([split[:, 0], split[:, 1]], axis=-1)
 
 
-def fold_kernel(nxt, end, extra, own, kept, got, *refs):
-    total = kept[...].astype(F32) + got[...].astype(F32)
+def fold_kernel(nxt, end, lanes, extra, own, *refs):
+    kept, got, refs = refs[:lanes], refs[lanes : 2 * lanes], refs[2 * lanes :]
+    head = 0
     if extra:
-        refs[-1][...] = refs[0][...] + refs[1][...]
-        refs = refs[2:-1]
+        more, refs = refs[0], refs[1:]
+        head = 2 * more.shape[0]
+        small = more[...] + joined(got[0][:head, :])
+        refs[-1][...] = small
+    totals = [a[...].astype(F32) + b[head:, :].astype(F32) for a, b in zip(kept, got)]
+    if nxt is None:
+        for ref, values in zip(refs, end(*totals)):
+            ref[...] = values.astype(ref.dtype)
+        return
+    for k, (total, (bit, inner)) in enumerate(zip(totals, nxt)):
+        keep, send = parted(total, inner, chosen(own, bit))
+        refs[2 * k][...] = keep.astype(BF16)
+        refs[2 * k + 1][head:, :] = send.astype(BF16)
+    if extra:
+        refs[1][:head, :] = halved(small)
+
+
+def fold(own, kept, got, extra, nxt, end, name):
+    ins = list(kept) + list(got)
     if nxt is not None:
-        bit, inner = nxt
-        keep, send = parted(total, inner, chosen(own, bit))
-        refs[0][...] = keep.astype(BF16)
-        refs[1][...] = send.astype(BF16)
-        return
-    for ref, values in zip(refs, end(total)):
-        ref[...] = values.astype(ref.dtype)
-
-
-def fold(own, kept, got, extra, nxt, end, name):
-    rows, width = kept.shape
-    ins = [kept, got[0]]
-    if nxt is not None:
-        shapes = [out((rows // 2, width), BF16)] * 2
+        head = 0 if extra is None else 2 * extra.shape[0]
+        shapes = []
+        for v in kept:
+            rows, width = v.shape
+            shapes += [out((rows // 2, width), BF16), out((head + rows // 2, width), BF16)]
     else:
-        shapes = jax.eval_shape(end, out(kept.shape, F32))
-        shapes = [out(s.shape, F32 if s.dtype == F32 else BF16) for s in shapes]
+        shapes = list(jax.eval_shape(end, *(out(v.shape, F32) for v in kept)))
     if extra is not None:
-        ins += [extra, got[1]]
-        shapes = shapes + [out(extra.shape, F32)]
+        ins.append(extra)
+        shapes.append(out(extra.shape, F32))
     return call(
-        functools.partial(fold_kernel, nxt, end, extra is not None),
+        functools.partial(fold_kernel, nxt, end, len(kept), extra is not None),
         (1,),
         [whole(v.shape) for v in ins],
         [(whole(s.shape), s) for s in shapes],
-        prefetch=1,
-        name=name,
+        us=1, prefetch=1, name=name,
     )(own, *ins)
+
+
+def place_kernel(block, parts, result):
+    peers, _, width = parts.shape
+    for p in range(peers):
+        for k in range(width // block):
+            at = (k * peers + p) * block
+            result[:, at : at + block] = parts[p, :, k * block : (k + 1) * block].astype(F32)
 
 
 def on_device(
@@ -624,11 +632,10 @@
         ],
         vmem=62, name="latent",
     )(counts, lat, out_grad.reshape(rows, width), gains, biases, w_query)
-    q_near = q_low
     qs = {0: q_low}
     bit = peers // 2
     qs[bit] = swap(q_low, "patch", bit)
-    dys = {0: dy}
+    dys = {0: dy, bit: swap(dy, "patch", bit)}
 
     group = slots // 2
     key_input, keyval = call(
@@ -650,7 +657,7 @@
         bit //= 2
         for j in list(qs):
             qs[j ^ bit] = swap(qs[j], "patch", bit)
-    qs = [qs[j] for j in range(peers)]
+    qs = [after(qs[0], dys[peers // 2])] + [qs[j] for j in range(1, peers)]
 
     pair = 2
     kv_block = leading((pair, keys, 2 * inner))
@@ -682,7 +689,7 @@
     )(*parts, lat, w_out, gains, biases)
     bit = peers // 2
     ffs = {0: ff_low, bit: swap(ff_low, "patch", bit)}
-    dys[bit] = swap(after(dy, ff_low), "patch", bit)
+    dys = spread({0: after(dy, ff_low), bit: after(dys[bit], ff_low)})
 
     halves = 2
     blocks = ff // (peers * halves * LANES)
@@ -690,10 +697,10 @@
     strided = chunk % LANES == 0
 
     def column(own, j, a, k):
-        p, y = own[0] ^ j, (own[1] % halves) ^ a
+        p, k = own[0] ^ j, a * blocks + k
         if strided:
-            return (((k // (chunk // LANES)) * halves + y) * peers + p) * (chunk // LANES) + k % (chunk // LANES)
-        return (p * halves + y) * blocks + k
+            return ((k // (chunk // LANES)) * peers + p) * (chunk // LANES) + k % (chunk // LANES)
+        return p * halves * blocks + k
 
     def weights(first, stride):
         ups = [
@@ -721,18 +728,11 @@
     )(own, ff_low, dy, *([w_up] * count), *([w_down] * count))
     ffs[peers // 2] = after(ffs[peers // 2], far[-1])
     ffs = spread(ffs)
-    ff_all = stacked(ffs)
-    ff_far = swap(ff_all, "img", 1)
-    dys[peers // 2] = after(dys[peers // 2], far[-1])
-    dys = spread(dys)
-    dy_all = stacked(dys)
-    dy_far = swap(dy_all, "img", 1)
-
-    def cross(values, *others):
-        values = after(tuple(values), *others)
+
+    def cross(values):
         return [swap(v, "patch", here + k) for k, v in enumerate(values)]
 
-    act_cross = cross(far[:1])
+    act_cross = cross(after(tuple(far[:here]), ffs[peers // 2]))
     near = call(
         functools.partial(feed_end_kernel, per_slot, count, here),
         (here, halves),
@@ -743,12 +743,11 @@
         + [(whole((rows + 4 * HEADS, inner)), out((rows + 4 * HEADS, inner), BF16)), (whole((2, width)), out((2, width), F32))],
         scratch=[pltpu.VMEM((rows, width), F32), pltpu.VMEM((rows, width), F32)],
         vmem=62, prefetch=1, name="feed_end",
-    )(own, counts, after(ff_low, ff_all, dy_all), dy, *([w_up] * count), *([w_down] * count),
+    )(own, counts, after(ff_low, *ffs[1:], *dys[1:]), dy, *([w_up] * count), *([w_down] * count),
       far[2 * here], far[2 * here + 1], hidden, attended, lse, w_out, gains)
     result, dhidden, dhid_low, datt_low, sums_ff = near[2 * here :]
     act_near, dpre_near = list(reversed(near[:here])), list(reversed(near[here : 2 * here]))
 
-    datt_low = after(datt_low, act_cross[0])
     das = {0: datt_low, peers // 2: swap(datt_low, "patch", peers // 2)}
     out_rows = width // shards // 2
     out_t = call(
@@ -758,11 +757,25 @@
         [(leading((shards // 2, out_rows, 2 * inner)), out((shards, out_rows, 2 * inner), BF16))],
         name="out_grad",
     )(after(dhid_low, datt_low), att_low)[0]
-    das[peers // 2] = after(das[peers // 2], out_t)
-    acts = act_near + act_cross
-    acts = [acts[0]] + [swap(acts[j], "patch", j) for j in range(1, here)] + list(acts[here:])
-    acts += [swap(after(far[k], das[peers // 2]), "patch", here + k) for k in range(1, here)]
+    near_swaps = lambda values: [values[0]] + [swap(values[j], "patch", j) for j in range(1, here)]
+
+    every = digits_of("img") + digits_of("patch")
+    ff_bits = digits_of("img")
+    ff_orders = [ff_bits[::-1], ff_bits[-2:] + ff_bits[:-2][::-1]]
+
+    def ff_lanes(rows):
+        return [(order, plan_of(rows, ff_bits, order)) for order in ff_orders]
+
+    acts = near_swaps(act_near) + act_cross
+    down_lanes = ff_lanes(width)
+    down_sum = Scatter(
+        own, outer(own, dys[:-1] + [after(dys[-1], out_t)], acts, width // 2, down_lanes, "down_grad"), down_lanes,
+        lambda *t: [jnp.concatenate(t, axis=1).astype(BF16)], name="down_fold",
+    )
+    down_sum.begin()
+    das[peers // 2] = after(das[peers // 2], *down_sum.both)
     das = spread(das)
+    dpres = near_swaps(dpre_near) + cross(after(tuple(far[here : 2 * here]), *down_sum.both))
 
     got = call(
         functools.partial(attend_back_kernel, peers, per_slot, scale),
@@ -771,29 +784,33 @@
         [(kv_block, out(keyval.shape, BF16))] + [(whole((rows, inner)), out((rows, inner), BF16))] * peers,
         scratch=[pltpu.VMEM((peers, padded, LANES), F32)],
         name="attend_back",
-    )(*qs, *das[:-1], after(das[-1], ff_far), keyval)
+    )(*qs, *das, keyval)
     dkv, dqs = got[0], got[1:]
-    dkv = after(dkv, dy_far, *acts)
-    act_all = stacked(acts, True)
-    act_far = swap(act_all, "img", 1)
-    dpres = dpre_near + [swap(after(far[here + k], dkv), "patch", here + k) for k in range(here)]
-    dpres = [dpres[0]] + [swap(dpres[j], "patch", j) for j in range(1, here)] + dpres[here:]
-
-    every = digits_of("img") + digits_of("patch")
+    dqs = [dqs[0]] + [swap(dqs[j], "patch", j) for j in range(1, peers)]
+
     low_bit, both = [("patch", 1)], [("patch", 2), ("img", 1)]
     last = [bit for bit in reversed(every) if bit not in low_bit + both]
     kv_order, qo_order = low_bit + both + last, low_bit + both[::-1] + last
-    kv_plan = plan_of(2 * inner, every, kv_order)
-    q_plan, qo_plan = plan_of(inner, every, qo_order), plan_of(2 * inner, every, qo_order)
+    kv_lanes = [(kv_order, plan_of(2 * inner, every, kv_order))]
     kv_sum = Scatter(
         own,
-        outer(
-            own, [after(dkv, act_all).reshape(-1, 2 * inner)], [key_input.reshape(-1, width)], 2 * inner // 4,
-            "keyval_grad", kv_order[0], kv_plan[0],
-        ),
-        kv_order, kv_plan, lambda t: [flipped(t)], name="keyval_fold",
+        outer(own, [dkv.reshape(-1, 2 * inner)], [key_input.reshape(-1, width)], 2 * inner // 4, kv_lanes, "keyval_grad"),
+        kv_lanes, lambda t: [t], name="keyval_fold",
     )
     kv_sum.begin()
+    mark = down_sum.finish(*kv_sum.both)
+    down_sum.begin()
+    up_lanes = ff_lanes(halves * part)
+
+    def up_end(*totals):
+        total = jnp.concatenate(totals, axis=1)
+        return [flipped(total)] if strided else [total.astype(BF16)]
+
+    up_sum = Scatter(
+        own, outer(own, dpres[:-1] + [after(dpres[-1], mark)], ffs, part, up_lanes, "up_grad"), up_lanes, up_end,
+        name="up_fold",
+    )
+    up_sum.begin()
 
     media_grad, dlat, sums_media = call(
         keyval_back_kernel,
@@ -808,23 +825,11 @@
             (whole((2, width)), out((2, width), F32)),
         ],
         name="keyval_back",
-    )(media, after(dkv, *kv_sum.both), w_keyval, gains)
-    dpres = list(after(tuple(dpres), kv_sum.finish(media_grad)))
-    dqs = [dqs[0]] + [swap(v, "patch", j + 1) for j, v in enumerate(after(tuple(dqs[1:]), *dpres))]
-    dpre_all = stacked(after(tuple(dpres), act_far), True)
-    dpre_far = swap(dpre_all, "img", 1)
-
-    rest = [("img", 1 << k) for k in range(1, log2(n_img))]
-    rest_digits = rest[::-1]
-    down_order, down_plan = rest + [("img", 1)], plan_of(width, rest_digits + [("img", 1)], rest + [("img", 1)])
-    down_sum = Scatter(
-        own,
-        outer(own, dys + [dy_far], acts + [after(act_far, dpre_all)], width // 2, "down_grad", down_order[0], down_plan[0]),
-        down_order, down_plan, None, name="down_fold",
-    )
+    )(media, after(dkv, *up_sum.both), w_keyval, gains)
+    mark = down_sum.finish(media_grad)
     down_sum.begin()
-    dqs = [dqs[0]] + list(after(tuple(dqs[1:]), *down_sum.both))
-    kv_sum.begin(*dqs)
+    mark = kv_sum.finish(mark)
+    kv_sum.begin()
 
     dq_low, latent_grad, sums = call(
         functools.partial(latent_back_kernel, peers),
@@ -837,72 +842,62 @@
             (whole((HEADS, width)), out((HEADS, width), F32)),
         ],
         name="latent_back",
-    )(*dqs, dlat, lat, dhidden, w_query, gains, sums_media, sums_ff)
+    )(*dqs, after(dlat, mark), lat, dhidden, w_query, gains, sums_media, sums_ff)
 
     q_rows = inner // shards
 
     def open_rows(total):
         other = total[q_rows:]
-        other = jnp.concatenate([other[:, :inner], other[:, inner:]], axis=0)
-        return [flipped(total[:q_rows]), flipped(other)]
-
-    qo_sum = Scatter(
-        own,
-        outer(own, [dq_low], [lat_low], inner // 2, "query_grad", qo_order[0], q_plan[0], more=out_t),
-        qo_order, qo_plan, open_rows, extra=sums, name="query_fold",
-    )
+        return [total[:q_rows], jnp.concatenate([other[:, :inner], other[:, inner:]], axis=0)]
+
+    q_plan, qo_plan = plan_of(inner, every, qo_order), plan_of(2 * inner, every, qo_order)
+    head = 2 * sums.shape[0]
+    qo_both = call(
+        functools.partial(query_kernel, qo_order[0], q_plan[0]),
+        (1,),
+        [whole(v.shape) for v in (dq_low, lat_low, out_t, sums)],
+        [(whole((inner, width)), out((inner, width), BF16)), (whole((head + inner, width)), out((head + inner, width), BF16))],
+        prefetch=1, name="query_grad",
+    )(own, dq_low, lat_low, out_t, sums)
+    qo_sum = Scatter(own, qo_both, [(qo_order, qo_plan)], open_rows, extra=sums, name="query_fold")
     qo_sum.begin()
-    mark = qo_sum.finish()
-    qo_sum.begin(dpre_far)
-    up_plan = plan_of(part, rest_digits, rest)
-    up_sum = Scatter(
-        own,
-        outer(own, dpres + [after(dpre_far, mark)], ffs + [ff_far], part // 2, "up_grad", rest[0], up_plan[0]),
-        rest, up_plan, lambda t: [flipped(t)] if strided else [t.astype(BF16)], name="up_fold",
-    )
-    up_sum.begin()
-    mark = up_sum.both[0]
-    for one in (down_sum, kv_sum, kv_sum, qo_sum, down_sum, up_sum, kv_sum, qo_sum):
+
+    mark = qo_sum.both[0]
+    if down_sum.steps == down_sum.at:
+        mark = down_sum.finish(mark)
+    for one in (qo_sum, up_sum, kv_sum, up_sum, qo_sum, kv_sum, qo_sum, kv_sum, qo_sum):
         mark = one.finish(mark)
-        one.begin()
+        if one.at < one.steps:
+            one.begin()
+    (up_sum,) = up_sum.run()
     (kv_sum,) = kv_sum.run()
-    (up_sum,) = up_sum.run()
     q_sum, out_sum = qo_sum.run()
+    (down,) = down_sum.run()
     small = lax.dynamic_slice_in_dim(
         qo_sum.extra, (own[1] * peers + own[0]) * (width // shards), width // shards, axis=1
     )
     if not strided:
-        have = lambda i, p: (p * halves + i % 2) * (n_img // 2) + i // 2
-        up_sum = lax.ppermute(
-            up_sum, ("img", "patch"), [(i * peers + p, have(i, p)) for i in range(n_img) for p in range(peers)]
-        )
-        up_sum = up_sum.astype(F32).T
-    up_grad = up_sum
-
-    while down_sum.at < len(down_sum.order):
-        down_sum.finish()
-        down_sum.begin()
-
-    kept, other = down_sum.both[0], down_sum.got[0]
-    kept, other = (v.reshape(peers, -1, part) for v in (kept, other))
-    odd = own[1] % 2 == 1
-    both = jnp.stack([jnp.where(odd, other, kept), jnp.where(odd, kept, other)], axis=1)
-    both = lax.all_to_all(both, "patch", 0, 0, tiled=True)
-    if strided:
-        both = both.reshape(peers, 2, -1, n_img // 2, chunk).transpose(3, 1, 0, 4, 2)
-    else:
-        both = both.transpose(0, 1, 3, 2)
-    down_grad = both.reshape(ff, width // shards).astype(F32)
+        pairs = [((b % n_img) * peers + b // n_img, b) for b in range(shards)]
+        up_sum = lax.ppermute(up_sum, ("img", "patch"), pairs).astype(F32).T
+
+    down = lax.all_to_all(down.reshape(peers, -1, halves * part), "patch", 0, 0, tiled=True)
+    down_t = call(
+        functools.partial(place_kernel, chunk if strided else halves * part),
+        (1,),
+        [whole(down.shape)],
+        [(whole((width // shards, ff)), out((width // shards, ff), F32))],
+        name="down_place",
+    )(down)[0]
 
     return (
         result.reshape(slots, per_slot, width),
         media_grad,
         latent_grad.reshape(slots, per_slot, width),
-        q_sum,
-        kv_sum,
-        out_sum,
-        up_grad,
-        down_grad,
+        q_sum.T,
+        kv_sum.T,
+        out_sum.T,
+        up_sum,
+        down_t.T,
         small[:3],
         small[3:6],
     )

time: 227 us -> 207 us (0.912)
  local copies, waits for them, and re-layouts: 22.3 us -> 9.86 us
  Pallas kernels: 83.2 us -> 74.1 us
  starting transfers between devices: 47.8 us -> 50.2 us
    unnamed x117 -> x86, local copies, waits for them, and re-layouts: 20.1 us -> 9.2 us
    pallas_call x22 -> x21, Pallas kernels: 34.2 us -> 28.1 us  [the longest x16 14 us: fold(): call(functools.partial(fold_kernel, nxt, end, len(kept), extra is not Non...]
    ppermute x48 -> x46, starting transfers between devices: 44.4 us -> 46.8 us  [swap(): return lax.ppermute(values, axis, [(k, k ^ bit) for k in range(n)])]
    ppermute x48 -> x46, waiting for transfers between devices: 70.3 us -> 70.2 us  [swap(): return lax.ppermute(values, axis, [(k, k ^ bit) for k in range(n)])]
  transfers between devices with their start and end apart: 49 -> 47, of which waited for: 14 -> 15; matrix products, arithmetic and copies ran while one was open for 2% -> 0% of each run, Pallas kernels for 29% -> 24%
where the time goes in v2:
time: 207 us; the launch traced here: 206 us
  Pallas kernels  74.1 us (36%)
  waiting for transfers between devices  70.2 us (34%)
  starting transfers between devices  50.2 us (24%)
  local copies, waits for them, and re-layouts  9.86 us (5%)
    ppermute x46, waiting for transfers between devices, swap(): return lax.ppermute(values, axis, [(k, k ^ bit) for k in range(n)])  70.2 us
    ppermute x46, starting transfers between devices, swap(): return lax.ppermute(values, axis, [(k, k ^ bit) for k in range(n)])  46.8 us
    pallas_call x16, Pallas kernels, fold(): call(functools.partial(fold_kernel, nxt, end, len(kept), extra is not Non...  14 us
    pallas_call x1, Pallas kernels, on_device(): call(functools.partial(feed_end_kernel, per_slot, count, here), (here, ha...  12.1 us
    pallas_call x3, Pallas kernels, outer(): call(functools.partial(outer_kernel, count, [(order[0], plan[0]) for orde...  11.8 us
    pallas_call x1, Pallas kernels, on_device(): call(functools.partial(feed_kernel, count, here), (here, halves), [whole(...  9.54 us
    unnamed x86, local copies, waits for them, and re-layouts  9.2 us
    pallas_call x1, Pallas kernels, on_device(): call(functools.partial(attend_back_kernel, peers, per_slot, scale), (slot...  5.67 us
  transfers between devices with their start and end apart: 47, of which 15 were waited for; matrix products, arithmetic and copies ran while one was open for 0% of the time, Pallas kernels for 24%

profile of v2, /device:TPU:0, one launch (start us, length us, event | category | flops | bytes accessed | tf_op | source)
XLA Modules:
  0.0 206.2 jit_solution(15059512493666380791)
XLA Ops:
  0.7 2.8 %latent.1 = (bf16[160,1024]{1,0:T(8,128)(2,1)}, bf16[160,512]{1,0:T(8,128)(2,1)}, bf16[160,1024]{1,0:T(8,128)(2,1)}) custom-call(s32[2]{0:T(128)} %counts.3, bf16[160,1024]{1,0:T(8,128)(2,1)} %bitcast.14, bf16[160,1024]{1,0:T(8,128)(2,1)} %bitcast.19, f32[3,1024]{1,0:T(4,128)} %refs_8_.1, f32[3,1024]{1,0:T(4,128)} %refs_7_.4, bf16[1024,512]{1,0:T(8,128)(2,1)} %refs_7_.7), custom_call_target="tpu_custom_call" | custom-call | bytes 200000 | tf_op jit(solution)/shard_map/latent/pallas_call | solution.py:624
  3.5 3.0 %collective-permute-start.2 = (bf16[160,512]{1,0:T(8,128)(2,1)}, bf16[160,512]{1,0:T(8,128)(2,1)S(1)}, u32[]{:S(2)}, u32[]{:S(2)}) collective-permute-start(bf16[160,512]{1,0:T(8,128)(2,1)} %get-tuple-element.149.refs_0_), channel_id=1, source_target_pairs={{0,2},{1,3},{2,0},{3,1},{4,6},{5,7},{6,4},{7,5},{8,10},{9,11},{10,... | collective-permute-start | bytes 491528 | tf_op jit(solution)/shard_map/ppermute | solution.py:22
  10.4 2.7 %media.3 = (bf16[10,80,1024]{2,1,0:T(8,128)(2,1)S(1)}, bf16[10,80,1024]{2,1,0:T(8,128)(2,1)S(1)}) custom-call(bf16[10,64,1024]{2,1,0:T(8,128)(2,1)S(1)} %copy-done.2, bf16[160,1024]{1,0:T(8,128)(2,1)S(1)} %copy-done.11, f32[3,1024]{1,0:T(4,128)S(1)} %copy-done.22, f32[3,1024]{1,0:T(4,128)S(1)} %copy-done.35, bf16[1024,1024]{1,0:T(8,128)(2,1)S(1)} %copy-done), custom_call_target="tpu_custom_call" | custom-call | bytes 200000 | tf_op jit(solution)/shard_map/media/pallas_call | solution.py:641
  14.8 3.1 %collective-permute-done.refs_2_ = bf16[160,1024]{1,0:T(8,128)(2,1)S(1)} collective-permute-done((bf16[160,1024]{1,0:T(8,128)(2,1)}, bf16[160,1024]{1,0:T(8,128)(2,1)S(1)}, u32[]{:S(2)}, u32[]{:S(2)}) %collective-permute-start) | collective-permute-done | bytes 327712 | tf_op jit(solution)/shard_map/ppermute | solution.py:22
  17.9 3.0 %attend.1 = (bf16[176,512]{1,0:T(8,128)(2,1)S(1)}, bf16[176,512]{1,0:T(8,128)(2,1)S(1)}, bf16[176,512]{1,0:T(8,128)(2,1)S(1)}, bf16[176,512]{1,0:T(8,128)(2,1)S(1)}) custom-call(bf16[160,512]{1,0:T(8,128)(2,1)S(1)} %copy-done.13, bf16[160,512]{1,0:T(8,128)(2,1)S(1)} %collective-permute-done.1.refs_1_, bf16[160,512]{1,0:T(8,128)(2,1)S(1)} %collective-permute-done.2.refs_2_, ...), custom_call_target="tpu_custom_call" | custom-call | bytes 200000 | tf_op jit(solution)/shard_map/attend/pallas_call | solution.py:666
  21.7 1.8 collective-permute-start.5
  23.6 5.6 %collective-permute-done.5.refs_2_ = bf16[176,512]{1,0:T(8,128)(2,1)S(1)} collective-permute-done((bf16[176,512]{1,0:T(8,128)(2,1)S(1)}, bf16[176,512]{1,0:T(8,128)(2,1)S(1)}, u32[]{:S(2)}, u32[]{:S(2)}) %collective-permute-start.5) | collective-permute-done | bytes 180256 | tf_op jit(solution)/shard_map/ppermute | solution.py:22
  29.2 2.8 %collective-permute-done.6.refs_3_ = bf16[176,512]{1,0:T(8,128)(2,1)S(1)} collective-permute-done((bf16[176,512]{1,0:T(8,128)(2,1)S(1)}, bf16[176,512]{1,0:T(8,128)(2,1)S(1)}, u32[]{:S(2)}, u32[]{:S(2)}) %collective-permute-start.6) | collective-permute-done | bytes 180256 | tf_op jit(solution)/shard_map/ppermute | solution.py:22
  32.7 3.8 %mix.1 = (f32[160,512]{1,0:T(8,128)}, bf16[160,512]{1,0:T(8,128)(2,1)}, f32[160,1024]{1,0:T(8,128)}, bf16[160,1024]{1,0:T(8,128)(2,1)}, f32[8,256]{1,0:T(8,128)}) custom-call(bf16[176,512]{1,0:T(8,128)(2,1)} %copy-done.33, bf16[176,512]{1,0:T(8,128)(2,1)} %copy-done.37, bf16[176,512]{1,0:T(8,128)(2,1)} %copy-done.38, bf16[176,512]{1,0:T(8,128)(2,1)} %copy-done.39, ...), custom_call_target="tpu_custom_call" | custom-call | bytes 200000 | tf_op jit(solution)/shard_map/mix/pallas_call | solution.py:676
  39.4 9.5 %feed.1 = (bf16[2,160,512]{2,1,0:T(8,128)(2,1)}, bf16[2,160,512]{2,1,0:T(8,128)(2,1)}, bf16[2,160,512]{2,1,0:T(8,128)(2,1)}, bf16[2,160,512]{2,1,0:T(8,128)(2,1)...) custom-call(s32[2]{0:T(128)} %pad_add_fusion.own, bf16[160,1024]{1,0:T(8,128)(2,1)} %get-tuple-element.162.ff_low.refs_4_, ...), custom_call_target="tpu_custom_call" | custom-call | bytes 200000 | tf_op jit(solution)/shard_map/feed/pallas_call | solution.py:722
  51.7 12.1 %feed_end.1 = (bf16[2,160,512]{2,1,0:T(8,128)(2,1)}, bf16[2,160,512]{2,1,0:T(8,128)(2,1)}, bf16[2,160,512]{2,1,0:T(8,128)(2,1)}, bf16[2,160,512]{2,1,0:T(8,128)(...) custom-call(s32[2]{0:T(128)} %pad_add_fusion.own, ...), custom_call_target="tpu_custom_call" | custom-call | bytes 200000 | tf_op jit(solution)/shard_map/feed_end/pallas_call | solution.py:736
  67.7 4.0 %down_grad.1 = (bf16[512,512]{1,0:T(8,128)(2,1)S(1)}, bf16[512,512]{1,0:T(8,128)(2,1)S(1)}, bf16[512,512]{1,0:T(8,128)(2,1)S(1)}, bf16[512,512]{1,0:T(8,128)(2,1)S(1)}) custom-call(s32[2]{0:T(128)S(1)} %copy-done.31, bf16[160,1024]{1,0:T(8,128)(2,1)S(1)} %copy-done.7, bf16[160,1024]{1,0:T(8,128)(2,1)} %collective-permute-done.10.refs_1_, ...), custom_call_target="tpu_custom_call" | custom-call | bytes 400000 | tf_op jit(solution)/shard_map/down_grad/pallas_call | solution.py:522
  73.4 5.7 %attend_back.1 = (bf16[10,80,1024]{2,1,0:T(8,128)(2,1)S(1)}, bf16[160,512]{1,0:T(8,128)(2,1)S(1)}, bf16[160,512]{1,0:T(8,128)(2,1)S(1)}, bf16[160,512]{1,0:T(8,128)(2,1)S(1)}, bf16[160,512]{1,0:T(8,128)(2,1)S(1)}) custom-call(bf16[160,512]{1,0:T(8,128)(2,1)S(1)} %copy-done.14, bf16[160,512]{1,0:T(8,128)(2,1)S(1)} %copy-done.18, ...), custom_call_target="tpu_custom_call" | custom-call | bytes 200000 | tf_op jit(solution)/shard_map/attend_back/pallas_call | solution.py:780
  79.1 3.9 %keyval_grad.1 = (bf16[512,1024]{1,0:T(8,128)(2,1)S(1)}, bf16[512,1024]{1,0:T(8,128)(2,1)S(1)}) custom-call(s32[2]{0:T(128)S(1)} %copy-done.31, bf16[800,1024]{1,0:T(8,128)(2,1)S(1)} %bitcast.13, bf16[800,1024]{1,0:T(8,128)(2,1)S(1)} %bitcast.17), custom_call_target="tpu_custom_call" | custom-call | bytes 400000 | tf_op jit(solution)/shard_map/keyval_grad/pallas_call | solution.py:522
  83.5 1.8 collective-permute-start.21
  88.4 9.1 %collective-permute-done.21.refs_2_ = bf16[512,512]{1,0:T(8,128)(2,1)S(1)} collective-permute-done((bf16[512,512]{1,0:T(8,128)(2,1)S(1)}, bf16[512,512]{1,0:T(8,128)(2,1)S(1)}, u32[]{:S(2)}, u32[]{:S(2)}) %collective-permute-start.21) | collective-permute-done | bytes 524320 | tf_op jit(solution)/shard_map/ppermute | solution.py:22
  102.8 4.4 %collective-permute-done.20.refs_3_ = bf16[2,160,512]{2,1,0:T(8,128)(2,1)S(1)} collective-permute-done((bf16[2,160,512]{2,1,0:T(8,128)(2,1)S(1)}, bf16[2,160,512]{2,1,0:T(8,128)(2,1)S(1)}, u32[]{:S(2)}, u32[]{:S(2)}) %collective-permute-start.20) | collective-permute-done | bytes 327712 | tf_op jit(solution)/shard_map/ppermute | solution.py:22
  109.0 3.9 %up_grad.1 = (bf16[512,512]{1,0:T(8,128)(2,1)S(1)}, bf16[512,512]{1,0:T(8,128)(2,1)S(1)}, bf16[512,512]{1,0:T(8,128)(2,1)S(1)}, bf16[512,512]{1,0:T(8,128)(2,1)S(1)}) custom-call(s32[2]{0:T(128)S(1)} %copy-done.31, bf16[2,160,512]{2,1,0:T(8,128)(2,1)S(1)} %copy-done.29, bf16[2,160,512]{2,1,0:T(8,128)(2,1)S(1)} %collective-permute-done.18.refs_1_, ...), custom_call_target="tpu_custom_call" | custom-call | bytes 400000 | tf_op jit(solution)/shard_map/up_grad/pallas_call | solution.py:522
  112.9 4.0 %keyval_back.1 = (bf16[10,64,1024]{2,1,0:T(8,128)(2,1)}, f32[160,1024]{1,0:T(8,128)S(1)}, f32[2,1024]{1,0:T(2,128)S(1)}) custom-call(bf16[10,64,1024]{2,1,0:T(8,128)(2,1)S(1)} %copy-done.3, bf16[10,80,1024]{2,1,0:T(8,128)(2,1)S(1)} %get-tuple-element.204.dkv, bf16[1024,1024]{1,0:T(8,128)(2,1)S(1)} %copy-done.1, f32[3,1024]{1,0:T(4,128)S(1)} %copy-done.23), custom_call_target="tpu_custom_call" | custom-call | bytes 200000 | tf_op jit(solution)/shard_map/keyval_back/pallas_call | solution.py:815
  122.0 1.9 collective-permute-start.32
  125.5 2.6 %collective-permute-start.29 = (bf16[128,512]{1,0:T(8,128)(2,1)S(1)}, bf16[128,512]{1,0:T(8,128)(2,1)S(1)}, u32[]{:S(2)}, u32[]{:S(2)}) collective-permute-start(bf16[128,512]{1,0:T(8,128)(2,1)S(1)} %get-tuple-element.234), channel_id=1, source_target_pairs={{0,16},{4,20},{8,24},{12,28},{16,0},{20,4},{24,8},{28,12},{1,17},{... | collective-permute-start | bytes 393224 | tf_op jit(solution)/shard_map/ppermute | solution.py:22
  128.5 12.2 %collective-permute-done.29.refs_2_ = bf16[128,512]{1,0:T(8,128)(2,1)S(1)} collective-permute-done((bf16[128,512]{1,0:T(8,128)(2,1)S(1)}, bf16[128,512]{1,0:T(8,128)(2,1)S(1)}, u32[]{:S(2)}, u32[]{:S(2)}) %collective-permute-start.29) | collective-permute-done | bytes 131104 | tf_op jit(solution)/shard_map/ppermute | solution.py:22
  147.0 3.6 %collective-permute-start.35 = (bf16[256,512]{1,0:T(8,128)(2,1)S(1)}, bf16[256,512]{1,0:T(8,128)(2,1)S(1)}, u32[]{:S(2)}, u32[]{:S(2)}) collective-permute-start(bf16[256,512]{1,0:T(8,128)(2,1)S(1)} %get-tuple-element.252), channel_id=1, source_target_pairs={{0,8},{4,12},{8,0},{12,4},{16,24},{20,28},{24,16},{28,20},{1,9},{5... | collective-permute-start | bytes 786440 | tf_op jit(solution)/shard_map/ppermute | solution.py:22
  152.1 5.5 %collective-permute-done.34.refs_1_ = bf16[256,1024]{1,0:T(8,128)(2,1)S(1)} collective-permute-done((bf16[256,1024]{1,0:T(8,128)(2,1)S(1)}, bf16[256,1024]{1,0:T(8,128)(2,1)S(1)}, u32[]{:S(2)}, u32[]{:S(2)}) %collective-permute-start.34) | collective-permute-done | bytes 524320 | tf_op jit(solution)/shard_map/ppermute | solution.py:22
  158.2 5.4 %collective-permute-done.36.refs_3_ = bf16[256,512]{1,0:T(8,128)(2,1)S(1)} collective-permute-done((bf16[256,512]{1,0:T(8,128)(2,1)S(1)}, bf16[256,512]{1,0:T(8,128)(2,1)S(1)}, u32[]{:S(2)}, u32[]{:S(2)}) %collective-permute-start.36) | collective-permute-done | bytes 262176 | tf_op jit(solution)/shard_map/ppermute | solution.py:22
  166.7 5.9 %collective-permute-done.38.refs_1_ = bf16[128,1024]{1,0:T(8,128)(2,1)S(1)} collective-permute-done((bf16[128,1024]{1,0:T(8,128)(2,1)S(1)}, bf16[128,1024]{1,0:T(8,128)(2,1)S(1)}, u32[]{:S(2)}, u32[]{:S(2)}) %collective-permute-start.38) | collective-permute-done | bytes 262176 | tf_op jit(solution)/shard_map/ppermute | solution.py:22
  173.8 3.6 %collective-permute-start.41 = (bf16[80,1024]{1,0:T(8,128)(2,1)S(1)}, bf16[80,1024]{1,0:T(8,128)(2,1)S(1)}, u32[]{:S(2)}, u32[]{:S(2)}) collective-permute-start(bf16[80,1024]{1,0:T(8,128)(2,1)S(1)} %get-tuple-element.270), channel_id=1, source_target_pairs={{0,8},{4,12},{8,0},{12,4},{16,24},{20,28},{24,16},{28,20},{1,9},{5... | collective-permute-start | bytes 491528 | tf_op jit(solution)/shard_map/ppermute | solution.py:22
  177.5 3.4 %all-to-all-start = ((bf16[4,32,1024]{2,1,0:T(8,128)(2,1)}), bf16[4,32,1024]{2,1,0:T(8,128)(2,1)S(1)}, u32[]{:S(2)}, u32[]{:S(2)}) async-start(bf16[4,32,1024]{2,1,0:T(8,128)(2,1)} %bitcast.11), calls=%async_computation | async-start | bytes 524288 | tf_op jit(solution)/shard_map/all_to_all | solution.py:883
  180.9 1.9 collective-permute-start.44
  185.1 1.9 collective-permute-start.42
  188.9 8.4 %collective-permute-done.44.refs_2_ = bf16[128,512]{1,0:T(8,128)(2,1)S(1)} collective-permute-done((bf16[128,512]{1,0:T(8,128)(2,1)S(1)}, bf16[128,512]{1,0:T(8,128)(2,1)S(1)}, u32[]{:S(2)}, u32[]{:S(2)}) %collective-permute-start.44) | collective-permute-done | bytes 131104 | tf_op jit(solution)/shard_map/ppermute | solution.py:22
  197.4 2.8 %collective-permute-done.45.refs_3_ = bf16[128,512]{1,0:T(8,128)(2,1)S(1)} collective-permute-done((bf16[128,512]{1,0:T(8,128)(2,1)S(1)}, bf16[128,512]{1,0:T(8,128)(2,1)S(1)}, u32[]{:S(2)}, u32[]{:S(2)}) %collective-permute-start.45) | collective-permute-done | bytes 131104 | tf_op jit(solution)/shard_map/ppermute | solution.py:22
  (182 shorter events, 58.8 us)
Async XLA Ops:
  3.5 10.8 %collective-permute-start.2 = (bf16[160,512]{1,0:T(8,128)(2,1)}, bf16[160,512]{1,0:T(8,128)(2,1)S(1)}, u32[]{:S(2)}, u32[]{:S(2)}) collective-permute-start(bf16[160,512]{1,0:T(8,128)(2,1)} %get-tuple-element.149.refs_0_), channel_id=1, source_target_pairs={{0,2},{1,3},{2,0},{3,1},{4,6},{5,7},{6,4},{7,5},{8,10},{9,11},{10,... | collective-permute-start | bytes 491528 | tf_op jit(solution)/shard_map/ppermute | solution.py:22
  6.5 11.4 %collective-permute-start = (bf16[160,1024]{1,0:T(8,128)(2,1)}, bf16[160,1024]{1,0:T(8,128)(2,1)S(1)}, u32[]{:S(2)}, u32[]{:S(2)}) collective-permute-start(bf16[160,1024]{1,0:T(8,128)(2,1)} %get-tuple-element.160.dy.refs_0_), channel_id=1, source_target_pairs={{0,2},{1,3},{2,0},{3,1},{4,6},{5,7},{6,4},{7,5},{8,10},{9,11},{10,... | collective-permute-start | bytes 983048 | tf_op jit(solution)/shard_map/ppermute | solution.py:22
  6.5 11.4 %collective-permute-start.1 = (bf16[160,512]{1,0:T(8,128)(2,1)}, bf16[160,512]{1,0:T(8,128)(2,1)S(1)}, u32[]{:S(2)}, u32[]{:S(2)}) collective-permute-start(bf16[160,512]{1,0:T(8,128)(2,1)} %get-tuple-element.149.refs_0_), channel_id=1, source_target_pairs={{0,1},{1,0},{2,3},{3,2},{4,5},{5,4},{6,7},{7,6},{8,9},{9,8},{10,11... | collective-permute-start | bytes 491528 | tf_op jit(solution)/shard_map/ppermute | solution.py:22
  36.5 12.5 %collective-permute-start.8 = (bf16[160,1024]{1,0:T(8,128)(2,1)}, bf16[160,1024]{1,0:T(8,128)(2,1)}, u32[]{:S(2)}, u32[]{:S(2)}) collective-permute-start(bf16[160,1024]{1,0:T(8,128)(2,1)} %get-tuple-element.162.ff_low.refs_4_), channel_id=1, source_target_pairs={{0,2},{1,3},{2,0},{3,1},{4,6},{5,7},{6,4},{7,5},{8,10},{9,11},{10,... | collective-permute-start | bytes 983048 | tf_op jit(solution)/shard_map/ppermute | solution.py:22
  38.8 12.1 %collective-permute-start.7 = (bf16[160,1024]{1,0:T(8,128)(2,1)}, bf16[160,1024]{1,0:T(8,128)(2,1)}, u32[]{:S(2)}, u32[]{:S(2)}) collective-permute-start(bf16[160,1024]{1,0:T(8,128)(2,1)} %get-tuple-element.162.ff_low.refs_4_), channel_id=1, source_target_pairs={{0,1},{1,0},{2,3},{3,2},{4,5},{5,4},{6,7},{7,6},{8,9},{9,8},{10,11... | collective-permute-start | bytes 983048 | tf_op jit(solution)/shard_map/ppermute | solution.py:22
  38.9 10.8 %collective-permute-start.10 = (bf16[160,1024]{1,0:T(8,128)(2,1)S(1)}, bf16[160,1024]{1,0:T(8,128)(2,1)}, u32[]{:S(2)}, u32[]{:S(2)}) collective-permute-start(bf16[160,1024]{1,0:T(8,128)(2,1)S(1)} %copy-done.6), channel_id=1, source_target_pairs={{0,1},{1,0},{2,3},{3,2},{4,5},{5,4},{6,7},{7,6},{8,9},{9,8},{10,11... | collective-permute-start | bytes 983048 | tf_op jit(solution)/shard_map/ppermute | solution.py:22
  39.4 11.6 %collective-permute-start.11 = (bf16[160,1024]{1,0:T(8,128)(2,1)}, bf16[160,1024]{1,0:T(8,128)(2,1)}, u32[]{:S(2)}, u32[]{:S(2)}) collective-permute-start(bf16[160,1024]{1,0:T(8,128)(2,1)} %copy-done.27), channel_id=1, source_target_pairs={{0,1},{1,0},{2,3},{3,2},{4,5},{5,4},{6,7},{7,6},{8,9},{9,8},{10,11... | collective-permute-start | bytes 983048 | tf_op jit(solution)/shard_map/ppermute | solution.py:22
  49.5 18.1 %collective-permute-start.15 = (bf16[2,160,512]{2,1,0:T(8,128)(2,1)}, bf16[2,160,512]{2,1,0:T(8,128)(2,1)}, u32[]{:S(2)}, u32[]{:S(2)}) collective-permute-start(bf16[2,160,512]{2,1,0:T(8,128)(2,1)} %get-tuple-element.177), channel_id=1, source_target_pairs={{0,2},{1,3},{2,0},{3,1},{4,6},{5,7},{6,4},{7,5},{8,10},{9,11},{10,... | collective-permute-start | bytes 983048 | tf_op jit(solution)/shard_map/ppermute | solution.py:22
  49.8 17.8 %collective-permute-start.16 = (bf16[2,160,512]{2,1,0:T(8,128)(2,1)}, bf16[2,160,512]{2,1,0:T(8,128)(2,1)}, u32[]{:S(2)}, u32[]{:S(2)}) collective-permute-start(bf16[2,160,512]{2,1,0:T(8,128)(2,1)} %get-tuple-element.178), channel_id=1, source_target_pairs={{0,3},{1,2},{2,1},{3,0},{4,7},{5,6},{6,5},{7,4},{8,11},{9,10},{10,... | collective-permute-start | bytes 983048 | tf_op jit(solution)/shard_map/ppermute | solution.py:22
  83.0 34.7 %collective-permute-start.28 = (bf16[512,1024]{1,0:T(8,128)(2,1)S(1)}, bf16[512,1024]{1,0:T(8,128)(2,1)S(1)}, u32[]{:S(2)}, u32[]{:S(2)}) collective-permute-start(bf16[512,1024]{1,0:T(8,128)(2,1)S(1)} %get-tuple-element.193), channel_id=1, source_target_pairs={{0,1},{1,0},{2,3},{3,2},{4,5},{5,4},{6,7},{7,6},{8,9},{9,8},{10,11... | collective-permute-start | bytes 3145736 | tf_op jit(solution)/shard_map/ppermute | solution.py:22
  83.5 14.0 %collective-permute-start.21 = (bf16[512,512]{1,0:T(8,128)(2,1)S(1)}, bf16[512,512]{1,0:T(8,128)(2,1)S(1)}, u32[]{:S(2)}, u32[]{:S(2)}) collective-permute-start(bf16[512,512]{1,0:T(8,128)(2,1)S(1)} %get-tuple-element.196), channel_id=1, source_target_pairs={{0,4},{4,0},{8,12},{12,8},{16,20},{20,16},{24,28},{28,24},{1,5},{5... | collective-permute-start | bytes 1572872 | tf_op jit(solution)/shard_map/ppermute | solution.py:22
  85.3 13.7 %collective-permute-start.22 = (bf16[512,512]{1,0:T(8,128)(2,1)S(1)}, bf16[512,512]{1,0:T(8,128)(2,1)S(1)}, u32[]{:S(2)}, u32[]{:S(2)}) collective-permute-start(bf16[512,512]{1,0:T(8,128)(2,1)S(1)} %get-tuple-element.197), channel_id=1, source_target_pairs={{0,8},{4,12},{8,0},{12,4},{16,24},{20,28},{24,16},{28,20},{1,9},{5... | collective-permute-start | bytes 1572872 | tf_op jit(solution)/shard_map/ppermute | solution.py:22
  86.8 14.7 %collective-permute-start.18 = (bf16[2,160,512]{2,1,0:T(8,128)(2,1)S(1)}, bf16[2,160,512]{2,1,0:T(8,128)(2,1)S(1)}, u32[]{:S(2)}, u32[]{:S(2)}) collective-permute-start(bf16[2,160,512]{2,1,0:T(8,128)(2,1)S(1)} %copy-done.42), channel_id=1, source_target_pairs={{0,1},{1,0},{2,3},{3,2},{4,5},{5,4},{6,7},{7,6},{8,9},{9,8},{10,11... | collective-permute-start | bytes 983048 | tf_op jit(solution)/shard_map/ppermute | solution.py:22
  86.8 15.3 %collective-permute-start.19 = (bf16[2,160,512]{2,1,0:T(8,128)(2,1)S(1)}, bf16[2,160,512]{2,1,0:T(8,128)(2,1)S(1)}, u32[]{:S(2)}, u32[]{:S(2)}) collective-permute-start(bf16[2,160,512]{2,1,0:T(8,128)(2,1)S(1)} %copy-done.41), channel_id=1, source_target_pairs={{0,2},{1,3},{2,0},{3,1},{4,6},{5,7},{6,4},{7,5},{8,10},{9,11},{10,... | collective-permute-start | bytes 983048 | tf_op jit(solution)/shard_map/ppermute | solution.py:22
  101.5 15.5 %collective-permute-start.27 = (bf16[256,512]{1,0:T(8,128)(2,1)S(1)}, bf16[256,512]{1,0:T(8,128)(2,1)S(1)}, u32[]{:S(2)}, u32[]{:S(2)}) collective-permute-start(bf16[256,512]{1,0:T(8,128)(2,1)S(1)} %get-tuple-element.217), channel_id=1, source_target_pairs={{0,4},{4,0},{8,12},{12,8},{16,20},{20,16},{24,28},{28,24},{1,5},{5... | collective-permute-start | bytes 786440 | tf_op jit(solution)/shard_map/ppermute | solution.py:22
  102.2 16.4 %collective-permute-start.23 = (bf16[160,512]{1,0:T(8,128)(2,1)S(1)}, bf16[160,512]{1,0:T(8,128)(2,1)S(1)}, u32[]{:S(2)}, u32[]{:S(2)}) collective-permute-start(bf16[160,512]{1,0:T(8,128)(2,1)S(1)} %get-tuple-element.207), channel_id=1, source_target_pairs={{0,1},{1,0},{2,3},{3,2},{4,5},{5,4},{6,7},{7,6},{8,9},{9,8},{10,11... | collective-permute-start | bytes 491528 | tf_op jit(solution)/shard_map/ppermute | solution.py:22
  107.2 11.4 %collective-permute-start.24 = (bf16[160,512]{1,0:T(8,128)(2,1)S(1)}, bf16[160,512]{1,0:T(8,128)(2,1)S(1)}, u32[]{:S(2)}, u32[]{:S(2)}) collective-permute-start(bf16[160,512]{1,0:T(8,128)(2,1)S(1)} %get-tuple-element.208), channel_id=1, source_target_pairs={{0,2},{1,3},{2,0},{3,1},{4,6},{5,7},{6,4},{7,5},{8,10},{9,11},{10,... | collective-permute-start | bytes 491528 | tf_op jit(solution)/shard_map/ppermute | solution.py:22
  121.5 22.1 %collective-permute-start.31 = (bf16[528,1024]{1,0:T(8,128)(2,1)S(1)}, bf16[528,1024]{1,0:T(8,128)(2,1)S(1)}, u32[]{:S(2)}, u32[]{:S(2)}) collective-permute-start(bf16[528,1024]{1,0:T(8,128)(2,1)S(1)} %get-tuple-element.237), channel_id=1, source_target_pairs={{0,1},{1,0},{2,3},{3,2},{4,5},{5,4},{6,7},{7,6},{8,9},{9,8},{10,11... | collective-permute-start | bytes 3244040 | tf_op jit(solution)/shard_map/ppermute | solution.py:22
  122.0 24.1 %collective-permute-start.32 = (bf16[512,512]{1,0:T(8,128)(2,1)S(1)}, bf16[512,512]{1,0:T(8,128)(2,1)S(1)}, u32[]{:S(2)}, u32[]{:S(2)}) collective-permute-start(bf16[512,512]{1,0:T(8,128)(2,1)S(1)} %get-tuple-element.241), channel_id=1, source_target_pairs={{0,4},{4,0},{8,12},{12,8},{16,20},{20,16},{24,28},{28,24},{1,5},{5... | collective-permute-start | bytes 1572872 | tf_op jit(solution)/shard_map/ppermute | solution.py:22
  124.0 22.1 %collective-permute-start.33 = (bf16[512,512]{1,0:T(8,128)(2,1)S(1)}, bf16[512,512]{1,0:T(8,128)(2,1)S(1)}, u32[]{:S(2)}, u32[]{:S(2)}) collective-permute-start(bf16[512,512]{1,0:T(8,128)(2,1)S(1)} %get-tuple-element.242), channel_id=1, source_target_pairs={{0,8},{4,12},{8,0},{12,4},{16,24},{20,28},{24,16},{28,20},{1,9},{5... | collective-permute-start | bytes 1572872 | tf_op jit(solution)/shard_map/ppermute | solution.py:22
  125.5 15.1 %collective-permute-start.29 = (bf16[128,512]{1,0:T(8,128)(2,1)S(1)}, bf16[128,512]{1,0:T(8,128)(2,1)S(1)}, u32[]{:S(2)}, u32[]{:S(2)}) collective-permute-start(bf16[128,512]{1,0:T(8,128)(2,1)S(1)} %get-tuple-element.234), channel_id=1, source_target_pairs={{0,16},{4,20},{8,24},{12,28},{16,0},{20,4},{24,8},{28,12},{1,17},{... | collective-permute-start | bytes 393224 | tf_op jit(solution)/shard_map/ppermute | solution.py:22
  128.1 14.2 %collective-permute-start.30 = (bf16[128,512]{1,0:T(8,128)(2,1)S(1)}, bf16[128,512]{1,0:T(8,128)(2,1)S(1)}, u32[]{:S(2)}, u32[]{:S(2)}) collective-permute-start(bf16[128,512]{1,0:T(8,128)(2,1)S(1)} %get-tuple-element.235), channel_id=1, source_target_pairs={{0,16},{4,20},{8,24},{12,28},{16,0},{20,4},{24,8},{28,12},{1,17},{... | collective-permute-start | bytes 393224 | tf_op jit(solution)/shard_map/ppermute | solution.py:22
  144.5 19.9 %collective-permute-start.37 = (bf16[272,1024]{1,0:T(8,128)(2,1)S(1)}, bf16[272,1024]{1,0:T(8,128)(2,1)S(1)}, u32[]{:S(2)}, u32[]{:S(2)}) collective-permute-start(bf16[272,1024]{1,0:T(8,128)(2,1)S(1)} %get-tuple-element.256), channel_id=1, source_target_pairs={{0,4},{4,0},{8,12},{12,8},{16,20},{20,16},{24,28},{28,24},{1,5},{5... | collective-permute-start | bytes 1671176 | tf_op jit(solution)/shard_map/ppermute | solution.py:22
  145.0 12.5 %collective-permute-start.34 = (bf16[256,1024]{1,0:T(8,128)(2,1)S(1)}, bf16[256,1024]{1,0:T(8,128)(2,1)S(1)}, u32[]{:S(2)}, u32[]{:S(2)}) collective-permute-start(bf16[256,1024]{1,0:T(8,128)(2,1)S(1)} %get-tuple-element.246), channel_id=1, source_target_pairs={{0,2},{1,3},{2,0},{3,1},{4,6},{5,7},{6,4},{7,5},{8,10},{9,11},{10,... | collective-permute-start | bytes 1572872 | tf_op jit(solution)/shard_map/ppermute | solution.py:22
  147.0 11.3 %collective-permute-start.35 = (bf16[256,512]{1,0:T(8,128)(2,1)S(1)}, bf16[256,512]{1,0:T(8,128)(2,1)S(1)}, u32[]{:S(2)}, u32[]{:S(2)}) collective-permute-start(bf16[256,512]{1,0:T(8,128)(2,1)S(1)} %get-tuple-element.252), channel_id=1, source_target_pairs={{0,8},{4,12},{8,0},{12,4},{16,24},{20,28},{24,16},{28,20},{1,9},{5... | collective-permute-start | bytes 786440 | tf_op jit(solution)/shard_map/ppermute | solution.py:22
  150.5 13.1 %collective-permute-start.36 = (bf16[256,512]{1,0:T(8,128)(2,1)S(1)}, bf16[256,512]{1,0:T(8,128)(2,1)S(1)}, u32[]{:S(2)}, u32[]{:S(2)}) collective-permute-start(bf16[256,512]{1,0:T(8,128)(2,1)S(1)} %get-tuple-element.253), channel_id=1, source_target_pairs={{0,4},{4,0},{8,12},{12,8},{16,20},{20,16},{24,28},{28,24},{1,5},{5... | collective-permute-start | bytes 786440 | tf_op jit(solution)/shard_map/ppermute | solution.py:22
  173.8 10.6 %collective-permute-start.41 = (bf16[80,1024]{1,0:T(8,128)(2,1)S(1)}, bf16[80,1024]{1,0:T(8,128)(2,1)S(1)}, u32[]{:S(2)}, u32[]{:S(2)}) collective-permute-start(bf16[80,1024]{1,0:T(8,128)(2,1)S(1)} %get-tuple-element.270), channel_id=1, source_target_pairs={{0,8},{4,12},{8,0},{12,4},{16,24},{20,28},{24,16},{28,20},{1,9},{5... | collective-permute-start | bytes 491528 | tf_op jit(solution)/shard_map/ppermute | solution.py:22
  177.5 10.6 %all-to-all-start = ((bf16[4,32,1024]{2,1,0:T(8,128)(2,1)}), bf16[4,32,1024]{2,1,0:T(8,128)(2,1)S(1)}, u32[]{:S(2)}, u32[]{:S(2)}) async-start(bf16[4,32,1024]{2,1,0:T(8,128)(2,1)} %bitcast.11), calls=%async_computation | async-start | bytes 524288 | tf_op jit(solution)/shard_map/all_to_all | solution.py:883
  180.9 16.5 %collective-permute-start.44 = (bf16[128,512]{1,0:T(8,128)(2,1)S(1)}, bf16[128,512]{1,0:T(8,128)(2,1)S(1)}, u32[]{:S(2)}, u32[]{:S(2)}) collective-permute-start(bf16[128,512]{1,0:T(8,128)(2,1)S(1)} %get-tuple-element.281), channel_id=1, source_target_pairs={{0,16},{4,20},{8,24},{12,28},{16,0},{20,4},{24,8},{28,12},{1,17},{... | collective-permute-start | bytes 393224 | tf_op jit(solution)/shard_map/ppermute | solution.py:22
  182.8 17.4 %collective-permute-start.45 = (bf16[128,512]{1,0:T(8,128)(2,1)S(1)}, bf16[128,512]{1,0:T(8,128)(2,1)S(1)}, u32[]{:S(2)}, u32[]{:S(2)}) collective-permute-start(bf16[128,512]{1,0:T(8,128)(2,1)S(1)} %get-tuple-element.282), channel_id=1, source_target_pairs={{0,16},{4,20},{8,24},{12,28},{16,0},{20,4},{24,8},{28,12},{1,17},{... | collective-permute-start | bytes 393224 | tf_op jit(solution)/shard_map/ppermute | solution.py:22
  185.1 19.2 %collective-permute-start.42 = (bf16[48,1024]{1,0:T(8,128)(2,1)S(1)}, bf16[48,1024]{1,0:T(8,128)(2,1)S(1)}, u32[]{:S(2)}, u32[]{:S(2)}) collective-permute-start(bf16[48,1024]{1,0:T(8,128)(2,1)S(1)} %get-tuple-element.273), channel_id=1, source_target_pairs={{0,16},{4,20},{8,24},{12,28},{16,0},{20,4},{24,8},{28,12},{1,17},{... | collective-permute-start | bytes 294920 | tf_op jit(solution)/shard_map/ppermute | solution.py:22
  187.0 16.1 %collective-permute-start.43 = (bf16[32,1024]{1,0:T(8,128)(2,1)S(1)}, bf16[32,1024]{1,0:T(8,128)(2,1)S(1)}, u32[]{:S(2)}, u32[]{:S(2)}) collective-permute-start(bf16[32,1024]{1,0:T(8,128)(2,1)S(1)} %get-tuple-element.276), channel_id=1, source_target_pairs={{0,16},{4,20},{8,24},{12,28},{16,0},{20,4},{24,8},{28,12},{1,17},{... | collective-permute-start | bytes 196616 | tf_op jit(solution)/shard_map/ppermute | solution.py:22
  (58 other events, 401.1 us)

commit v3 on v2

--- a/solution.py
+++ b/solution.py
@@ -15,6 +15,10 @@
 F32 = jnp.float32
 BF16 = jnp.bfloat16
 MIB = 1024 * 1024
+TIMES = dict(latent=2.9, media=2.7, attend=3.1, mix=3.8, feed=9.6, feed_end=12.0, down_grad=4.0, attend_back=1.7, keyval_grad=3.8, up_grad=4.0, keyval_back=4.0, latent_back=1.6, query_grad=1.5)
+RATE = 2e+09
+ORDER = "OGXBVDWPKDLRUUQDKQKQUKQKQ"
+KV_ORDER, QO_ORDER = "cxyz", "czxy"
 
 
 def swap(values, axis, bit):
@@ -85,6 +89,8 @@
             kept = after(kept, *others)
         nxt = None
         if self.at < self.steps:
+            if all(order[self.at :] == self.lanes[0][0][self.at :] for order, _ in self.lanes):
+                self.lanes = self.lanes[:1]
             nxt = [(order[self.at], plan[self.at]) for order, plan in self.lanes]
         values = fold(self.own, kept, self.got, self.extra, nxt, self.end, self.name)
         if self.extra is not None:
@@ -97,10 +103,10 @@
         return values[0]
 
     def run(self):
-        while self.open or self.at < self.steps:
-            if not self.open:
+        while self.open:
+            self.finish()
+            if self.at < self.steps:
                 self.begin()
-            self.finish()
         return self.values
 
 
@@ -168,7 +174,7 @@
     return values.T[:b, :a]
 
 
-def call(kernel, grid, ins, outs, scratch=(), vmem=40, us=2, prefetch=0, name=None):
+def call(kernel, grid, ins, outs, scratch=(), vmem=40, prefetch=0, name=None):
     return pl.pallas_call(
         kernel,
         grid_spec=pltpu.PrefetchScalarGridSpec(
@@ -182,7 +188,7 @@
         compiler_params=pltpu.CompilerParams(
             vmem_limit_bytes=vmem * MIB, dimension_semantics=("arbitrary",) * len(grid)
         ),
-        cost_estimate=pl.CostEstimate(flops=0, bytes_accessed=int(us * 1e5), transcendentals=0),
+        cost_estimate=pl.CostEstimate(flops=int(TIMES.get(name, 0.8) * RATE), bytes_accessed=100000, transcendentals=0),
         name=name,
     )
 
@@ -525,7 +531,7 @@
         [left_spec(v) for v in lefts] + [whole(v.shape) for v in rights],
         [(spec, out((a // 2, part), BF16))] * (2 * len(lanes)),
         scratch=[pltpu.VMEM((total, b), BF16)],
-        us=4, prefetch=1, name=name,
+        prefetch=1, name=name,
     )(own, *lefts, *rights)
 
 
@@ -565,6 +571,8 @@
         for ref, values in zip(refs, end(*totals)):
             ref[...] = values.astype(ref.dtype)
         return
+    if len(nxt) < len(totals):
+        totals = [jnp.concatenate(totals, axis=1)]
     for k, (total, (bit, inner)) in enumerate(zip(totals, nxt)):
         keep, send = parted(total, inner, chosen(own, bit))
         refs[2 * k][...] = keep.astype(BF16)
@@ -578,8 +586,8 @@
     if nxt is not None:
         head = 0 if extra is None else 2 * extra.shape[0]
         shapes = []
-        for v in kept:
-            rows, width = v.shape
+        for _ in nxt:
+            rows, width = kept[0].shape[0], kept[0].shape[1] * len(kept) // len(nxt)
             shapes += [out((rows // 2, width), BF16), out((head + rows // 2, width), BF16)]
     else:
         shapes = list(jax.eval_shape(end, *(out(v.shape, F32) for v in kept)))
@@ -591,7 +599,7 @@
         (1,),
         [whole(v.shape) for v in ins],
         [(whole(s.shape), s) for s in shapes],
-        us=1, prefetch=1, name=name,
+        prefetch=1, name=name,
     )(own, *ins)
 
 
@@ -635,7 +643,6 @@
     qs = {0: q_low}
     bit = peers // 2
     qs[bit] = swap(q_low, "patch", bit)
-    dys = {0: dy, bit: swap(dy, "patch", bit)}
 
     group = slots // 2
     key_input, keyval = call(
@@ -657,7 +664,7 @@
         bit //= 2
         for j in list(qs):
             qs[j ^ bit] = swap(qs[j], "patch", bit)
-    qs = [after(qs[0], dys[peers // 2])] + [qs[j] for j in range(1, peers)]
+    qs = [qs[j] for j in range(peers)]
 
     pair = 2
     kv_block = leading((pair, keys, 2 * inner))
@@ -671,7 +678,8 @@
         scratch=[pltpu.VMEM((peers, padded, LANES), F32)],
         name="attend",
     )(*qs, keyval)
-    parts = [parts[0]] + [swap(parts[j], "patch", j) for j in range(1, peers)]
+    dys = {0: dy, peers // 2: swap(dy, "patch", peers // 2)}
+    parts = [parts[0]] + [swap(after(parts[j], dys[peers // 2]), "patch", j) for j in range(1, peers)]
 
     attended, att_low, hidden, ff_low, lse = call(
         functools.partial(mix_kernel, peers),
@@ -750,129 +758,145 @@
 
     das = {0: datt_low, peers // 2: swap(datt_low, "patch", peers // 2)}
     out_rows = width // shards // 2
-    out_t = call(
-        functools.partial(side_by_side_kernel, out_rows),
-        (2,),
-        [pl.BlockSpec((rows, width // 2), lambda g: (0, g)), whole((rows, inner))],
-        [(leading((shards // 2, out_rows, 2 * inner)), out((shards, out_rows, 2 * inner), BF16))],
-        name="out_grad",
-    )(after(dhid_low, datt_low), att_low)[0]
-    near_swaps = lambda values: [values[0]] + [swap(values[j], "patch", j) for j in range(1, here)]
-
-    every = digits_of("img") + digits_of("patch")
-    ff_bits = digits_of("img")
+    q_rows = inner // shards
+    every, ff_bits = digits_of("img") + digits_of("patch"), digits_of("img")
     ff_orders = [ff_bits[::-1], ff_bits[-2:] + ff_bits[:-2][::-1]]
+    named = {"c": ("patch", 1), "x": ("patch", 2), "y": ("img", 1), "z": ("img", 2)}
+
+    def order_of(letters):
+        head = [named[k] for k in letters]
+        return head + [bit for bit in reversed(every) if bit not in head]
 
     def ff_lanes(rows):
         return [(order, plan_of(rows, ff_bits, order)) for order in ff_orders]
 
+    def near_swaps(values):
+        return [values[0]] + [swap(values[j], "patch", j) for j in range(1, here)]
+
+    kv_order, qo_order = order_of(KV_ORDER), order_of(QO_ORDER)
     acts = near_swaps(act_near) + act_cross
-    down_lanes = ff_lanes(width)
-    down_sum = Scatter(
-        own, outer(own, dys[:-1] + [after(dys[-1], out_t)], acts, width // 2, down_lanes, "down_grad"), down_lanes,
-        lambda *t: [jnp.concatenate(t, axis=1).astype(BF16)], name="down_fold",
-    )
-    down_sum.begin()
-    das[peers // 2] = after(das[peers // 2], *down_sum.both)
-    das = spread(das)
-    dpres = near_swaps(dpre_near) + cross(after(tuple(far[here : 2 * here]), *down_sum.both))
-
-    got = call(
-        functools.partial(attend_back_kernel, peers, per_slot, scale),
-        (slots // pair,),
-        [whole((rows, inner))] * peers + [whole((rows + 4 * HEADS, inner))] * peers + [kv_block],
-        [(kv_block, out(keyval.shape, BF16))] + [(whole((rows, inner)), out((rows, inner), BF16))] * peers,
-        scratch=[pltpu.VMEM((peers, padded, LANES), F32)],
-        name="attend_back",
-    )(*qs, *das, keyval)
-    dkv, dqs = got[0], got[1:]
-    dqs = [dqs[0]] + [swap(dqs[j], "patch", j) for j in range(1, peers)]
-
-    low_bit, both = [("patch", 1)], [("patch", 2), ("img", 1)]
-    last = [bit for bit in reversed(every) if bit not in low_bit + both]
-    kv_order, qo_order = low_bit + both + last, low_bit + both[::-1] + last
-    kv_lanes = [(kv_order, plan_of(2 * inner, every, kv_order))]
-    kv_sum = Scatter(
-        own,
-        outer(own, [dkv.reshape(-1, 2 * inner)], [key_input.reshape(-1, width)], 2 * inner // 4, kv_lanes, "keyval_grad"),
-        kv_lanes, lambda t: [t], name="keyval_fold",
-    )
-    kv_sum.begin()
-    mark = down_sum.finish(*kv_sum.both)
-    down_sum.begin()
-    up_lanes = ff_lanes(halves * part)
-
-    def up_end(*totals):
-        total = jnp.concatenate(totals, axis=1)
-        return [flipped(total)] if strided else [total.astype(BF16)]
-
-    up_sum = Scatter(
-        own, outer(own, dpres[:-1] + [after(dpres[-1], mark)], ffs, part, up_lanes, "up_grad"), up_lanes, up_end,
-        name="up_fold",
-    )
-    up_sum.begin()
-
-    media_grad, dlat, sums_media = call(
-        keyval_back_kernel,
-        (slots // group,),
-        [
-            leading((group, patch_rows, width)), leading((group, keys, 2 * inner)),
-            whole(w_keyval.shape), gain_spec,
-        ],
-        [
-            (leading((group, patch_rows, width)), out(media.shape, BF16)),
-            (leading((group * per_slot, width)), out((rows, width), F32)),
-            (whole((2, width)), out((2, width), F32)),
-        ],
-        name="keyval_back",
-    )(media, after(dkv, *up_sum.both), w_keyval, gains)
-    mark = down_sum.finish(media_grad)
-    down_sum.begin()
-    mark = kv_sum.finish(mark)
-    kv_sum.begin()
-
-    dq_low, latent_grad, sums = call(
-        functools.partial(latent_back_kernel, peers),
-        (1,),
-        [whole((rows, inner))] * peers
-        + [whole((rows, width))] * 3 + [whole(w_query.shape), gain_spec, whole((2, width)), whole((2, width))],
-        [
-            (whole((rows, inner)), out((rows, inner), BF16)),
-            (whole((rows, width)), out((rows, width), BF16)),
-            (whole((HEADS, width)), out((HEADS, width), F32)),
-        ],
-        name="latent_back",
-    )(*dqs, after(dlat, mark), lat, dhidden, w_query, gains, sums_media, sums_ff)
-
-    q_rows = inner // shards
+    dpre_first = near_swaps(dpre_near)
+    got, sums_of = {}, {}
+
+    def out_grad(mark):
+        got["out_t"] = call(
+            functools.partial(side_by_side_kernel, out_rows),
+            (2,),
+            [pl.BlockSpec((rows, width // 2), lambda g: (0, g)), whole((rows, inner))],
+            [(leading((shards // 2, out_rows, 2 * inner)), out((shards, out_rows, 2 * inner), BF16))],
+            name="out_grad",
+        )(after(dhid_low, mark), att_low)[0]
+        return got["out_t"]
+
+    def begun(letter, scatter):
+        sums_of[letter] = scatter
+        mark = scatter.both[0]
+        scatter.begin()
+        return mark
+
+    def down_grad(mark):
+        lanes = ff_lanes(width)
+        both = outer(own, dys[:-1] + [after(dys[-1], mark)], acts, width // 2, lanes, "down_grad")
+        return begun("D", Scatter(own, both, lanes, lambda t: [t.astype(BF16)], name="down_fold"))
+
+    def send_dpre(mark):
+        got["dpres"] = dpre_first + cross(after(tuple(far[here : 2 * here]), mark))
+        return mark
+
+    def attend_back(mark):
+        near_das = spread({0: das[0], peers // 2: after(das[peers // 2], mark)})
+        values = call(
+            functools.partial(attend_back_kernel, peers, per_slot, scale),
+            (slots // pair,),
+            [whole((rows, inner))] * peers + [whole((rows + 4 * HEADS, inner))] * peers + [kv_block],
+            [(kv_block, out(keyval.shape, BF16))] + [(whole((rows, inner)), out((rows, inner), BF16))] * peers,
+            scratch=[pltpu.VMEM((peers, padded, LANES), F32)],
+            name="attend_back",
+        )(*qs, *near_das, keyval)
+        got["dkv"], dqs = values[0], values[1:]
+        got["dqs"] = [dqs[0]] + [swap(dqs[j], "patch", j) for j in range(1, peers)]
+        return got["dkv"]
+
+    def keyval_back(mark):
+        got["media_grad"], got["dlat"], got["sums_media"] = call(
+            keyval_back_kernel,
+            (slots // group,),
+            [
+                leading((group, patch_rows, width)), leading((group, keys, 2 * inner)),
+                whole(w_keyval.shape), gain_spec,
+            ],
+            [
+                (leading((group, patch_rows, width)), out(media.shape, BF16)),
+                (leading((group * per_slot, width)), out((rows, width), F32)),
+                (whole((2, width)), out((2, width), F32)),
+            ],
+            name="keyval_back",
+        )(media, after(got["dkv"], mark), w_keyval, gains)
+        return got["sums_media"]
+
+    def keyval_grad(mark):
+        lanes = [(kv_order, plan_of(2 * inner, every, kv_order))]
+        both = outer(
+            own, [after(got["dkv"], mark).reshape(-1, 2 * inner)], [key_input.reshape(-1, width)], 2 * inner // 4,
+            lanes, "keyval_grad",
+        )
+        return begun("K", Scatter(own, both, lanes, lambda t: [t], name="keyval_fold"))
+
+    def up_grad(mark):
+        lanes, dpres = ff_lanes(halves * part), got["dpres"]
+        both = outer(own, dpres[:-1] + [after(dpres[-1], mark)], ffs, part, lanes, "up_grad")
+        end = lambda t: [flipped(t)] if strided else [t.astype(BF16)]
+        return begun("U", Scatter(own, both, lanes, end, name="up_fold"))
+
+    def latent_back(mark):
+        got["dq_low"], got["latent_grad"], got["sums"] = call(
+            functools.partial(latent_back_kernel, peers),
+            (1,),
+            [whole((rows, inner))] * peers
+            + [whole((rows, width))] * 3 + [whole(w_query.shape), gain_spec, whole((2, width)), whole((2, width))],
+            [
+                (whole((rows, inner)), out((rows, inner), BF16)),
+                (whole((rows, width)), out((rows, width), BF16)),
+                (whole((HEADS, width)), out((HEADS, width), F32)),
+            ],
+            name="latent_back",
+        )(*got["dqs"], after(got["dlat"], mark), lat, dhidden, w_query, gains, got["sums_media"], sums_ff)
+        return got["dq_low"]
 
     def open_rows(total):
         other = total[q_rows:]
         return [total[:q_rows], jnp.concatenate([other[:, :inner], other[:, inner:]], axis=0)]
 
-    q_plan, qo_plan = plan_of(inner, every, qo_order), plan_of(2 * inner, every, qo_order)
-    head = 2 * sums.shape[0]
-    qo_both = call(
-        functools.partial(query_kernel, qo_order[0], q_plan[0]),
-        (1,),
-        [whole(v.shape) for v in (dq_low, lat_low, out_t, sums)],
-        [(whole((inner, width)), out((inner, width), BF16)), (whole((head + inner, width)), out((head + inner, width), BF16))],
-        prefetch=1, name="query_grad",
-    )(own, dq_low, lat_low, out_t, sums)
-    qo_sum = Scatter(own, qo_both, [(qo_order, qo_plan)], open_rows, extra=sums, name="query_fold")
-    qo_sum.begin()
-
-    mark = qo_sum.both[0]
-    if down_sum.steps == down_sum.at:
-        mark = down_sum.finish(mark)
-    for one in (qo_sum, up_sum, kv_sum, up_sum, qo_sum, kv_sum, qo_sum, kv_sum, qo_sum):
-        mark = one.finish(mark)
-        if one.at < one.steps:
-            one.begin()
-    (up_sum,) = up_sum.run()
-    (kv_sum,) = kv_sum.run()
-    q_sum, out_sum = qo_sum.run()
-    (down,) = down_sum.run()
+    def query_grad(mark):
+        q_plan, qo_plan = plan_of(inner, every, qo_order), plan_of(2 * inner, every, qo_order)
+        sums = got["sums"]
+        tall = 2 * sums.shape[0] + inner
+        ins = (after(got["dq_low"], mark), lat_low, got["out_t"], sums)
+        both = call(
+            functools.partial(query_kernel, qo_order[0], q_plan[0]),
+            (1,),
+            [whole(v.shape) for v in ins],
+            [(whole((inner, width)), out((inner, width), BF16)), (whole((tall, width)), out((tall, width), BF16))],
+            prefetch=1, name="query_grad",
+        )(own, *ins)
+        return begun("Q", Scatter(own, both, [(qo_order, qo_plan)], open_rows, extra=sums, name="query_fold"))
+
+    tasks = dict(
+        O=out_grad, G=down_grad, X=send_dpre, B=attend_back, V=keyval_back, W=keyval_grad, P=up_grad, L=latent_back,
+        R=query_grad,
+    )
+    mark = datt_low
+    for letter in ORDER:
+        if letter in tasks:
+            mark = tasks[letter](mark)
+        else:
+            one = sums_of[letter]
+            mark = one.finish(mark)
+            if one.at < one.steps:
+                one.begin()
+    media_grad, latent_grad = got["media_grad"], got["latent_grad"]
+    qo_sum = sums_of["Q"]
+    (up_sum,), (kv_sum,), (down,), (q_sum, out_sum) = (sums_of[k].run() for k in "UKDQ")
     small = lax.dynamic_slice_in_dim(
         qo_sum.extra, (own[1] * peers + own[0]) * (width // shards), width // shards, axis=1
     )

time: 207 us -> 179 us (0.86)
  waiting for transfers between devices: 70.2 us -> 52.2 us
  starting transfers between devices: 50.2 us -> 37.4 us
  local copies, waits for them, and re-layouts: 9.86 us -> 13.7 us
    ppermute x46 -> x44, waiting for transfers between devices: 70.2 us -> 52.2 us  [swap(): return lax.ppermute(values, axis, [(k, k ^ bit) for k in range(n)])]
    ppermute x46 -> x44, starting transfers between devices: 46.8 us -> 34 us  [swap(): return lax.ppermute(values, axis, [(k, k ^ bit) for k in range(n)])]
    unnamed x86 -> x112, local copies, waits for them, and re-layouts: 9.2 us -> 13 us
  transfers between devices with their start and end apart: 47 -> 45, of which waited for: 15 -> 16; matrix products, arithmetic and copies ran while one was open for 0% -> 0% of each run, Pallas kernels for 24% -> 37%
where the time goes in v3:
time: 179 us; the launch traced here: 178 us
  Pallas kernels  73.1 us (41%)
  waiting for transfers between devices  52.2 us (29%)
  starting transfers between devices  37.4 us (21%)
  local copies, waits for them, and re-layouts  13.7 us (8%)
    ppermute x44, waiting for transfers between devices, swap(): return lax.ppermute(values, axis, [(k, k ^ bit) for k in range(n)])  52.2 us
    ppermute x44, starting transfers between devices, swap(): return lax.ppermute(values, axis, [(k, k ^ bit) for k in range(n)])  34 us
    pallas_call x16, Pallas kernels, fold(): call(functools.partial(fold_kernel, nxt, end, len(kept), extra is not Non...  14 us
    unnamed x112, local copies, waits for them, and re-layouts  13 us
    pallas_call x1, Pallas kernels, on_device(): call(functools.partial(feed_end_kernel, per_slot, count, here), (here, ha...  12 us
    pallas_call x3, Pallas kernels, outer(): call(functools.partial(outer_kernel, count, [(order[0], plan[0]) for orde...  10.9 us
    pallas_call x1, Pallas kernels, on_device(): call(functools.partial(feed_kernel, count, here), (here, halves), [whole(...  9.57 us
    pallas_call x1, Pallas kernels, attend_back(): call(functools.partial(attend_back_kernel, peers, per_slot, scale), (slot...  5.64 us
  transfers between devices with their start and end apart: 45, of which 16 were waited for; matrix products, arithmetic and copies ran while one was open for 0% of the time, Pallas kernels for 37%

profile of v3, /device:TPU:0, one launch (start us, length us, event | category | flops | bytes accessed | tf_op | source)
XLA Modules:
  0.0 178.3 jit_solution(1391604428902080509)
XLA Ops:
  0.7 2.9 %latent.1 = (bf16[160,1024]{1,0:T(8,128)(2,1)}, bf16[160,512]{1,0:T(8,128)(2,1)}, bf16[160,1024]{1,0:T(8,128)(2,1)}) custom-call(s32[2]{0:T(128)} %counts.3, bf16[160,1024]{1,0:T(8,128)(2,1)} %bitcast.13, bf16[160,1024]{1,0:T(8,128)(2,1)} %bitcast.18, f32[3,1024]{1,0:T(4,128)} %refs_8_.1, f32[3,1024]{1,0:T(4,128)} %refs_7_.4, bf16[1024,512]{1,0:T(8,128)(2,1)} %refs_7_.7), custom_call_target="tpu_custom_call" | custom-call | flops 5800000000 | bytes 100000 | tf_op jit(solution)/shard_map/latent/pallas_call | solution.py:632
  3.6 3.0 %collective-permute-start.1 = (bf16[160,512]{1,0:T(8,128)(2,1)}, bf16[160,512]{1,0:T(8,128)(2,1)S(1)}, u32[]{:S(2)}, u32[]{:S(2)}) collective-permute-start(bf16[160,512]{1,0:T(8,128)(2,1)} %get-tuple-element.144.refs_0_), channel_id=1, source_target_pairs={{0,2},{1,3},{2,0},{3,1},{4,6},{5,7},{6,4},{7,5},{8,10},{9,11},{10,... | collective-permute-start | bytes 491528 | tf_op jit(solution)/shard_map/ppermute | solution.py:26
  6.6 1.6 copy-done
  9.2 2.7 %media.3 = (bf16[10,80,1024]{2,1,0:T(8,128)(2,1)S(1)}, bf16[10,80,1024]{2,1,0:T(8,128)(2,1)S(1)}) custom-call(bf16[10,64,1024]{2,1,0:T(8,128)(2,1)S(1)} %copy-done.2, bf16[160,1024]{1,0:T(8,128)(2,1)S(1)} %copy-done.42, f32[3,1024]{1,0:T(4,128)S(1)} %copy-done.22, f32[3,1024]{1,0:T(4,128)S(1)} %copy-done.21, bf16[1024,1024]{1,0:T(8,128)(2,1)S(1)} %copy-done), custom_call_target="tpu_custom_call" | custom-call | flops 5400000000 | bytes 100000 | tf_op jit(solution)/shard_map/media/pallas_call | solution.py:648
  14.6 3.0 %attend.1 = (bf16[176,512]{1,0:T(8,128)(2,1)S(1)}, bf16[176,512]{1,0:T(8,128)(2,1)S(1)}, bf16[176,512]{1,0:T(8,128)(2,1)S(1)}, bf16[176,512]{1,0:T(8,128)(2,1)S(1)}) custom-call(bf16[160,512]{1,0:T(8,128)(2,1)S(1)} %copy-done.13, bf16[160,512]{1,0:T(8,128)(2,1)S(1)} %collective-permute-done.refs_1_, bf16[160,512]{1,0:T(8,128)(2,1)S(1)} %collective-permute-done.1.refs_2_, ...), custom_call_target="tpu_custom_call" | custom-call | flops 6200000000 | bytes 100000 | tf_op jit(solution)/shard_map/attend/pallas_call | solution.py:673
  18.2 5.0 %collective-permute-done.3.refs_2_ = bf16[160,1024]{1,0:T(8,128)(2,1)S(1)} collective-permute-done((bf16[160,1024]{1,0:T(8,128)(2,1)S(1)}, bf16[160,1024]{1,0:T(8,128)(2,1)S(1)}, u32[]{:S(2)}, u32[]{:S(2)}) %collective-permute-start.3) | collective-permute-done | bytes 327712 | tf_op jit(solution)/shard_map/ppermute | solution.py:26
  26.4 4.4 %collective-permute-done.6.refs_3_ = bf16[176,512]{1,0:T(8,128)(2,1)S(1)} collective-permute-done((bf16[176,512]{1,0:T(8,128)(2,1)S(1)}, bf16[176,512]{1,0:T(8,128)(2,1)S(1)}, u32[]{:S(2)}, u32[]{:S(2)}) %collective-permute-start.6) | collective-permute-done | bytes 180256 | tf_op jit(solution)/shard_map/ppermute | solution.py:26
  30.8 2.7 %collective-permute-done.5.refs_2_ = bf16[176,512]{1,0:T(8,128)(2,1)S(1)} collective-permute-done((bf16[176,512]{1,0:T(8,128)(2,1)S(1)}, bf16[176,512]{1,0:T(8,128)(2,1)S(1)}, u32[]{:S(2)}, u32[]{:S(2)}) %collective-permute-start.5) | collective-permute-done | bytes 180256 | tf_op jit(solution)/shard_map/ppermute | solution.py:26
  34.2 3.8 %mix.1 = (f32[160,512]{1,0:T(8,128)}, bf16[160,512]{1,0:T(8,128)(2,1)}, f32[160,1024]{1,0:T(8,128)}, bf16[160,1024]{1,0:T(8,128)(2,1)}, f32[8,256]{1,0:T(8,128)}) custom-call(bf16[176,512]{1,0:T(8,128)(2,1)} %copy-done.48, bf16[176,512]{1,0:T(8,128)(2,1)} %copy-done.55, bf16[176,512]{1,0:T(8,128)(2,1)} %copy-done.54, bf16[176,512]{1,0:T(8,128)(2,1)} %copy-done.53, ...), custom_call_target="tpu_custom_call" | custom-call | flops 7600000000 | bytes 100000 | tf_op jit(solution)/shard_map/mix/pallas_call | solution.py:684
  40.0 9.6 %feed.1 = (bf16[2,160,512]{2,1,0:T(8,128)(2,1)}, bf16[2,160,512]{2,1,0:T(8,128)(2,1)}, bf16[2,160,512]{2,1,0:T(8,128)(2,1)}, bf16[2,160,512]{2,1,0:T(8,128)(2,1)...) custom-call(s32[2]{0:T(128)} %pad_add_fusion.own, bf16[160,1024]{1,0:T(8,128)(2,1)} %get-tuple-element.161.ff_low.refs_4_, ...), custom_call_target="tpu_custom_call" | custom-call | flops 19200000000 | bytes 100000 | tf_op jit(solution)/shard_map/feed/pallas_call | solution.py:730
  52.4 12.0 %feed_end.1 = (bf16[2,160,512]{2,1,0:T(8,128)(2,1)}, bf16[2,160,512]{2,1,0:T(8,128)(2,1)}, bf16[2,160,512]{2,1,0:T(8,128)(2,1)}, bf16[2,160,512]{2,1,0:T(8,128)(...) custom-call(s32[2]{0:T(128)} %pad_add_fusion.own, ...), custom_call_target="tpu_custom_call" | custom-call | flops 24000000000 | bytes 100000 | tf_op jit(solution)/shard_map/feed_end/pallas_call | solution.py:744
  68.8 4.3 %down_grad.1 = (bf16[512,512]{1,0:T(8,128)(2,1)S(1)}, bf16[512,512]{1,0:T(8,128)(2,1)S(1)}, bf16[512,512]{1,0:T(8,128)(2,1)S(1)}, bf16[512,512]{1,0:T(8,128)(2,1)S(1)}) custom-call(s32[2]{0:T(128)S(1)} %copy-done.26, bf16[160,1024]{1,0:T(8,128)(2,1)S(1)} %copy-done.9, bf16[160,1024]{1,0:T(8,128)(2,1)} %collective-permute-done.10.refs_1_, ...), custom_call_target="tpu_custom_call" | custom-call | flops 8000000000 | bytes 100000 | tf_op jit(solution)/shard_map/down_grad/pallas_call | solution.py:528
  73.8 1.5 collective-permute-start.25
  75.3 1.8 collective-permute-start.21
  77.1 1.6 collective-permute-start.22
  79.0 5.6 %attend_back.1 = (bf16[10,80,1024]{2,1,0:T(8,128)(2,1)S(1)}, bf16[160,512]{1,0:T(8,128)(2,1)S(1)}, bf16[160,512]{1,0:T(8,128)(2,1)S(1)}, bf16[160,512]{1,0:T(8,128)(2,1)S(1)}, bf16[160,512]{1,0:T(8,128)(2,1)S(1)}) custom-call(bf16[160,512]{1,0:T(8,128)(2,1)S(1)} %copy-done.14, bf16[160,512]{1,0:T(8,128)(2,1)S(1)} %copy-done.18, ...), custom_call_target="tpu_custom_call" | custom-call | flops 3400000000 | bytes 100000 | tf_op jit(solution)/shard_map/attend_back/pallas_call | solution.py:808
  84.7 4.2 %keyval_back.1 = (bf16[10,64,1024]{2,1,0:T(8,128)(2,1)}, f32[160,1024]{1,0:T(8,128)S(1)}, f32[2,1024]{1,0:T(2,128)S(1)}) custom-call(bf16[10,64,1024]{2,1,0:T(8,128)(2,1)S(1)} %copy-done.2, bf16[10,80,1024]{2,1,0:T(8,128)(2,1)S(1)} %get-tuple-element.198.dkv, bf16[1024,1024]{1,0:T(8,128)(2,1)S(1)} %copy-done.1, f32[3,1024]{1,0:T(4,128)S(1)} %copy-done.23), custom_call_target="tpu_custom_call" | custom-call | flops 8000000000 | bytes 100000 | tf_op jit(solution)/shard_map/keyval_back/pallas_call | solution.py:821
  91.7 3.9 %keyval_grad.1 = (bf16[512,1024]{1,0:T(8,128)(2,1)S(1)}, bf16[512,1024]{1,0:T(8,128)(2,1)S(1)}) custom-call(s32[2]{0:T(128)S(1)} %copy-done.26, bf16[800,1024]{1,0:T(8,128)(2,1)S(1)} %bitcast.17, bf16[800,1024]{1,0:T(8,128)(2,1)S(1)} %bitcast.16), custom_call_target="tpu_custom_call" | custom-call | flops 7600000000 | bytes 100000 | tf_op jit(solution)/shard_map/keyval_grad/pallas_call | solution.py:528
  96.5 1.6 collective-permute-start.27
  98.6 2.7 %up_grad.1 = (bf16[512,512]{1,0:T(8,128)(2,1)S(1)}, bf16[512,512]{1,0:T(8,128)(2,1)S(1)}, bf16[512,512]{1,0:T(8,128)(2,1)S(1)}, bf16[512,512]{1,0:T(8,128)(2,1)S(1)}) custom-call(s32[2]{0:T(128)S(1)} %copy-done.26, bf16[2,160,512]{2,1,0:T(8,128)(2,1)S(1)} %copy-done.46, bf16[2,160,512]{2,1,0:T(8,128)(2,1)S(1)} %collective-permute-done.23.refs_1_, ...), custom_call_target="tpu_custom_call" | custom-call | flops 8000000000 | bytes 100000 | tf_op jit(solution)/shard_map/up_grad/pallas_call | solution.py:528
  102.8 1.7 collective-permute-done.27.refs_2_
  110.8 7.2 %collective-permute-done.29.refs_2_ = bf16[512,512]{1,0:T(8,128)(2,1)S(1)} collective-permute-done((bf16[512,512]{1,0:T(8,128)(2,1)S(1)}, bf16[512,512]{1,0:T(8,128)(2,1)S(1)}, u32[]{:S(2)}, u32[]{:S(2)}) %collective-permute-start.29) | collective-permute-done | bytes 524320 | tf_op jit(solution)/shard_map/ppermute | solution.py:26
  121.6 2.6 %collective-permute-start.34 = (bf16[128,1024]{1,0:T(8,128)(2,1)S(1)}, bf16[128,1024]{1,0:T(8,128)(2,1)S(1)}, u32[]{:S(2)}, u32[]{:S(2)}) collective-permute-start(bf16[128,1024]{1,0:T(8,128)(2,1)S(1)} %get-tuple-element.246), channel_id=1, source_target_pairs={{0,16},{4,20},{8,24},{12,28},{16,0},{20,4},{24,8},{28,12},{1,17},{... | collective-permute-start | bytes 786440 | tf_op jit(solution)/shard_map/ppermute | solution.py:26
  124.2 1.6 collective-permute-start.35
  125.8 7.0 %collective-permute-done.31.refs_2_ = bf16[256,512]{1,0:T(8,128)(2,1)S(1)} collective-permute-done((bf16[256,512]{1,0:T(8,128)(2,1)S(1)}, bf16[256,512]{1,0:T(8,128)(2,1)S(1)}, u32[]{:S(2)}, u32[]{:S(2)}) %collective-permute-start.31) | collective-permute-done | bytes 262176 | tf_op jit(solution)/shard_map/ppermute | solution.py:26
  137.3 3.4 %all-to-all-start = ((bf16[4,32,1024]{2,1,0:T(8,128)(2,1)}), bf16[4,32,1024]{2,1,0:T(8,128)(2,1)S(1)}, u32[]{:S(2)}, u32[]{:S(2)}) async-start(bf16[4,32,1024]{2,1,0:T(8,128)(2,1)} %bitcast.11), calls=%async_computation | async-start | bytes 524288 | tf_op jit(solution)/shard_map/all_to_all | solution.py:907
  144.6 8.5 %collective-permute-done.36.refs_1_ = bf16[272,1024]{1,0:T(8,128)(2,1)S(1)} collective-permute-done((bf16[272,1024]{1,0:T(8,128)(2,1)S(1)}, bf16[272,1024]{1,0:T(8,128)(2,1)S(1)}, u32[]{:S(2)}, u32[]{:S(2)}) %collective-permute-start.36) | collective-permute-done | bytes 557088 | tf_op jit(solution)/shard_map/ppermute | solution.py:26
  156.0 6.2 %collective-permute-done.38.refs_1_ = bf16[144,1024]{1,0:T(8,128)(2,1)S(1)} collective-permute-done((bf16[144,1024]{1,0:T(8,128)(2,1)S(1)}, bf16[144,1024]{1,0:T(8,128)(2,1)S(1)}, u32[]{:S(2)}, u32[]{:S(2)}) %collective-permute-start.38) | collective-permute-done | bytes 294944 | tf_op jit(solution)/shard_map/ppermute | solution.py:26
  162.8 3.4 %collective-permute-start.41 = (bf16[80,1024]{1,0:T(8,128)(2,1)S(1)}, bf16[80,1024]{1,0:T(8,128)(2,1)S(1)}, u32[]{:S(2)}, u32[]{:S(2)}) collective-permute-start(bf16[80,1024]{1,0:T(8,128)(2,1)S(1)} %get-tuple-element.267), channel_id=1, source_target_pairs={{0,4},{4,0},{8,12},{12,8},{16,20},{20,16},{24,28},{28,24},{1,5},{5... | collective-permute-start | bytes 491528 | tf_op jit(solution)/shard_map/ppermute | solution.py:26
  166.3 1.5 up_fold.5
  170.2 1.9 %collective-permute-start.43 = (bf16[48,1024]{1,0:T(8,128)(2,1)S(1)}, bf16[48,1024]{1,0:T(8,128)(2,1)S(1)}, u32[]{:S(2)}, u32[]{:S(2)}) collective-permute-start(bf16[48,1024]{1,0:T(8,128)(2,1)S(1)} %get-tuple-element.273), channel_id=1, source_target_pairs={{0,16},{4,20},{8,24},{12,28},{16,0},{20,4},{24,8},{28,12},{1,17},{... | collective-permute-start | bytes 294920 | tf_op jit(solution)/shard_map/ppermute | solution.py:26
  172.1 3.2 %collective-permute-done.42.refs_1_ = bf16[32,1024]{1,0:T(8,128)(2,1)S(1)} collective-permute-done((bf16[32,1024]{1,0:T(8,128)(2,1)S(1)}, bf16[32,1024]{1,0:T(8,128)(2,1)S(1)}, u32[]{:S(2)}, u32[]{:S(2)}) %collective-permute-start.42) | collective-permute-done | bytes 65568 | tf_op jit(solution)/shard_map/ppermute | solution.py:26
  (204 shorter events, 51.1 us)
Async XLA Ops:
  3.6 9.4 %collective-permute-start.1 = (bf16[160,512]{1,0:T(8,128)(2,1)}, bf16[160,512]{1,0:T(8,128)(2,1)S(1)}, u32[]{:S(2)}, u32[]{:S(2)}) collective-permute-start(bf16[160,512]{1,0:T(8,128)(2,1)} %get-tuple-element.144.refs_0_), channel_id=1, source_target_pairs={{0,2},{1,3},{2,0},{3,1},{4,6},{5,7},{6,4},{7,5},{8,10},{9,11},{10,... | collective-permute-start | bytes 491528 | tf_op jit(solution)/shard_map/ppermute | solution.py:26
  13.5 9.7 %collective-permute-start.3 = (bf16[160,1024]{1,0:T(8,128)(2,1)S(1)}, bf16[160,1024]{1,0:T(8,128)(2,1)S(1)}, u32[]{:S(2)}, u32[]{:S(2)}) collective-permute-start(bf16[160,1024]{1,0:T(8,128)(2,1)S(1)} %copy-done.8), channel_id=1, source_target_pairs={{0,2},{1,3},{2,0},{3,1},{4,6},{5,7},{6,4},{7,5},{8,10},{9,11},{10,... | collective-permute-start | bytes 983048 | tf_op jit(solution)/shard_map/ppermute | solution.py:26
  23.9 9.5 %collective-permute-start.5 = (bf16[176,512]{1,0:T(8,128)(2,1)S(1)}, bf16[176,512]{1,0:T(8,128)(2,1)S(1)}, u32[]{:S(2)}, u32[]{:S(2)}) collective-permute-start(bf16[176,512]{1,0:T(8,128)(2,1)S(1)} %get-tuple-element.153), channel_id=1, source_target_pairs={{0,2},{1,3},{2,0},{3,1},{4,6},{5,7},{6,4},{7,5},{8,10},{9,11},{10,... | collective-permute-start | bytes 540680 | tf_op jit(solution)/shard_map/ppermute | solution.py:26
  24.8 8.7 %collective-permute-start.4 = (bf16[176,512]{1,0:T(8,128)(2,1)S(1)}, bf16[176,512]{1,0:T(8,128)(2,1)S(1)}, u32[]{:S(2)}, u32[]{:S(2)}) collective-permute-start(bf16[176,512]{1,0:T(8,128)(2,1)S(1)} %get-tuple-element.151), channel_id=1, source_target_pairs={{0,1},{1,0},{2,3},{3,2},{4,5},{5,4},{6,7},{7,6},{8,9},{9,8},{10,11... | collective-permute-start | bytes 540680 | tf_op jit(solution)/shard_map/ppermute | solution.py:26
  38.0 11.6 %collective-permute-start.8 = (bf16[160,1024]{1,0:T(8,128)(2,1)}, bf16[160,1024]{1,0:T(8,128)(2,1)S(1)}, u32[]{:S(2)}, u32[]{:S(2)}) collective-permute-start(bf16[160,1024]{1,0:T(8,128)(2,1)} %get-tuple-element.161.ff_low.refs_4_), channel_id=1, source_target_pairs={{0,2},{1,3},{2,0},{3,1},{4,6},{5,7},{6,4},{7,5},{8,10},{9,11},{10,... | collective-permute-start | bytes 983048 | tf_op jit(solution)/shard_map/ppermute | solution.py:26
  39.5 12.1 %collective-permute-start.7 = (bf16[160,1024]{1,0:T(8,128)(2,1)}, bf16[160,1024]{1,0:T(8,128)(2,1)S(1)}, u32[]{:S(2)}, u32[]{:S(2)}) collective-permute-start(bf16[160,1024]{1,0:T(8,128)(2,1)} %get-tuple-element.161.ff_low.refs_4_), channel_id=1, source_target_pairs={{0,1},{1,0},{2,3},{3,2},{4,5},{5,4},{6,7},{7,6},{8,9},{9,8},{10,11... | collective-permute-start | bytes 983048 | tf_op jit(solution)/shard_map/ppermute | solution.py:26
  39.5 11.2 %collective-permute-start.11 = (bf16[160,1024]{1,0:T(8,128)(2,1)}, bf16[160,1024]{1,0:T(8,128)(2,1)}, u32[]{:S(2)}, u32[]{:S(2)}) collective-permute-start(bf16[160,1024]{1,0:T(8,128)(2,1)} %copy-done.10), channel_id=1, source_target_pairs={{0,1},{1,0},{2,3},{3,2},{4,5},{5,4},{6,7},{7,6},{8,9},{9,8},{10,11... | collective-permute-start | bytes 983048 | tf_op jit(solution)/shard_map/ppermute | solution.py:26
  40.0 11.6 %collective-permute-start.10 = (bf16[160,1024]{1,0:T(8,128)(2,1)}, bf16[160,1024]{1,0:T(8,128)(2,1)}, u32[]{:S(2)}, u32[]{:S(2)}) collective-permute-start(bf16[160,1024]{1,0:T(8,128)(2,1)} %get-tuple-element.159.dy.refs_0_), channel_id=1, source_target_pairs={{0,1},{1,0},{2,3},{3,2},{4,5},{5,4},{6,7},{7,6},{8,9},{9,8},{10,11... | collective-permute-start | bytes 983048 | tf_op jit(solution)/shard_map/ppermute | solution.py:26
  50.2 18.2 %collective-permute-start.15 = (bf16[2,160,512]{2,1,0:T(8,128)(2,1)}, bf16[2,160,512]{2,1,0:T(8,128)(2,1)}, u32[]{:S(2)}, u32[]{:S(2)}) collective-permute-start(bf16[2,160,512]{2,1,0:T(8,128)(2,1)} %get-tuple-element.176), channel_id=1, source_target_pairs={{0,2},{1,3},{2,0},{3,1},{4,6},{5,7},{6,4},{7,5},{8,10},{9,11},{10,... | collective-permute-start | bytes 983048 | tf_op jit(solution)/shard_map/ppermute | solution.py:26
  50.7 17.6 %collective-permute-start.16 = (bf16[2,160,512]{2,1,0:T(8,128)(2,1)}, bf16[2,160,512]{2,1,0:T(8,128)(2,1)}, u32[]{:S(2)}, u32[]{:S(2)}) collective-permute-start(bf16[2,160,512]{2,1,0:T(8,128)(2,1)} %get-tuple-element.177), channel_id=1, source_target_pairs={{0,3},{1,2},{2,1},{3,0},{4,7},{5,6},{6,5},{7,4},{8,11},{9,10},{10,... | collective-permute-start | bytes 983048 | tf_op jit(solution)/shard_map/ppermute | solution.py:26
  65.2 8.0 %collective-permute-start.13 = (bf16[192,512]{1,0:T(8,128)(2,1)}, bf16[192,512]{1,0:T(8,128)(2,1)S(1)}, u32[]{:S(2)}, u32[]{:S(2)}) collective-permute-start(bf16[192,512]{1,0:T(8,128)(2,1)} %get-tuple-element.167.refs_4_), channel_id=1, source_target_pairs={{0,2},{1,3},{2,0},{3,1},{4,6},{5,7},{6,4},{7,5},{8,10},{9,11},{10,... | collective-permute-start | bytes 589832 | tf_op jit(solution)/shard_map/ppermute | solution.py:26
  65.7 11.4 %collective-permute-start.12 = (bf16[192,512]{1,0:T(8,128)(2,1)}, bf16[192,512]{1,0:T(8,128)(2,1)S(1)}, u32[]{:S(2)}, u32[]{:S(2)}) collective-permute-start(bf16[192,512]{1,0:T(8,128)(2,1)} %get-tuple-element.167.refs_4_), channel_id=1, source_target_pairs={{0,1},{1,0},{2,3},{3,2},{4,5},{5,4},{6,7},{7,6},{8,9},{9,8},{10,11... | collective-permute-start | bytes 589832 | tf_op jit(solution)/shard_map/ppermute | solution.py:26
  73.7 22.8 %collective-permute-start.23 = (bf16[2,160,512]{2,1,0:T(8,128)(2,1)S(1)}, bf16[2,160,512]{2,1,0:T(8,128)(2,1)S(1)}, u32[]{:S(2)}, u32[]{:S(2)}) collective-permute-start(bf16[2,160,512]{2,1,0:T(8,128)(2,1)S(1)} %copy-done.52), channel_id=1, source_target_pairs={{0,1},{1,0},{2,3},{3,2},{4,5},{5,4},{6,7},{7,6},{8,9},{9,8},{10,11... | collective-permute-start | bytes 983048 | tf_op jit(solution)/shard_map/ppermute | solution.py:26
  73.8 22.3 %collective-permute-start.25 = (bf16[2,160,512]{2,1,0:T(8,128)(2,1)S(1)}, bf16[2,160,512]{2,1,0:T(8,128)(2,1)S(1)}, u32[]{:S(2)}, u32[]{:S(2)}) collective-permute-start(bf16[2,160,512]{2,1,0:T(8,128)(2,1)S(1)} %copy-done.51), channel_id=1, source_target_pairs={{0,3},{1,2},{2,1},{3,0},{4,7},{5,6},{6,5},{7,4},{8,11},{9,10},{10,... | collective-permute-start | bytes 983048 | tf_op jit(solution)/shard_map/ppermute | solution.py:26
  75.3 13.9 %collective-permute-start.21 = (bf16[512,512]{1,0:T(8,128)(2,1)S(1)}, bf16[512,512]{1,0:T(8,128)(2,1)S(1)}, u32[]{:S(2)}, u32[]{:S(2)}) collective-permute-start(bf16[512,512]{1,0:T(8,128)(2,1)S(1)} %get-tuple-element.194), channel_id=1, source_target_pairs={{0,4},{4,0},{8,12},{12,8},{16,20},{20,16},{24,28},{28,24},{1,5},{5... | collective-permute-start | bytes 1572872 | tf_op jit(solution)/shard_map/ppermute | solution.py:26
  77.1 13.6 %collective-permute-start.22 = (bf16[512,512]{1,0:T(8,128)(2,1)S(1)}, bf16[512,512]{1,0:T(8,128)(2,1)S(1)}, u32[]{:S(2)}, u32[]{:S(2)}) collective-permute-start(bf16[512,512]{1,0:T(8,128)(2,1)S(1)} %get-tuple-element.195), channel_id=1, source_target_pairs={{0,8},{4,12},{8,0},{12,4},{16,24},{20,28},{24,16},{28,20},{1,9},{5... | collective-permute-start | bytes 1572872 | tf_op jit(solution)/shard_map/ppermute | solution.py:26
  78.7 19.4 %collective-permute-start.24 = (bf16[2,160,512]{2,1,0:T(8,128)(2,1)S(1)}, bf16[2,160,512]{2,1,0:T(8,128)(2,1)S(1)}, u32[]{:S(2)}, u32[]{:S(2)}) collective-permute-start(bf16[2,160,512]{2,1,0:T(8,128)(2,1)S(1)} %copy-done.50), channel_id=1, source_target_pairs={{0,2},{1,3},{2,0},{3,1},{4,6},{5,7},{6,4},{7,5},{8,10},{9,11},{10,... | collective-permute-start | bytes 983048 | tf_op jit(solution)/shard_map/ppermute | solution.py:26
  95.6 11.7 %collective-permute-start.18 = (bf16[160,512]{1,0:T(8,128)(2,1)S(1)}, bf16[160,512]{1,0:T(8,128)(2,1)S(1)}, u32[]{:S(2)}, u32[]{:S(2)}) collective-permute-start(bf16[160,512]{1,0:T(8,128)(2,1)S(1)} %get-tuple-element.184), channel_id=1, source_target_pairs={{0,1},{1,0},{2,3},{3,2},{4,5},{5,4},{6,7},{7,6},{8,9},{9,8},{10,11... | collective-permute-start | bytes 491528 | tf_op jit(solution)/shard_map/ppermute | solution.py:26
  96.1 11.2 %collective-permute-start.19 = (bf16[160,512]{1,0:T(8,128)(2,1)S(1)}, bf16[160,512]{1,0:T(8,128)(2,1)S(1)}, u32[]{:S(2)}, u32[]{:S(2)}) collective-permute-start(bf16[160,512]{1,0:T(8,128)(2,1)S(1)} %get-tuple-element.185), channel_id=1, source_target_pairs={{0,2},{1,3},{2,0},{3,1},{4,6},{5,7},{6,4},{7,5},{8,10},{9,11},{10,... | collective-permute-start | bytes 491528 | tf_op jit(solution)/shard_map/ppermute | solution.py:26
  96.5 8.0 %collective-permute-start.27 = (bf16[256,512]{1,0:T(8,128)(2,1)S(1)}, bf16[256,512]{1,0:T(8,128)(2,1)S(1)}, u32[]{:S(2)}, u32[]{:S(2)}) collective-permute-start(bf16[256,512]{1,0:T(8,128)(2,1)S(1)} %get-tuple-element.216), channel_id=1, source_target_pairs={{0,8},{4,12},{8,0},{12,4},{16,24},{20,28},{24,16},{28,20},{1,9},{5... | collective-permute-start | bytes 786440 | tf_op jit(solution)/shard_map/ppermute | solution.py:26
  104.5 13.5 %collective-permute-start.29 = (bf16[512,512]{1,0:T(8,128)(2,1)S(1)}, bf16[512,512]{1,0:T(8,128)(2,1)S(1)}, u32[]{:S(2)}, u32[]{:S(2)}) collective-permute-start(bf16[512,512]{1,0:T(8,128)(2,1)S(1)} %get-tuple-element.231), channel_id=1, source_target_pairs={{0,4},{4,0},{8,12},{12,8},{16,20},{20,16},{24,28},{28,24},{1,5},{5... | collective-permute-start | bytes 1572872 | tf_op jit(solution)/shard_map/ppermute | solution.py:26
  105.8 13.4 %collective-permute-start.30 = (bf16[512,512]{1,0:T(8,128)(2,1)S(1)}, bf16[512,512]{1,0:T(8,128)(2,1)S(1)}, u32[]{:S(2)}, u32[]{:S(2)}) collective-permute-start(bf16[512,512]{1,0:T(8,128)(2,1)S(1)} %get-tuple-element.232), channel_id=1, source_target_pairs={{0,8},{4,12},{8,0},{12,4},{16,24},{20,28},{24,16},{28,20},{1,9},{5... | collective-permute-start | bytes 1572872 | tf_op jit(solution)/shard_map/ppermute | solution.py:26
  110.6 23.6 %collective-permute-start.33 = (bf16[528,1024]{1,0:T(8,128)(2,1)S(1)}, bf16[528,1024]{1,0:T(8,128)(2,1)S(1)}, u32[]{:S(2)}, u32[]{:S(2)}) collective-permute-start(bf16[528,1024]{1,0:T(8,128)(2,1)S(1)} %get-tuple-element.243), channel_id=1, source_target_pairs={{0,1},{1,0},{2,3},{3,2},{4,5},{5,4},{6,7},{7,6},{8,9},{9,8},{10,11... | collective-permute-start | bytes 3244040 | tf_op jit(solution)/shard_map/ppermute | solution.py:26
  120.1 12.6 %collective-permute-start.31 = (bf16[256,512]{1,0:T(8,128)(2,1)S(1)}, bf16[256,512]{1,0:T(8,128)(2,1)S(1)}, u32[]{:S(2)}, u32[]{:S(2)}) collective-permute-start(bf16[256,512]{1,0:T(8,128)(2,1)S(1)} %get-tuple-element.239), channel_id=1, source_target_pairs={{0,8},{4,12},{8,0},{12,4},{16,24},{20,28},{24,16},{28,20},{1,9},{5... | collective-permute-start | bytes 786440 | tf_op jit(solution)/shard_map/ppermute | solution.py:26
  120.6 12.1 %collective-permute-start.32 = (bf16[256,512]{1,0:T(8,128)(2,1)S(1)}, bf16[256,512]{1,0:T(8,128)(2,1)S(1)}, u32[]{:S(2)}, u32[]{:S(2)}) collective-permute-start(bf16[256,512]{1,0:T(8,128)(2,1)S(1)} %get-tuple-element.240), channel_id=1, source_target_pairs={{0,4},{4,0},{8,12},{12,8},{16,20},{20,16},{24,28},{28,24},{1,5},{5... | collective-permute-start | bytes 786440 | tf_op jit(solution)/shard_map/ppermute | solution.py:26
  121.6 14.3 %collective-permute-start.34 = (bf16[128,1024]{1,0:T(8,128)(2,1)S(1)}, bf16[128,1024]{1,0:T(8,128)(2,1)S(1)}, u32[]{:S(2)}, u32[]{:S(2)}) collective-permute-start(bf16[128,1024]{1,0:T(8,128)(2,1)S(1)} %get-tuple-element.246), channel_id=1, source_target_pairs={{0,16},{4,20},{8,24},{12,28},{16,0},{20,4},{24,8},{28,12},{1,17},{... | collective-permute-start | bytes 786440 | tf_op jit(solution)/shard_map/ppermute | solution.py:26
  124.2 16.5 %collective-permute-start.35 = (bf16[256,1024]{1,0:T(8,128)(2,1)S(1)}, bf16[256,1024]{1,0:T(8,128)(2,1)S(1)}, u32[]{:S(2)}, u32[]{:S(2)}) collective-permute-start(bf16[256,1024]{1,0:T(8,128)(2,1)S(1)} %get-tuple-element.248), channel_id=1, source_target_pairs={{0,2},{1,3},{2,0},{3,1},{4,6},{5,7},{6,4},{7,5},{8,10},{9,11},{10,... | collective-permute-start | bytes 1572872 | tf_op jit(solution)/shard_map/ppermute | solution.py:26
  135.9 17.1 %collective-permute-start.36 = (bf16[272,1024]{1,0:T(8,128)(2,1)S(1)}, bf16[272,1024]{1,0:T(8,128)(2,1)S(1)}, u32[]{:S(2)}, u32[]{:S(2)}) collective-permute-start(bf16[272,1024]{1,0:T(8,128)(2,1)S(1)} %get-tuple-element.251), channel_id=1, source_target_pairs={{0,8},{4,12},{8,0},{12,4},{16,24},{20,28},{24,16},{28,20},{1,9},{5... | collective-permute-start | bytes 1671176 | tf_op jit(solution)/shard_map/ppermute | solution.py:26
  135.9 30.3 %collective-permute-start.39 = (bf16[128,1024]{1,0:T(8,128)(2,1)S(1)}, bf16[128,1024]{1,0:T(8,128)(2,1)S(1)}, u32[]{:S(2)}, u32[]{:S(2)}) collective-permute-start(bf16[128,1024]{1,0:T(8,128)(2,1)S(1)} %get-tuple-element.262), channel_id=1, source_target_pairs={{0,16},{4,20},{8,24},{12,28},{16,0},{20,4},{24,8},{28,12},{1,17},{... | collective-permute-start | bytes 786440 | tf_op jit(solution)/shard_map/ppermute | solution.py:26
  137.3 17.1 %all-to-all-start = ((bf16[4,32,1024]{2,1,0:T(8,128)(2,1)}), bf16[4,32,1024]{2,1,0:T(8,128)(2,1)S(1)}, u32[]{:S(2)}, u32[]{:S(2)}) async-start(bf16[4,32,1024]{2,1,0:T(8,128)(2,1)} %bitcast.11), calls=%async_computation | async-start | bytes 524288 | tf_op jit(solution)/shard_map/all_to_all | solution.py:907
  143.2 12.1 %collective-permute-start.37 = (bf16[128,1024]{1,0:T(8,128)(2,1)S(1)}, bf16[128,1024]{1,0:T(8,128)(2,1)S(1)}, u32[]{:S(2)}, u32[]{:S(2)}) collective-permute-start(bf16[128,1024]{1,0:T(8,128)(2,1)S(1)} %get-tuple-element.255), channel_id=1, source_target_pairs={{0,4},{4,0},{8,12},{12,8},{16,20},{20,16},{24,28},{28,24},{1,5},{5... | collective-permute-start | bytes 786440 | tf_op jit(solution)/shard_map/ppermute | solution.py:26
  156.0 11.8 %collective-permute-start.40 = (bf16[64,1024]{1,0:T(8,128)(2,1)S(1)}, bf16[64,1024]{1,0:T(8,128)(2,1)S(1)}, u32[]{:S(2)}, u32[]{:S(2)}) collective-permute-start(bf16[64,1024]{1,0:T(8,128)(2,1)S(1)} %get-tuple-element.264), channel_id=1, source_target_pairs={{0,8},{4,12},{8,0},{12,4},{16,24},{20,28},{24,16},{28,20},{1,9},{5... | collective-permute-start | bytes 393224 | tf_op jit(solution)/shard_map/ppermute | solution.py:26
  (69 other events, 314.9 us)

commit v4 on v3

--- a/solution.py
+++ b/solution.py
@@ -15,10 +15,10 @@
 F32 = jnp.float32
 BF16 = jnp.bfloat16
 MIB = 1024 * 1024
-TIMES = dict(latent=2.9, media=2.7, attend=3.1, mix=3.8, feed=9.6, feed_end=12.0, down_grad=4.0, attend_back=1.7, keyval_grad=3.8, up_grad=4.0, keyval_back=4.0, latent_back=1.6, query_grad=1.5)
+TIMES = dict(latent=2.9, media=2.7, attend=3.1, mix=3.8, feed=0.1, feed_end=36.0, down_grad=4.0, attend_back=1.7, keyval_grad=11.4, up_grad=4.0, keyval_back=4.0, latent_back=1.6, query_grad=1.5, pair=0.8, down_fold=0.8, up_fold=0.8, keyval_fold=0.8, query_fold=1.6, out_grad=0.8)
 RATE = 2e+09
-ORDER = "OGXBVDWPKDLRUUQDKQKQUKQKQ"
-KV_ORDER, QO_ORDER = "cxyz", "czxy"
+ORDER = "OGXBVDWYPKDLRUUQDKQKUQKQKQ"
+KV_ORDER, QO_ORDER = "cxyz", "cyzx"
 
 
 def swap(values, axis, bit):
@@ -407,7 +407,8 @@
 
 def attend_back_kernel(peers, per_slot, scale, *refs):
     qs, das, kv, dkv = refs[:peers], refs[peers : 2 * peers], refs[2 * peers], refs[2 * peers + 1]
-    dqs, held = refs[2 * peers + 2 : 3 * peers + 2], refs[3 * peers + 2]
+    (near, cross), held = refs[2 * peers + 2 : 2 * peers + 4], refs[2 * peers + 4]
+    dqs = [(cross if i % 2 else near, i // 2) for i in range(peers)]
     n, inner = kv.shape[0], kv.shape[2] // 2
     step = pl.program_id(0)
     items = [(s, t) for s in range(n) for t in range(inner // LANES)]
@@ -444,7 +445,14 @@
     for (s, t), ds in zip(items, dscores):
         dq = (unpaired(dot(ds, kv[s, :, cuts[t]])) * scale).astype(BF16)
         for i in range(peers):
-            dqs[i][pl.ds(rows[s], per_slot), cuts[t]] = dq[i * per_slot : (i + 1) * per_slot]
+            ref, at = dqs[i]
+            ref[at, pl.ds(rows[s], per_slot), cuts[t]] = dq[i * per_slot : (i + 1) * per_slot]
+
+
+def pair_kernel(near, other, mine, sent):
+    total = near[...].astype(F32) + other[...].astype(F32)
+    mine[...] = total[0].astype(BF16)
+    sent[...] = total[1].astype(BF16)
 
 
 def keyval_back_kernel(media, dkv, w_keyval, gain, media_grad, dlat, sums):
@@ -678,8 +686,8 @@
         scratch=[pltpu.VMEM((peers, padded, LANES), F32)],
         name="attend",
     )(*qs, keyval)
-    dys = {0: dy, peers // 2: swap(dy, "patch", peers // 2)}
-    parts = [parts[0]] + [swap(after(parts[j], dys[peers // 2]), "patch", j) for j in range(1, peers)]
+    parts = [parts[0]] + [swap(parts[j], "patch", j) for j in range(1, peers)]
+    dys = {0: dy, peers // 2: swap(after(dy, *parts[1:]), "patch", peers // 2)}
 
     attended, att_low, hidden, ff_low, lse = call(
         functools.partial(mix_kernel, peers),
@@ -697,7 +705,6 @@
     )(*parts, lat, w_out, gains, biases)
     bit = peers // 2
     ffs = {0: ff_low, bit: swap(ff_low, "patch", bit)}
-    dys = spread({0: after(dy, ff_low), bit: after(dys[bit], ff_low)})
 
     halves = 2
     blocks = ff // (peers * halves * LANES)
@@ -734,7 +741,8 @@
         [columns] * (2 * here) + [wide, wide],
         vmem=62, prefetch=1, name="feed",
     )(own, ff_low, dy, *([w_up] * count), *([w_down] * count))
-    ffs[peers // 2] = after(ffs[peers // 2], far[-1])
+    dys = spread({0: after(dy, ff_low), bit: after(dys[bit], far[-1])})
+    ffs[peers // 2] = after(ffs[peers // 2], dys[bit])
     ffs = spread(ffs)
 
     def cross(values):
@@ -809,13 +817,26 @@
             functools.partial(attend_back_kernel, peers, per_slot, scale),
             (slots // pair,),
             [whole((rows, inner))] * peers + [whole((rows + 4 * HEADS, inner))] * peers + [kv_block],
-            [(kv_block, out(keyval.shape, BF16))] + [(whole((rows, inner)), out((rows, inner), BF16))] * peers,
+            [(kv_block, out(keyval.shape, BF16))]
+            + [(whole((here, rows, inner)), out((here, rows, inner), BF16))] * 2,
             scratch=[pltpu.VMEM((peers, padded, LANES), F32)],
             name="attend_back",
         )(*qs, *near_das, keyval)
-        got["dkv"], dqs = values[0], values[1:]
-        got["dqs"] = [dqs[0]] + [swap(dqs[j], "patch", j) for j in range(1, peers)]
+        got["dkv"], near_dq, cross_dq = values
+        got["pair"] = (near_dq, swap(cross_dq, "patch", 1))
         return got["dkv"]
+
+    def pair_dq(mark):
+        near_dq, other = got["pair"]
+        mine, sent = call(
+            pair_kernel,
+            (1,),
+            [whole(near_dq.shape)] * 2,
+            [(whole((rows, inner)), out((rows, inner), BF16))] * 2,
+            name="pair",
+        )(after(near_dq, mark), other)
+        got["dqs"] = [mine, swap(sent, "patch", here)]
+        return mine
 
     def keyval_back(mark):
         got["media_grad"], got["dlat"], got["sums_media"] = call(
@@ -850,9 +871,9 @@
 
     def latent_back(mark):
         got["dq_low"], got["latent_grad"], got["sums"] = call(
-            functools.partial(latent_back_kernel, peers),
+            functools.partial(latent_back_kernel, here),
             (1,),
-            [whole((rows, inner))] * peers
+            [whole((rows, inner))] * here
             + [whole((rows, width))] * 3 + [whole(w_query.shape), gain_spec, whole((2, width)), whole((2, width))],
             [
                 (whole((rows, inner)), out((rows, inner), BF16)),
@@ -882,7 +903,7 @@
         return begun("Q", Scatter(own, both, [(qo_order, qo_plan)], open_rows, extra=sums, name="query_fold"))
 
     tasks = dict(
-        O=out_grad, G=down_grad, X=send_dpre, B=attend_back, V=keyval_back, W=keyval_grad, P=up_grad, L=latent_back,
+        O=out_grad, G=down_grad, X=send_dpre, B=attend_back, Y=pair_dq, V=keyval_back, W=keyval_grad, P=up_grad, L=latent_back,
         R=query_grad,
     )
     mark = datt_low

time: 179 us -> 172 us (0.961)
  starting transfers between devices: 37.4 us -> 33.3 us
  waiting for transfers between devices: 52.2 us -> 49.7 us
    ppermute x44 -> x43, starting transfers between devices: 34 us -> 29.9 us  [swap(): return lax.ppermute(values, axis, [(k, k ^ bit) for k in range(n)])]
    ppermute x44 -> x43, waiting for transfers between devices: 52.2 us -> 49.7 us  [swap(): return lax.ppermute(values, axis, [(k, k ^ bit) for k in range(n)])]
    unnamed x112 -> x100, local copies, waits for them, and re-layouts: 13 us -> 11.5 us
  transfers between devices with their start and end apart: 45 -> 44, of which waited for: 16 -> 16; matrix products, arithmetic and copies ran while one was open for 0% -> 0% of each run, Pallas kernels for 37% -> 39%
where the time goes in v4:
time: 172 us; the launch traced here: 171 us
  Pallas kernels  74.2 us (43%)
  waiting for transfers between devices  49.7 us (29%)
  starting transfers between devices  33.3 us (19%)
  local copies, waits for them, and re-layouts  12.2 us (7%)
    ppermute x43, waiting for transfers between devices, swap(): return lax.ppermute(values, axis, [(k, k ^ bit) for k in range(n)])  49.7 us
    ppermute x43, starting transfers between devices, swap(): return lax.ppermute(values, axis, [(k, k ^ bit) for k in range(n)])  29.9 us
    pallas_call x16, Pallas kernels, fold(): call(functools.partial(fold_kernel, nxt, end, len(kept), extra is not Non...  14 us
    pallas_call x1, Pallas kernels, on_device(): call(functools.partial(feed_end_kernel, per_slot, count, here), (here, ha...  12 us
    pallas_call x3, Pallas kernels, outer(): call(functools.partial(outer_kernel, count, [(order[0], plan[0]) for orde...  11.8 us
    unnamed x100, local copies, waits for them, and re-layouts  11.5 us
    pallas_call x1, Pallas kernels, on_device(): call(functools.partial(feed_kernel, count, here), (here, halves), [whole(...  9.57 us
    pallas_call x1, Pallas kernels, attend_back(): call(functools.partial(attend_back_kernel, peers, per_slot, scale), (slot...  5.66 us
  transfers between devices with their start and end apart: 44, of which 16 were waited for; matrix products, arithmetic and copies ran while one was open for 0% of the time, Pallas kernels for 39%

profile of v4, /device:TPU:0, one launch (start us, length us, event | category | flops | bytes accessed | tf_op | source)
XLA Modules:
  0.0 171.3 jit_solution(15732640096387284231)
XLA Ops:
  0.7 2.9 %latent.1 = (bf16[160,1024]{1,0:T(8,128)(2,1)}, bf16[160,512]{1,0:T(8,128)(2,1)}, bf16[160,1024]{1,0:T(8,128)(2,1)}) custom-call(s32[2]{0:T(128)} %counts.3, bf16[160,1024]{1,0:T(8,128)(2,1)} %bitcast.13, bf16[160,1024]{1,0:T(8,128)(2,1)} %bitcast.18, f32[3,1024]{1,0:T(4,128)} %refs_6_.7, f32[3,1024]{1,0:T(4,128)} %refs_7_.3, bf16[1024,512]{1,0:T(8,128)(2,1)} %refs_5_.7), custom_call_target="tpu_custom_call" | custom-call | flops 5800000000 | bytes 100000 | tf_op jit(solution)/shard_map/latent/pallas_call | solution.py:640
  3.6 3.0 %collective-permute-start.1 = (bf16[160,512]{1,0:T(8,128)(2,1)}, bf16[160,512]{1,0:T(8,128)(2,1)S(1)}, u32[]{:S(2)}, u32[]{:S(2)}) collective-permute-start(bf16[160,512]{1,0:T(8,128)(2,1)} %get-tuple-element.143.refs_0_), channel_id=1, source_target_pairs={{0,2},{1,3},{2,0},{3,1},{4,6},{5,7},{6,4},{7,5},{8,10},{9,11},{10,... | collective-permute-start | bytes 491528 | tf_op jit(solution)/shard_map/ppermute | solution.py:26
  6.6 1.6 copy-done.4
  9.2 2.7 %media.3 = (bf16[10,80,1024]{2,1,0:T(8,128)(2,1)S(1)}, bf16[10,80,1024]{2,1,0:T(8,128)(2,1)S(1)}) custom-call(bf16[10,64,1024]{2,1,0:T(8,128)(2,1)S(1)} %copy-done.6, bf16[160,1024]{1,0:T(8,128)(2,1)S(1)} %copy-done.38, f32[3,1024]{1,0:T(4,128)S(1)} %copy-done.23, f32[3,1024]{1,0:T(4,128)S(1)} %copy-done.22, bf16[1024,1024]{1,0:T(8,128)(2,1)S(1)} %copy-done.4), custom_call_target="tpu_custom_call" | custom-call | flops 5400000000 | bytes 100000 | tf_op jit(solution)/shard_map/media/pallas_call | solution.py:656
  14.7 2.9 %attend.1 = (bf16[176,512]{1,0:T(8,128)(2,1)S(1)}, bf16[176,512]{1,0:T(8,128)(2,1)S(1)}, bf16[176,512]{1,0:T(8,128)(2,1)S(1)}, bf16[176,512]{1,0:T(8,128)(2,1)S(1)}) custom-call(bf16[160,512]{1,0:T(8,128)(2,1)S(1)} %copy-done.14, bf16[160,512]{1,0:T(8,128)(2,1)S(1)} %collective-permute-done.refs_1_, bf16[160,512]{1,0:T(8,128)(2,1)S(1)} %collective-permute-done.1.refs_2_, ...), custom_call_target="tpu_custom_call" | custom-call | flops 6200000000 | bytes 100000 | tf_op jit(solution)/shard_map/attend/pallas_call | solution.py:681
  18.7 1.5 collective-permute-start.5
  20.2 5.9 %collective-permute-done.4.refs_2_ = bf16[176,512]{1,0:T(8,128)(2,1)S(1)} collective-permute-done((bf16[176,512]{1,0:T(8,128)(2,1)S(1)}, bf16[176,512]{1,0:T(8,128)(2,1)S(1)}, u32[]{:S(2)}, u32[]{:S(2)}) %collective-permute-start.4) | collective-permute-done | bytes 180256 | tf_op jit(solution)/shard_map/ppermute | solution.py:26
  26.1 2.2 %collective-permute-done.5.refs_3_ = bf16[176,512]{1,0:T(8,128)(2,1)S(1)} collective-permute-done((bf16[176,512]{1,0:T(8,128)(2,1)S(1)}, bf16[176,512]{1,0:T(8,128)(2,1)S(1)}, u32[]{:S(2)}, u32[]{:S(2)}) %collective-permute-start.5) | collective-permute-done | bytes 180256 | tf_op jit(solution)/shard_map/ppermute | solution.py:26
  29.6 3.8 %mix.1 = (f32[160,512]{1,0:T(8,128)}, bf16[160,512]{1,0:T(8,128)(2,1)}, f32[160,1024]{1,0:T(8,128)}, bf16[160,1024]{1,0:T(8,128)(2,1)}, f32[8,256]{1,0:T(8,128)}) custom-call(bf16[176,512]{1,0:T(8,128)(2,1)} %copy-done.42, bf16[176,512]{1,0:T(8,128)(2,1)} %copy-done.47, bf16[176,512]{1,0:T(8,128)(2,1)} %copy-done.48, bf16[176,512]{1,0:T(8,128)(2,1)} %copy-done.49, ...), custom_call_target="tpu_custom_call" | custom-call | flops 7600000000 | bytes 100000 | tf_op jit(solution)/shard_map/mix/pallas_call | solution.py:692
  33.4 1.5 collective-permute-start.7
  36.0 9.6 %feed.1 = (bf16[2,160,512]{2,1,0:T(8,128)(2,1)}, bf16[2,160,512]{2,1,0:T(8,128)(2,1)}, bf16[2,160,512]{2,1,0:T(8,128)(2,1)}, bf16[2,160,512]{2,1,0:T(8,128)(2,1)...) custom-call(s32[2]{0:T(128)} %pad_add_fusion.own, bf16[160,1024]{1,0:T(8,128)(2,1)} %get-tuple-element.158.ff_low.refs_4_, ...), custom_call_target="tpu_custom_call" | custom-call | flops 200000000 | bytes 100000 | tf_op jit(solution)/shard_map/feed/pallas_call | solution.py:737
  49.7 12.0 %feed_end.1 = (bf16[2,160,512]{2,1,0:T(8,128)(2,1)}, bf16[2,160,512]{2,1,0:T(8,128)(2,1)}, bf16[2,160,512]{2,1,0:T(8,128)(2,1)}, bf16[2,160,512]{2,1,0:T(8,128)(...) custom-call(s32[2]{0:T(128)} %pad_add_fusion.own, ...), custom_call_target="tpu_custom_call" | custom-call | flops 71999995904 | bytes 100000 | tf_op jit(solution)/shard_map/feed_end/pallas_call | solution.py:752
  66.0 4.2 %down_grad.1 = (bf16[512,512]{1,0:T(8,128)(2,1)S(1)}, bf16[512,512]{1,0:T(8,128)(2,1)S(1)}, bf16[512,512]{1,0:T(8,128)(2,1)S(1)}, bf16[512,512]{1,0:T(8,128)(2,1)S(1)}) custom-call(s32[2]{0:T(128)S(1)} %copy-done.3, bf16[160,1024]{1,0:T(8,128)(2,1)S(1)} %copy-done.2, bf16[160,1024]{1,0:T(8,128)(2,1)} %collective-permute-done.10.refs_1_, ...), custom_call_target="tpu_custom_call" | custom-call | flops 8000000000 | bytes 100000 | tf_op jit(solution)/shard_map/down_grad/pallas_call | solution.py:536
  70.8 1.8 %collective-permute-start.24 = (bf16[2,160,512]{2,1,0:T(8,128)(2,1)S(1)}, bf16[2,160,512]{2,1,0:T(8,128)(2,1)S(1)}, u32[]{:S(2)}, u32[]{:S(2)}) collective-permute-start(bf16[2,160,512]{2,1,0:T(8,128)(2,1)S(1)} %copy-done.45), channel_id=1, source_target_pairs={{0,3},{1,2},{2,1},{3,0},{4,7},{5,6},{6,5},{7,4},{8,11},{9,10},{10,... | collective-permute-start | bytes 983048 | tf_op jit(solution)/shard_map/ppermute | solution.py:26
  72.6 1.5 collective-permute-start.18
  74.1 1.6 collective-permute-start.19
  76.3 5.7 %attend_back.1 = (bf16[10,80,1024]{2,1,0:T(8,128)(2,1)S(1)}, bf16[2,160,512]{2,1,0:T(8,128)(2,1)S(1)}, bf16[2,160,512]{2,1,0:T(8,128)(2,1)S(1)}) custom-call(bf16[160,512]{1,0:T(8,128)(2,1)S(1)} %copy-done.15, bf16[160,512]{1,0:T(8,128)(2,1)S(1)} %copy-done.19, bf16[160,512]{1,0:T(8,128)(2,1)S(1)} %copy-done.17, bf16[160,512]{1,0:T(8,128)(2,1)S(1)} %copy-done.21, ...), custom_call_target="tpu_custom_call" | custom-call | flops 3400000000 | bytes 100000 | tf_op jit(solution)/shard_map/attend_back/pallas_call | solution.py:816
  82.0 4.2 %keyval_back.1 = (bf16[10,64,1024]{2,1,0:T(8,128)(2,1)}, f32[160,1024]{1,0:T(8,128)S(1)}, f32[2,1024]{1,0:T(2,128)S(1)}) custom-call(bf16[10,64,1024]{2,1,0:T(8,128)(2,1)S(1)} %copy-done.6, bf16[10,80,1024]{2,1,0:T(8,128)(2,1)S(1)} %get-tuple-element.190.dkv, bf16[1024,1024]{1,0:T(8,128)(2,1)S(1)} %copy-done.5, f32[3,1024]{1,0:T(4,128)S(1)} %copy-done.24), custom_call_target="tpu_custom_call" | custom-call | flops 8000000000 | bytes 100000 | tf_op jit(solution)/shard_map/keyval_back/pallas_call | solution.py:842
  88.7 3.9 %keyval_grad.1 = (bf16[512,1024]{1,0:T(8,128)(2,1)S(1)}, bf16[512,1024]{1,0:T(8,128)(2,1)S(1)}) custom-call(s32[2]{0:T(128)S(1)} %copy-done.3, bf16[800,1024]{1,0:T(8,128)(2,1)S(1)} %bitcast.17, bf16[800,1024]{1,0:T(8,128)(2,1)S(1)} %bitcast.16), custom_call_target="tpu_custom_call" | custom-call | flops 22799998976 | bytes 100000 | tf_op jit(solution)/shard_map/keyval_grad/pallas_call | solution.py:536
  92.8 1.6 collective-permute-start.26
  95.3 3.7 %up_grad.1 = (bf16[512,512]{1,0:T(8,128)(2,1)S(1)}, bf16[512,512]{1,0:T(8,128)(2,1)S(1)}, bf16[512,512]{1,0:T(8,128)(2,1)S(1)}, bf16[512,512]{1,0:T(8,128)(2,1)S(1)}) custom-call(s32[2]{0:T(128)S(1)} %copy-done.3, bf16[2,160,512]{2,1,0:T(8,128)(2,1)S(1)} %copy-done.40, bf16[2,160,512]{2,1,0:T(8,128)(2,1)S(1)} %collective-permute-done.22.refs_1_, ...), custom_call_target="tpu_custom_call" | custom-call | flops 8000000000 | bytes 100000 | tf_op jit(solution)/shard_map/up_grad/pallas_call | solution.py:536
  104.3 1.9 %collective-permute-done.21.refs_1_ = bf16[160,512]{1,0:T(8,128)(2,1)S(1)} collective-permute-done((bf16[160,512]{1,0:T(8,128)(2,1)S(1)}, bf16[160,512]{1,0:T(8,128)(2,1)S(1)}, u32[]{:S(2)}, u32[]{:S(2)}) %collective-permute-start.21) | collective-permute-done | bytes 163872 | tf_op jit(solution)/shard_map/ppermute | solution.py:26
  106.2 1.5 latent_back.1
  109.2 4.9 %collective-permute-done.28.refs_2_ = bf16[512,512]{1,0:T(8,128)(2,1)S(1)} collective-permute-done((bf16[512,512]{1,0:T(8,128)(2,1)S(1)}, bf16[512,512]{1,0:T(8,128)(2,1)S(1)}, u32[]{:S(2)}, u32[]{:S(2)}) %collective-permute-start.28) | collective-permute-done | bytes 524320 | tf_op jit(solution)/shard_map/ppermute | solution.py:26
  116.3 2.6 %collective-permute-start.33 = (bf16[128,1024]{1,0:T(8,128)(2,1)S(1)}, bf16[128,1024]{1,0:T(8,128)(2,1)S(1)}, u32[]{:S(2)}, u32[]{:S(2)}) collective-permute-start(bf16[128,1024]{1,0:T(8,128)(2,1)S(1)} %get-tuple-element.244), channel_id=1, source_target_pairs={{0,16},{4,20},{8,24},{12,28},{16,0},{20,4},{24,8},{28,12},{1,17},{... | collective-permute-start | bytes 786440 | tf_op jit(solution)/shard_map/ppermute | solution.py:26
  119.4 8.8 %collective-permute-done.30.refs_2_ = bf16[256,512]{1,0:T(8,128)(2,1)S(1)} collective-permute-done((bf16[256,512]{1,0:T(8,128)(2,1)S(1)}, bf16[256,512]{1,0:T(8,128)(2,1)S(1)}, u32[]{:S(2)}, u32[]{:S(2)}) %collective-permute-start.30) | collective-permute-done | bytes 262176 | tf_op jit(solution)/shard_map/ppermute | solution.py:26
  135.4 3.4 %all-to-all-start = ((bf16[4,32,1024]{2,1,0:T(8,128)(2,1)}), bf16[4,32,1024]{2,1,0:T(8,128)(2,1)S(1)}, u32[]{:S(2)}, u32[]{:S(2)}) async-start(bf16[4,32,1024]{2,1,0:T(8,128)(2,1)} %bitcast.11), calls=%async_computation | async-start | bytes 524288 | tf_op jit(solution)/shard_map/all_to_all | solution.py:928
  138.8 8.0 %collective-permute-done.35.refs_1_ = bf16[272,1024]{1,0:T(8,128)(2,1)S(1)} collective-permute-done((bf16[272,1024]{1,0:T(8,128)(2,1)S(1)}, bf16[272,1024]{1,0:T(8,128)(2,1)S(1)}, u32[]{:S(2)}, u32[]{:S(2)}) %collective-permute-start.35) | collective-permute-done | bytes 557088 | tf_op jit(solution)/shard_map/ppermute | solution.py:26
  150.6 1.5 up_fold.5
  152.8 3.9 %collective-permute-done.38.refs_1_ = bf16[144,1024]{1,0:T(8,128)(2,1)S(1)} collective-permute-done((bf16[144,1024]{1,0:T(8,128)(2,1)S(1)}, bf16[144,1024]{1,0:T(8,128)(2,1)S(1)}, u32[]{:S(2)}, u32[]{:S(2)}) %collective-permute-start.38) | collective-permute-done | bytes 294944 | tf_op jit(solution)/shard_map/ppermute | solution.py:26
  159.5 3.3 %collective-permute-done.40.refs_1_ = bf16[80,1024]{1,0:T(8,128)(2,1)S(1)} collective-permute-done((bf16[80,1024]{1,0:T(8,128)(2,1)S(1)}, bf16[80,1024]{1,0:T(8,128)(2,1)S(1)}, u32[]{:S(2)}, u32[]{:S(2)}) %collective-permute-start.40) | collective-permute-done | bytes 163872 | tf_op jit(solution)/shard_map/ppermute | solution.py:26
  166.0 3.4 %collective-permute-done.42.refs_1_ = bf16[48,1024]{1,0:T(8,128)(2,1)S(1)} collective-permute-done((bf16[48,1024]{1,0:T(8,128)(2,1)S(1)}, bf16[48,1024]{1,0:T(8,128)(2,1)S(1)}, u32[]{:S(2)}, u32[]{:S(2)}) %collective-permute-start.42) | collective-permute-done | bytes 98336 | tf_op jit(solution)/shard_map/ppermute | solution.py:26
  (191 shorter events, 49.2 us)
Async XLA Ops:
  3.6 9.5 %collective-permute-start.1 = (bf16[160,512]{1,0:T(8,128)(2,1)}, bf16[160,512]{1,0:T(8,128)(2,1)S(1)}, u32[]{:S(2)}, u32[]{:S(2)}) collective-permute-start(bf16[160,512]{1,0:T(8,128)(2,1)} %get-tuple-element.143.refs_0_), channel_id=1, source_target_pairs={{0,2},{1,3},{2,0},{3,1},{4,6},{5,7},{6,4},{7,5},{8,10},{9,11},{10,... | collective-permute-start | bytes 491528 | tf_op jit(solution)/shard_map/ppermute | solution.py:26
  6.6 7.1 %collective-permute-start = (bf16[160,512]{1,0:T(8,128)(2,1)}, bf16[160,512]{1,0:T(8,128)(2,1)S(1)}, u32[]{:S(2)}, u32[]{:S(2)}) collective-permute-start(bf16[160,512]{1,0:T(8,128)(2,1)} %get-tuple-element.143.refs_0_), channel_id=1, source_target_pairs={{0,1},{1,0},{2,3},{3,2},{4,5},{5,4},{6,7},{7,6},{8,9},{9,8},{10,11... | collective-permute-start | bytes 491528 | tf_op jit(solution)/shard_map/ppermute | solution.py:26
  18.7 7.4 %collective-permute-start.4 = (bf16[176,512]{1,0:T(8,128)(2,1)S(1)}, bf16[176,512]{1,0:T(8,128)(2,1)S(1)}, u32[]{:S(2)}, u32[]{:S(2)}) collective-permute-start(bf16[176,512]{1,0:T(8,128)(2,1)S(1)} %get-tuple-element.149), channel_id=1, source_target_pairs={{0,2},{1,3},{2,0},{3,1},{4,6},{5,7},{6,4},{7,5},{8,10},{9,11},{10,... | collective-permute-start | bytes 540680 | tf_op jit(solution)/shard_map/ppermute | solution.py:26
  18.7 9.6 %collective-permute-start.5 = (bf16[176,512]{1,0:T(8,128)(2,1)S(1)}, bf16[176,512]{1,0:T(8,128)(2,1)S(1)}, u32[]{:S(2)}, u32[]{:S(2)}) collective-permute-start(bf16[176,512]{1,0:T(8,128)(2,1)S(1)} %get-tuple-element.150), channel_id=1, source_target_pairs={{0,3},{1,2},{2,1},{3,0},{4,7},{5,6},{6,5},{7,4},{8,11},{9,10},{10,... | collective-permute-start | bytes 540680 | tf_op jit(solution)/shard_map/ppermute | solution.py:26
  29.0 16.5 %collective-permute-start.8 = (bf16[160,1024]{1,0:T(8,128)(2,1)S(1)}, bf16[160,1024]{1,0:T(8,128)(2,1)}, u32[]{:S(2)}, u32[]{:S(2)}) collective-permute-start(bf16[160,1024]{1,0:T(8,128)(2,1)S(1)} %copy-done.1), channel_id=1, source_target_pairs={{0,2},{1,3},{2,0},{3,1},{4,6},{5,7},{6,4},{7,5},{8,10},{9,11},{10,... | collective-permute-start | bytes 983048 | tf_op jit(solution)/shard_map/ppermute | solution.py:26
  33.4 12.9 %collective-permute-start.7 = (bf16[160,1024]{1,0:T(8,128)(2,1)}, bf16[160,1024]{1,0:T(8,128)(2,1)S(1)}, u32[]{:S(2)}, u32[]{:S(2)}) collective-permute-start(bf16[160,1024]{1,0:T(8,128)(2,1)} %get-tuple-element.158.ff_low.refs_4_), channel_id=1, source_target_pairs={{0,2},{1,3},{2,0},{3,1},{4,6},{5,7},{6,4},{7,5},{8,10},{9,11},{10,... | collective-permute-start | bytes 983048 | tf_op jit(solution)/shard_map/ppermute | solution.py:26
  35.5 12.7 %collective-permute-start.6 = (bf16[160,1024]{1,0:T(8,128)(2,1)}, bf16[160,1024]{1,0:T(8,128)(2,1)}, u32[]{:S(2)}, u32[]{:S(2)}) collective-permute-start(bf16[160,1024]{1,0:T(8,128)(2,1)} %get-tuple-element.158.ff_low.refs_4_), channel_id=1, source_target_pairs={{0,1},{1,0},{2,3},{3,2},{4,5},{5,4},{6,7},{7,6},{8,9},{9,8},{10,11... | collective-permute-start | bytes 983048 | tf_op jit(solution)/shard_map/ppermute | solution.py:26
  35.6 11.5 %collective-permute-start.10 = (bf16[160,1024]{1,0:T(8,128)(2,1)S(1)}, bf16[160,1024]{1,0:T(8,128)(2,1)}, u32[]{:S(2)}, u32[]{:S(2)}) collective-permute-start(bf16[160,1024]{1,0:T(8,128)(2,1)S(1)} %copy-done.1), channel_id=1, source_target_pairs={{0,1},{1,0},{2,3},{3,2},{4,5},{5,4},{6,7},{7,6},{8,9},{9,8},{10,11... | collective-permute-start | bytes 983048 | tf_op jit(solution)/shard_map/ppermute | solution.py:26
  46.8 18.7 %collective-permute-start.15 = (bf16[2,160,512]{2,1,0:T(8,128)(2,1)}, bf16[2,160,512]{2,1,0:T(8,128)(2,1)}, u32[]{:S(2)}, u32[]{:S(2)}) collective-permute-start(bf16[2,160,512]{2,1,0:T(8,128)(2,1)} %get-tuple-element.173), channel_id=1, source_target_pairs={{0,2},{1,3},{2,0},{3,1},{4,6},{5,7},{6,4},{7,5},{8,10},{9,11},{10,... | collective-permute-start | bytes 983048 | tf_op jit(solution)/shard_map/ppermute | solution.py:26
  47.1 18.4 %collective-permute-start.16 = (bf16[2,160,512]{2,1,0:T(8,128)(2,1)}, bf16[2,160,512]{2,1,0:T(8,128)(2,1)S(1)}, u32[]{:S(2)}, u32[]{:S(2)}) collective-permute-start(bf16[2,160,512]{2,1,0:T(8,128)(2,1)} %get-tuple-element.174), channel_id=1, source_target_pairs={{0,3},{1,2},{2,1},{3,0},{4,7},{5,6},{6,5},{7,4},{8,11},{9,10},{10,... | collective-permute-start | bytes 983048 | tf_op jit(solution)/shard_map/ppermute | solution.py:26
  62.5 7.6 %collective-permute-start.13 = (bf16[192,512]{1,0:T(8,128)(2,1)}, bf16[192,512]{1,0:T(8,128)(2,1)S(1)}, u32[]{:S(2)}, u32[]{:S(2)}) collective-permute-start(bf16[192,512]{1,0:T(8,128)(2,1)} %get-tuple-element.164.refs_4_), channel_id=1, source_target_pairs={{0,2},{1,3},{2,0},{3,1},{4,6},{5,7},{6,4},{7,5},{8,10},{9,11},{10,... | collective-permute-start | bytes 589832 | tf_op jit(solution)/shard_map/ppermute | solution.py:26
  62.8 11.3 %collective-permute-start.12 = (bf16[192,512]{1,0:T(8,128)(2,1)}, bf16[192,512]{1,0:T(8,128)(2,1)S(1)}, u32[]{:S(2)}, u32[]{:S(2)}) collective-permute-start(bf16[192,512]{1,0:T(8,128)(2,1)} %get-tuple-element.164.refs_4_), channel_id=1, source_target_pairs={{0,1},{1,0},{2,3},{3,2},{4,5},{5,4},{6,7},{7,6},{8,9},{9,8},{10,11... | collective-permute-start | bytes 589832 | tf_op jit(solution)/shard_map/ppermute | solution.py:26
  70.7 24.5 %collective-permute-start.22 = (bf16[2,160,512]{2,1,0:T(8,128)(2,1)S(1)}, bf16[2,160,512]{2,1,0:T(8,128)(2,1)S(1)}, u32[]{:S(2)}, u32[]{:S(2)}) collective-permute-start(bf16[2,160,512]{2,1,0:T(8,128)(2,1)S(1)} %copy-done.46), channel_id=1, source_target_pairs={{0,1},{1,0},{2,3},{3,2},{4,5},{5,4},{6,7},{7,6},{8,9},{9,8},{10,11... | collective-permute-start | bytes 983048 | tf_op jit(solution)/shard_map/ppermute | solution.py:26
  70.8 22.0 %collective-permute-start.24 = (bf16[2,160,512]{2,1,0:T(8,128)(2,1)S(1)}, bf16[2,160,512]{2,1,0:T(8,128)(2,1)S(1)}, u32[]{:S(2)}, u32[]{:S(2)}) collective-permute-start(bf16[2,160,512]{2,1,0:T(8,128)(2,1)S(1)} %copy-done.45), channel_id=1, source_target_pairs={{0,3},{1,2},{2,1},{3,0},{4,7},{5,6},{6,5},{7,4},{8,11},{9,10},{10,... | collective-permute-start | bytes 983048 | tf_op jit(solution)/shard_map/ppermute | solution.py:26
  72.6 13.9 %collective-permute-start.18 = (bf16[512,512]{1,0:T(8,128)(2,1)S(1)}, bf16[512,512]{1,0:T(8,128)(2,1)S(1)}, u32[]{:S(2)}, u32[]{:S(2)}) collective-permute-start(bf16[512,512]{1,0:T(8,128)(2,1)S(1)} %get-tuple-element.187), channel_id=1, source_target_pairs={{0,4},{4,0},{8,12},{12,8},{16,20},{20,16},{24,28},{28,24},{1,5},{5... | collective-permute-start | bytes 1572872 | tf_op jit(solution)/shard_map/ppermute | solution.py:26
  74.1 13.6 %collective-permute-start.19 = (bf16[512,512]{1,0:T(8,128)(2,1)S(1)}, bf16[512,512]{1,0:T(8,128)(2,1)S(1)}, u32[]{:S(2)}, u32[]{:S(2)}) collective-permute-start(bf16[512,512]{1,0:T(8,128)(2,1)S(1)} %get-tuple-element.188), channel_id=1, source_target_pairs={{0,8},{4,12},{8,0},{12,4},{16,24},{20,28},{24,16},{28,20},{1,9},{5... | collective-permute-start | bytes 1572872 | tf_op jit(solution)/shard_map/ppermute | solution.py:26
  75.7 19.5 %collective-permute-start.23 = (bf16[2,160,512]{2,1,0:T(8,128)(2,1)S(1)}, bf16[2,160,512]{2,1,0:T(8,128)(2,1)S(1)}, u32[]{:S(2)}, u32[]{:S(2)}) collective-permute-start(bf16[2,160,512]{2,1,0:T(8,128)(2,1)S(1)} %copy-done.44), channel_id=1, source_target_pairs={{0,2},{1,3},{2,0},{3,1},{4,6},{5,7},{6,4},{7,5},{8,10},{9,11},{10,... | collective-permute-start | bytes 983048 | tf_op jit(solution)/shard_map/ppermute | solution.py:26
  92.6 8.2 %collective-permute-start.25 = (bf16[512,1024]{1,0:T(8,128)(2,1)S(1)}, bf16[512,1024]{1,0:T(8,128)(2,1)S(1)}, u32[]{:S(2)}, u32[]{:S(2)}) collective-permute-start(bf16[512,1024]{1,0:T(8,128)(2,1)S(1)} %get-tuple-element.208), channel_id=1, source_target_pairs={{0,1},{1,0},{2,3},{3,2},{4,5},{5,4},{6,7},{7,6},{8,9},{9,8},{10,11... | collective-permute-start | bytes 3145736 | tf_op jit(solution)/shard_map/ppermute | solution.py:26
  92.8 9.4 %collective-permute-start.26 = (bf16[256,512]{1,0:T(8,128)(2,1)S(1)}, bf16[256,512]{1,0:T(8,128)(2,1)S(1)}, u32[]{:S(2)}, u32[]{:S(2)}) collective-permute-start(bf16[256,512]{1,0:T(8,128)(2,1)S(1)} %get-tuple-element.214), channel_id=1, source_target_pairs={{0,8},{4,12},{8,0},{12,4},{16,24},{20,28},{24,16},{28,20},{1,9},{5... | collective-permute-start | bytes 786440 | tf_op jit(solution)/shard_map/ppermute | solution.py:26
  94.4 9.2 %collective-permute-start.27 = (bf16[256,512]{1,0:T(8,128)(2,1)S(1)}, bf16[256,512]{1,0:T(8,128)(2,1)S(1)}, u32[]{:S(2)}, u32[]{:S(2)}) collective-permute-start(bf16[256,512]{1,0:T(8,128)(2,1)S(1)} %get-tuple-element.215), channel_id=1, source_target_pairs={{0,4},{4,0},{8,12},{12,8},{16,20},{20,16},{24,28},{28,24},{1,5},{5... | collective-permute-start | bytes 786440 | tf_op jit(solution)/shard_map/ppermute | solution.py:26
  99.0 15.1 %collective-permute-start.28 = (bf16[512,512]{1,0:T(8,128)(2,1)S(1)}, bf16[512,512]{1,0:T(8,128)(2,1)S(1)}, u32[]{:S(2)}, u32[]{:S(2)}) collective-permute-start(bf16[512,512]{1,0:T(8,128)(2,1)S(1)} %get-tuple-element.229), channel_id=1, source_target_pairs={{0,4},{4,0},{8,12},{12,8},{16,20},{20,16},{24,28},{28,24},{1,5},{5... | collective-permute-start | bytes 1572872 | tf_op jit(solution)/shard_map/ppermute | solution.py:26
  100.3 13.8 %collective-permute-start.29 = (bf16[512,512]{1,0:T(8,128)(2,1)S(1)}, bf16[512,512]{1,0:T(8,128)(2,1)S(1)}, u32[]{:S(2)}, u32[]{:S(2)}) collective-permute-start(bf16[512,512]{1,0:T(8,128)(2,1)S(1)} %get-tuple-element.230), channel_id=1, source_target_pairs={{0,8},{4,12},{8,0},{12,4},{16,24},{20,28},{24,16},{28,20},{1,9},{5... | collective-permute-start | bytes 1572872 | tf_op jit(solution)/shard_map/ppermute | solution.py:26
  109.1 20.5 %collective-permute-start.32 = (bf16[528,1024]{1,0:T(8,128)(2,1)S(1)}, bf16[528,1024]{1,0:T(8,128)(2,1)S(1)}, u32[]{:S(2)}, u32[]{:S(2)}) collective-permute-start(bf16[528,1024]{1,0:T(8,128)(2,1)S(1)} %get-tuple-element.241), channel_id=1, source_target_pairs={{0,1},{1,0},{2,3},{3,2},{4,5},{5,4},{6,7},{7,6},{8,9},{9,8},{10,11... | collective-permute-start | bytes 3244040 | tf_op jit(solution)/shard_map/ppermute | solution.py:26
  114.9 13.2 %collective-permute-start.30 = (bf16[256,512]{1,0:T(8,128)(2,1)S(1)}, bf16[256,512]{1,0:T(8,128)(2,1)S(1)}, u32[]{:S(2)}, u32[]{:S(2)}) collective-permute-start(bf16[256,512]{1,0:T(8,128)(2,1)S(1)} %get-tuple-element.237), channel_id=1, source_target_pairs={{0,8},{4,12},{8,0},{12,4},{16,24},{20,28},{24,16},{28,20},{1,9},{5... | collective-permute-start | bytes 786440 | tf_op jit(solution)/shard_map/ppermute | solution.py:26
  115.5 12.7 %collective-permute-start.31 = (bf16[256,512]{1,0:T(8,128)(2,1)S(1)}, bf16[256,512]{1,0:T(8,128)(2,1)S(1)}, u32[]{:S(2)}, u32[]{:S(2)}) collective-permute-start(bf16[256,512]{1,0:T(8,128)(2,1)S(1)} %get-tuple-element.238), channel_id=1, source_target_pairs={{0,4},{4,0},{8,12},{12,8},{16,20},{20,16},{24,28},{28,24},{1,5},{5... | collective-permute-start | bytes 786440 | tf_op jit(solution)/shard_map/ppermute | solution.py:26
  116.3 15.8 %collective-permute-start.33 = (bf16[128,1024]{1,0:T(8,128)(2,1)S(1)}, bf16[128,1024]{1,0:T(8,128)(2,1)S(1)}, u32[]{:S(2)}, u32[]{:S(2)}) collective-permute-start(bf16[128,1024]{1,0:T(8,128)(2,1)S(1)} %get-tuple-element.244), channel_id=1, source_target_pairs={{0,16},{4,20},{8,24},{12,28},{16,0},{20,4},{24,8},{28,12},{1,17},{... | collective-permute-start | bytes 786440 | tf_op jit(solution)/shard_map/ppermute | solution.py:26
  118.9 14.6 %collective-permute-start.34 = (bf16[256,1024]{1,0:T(8,128)(2,1)S(1)}, bf16[256,1024]{1,0:T(8,128)(2,1)S(1)}, u32[]{:S(2)}, u32[]{:S(2)}) collective-permute-start(bf16[256,1024]{1,0:T(8,128)(2,1)S(1)} %get-tuple-element.246), channel_id=1, source_target_pairs={{0,2},{1,3},{2,0},{3,1},{4,6},{5,7},{6,4},{7,5},{8,10},{9,11},{10,... | collective-permute-start | bytes 1572872 | tf_op jit(solution)/shard_map/ppermute | solution.py:26
  131.3 15.5 %collective-permute-start.35 = (bf16[272,1024]{1,0:T(8,128)(2,1)S(1)}, bf16[272,1024]{1,0:T(8,128)(2,1)S(1)}, u32[]{:S(2)}, u32[]{:S(2)}) collective-permute-start(bf16[272,1024]{1,0:T(8,128)(2,1)S(1)} %get-tuple-element.249), channel_id=1, source_target_pairs={{0,4},{4,0},{8,12},{12,8},{16,20},{20,16},{24,28},{28,24},{1,5},{5... | collective-permute-start | bytes 1671176 | tf_op jit(solution)/shard_map/ppermute | solution.py:26
  132.1 18.4 %collective-permute-start.37 = (bf16[128,1024]{1,0:T(8,128)(2,1)S(1)}, bf16[128,1024]{1,0:T(8,128)(2,1)S(1)}, u32[]{:S(2)}, u32[]{:S(2)}) collective-permute-start(bf16[128,1024]{1,0:T(8,128)(2,1)S(1)} %get-tuple-element.256), channel_id=1, source_target_pairs={{0,16},{4,20},{8,24},{12,28},{16,0},{20,4},{24,8},{28,12},{1,17},{... | collective-permute-start | bytes 786440 | tf_op jit(solution)/shard_map/ppermute | solution.py:26
  134.1 15.8 %collective-permute-start.36 = (bf16[128,1024]{1,0:T(8,128)(2,1)S(1)}, bf16[128,1024]{1,0:T(8,128)(2,1)S(1)}, u32[]{:S(2)}, u32[]{:S(2)}) collective-permute-start(bf16[128,1024]{1,0:T(8,128)(2,1)S(1)} %get-tuple-element.253), channel_id=1, source_target_pairs={{0,4},{4,0},{8,12},{12,8},{16,20},{20,16},{24,28},{28,24},{1,5},{5... | collective-permute-start | bytes 786440 | tf_op jit(solution)/shard_map/ppermute | solution.py:26
  135.4 22.6 %all-to-all-start = ((bf16[4,32,1024]{2,1,0:T(8,128)(2,1)}), bf16[4,32,1024]{2,1,0:T(8,128)(2,1)S(1)}, u32[]{:S(2)}, u32[]{:S(2)}) async-start(bf16[4,32,1024]{2,1,0:T(8,128)(2,1)} %bitcast.11), calls=%async_computation | async-start | bytes 524288 | tf_op jit(solution)/shard_map/all_to_all | solution.py:928
  148.6 8.2 %collective-permute-start.38 = (bf16[144,1024]{1,0:T(8,128)(2,1)S(1)}, bf16[144,1024]{1,0:T(8,128)(2,1)S(1)}, u32[]{:S(2)}, u32[]{:S(2)}) collective-permute-start(bf16[144,1024]{1,0:T(8,128)(2,1)S(1)} %get-tuple-element.258), channel_id=1, source_target_pairs={{0,8},{4,12},{8,0},{12,4},{16,24},{20,28},{24,16},{28,20},{1,9},{5... | collective-permute-start | bytes 884744 | tf_op jit(solution)/shard_map/ppermute | solution.py:26
  (62 other events, 268.0 us)

commit v5 on v4

--- a/solution.py
+++ b/solution.py
@@ -17,8 +17,8 @@
 MIB = 1024 * 1024
 TIMES = dict(latent=2.9, media=2.7, attend=3.1, mix=3.8, feed=0.1, feed_end=36.0, down_grad=4.0, attend_back=1.7, keyval_grad=11.4, up_grad=4.0, keyval_back=4.0, latent_back=1.6, query_grad=1.5, pair=0.8, down_fold=0.8, up_fold=0.8, keyval_fold=0.8, query_fold=1.6, out_grad=0.8)
 RATE = 2e+09
-ORDER = "OGXBVDWYPKDLRUUQDKQKUQKQKQ"
-KV_ORDER, QO_ORDER = "cxyz", "cyzx"
+ORDER = "OGXBVDWYPKDLRUDUKQQKUQKQKQ"
+KV_ORDER, QO_ORDER = "cxyz", "cxyz"
 
 
 def swap(values, axis, bit):
@@ -664,7 +664,7 @@
             (leading((group, keys, width)), out((slots, keys, width), BF16)),
             (leading((group, keys, 2 * inner)), out((slots, keys, 2 * inner), BF16)),
         ],
-        name="media",
+        vmem=62, name="media",
     )(media, lat_low, gains, biases, w_keyval)
     first = after(qs[bit], keyval)
     qs[bit] = first

time: 172 us -> 165 us (0.959)
  waiting for transfers between devices: 49.7 us -> 36.7 us
  starting transfers between devices: 33.3 us -> 44 us
  local copies, waits for them, and re-layouts: 12.2 us -> 5.89 us
    ppermute x43, waiting for transfers between devices: 49.7 us -> 36.7 us  [swap(): return lax.ppermute(values, axis, [(k, k ^ bit) for k in range(n)])]
    ppermute x43, starting transfers between devices: 29.9 us -> 40.5 us  [swap(): return lax.ppermute(values, axis, [(k, k ^ bit) for k in range(n)])]
    unnamed x100 -> x74, local copies, waits for them, and re-layouts: 11.5 us -> 5.23 us
    pallas_call x1, Pallas kernels: 2.72 us -> 5.53 us  [on_device(): call(media_kernel, (slots // group,), [leading((group, patch_rows, width)...]
  transfers between devices with their start and end apart: 44 -> 44, of which waited for: 16 -> 18; matrix products, arithmetic and copies ran while one was open for 0% -> 0% of each run, Pallas kernels for 39% -> 41%
where the time goes in v5:
time: 165 us; the launch traced here: 164 us
  Pallas kernels  75.9 us (46%)
  starting transfers between devices  44 us (27%)
  waiting for transfers between devices  36.7 us (22%)
  local copies, waits for them, and re-layouts  5.89 us (4%)
    ppermute x43, starting transfers between devices, swap(): return lax.ppermute(values, axis, [(k, k ^ bit) for k in range(n)])  40.5 us
    ppermute x43, waiting for transfers between devices, swap(): return lax.ppermute(values, axis, [(k, k ^ bit) for k in range(n)])  36.7 us
    pallas_call x16, Pallas kernels, fold(): call(functools.partial(fold_kernel, nxt, end, len(kept), extra is not Non...  14 us
    pallas_call x1, Pallas kernels, on_device(): call(functools.partial(feed_end_kernel, per_slot, count, here), (here, ha...  12 us
    pallas_call x3, Pallas kernels, outer(): call(functools.partial(outer_kernel, count, [(order[0], plan[0]) for orde...  10.7 us
    pallas_call x1, Pallas kernels, on_device(): call(functools.partial(feed_kernel, count, here), (here, halves), [whole(...  9.51 us
    pallas_call x1, Pallas kernels, attend_back(): call(functools.partial(attend_back_kernel, peers, per_slot, scale), (slot...  5.67 us
    pallas_call x1, Pallas kernels, on_device(): call(media_kernel, (slots // group,), [leading((group, patch_rows, width)...  5.53 us
  transfers between devices with their start and end apart: 44, of which 18 were waited for; matrix products, arithmetic and copies ran while one was open for 0% of the time, Pallas kernels for 41%

profile of v5, /device:TPU:0, one launch (start us, length us, event | category | flops | bytes accessed | tf_op | source)
XLA Modules:
  0.0 164.1 jit_solution(1106849861071115119)
XLA Ops:
  0.6 2.8 %latent.1 = (bf16[160,1024]{1,0:T(8,128)(2,1)}, bf16[160,512]{1,0:T(8,128)(2,1)}, bf16[160,1024]{1,0:T(8,128)(2,1)}) custom-call(s32[2]{0:T(128)} %counts.3, bf16[160,1024]{1,0:T(8,128)(2,1)} %bitcast.13, bf16[160,1024]{1,0:T(8,128)(2,1)} %bitcast.18, f32[3,1024]{1,0:T(4,128)} %refs_6_.7, f32[3,1024]{1,0:T(4,128)} %refs_7_.3, bf16[1024,512]{1,0:T(8,128)(2,1)} %refs_5_.7), custom_call_target="tpu_custom_call" | custom-call | flops 5800000000 | bytes 100000 | tf_op jit(solution)/shard_map/latent/pallas_call | solution.py:640
  3.5 3.0 %collective-permute-start.1 = (bf16[160,512]{1,0:T(8,128)(2,1)}, bf16[160,512]{1,0:T(8,128)(2,1)S(1)}, u32[]{:S(2)}, u32[]{:S(2)}) collective-permute-start(bf16[160,512]{1,0:T(8,128)(2,1)} %get-tuple-element.142.refs_0_), channel_id=1, source_target_pairs={{0,2},{1,3},{2,0},{3,1},{4,6},{5,7},{6,4},{7,5},{8,10},{9,11},{10,... | collective-permute-start | bytes 491528 | tf_op jit(solution)/shard_map/ppermute | solution.py:26
  6.5 5.5 %media.3 = (bf16[10,80,1024]{2,1,0:T(8,128)(2,1)}, bf16[10,80,1024]{2,1,0:T(8,128)(2,1)}) custom-call(bf16[10,64,1024]{2,1,0:T(8,128)(2,1)} %media.5, bf16[160,1024]{1,0:T(8,128)(2,1)} %get-tuple-element.143.lat_low, f32[3,1024]{1,0:T(4,128)} %refs_6_.7, f32[3,1024]{1,0:T(4,128)} %refs_7_.3, bf16[1024,1024]{1,0:T(8,128)(2,1)} %w_keyval.3), custom_call_target="tpu_custom_call" | custom-call | flops 5400000000 | bytes 100000 | tf_op jit(solution)/shard_map/media/pallas_call | solution.py:656
  15.0 3.0 %attend.1 = (bf16[176,512]{1,0:T(8,128)(2,1)S(1)}, bf16[176,512]{1,0:T(8,128)(2,1)S(1)}, bf16[176,512]{1,0:T(8,128)(2,1)S(1)}, bf16[176,512]{1,0:T(8,128)(2,1)S(1)}) custom-call(bf16[160,512]{1,0:T(8,128)(2,1)S(1)} %copy-done.11, bf16[160,512]{1,0:T(8,128)(2,1)S(1)} %collective-permute-done.refs_1_, bf16[160,512]{1,0:T(8,128)(2,1)S(1)} %collective-permute-done.1.refs_2_, ...), custom_call_target="tpu_custom_call" | custom-call | flops 6200000000 | bytes 100000 | tf_op jit(solution)/shard_map/attend/pallas_call | solution.py:681
  20.6 5.9 %collective-permute-done.4.refs_2_ = bf16[176,512]{1,0:T(8,128)(2,1)S(1)} collective-permute-done((bf16[176,512]{1,0:T(8,128)(2,1)S(1)}, bf16[176,512]{1,0:T(8,128)(2,1)S(1)}, u32[]{:S(2)}, u32[]{:S(2)}) %collective-permute-start.4) | collective-permute-done | bytes 180256 | tf_op jit(solution)/shard_map/ppermute | solution.py:26
  26.5 2.2 %collective-permute-done.5.refs_3_ = bf16[176,512]{1,0:T(8,128)(2,1)S(1)} collective-permute-done((bf16[176,512]{1,0:T(8,128)(2,1)S(1)}, bf16[176,512]{1,0:T(8,128)(2,1)S(1)}, u32[]{:S(2)}, u32[]{:S(2)}) %collective-permute-start.5) | collective-permute-done | bytes 180256 | tf_op jit(solution)/shard_map/ppermute | solution.py:26
  29.4 3.9 %mix.1 = (f32[160,512]{1,0:T(8,128)}, bf16[160,512]{1,0:T(8,128)(2,1)}, f32[160,1024]{1,0:T(8,128)}, bf16[160,1024]{1,0:T(8,128)(2,1)}, f32[8,256]{1,0:T(8,128)}) custom-call(bf16[176,512]{1,0:T(8,128)(2,1)} %copy-done.29, bf16[176,512]{1,0:T(8,128)(2,1)} %copy-done.34, bf16[176,512]{1,0:T(8,128)(2,1)} %copy-done.35, bf16[176,512]{1,0:T(8,128)(2,1)} %copy-done.36, ...), custom_call_target="tpu_custom_call" | custom-call | flops 7600000000 | bytes 100000 | tf_op jit(solution)/shard_map/mix/pallas_call | solution.py:692
  35.7 9.5 %feed.1 = (bf16[2,160,512]{2,1,0:T(8,128)(2,1)}, bf16[2,160,512]{2,1,0:T(8,128)(2,1)}, bf16[2,160,512]{2,1,0:T(8,128)(2,1)}, bf16[2,160,512]{2,1,0:T(8,128)(2,1)...) custom-call(s32[2]{0:T(128)} %pad_add_fusion.own, bf16[160,1024]{1,0:T(8,128)(2,1)} %get-tuple-element.157.ff_low.refs_4_, ...), custom_call_target="tpu_custom_call" | custom-call | flops 200000000 | bytes 100000 | tf_op jit(solution)/shard_map/feed/pallas_call | solution.py:737
  48.8 12.0 %feed_end.1 = (bf16[2,160,512]{2,1,0:T(8,128)(2,1)}, bf16[2,160,512]{2,1,0:T(8,128)(2,1)}, bf16[2,160,512]{2,1,0:T(8,128)(2,1)}, bf16[2,160,512]{2,1,0:T(8,128)(...) custom-call(s32[2]{0:T(128)} %pad_add_fusion.own, ...), custom_call_target="tpu_custom_call" | custom-call | flops 71999995904 | bytes 100000 | tf_op jit(solution)/shard_map/feed_end/pallas_call | solution.py:752
  65.0 4.1 %down_grad.1 = (bf16[512,512]{1,0:T(8,128)(2,1)S(1)}, bf16[512,512]{1,0:T(8,128)(2,1)S(1)}, bf16[512,512]{1,0:T(8,128)(2,1)S(1)}, bf16[512,512]{1,0:T(8,128)(2,1)S(1)}) custom-call(s32[2]{0:T(128)S(1)} %copy-done.3, bf16[160,1024]{1,0:T(8,128)(2,1)S(1)} %copy-done.2, bf16[160,1024]{1,0:T(8,128)(2,1)S(1)} %collective-permute-done.10.refs_1_, ...), custom_call_target="tpu_custom_call" | custom-call | flops 8000000000 | bytes 100000 | tf_op jit(solution)/shard_map/down_grad/pallas_call | solution.py:536
  69.8 1.6 collective-permute-start.24
  71.4 1.5 collective-permute-start.18
  73.0 1.6 collective-permute-start.19
  75.1 5.7 %attend_back.1 = (bf16[10,80,1024]{2,1,0:T(8,128)(2,1)S(1)}, bf16[2,160,512]{2,1,0:T(8,128)(2,1)S(1)}, bf16[2,160,512]{2,1,0:T(8,128)(2,1)S(1)}) custom-call(bf16[160,512]{1,0:T(8,128)(2,1)S(1)} %copy-done.12, bf16[160,512]{1,0:T(8,128)(2,1)S(1)} %copy-done.16, bf16[160,512]{1,0:T(8,128)(2,1)S(1)} %copy-done.14, bf16[160,512]{1,0:T(8,128)(2,1)S(1)} %copy-done.18, ...), custom_call_target="tpu_custom_call" | custom-call | flops 3400000000 | bytes 100000 | tf_op jit(solution)/shard_map/attend_back/pallas_call | solution.py:816
  80.8 4.2 %keyval_back.1 = (bf16[10,64,1024]{2,1,0:T(8,128)(2,1)}, f32[160,1024]{1,0:T(8,128)S(1)}, f32[2,1024]{1,0:T(2,128)S(1)}) custom-call(bf16[10,64,1024]{2,1,0:T(8,128)(2,1)S(1)} %copy-done.5, bf16[10,80,1024]{2,1,0:T(8,128)(2,1)S(1)} %get-tuple-element.189.dkv, bf16[1024,1024]{1,0:T(8,128)(2,1)S(1)} %copy-done.4, f32[3,1024]{1,0:T(4,128)S(1)} %copy-done.19), custom_call_target="tpu_custom_call" | custom-call | flops 8000000000 | bytes 100000 | tf_op jit(solution)/shard_map/keyval_back/pallas_call | solution.py:842
  87.5 3.9 %keyval_grad.1 = (bf16[512,1024]{1,0:T(8,128)(2,1)S(1)}, bf16[512,1024]{1,0:T(8,128)(2,1)S(1)}) custom-call(s32[2]{0:T(128)S(1)} %copy-done.3, bf16[800,1024]{1,0:T(8,128)(2,1)S(1)} %bitcast.17, bf16[800,1024]{1,0:T(8,128)(2,1)S(1)} %bitcast.16), custom_call_target="tpu_custom_call" | custom-call | flops 22799998976 | bytes 100000 | tf_op jit(solution)/shard_map/keyval_grad/pallas_call | solution.py:536
  91.6 1.6 collective-permute-start.26
  94.1 2.7 %up_grad.1 = (bf16[512,512]{1,0:T(8,128)(2,1)S(1)}, bf16[512,512]{1,0:T(8,128)(2,1)S(1)}, bf16[512,512]{1,0:T(8,128)(2,1)S(1)}, bf16[512,512]{1,0:T(8,128)(2,1)S(1)}) custom-call(s32[2]{0:T(128)S(1)} %copy-done.3, bf16[2,160,512]{2,1,0:T(8,128)(2,1)S(1)} %copy-done.27, bf16[2,160,512]{2,1,0:T(8,128)(2,1)S(1)} %collective-permute-done.22.refs_1_, ...), custom_call_target="tpu_custom_call" | custom-call | flops 8000000000 | bytes 100000 | tf_op jit(solution)/shard_map/up_grad/pallas_call | solution.py:536
  100.4 2.0 %collective-permute-done.27.refs_3_ = bf16[256,512]{1,0:T(8,128)(2,1)S(1)} collective-permute-done((bf16[256,512]{1,0:T(8,128)(2,1)S(1)}, bf16[256,512]{1,0:T(8,128)(2,1)S(1)}, u32[]{:S(2)}, u32[]{:S(2)}) %collective-permute-start.27) | collective-permute-done | bytes 262176 | tf_op jit(solution)/shard_map/ppermute | solution.py:26
  104.0 1.5 latent_back.1
  107.0 2.6 %collective-permute-start.30 = (bf16[128,1024]{1,0:T(8,128)(2,1)S(1)}, bf16[128,1024]{1,0:T(8,128)(2,1)S(1)}, u32[]{:S(2)}, u32[]{:S(2)}) collective-permute-start(bf16[128,1024]{1,0:T(8,128)(2,1)S(1)} %get-tuple-element.233), channel_id=1, source_target_pairs={{0,16},{4,20},{8,24},{12,28},{16,0},{20,4},{24,8},{28,12},{1,17},{... | collective-permute-start | bytes 786440 | tf_op jit(solution)/shard_map/ppermute | solution.py:26
  110.2 2.6 %collective-permute-done.28.refs_2_ = bf16[512,512]{1,0:T(8,128)(2,1)S(1)} collective-permute-done((bf16[512,512]{1,0:T(8,128)(2,1)S(1)}, bf16[512,512]{1,0:T(8,128)(2,1)S(1)}, u32[]{:S(2)}, u32[]{:S(2)}) %collective-permute-start.28) | collective-permute-done | bytes 524320 | tf_op jit(solution)/shard_map/ppermute | solution.py:26
  115.2 7.2 %collective-permute-done.30.refs_1_ = bf16[128,1024]{1,0:T(8,128)(2,1)S(1)} collective-permute-done((bf16[128,1024]{1,0:T(8,128)(2,1)S(1)}, bf16[128,1024]{1,0:T(8,128)(2,1)S(1)}, u32[]{:S(2)}, u32[]{:S(2)}) %collective-permute-start.30) | collective-permute-done | bytes 262176 | tf_op jit(solution)/shard_map/ppermute | solution.py:26
  127.3 2.9 %collective-permute-start.37 = (bf16[128,1024]{1,0:T(8,128)(2,1)S(1)}, bf16[128,1024]{1,0:T(8,128)(2,1)S(1)}, u32[]{:S(2)}, u32[]{:S(2)}) collective-permute-start(bf16[128,1024]{1,0:T(8,128)(2,1)S(1)} %get-tuple-element.254), channel_id=1, source_target_pairs={{0,16},{4,20},{8,24},{12,28},{16,0},{20,4},{24,8},{28,12},{1,17},{... | collective-permute-start | bytes 786440 | tf_op jit(solution)/shard_map/ppermute | solution.py:26
  130.2 3.4 %all-to-all-start = ((bf16[4,32,1024]{2,1,0:T(8,128)(2,1)}), bf16[4,32,1024]{2,1,0:T(8,128)(2,1)S(1)}, u32[]{:S(2)}, u32[]{:S(2)}) async-start(bf16[4,32,1024]{2,1,0:T(8,128)(2,1)} %bitcast.11), calls=%async_computation | async-start | bytes 524288 | tf_op jit(solution)/shard_map/all_to_all | solution.py:928
  134.5 7.1 %collective-permute-done.35.refs_1_ = bf16[272,1024]{1,0:T(8,128)(2,1)S(1)} collective-permute-done((bf16[272,1024]{1,0:T(8,128)(2,1)S(1)}, bf16[272,1024]{1,0:T(8,128)(2,1)S(1)}, u32[]{:S(2)}, u32[]{:S(2)}) %collective-permute-start.35) | collective-permute-done | bytes 557088 | tf_op jit(solution)/shard_map/ppermute | solution.py:26
  144.0 1.5 up_fold.5
  145.5 2.0 %collective-permute-start.39 = (bf16[64,1024]{1,0:T(8,128)(2,1)S(1)}, bf16[64,1024]{1,0:T(8,128)(2,1)S(1)}, u32[]{:S(2)}, u32[]{:S(2)}) collective-permute-start(bf16[64,1024]{1,0:T(8,128)(2,1)S(1)} %get-tuple-element.260), channel_id=1, source_target_pairs={{0,8},{4,12},{8,0},{12,4},{16,24},{20,28},{24,16},{28,20},{1,9},{5... | collective-permute-start | bytes 393224 | tf_op jit(solution)/shard_map/ppermute | solution.py:26
  147.5 1.6 collective-permute-done.38.refs_1_
  149.7 2.0 %collective-permute-start.40 = (bf16[80,1024]{1,0:T(8,128)(2,1)S(1)}, bf16[80,1024]{1,0:T(8,128)(2,1)S(1)}, u32[]{:S(2)}, u32[]{:S(2)}) collective-permute-start(bf16[80,1024]{1,0:T(8,128)(2,1)S(1)} %get-tuple-element.263), channel_id=1, source_target_pairs={{0,8},{4,12},{8,0},{12,4},{16,24},{20,28},{24,16},{28,20},{1,9},{5... | collective-permute-start | bytes 491528 | tf_op jit(solution)/shard_map/ppermute | solution.py:26
  153.2 2.9 %collective-permute-start.41 = (bf16[32,1024]{1,0:T(8,128)(2,1)S(1)}, bf16[32,1024]{1,0:T(8,128)(2,1)S(1)}, u32[]{:S(2)}, u32[]{:S(2)}) collective-permute-start(bf16[32,1024]{1,0:T(8,128)(2,1)S(1)} %get-tuple-element.267), channel_id=1, source_target_pairs={{0,16},{4,20},{8,24},{12,28},{16,0},{20,4},{24,8},{28,12},{1,17},{... | collective-permute-start | bytes 196616 | tf_op jit(solution)/shard_map/ppermute | solution.py:26
  156.7 2.4 %collective-permute-start.42 = (bf16[48,1024]{1,0:T(8,128)(2,1)S(1)}, bf16[48,1024]{1,0:T(8,128)(2,1)S(1)}, u32[]{:S(2)}, u32[]{:S(2)}) collective-permute-start(bf16[48,1024]{1,0:T(8,128)(2,1)S(1)} %get-tuple-element.269), channel_id=1, source_target_pairs={{0,16},{4,20},{8,24},{12,28},{16,0},{20,4},{24,8},{28,12},{1,17},{... | collective-permute-start | bytes 294920 | tf_op jit(solution)/shard_map/ppermute | solution.py:26
  (165 shorter events, 46.4 us)
Async XLA Ops:
  3.5 8.5 %collective-permute-start.1 = (bf16[160,512]{1,0:T(8,128)(2,1)}, bf16[160,512]{1,0:T(8,128)(2,1)S(1)}, u32[]{:S(2)}, u32[]{:S(2)}) collective-permute-start(bf16[160,512]{1,0:T(8,128)(2,1)} %get-tuple-element.142.refs_0_), channel_id=1, source_target_pairs={{0,2},{1,3},{2,0},{3,1},{4,6},{5,7},{6,4},{7,5},{8,10},{9,11},{10,... | collective-permute-start | bytes 491528 | tf_op jit(solution)/shard_map/ppermute | solution.py:26
  19.1 7.4 %collective-permute-start.4 = (bf16[176,512]{1,0:T(8,128)(2,1)S(1)}, bf16[176,512]{1,0:T(8,128)(2,1)S(1)}, u32[]{:S(2)}, u32[]{:S(2)}) collective-permute-start(bf16[176,512]{1,0:T(8,128)(2,1)S(1)} %get-tuple-element.148), channel_id=1, source_target_pairs={{0,2},{1,3},{2,0},{3,1},{4,6},{5,7},{6,4},{7,5},{8,10},{9,11},{10,... | collective-permute-start | bytes 540680 | tf_op jit(solution)/shard_map/ppermute | solution.py:26
  19.3 9.4 %collective-permute-start.5 = (bf16[176,512]{1,0:T(8,128)(2,1)S(1)}, bf16[176,512]{1,0:T(8,128)(2,1)S(1)}, u32[]{:S(2)}, u32[]{:S(2)}) collective-permute-start(bf16[176,512]{1,0:T(8,128)(2,1)S(1)} %get-tuple-element.149), channel_id=1, source_target_pairs={{0,3},{1,2},{2,1},{3,0},{4,7},{5,6},{6,5},{7,4},{8,11},{9,10},{10,... | collective-permute-start | bytes 540680 | tf_op jit(solution)/shard_map/ppermute | solution.py:26
  28.7 16.5 %collective-permute-start.8 = (bf16[160,1024]{1,0:T(8,128)(2,1)S(1)}, bf16[160,1024]{1,0:T(8,128)(2,1)S(1)}, u32[]{:S(2)}, u32[]{:S(2)}) collective-permute-start(bf16[160,1024]{1,0:T(8,128)(2,1)S(1)} %copy-done.1), channel_id=1, source_target_pairs={{0,2},{1,3},{2,0},{3,1},{4,6},{5,7},{6,4},{7,5},{8,10},{9,11},{10,... | collective-permute-start | bytes 983048 | tf_op jit(solution)/shard_map/ppermute | solution.py:26
  33.2 12.8 %collective-permute-start.7 = (bf16[160,1024]{1,0:T(8,128)(2,1)}, bf16[160,1024]{1,0:T(8,128)(2,1)S(1)}, u32[]{:S(2)}, u32[]{:S(2)}) collective-permute-start(bf16[160,1024]{1,0:T(8,128)(2,1)} %get-tuple-element.157.ff_low.refs_4_), channel_id=1, source_target_pairs={{0,2},{1,3},{2,0},{3,1},{4,6},{5,7},{6,4},{7,5},{8,10},{9,11},{10,... | collective-permute-start | bytes 983048 | tf_op jit(solution)/shard_map/ppermute | solution.py:26
  35.2 12.7 %collective-permute-start.6 = (bf16[160,1024]{1,0:T(8,128)(2,1)}, bf16[160,1024]{1,0:T(8,128)(2,1)S(1)}, u32[]{:S(2)}, u32[]{:S(2)}) collective-permute-start(bf16[160,1024]{1,0:T(8,128)(2,1)} %get-tuple-element.157.ff_low.refs_4_), channel_id=1, source_target_pairs={{0,1},{1,0},{2,3},{3,2},{4,5},{5,4},{6,7},{7,6},{8,9},{9,8},{10,11... | collective-permute-start | bytes 983048 | tf_op jit(solution)/shard_map/ppermute | solution.py:26
  35.3 11.7 %collective-permute-start.10 = (bf16[160,1024]{1,0:T(8,128)(2,1)S(1)}, bf16[160,1024]{1,0:T(8,128)(2,1)S(1)}, u32[]{:S(2)}, u32[]{:S(2)}) collective-permute-start(bf16[160,1024]{1,0:T(8,128)(2,1)S(1)} %copy-done.1), channel_id=1, source_target_pairs={{0,1},{1,0},{2,3},{3,2},{4,5},{5,4},{6,7},{7,6},{8,9},{9,8},{10,11... | collective-permute-start | bytes 983048 | tf_op jit(solution)/shard_map/ppermute | solution.py:26
  46.5 18.1 %collective-permute-start.15 = (bf16[2,160,512]{2,1,0:T(8,128)(2,1)}, bf16[2,160,512]{2,1,0:T(8,128)(2,1)}, u32[]{:S(2)}, u32[]{:S(2)}) collective-permute-start(bf16[2,160,512]{2,1,0:T(8,128)(2,1)} %get-tuple-element.172), channel_id=1, source_target_pairs={{0,2},{1,3},{2,0},{3,1},{4,6},{5,7},{6,4},{7,5},{8,10},{9,11},{10,... | collective-permute-start | bytes 983048 | tf_op jit(solution)/shard_map/ppermute | solution.py:26
  46.9 17.6 %collective-permute-start.16 = (bf16[2,160,512]{2,1,0:T(8,128)(2,1)}, bf16[2,160,512]{2,1,0:T(8,128)(2,1)S(1)}, u32[]{:S(2)}, u32[]{:S(2)}) collective-permute-start(bf16[2,160,512]{2,1,0:T(8,128)(2,1)} %get-tuple-element.173), channel_id=1, source_target_pairs={{0,3},{1,2},{2,1},{3,0},{4,7},{5,6},{6,5},{7,4},{8,11},{9,10},{10,... | collective-permute-start | bytes 983048 | tf_op jit(solution)/shard_map/ppermute | solution.py:26
  61.5 7.7 %collective-permute-start.13 = (bf16[192,512]{1,0:T(8,128)(2,1)}, bf16[192,512]{1,0:T(8,128)(2,1)S(1)}, u32[]{:S(2)}, u32[]{:S(2)}) collective-permute-start(bf16[192,512]{1,0:T(8,128)(2,1)} %get-tuple-element.163.refs_4_), channel_id=1, source_target_pairs={{0,2},{1,3},{2,0},{3,1},{4,6},{5,7},{6,4},{7,5},{8,10},{9,11},{10,... | collective-permute-start | bytes 589832 | tf_op jit(solution)/shard_map/ppermute | solution.py:26
  61.9 11.1 %collective-permute-start.12 = (bf16[192,512]{1,0:T(8,128)(2,1)}, bf16[192,512]{1,0:T(8,128)(2,1)S(1)}, u32[]{:S(2)}, u32[]{:S(2)}) collective-permute-start(bf16[192,512]{1,0:T(8,128)(2,1)} %get-tuple-element.163.refs_4_), channel_id=1, source_target_pairs={{0,1},{1,0},{2,3},{3,2},{4,5},{5,4},{6,7},{7,6},{8,9},{9,8},{10,11... | collective-permute-start | bytes 589832 | tf_op jit(solution)/shard_map/ppermute | solution.py:26
  69.7 24.3 %collective-permute-start.22 = (bf16[2,160,512]{2,1,0:T(8,128)(2,1)S(1)}, bf16[2,160,512]{2,1,0:T(8,128)(2,1)S(1)}, u32[]{:S(2)}, u32[]{:S(2)}) collective-permute-start(bf16[2,160,512]{2,1,0:T(8,128)(2,1)S(1)} %copy-done.33), channel_id=1, source_target_pairs={{0,1},{1,0},{2,3},{3,2},{4,5},{5,4},{6,7},{7,6},{8,9},{9,8},{10,11... | collective-permute-start | bytes 983048 | tf_op jit(solution)/shard_map/ppermute | solution.py:26
  69.8 21.8 %collective-permute-start.24 = (bf16[2,160,512]{2,1,0:T(8,128)(2,1)S(1)}, bf16[2,160,512]{2,1,0:T(8,128)(2,1)S(1)}, u32[]{:S(2)}, u32[]{:S(2)}) collective-permute-start(bf16[2,160,512]{2,1,0:T(8,128)(2,1)S(1)} %copy-done.32), channel_id=1, source_target_pairs={{0,3},{1,2},{2,1},{3,0},{4,7},{5,6},{6,5},{7,4},{8,11},{9,10},{10,... | collective-permute-start | bytes 983048 | tf_op jit(solution)/shard_map/ppermute | solution.py:26
  71.4 13.9 %collective-permute-start.18 = (bf16[512,512]{1,0:T(8,128)(2,1)S(1)}, bf16[512,512]{1,0:T(8,128)(2,1)S(1)}, u32[]{:S(2)}, u32[]{:S(2)}) collective-permute-start(bf16[512,512]{1,0:T(8,128)(2,1)S(1)} %get-tuple-element.186), channel_id=1, source_target_pairs={{0,4},{4,0},{8,12},{12,8},{16,20},{20,16},{24,28},{28,24},{1,5},{5... | collective-permute-start | bytes 1572872 | tf_op jit(solution)/shard_map/ppermute | solution.py:26
  73.0 13.6 %collective-permute-start.19 = (bf16[512,512]{1,0:T(8,128)(2,1)S(1)}, bf16[512,512]{1,0:T(8,128)(2,1)S(1)}, u32[]{:S(2)}, u32[]{:S(2)}) collective-permute-start(bf16[512,512]{1,0:T(8,128)(2,1)S(1)} %get-tuple-element.187), channel_id=1, source_target_pairs={{0,8},{4,12},{8,0},{12,4},{16,24},{20,28},{24,16},{28,20},{1,9},{5... | collective-permute-start | bytes 1572872 | tf_op jit(solution)/shard_map/ppermute | solution.py:26
  74.5 19.5 %collective-permute-start.23 = (bf16[2,160,512]{2,1,0:T(8,128)(2,1)S(1)}, bf16[2,160,512]{2,1,0:T(8,128)(2,1)S(1)}, u32[]{:S(2)}, u32[]{:S(2)}) collective-permute-start(bf16[2,160,512]{2,1,0:T(8,128)(2,1)S(1)} %copy-done.31), channel_id=1, source_target_pairs={{0,2},{1,3},{2,0},{3,1},{4,6},{5,7},{6,4},{7,5},{8,10},{9,11},{10,... | collective-permute-start | bytes 983048 | tf_op jit(solution)/shard_map/ppermute | solution.py:26
  91.4 7.2 %collective-permute-start.25 = (bf16[512,1024]{1,0:T(8,128)(2,1)S(1)}, bf16[512,1024]{1,0:T(8,128)(2,1)S(1)}, u32[]{:S(2)}, u32[]{:S(2)}) collective-permute-start(bf16[512,1024]{1,0:T(8,128)(2,1)S(1)} %get-tuple-element.207), channel_id=1, source_target_pairs={{0,1},{1,0},{2,3},{3,2},{4,5},{5,4},{6,7},{7,6},{8,9},{9,8},{10,11... | collective-permute-start | bytes 3145736 | tf_op jit(solution)/shard_map/ppermute | solution.py:26
  91.6 8.8 %collective-permute-start.26 = (bf16[256,512]{1,0:T(8,128)(2,1)S(1)}, bf16[256,512]{1,0:T(8,128)(2,1)S(1)}, u32[]{:S(2)}, u32[]{:S(2)}) collective-permute-start(bf16[256,512]{1,0:T(8,128)(2,1)S(1)} %get-tuple-element.213), channel_id=1, source_target_pairs={{0,8},{4,12},{8,0},{12,4},{16,24},{20,28},{24,16},{28,20},{1,9},{5... | collective-permute-start | bytes 786440 | tf_op jit(solution)/shard_map/ppermute | solution.py:26
  93.2 9.2 %collective-permute-start.27 = (bf16[256,512]{1,0:T(8,128)(2,1)S(1)}, bf16[256,512]{1,0:T(8,128)(2,1)S(1)}, u32[]{:S(2)}, u32[]{:S(2)}) collective-permute-start(bf16[256,512]{1,0:T(8,128)(2,1)S(1)} %get-tuple-element.214), channel_id=1, source_target_pairs={{0,4},{4,0},{8,12},{12,8},{16,20},{20,16},{24,28},{28,24},{1,5},{5... | collective-permute-start | bytes 786440 | tf_op jit(solution)/shard_map/ppermute | solution.py:26
  96.8 16.0 %collective-permute-start.28 = (bf16[512,512]{1,0:T(8,128)(2,1)S(1)}, bf16[512,512]{1,0:T(8,128)(2,1)S(1)}, u32[]{:S(2)}, u32[]{:S(2)}) collective-permute-start(bf16[512,512]{1,0:T(8,128)(2,1)S(1)} %get-tuple-element.228), channel_id=1, source_target_pairs={{0,4},{4,0},{8,12},{12,8},{16,20},{20,16},{24,28},{28,24},{1,5},{5... | collective-permute-start | bytes 1572872 | tf_op jit(solution)/shard_map/ppermute | solution.py:26
  98.1 15.2 %collective-permute-start.29 = (bf16[512,512]{1,0:T(8,128)(2,1)S(1)}, bf16[512,512]{1,0:T(8,128)(2,1)S(1)}, u32[]{:S(2)}, u32[]{:S(2)}) collective-permute-start(bf16[512,512]{1,0:T(8,128)(2,1)S(1)} %get-tuple-element.229), channel_id=1, source_target_pairs={{0,8},{4,12},{8,0},{12,4},{16,24},{20,28},{24,16},{28,20},{1,9},{5... | collective-permute-start | bytes 1572872 | tf_op jit(solution)/shard_map/ppermute | solution.py:26
  106.9 18.8 %collective-permute-start.34 = (bf16[528,1024]{1,0:T(8,128)(2,1)S(1)}, bf16[528,1024]{1,0:T(8,128)(2,1)S(1)}, u32[]{:S(2)}, u32[]{:S(2)}) collective-permute-start(bf16[528,1024]{1,0:T(8,128)(2,1)S(1)} %get-tuple-element.245), channel_id=1, source_target_pairs={{0,1},{1,0},{2,3},{3,2},{4,5},{5,4},{6,7},{7,6},{8,9},{9,8},{10,11... | collective-permute-start | bytes 3244040 | tf_op jit(solution)/shard_map/ppermute | solution.py:26
  107.0 15.4 %collective-permute-start.30 = (bf16[128,1024]{1,0:T(8,128)(2,1)S(1)}, bf16[128,1024]{1,0:T(8,128)(2,1)S(1)}, u32[]{:S(2)}, u32[]{:S(2)}) collective-permute-start(bf16[128,1024]{1,0:T(8,128)(2,1)S(1)} %get-tuple-element.233), channel_id=1, source_target_pairs={{0,16},{4,20},{8,24},{12,28},{16,0},{20,4},{24,8},{28,12},{1,17},{... | collective-permute-start | bytes 786440 | tf_op jit(solution)/shard_map/ppermute | solution.py:26
  109.7 15.4 %collective-permute-start.33 = (bf16[256,1024]{1,0:T(8,128)(2,1)S(1)}, bf16[256,1024]{1,0:T(8,128)(2,1)S(1)}, u32[]{:S(2)}, u32[]{:S(2)}) collective-permute-start(bf16[256,1024]{1,0:T(8,128)(2,1)S(1)} %get-tuple-element.242), channel_id=1, source_target_pairs={{0,2},{1,3},{2,0},{3,1},{4,6},{5,7},{6,4},{7,5},{8,10},{9,11},{10,... | collective-permute-start | bytes 1572872 | tf_op jit(solution)/shard_map/ppermute | solution.py:26
  114.2 10.1 %collective-permute-start.31 = (bf16[256,512]{1,0:T(8,128)(2,1)S(1)}, bf16[256,512]{1,0:T(8,128)(2,1)S(1)}, u32[]{:S(2)}, u32[]{:S(2)}) collective-permute-start(bf16[256,512]{1,0:T(8,128)(2,1)S(1)} %get-tuple-element.238), channel_id=1, source_target_pairs={{0,8},{4,12},{8,0},{12,4},{16,24},{20,28},{24,16},{28,20},{1,9},{5... | collective-permute-start | bytes 786440 | tf_op jit(solution)/shard_map/ppermute | solution.py:26
  114.5 9.8 %collective-permute-start.32 = (bf16[256,512]{1,0:T(8,128)(2,1)S(1)}, bf16[256,512]{1,0:T(8,128)(2,1)S(1)}, u32[]{:S(2)}, u32[]{:S(2)}) collective-permute-start(bf16[256,512]{1,0:T(8,128)(2,1)S(1)} %get-tuple-element.239), channel_id=1, source_target_pairs={{0,4},{4,0},{8,12},{12,8},{16,20},{20,16},{24,28},{28,24},{1,5},{5... | collective-permute-start | bytes 786440 | tf_op jit(solution)/shard_map/ppermute | solution.py:26
  126.7 14.9 %collective-permute-start.35 = (bf16[272,1024]{1,0:T(8,128)(2,1)S(1)}, bf16[272,1024]{1,0:T(8,128)(2,1)S(1)}, u32[]{:S(2)}, u32[]{:S(2)}) collective-permute-start(bf16[272,1024]{1,0:T(8,128)(2,1)S(1)} %get-tuple-element.247), channel_id=1, source_target_pairs={{0,2},{1,3},{2,0},{3,1},{4,6},{5,7},{6,4},{7,5},{8,10},{9,11},{10,... | collective-permute-start | bytes 1671176 | tf_op jit(solution)/shard_map/ppermute | solution.py:26
  127.3 16.7 %collective-permute-start.37 = (bf16[128,1024]{1,0:T(8,128)(2,1)S(1)}, bf16[128,1024]{1,0:T(8,128)(2,1)S(1)}, u32[]{:S(2)}, u32[]{:S(2)}) collective-permute-start(bf16[128,1024]{1,0:T(8,128)(2,1)S(1)} %get-tuple-element.254), channel_id=1, source_target_pairs={{0,16},{4,20},{8,24},{12,28},{16,0},{20,4},{24,8},{28,12},{1,17},{... | collective-permute-start | bytes 786440 | tf_op jit(solution)/shard_map/ppermute | solution.py:26
  130.2 21.6 %all-to-all-start = ((bf16[4,32,1024]{2,1,0:T(8,128)(2,1)}), bf16[4,32,1024]{2,1,0:T(8,128)(2,1)S(1)}, u32[]{:S(2)}, u32[]{:S(2)}) async-start(bf16[4,32,1024]{2,1,0:T(8,128)(2,1)} %bitcast.11), calls=%async_computation | async-start | bytes 524288 | tf_op jit(solution)/shard_map/all_to_all | solution.py:928
  133.6 9.8 %collective-permute-start.36 = (bf16[128,1024]{1,0:T(8,128)(2,1)S(1)}, bf16[128,1024]{1,0:T(8,128)(2,1)S(1)}, u32[]{:S(2)}, u32[]{:S(2)}) collective-permute-start(bf16[128,1024]{1,0:T(8,128)(2,1)S(1)} %get-tuple-element.251), channel_id=1, source_target_pairs={{0,4},{4,0},{8,12},{12,8},{16,20},{20,16},{24,28},{28,24},{1,5},{5... | collective-permute-start | bytes 786440 | tf_op jit(solution)/shard_map/ppermute | solution.py:26
  145.5 7.1 %collective-permute-start.39 = (bf16[64,1024]{1,0:T(8,128)(2,1)S(1)}, bf16[64,1024]{1,0:T(8,128)(2,1)S(1)}, u32[]{:S(2)}, u32[]{:S(2)}) collective-permute-start(bf16[64,1024]{1,0:T(8,128)(2,1)S(1)} %get-tuple-element.260), channel_id=1, source_target_pairs={{0,8},{4,12},{8,0},{12,4},{16,24},{20,28},{24,16},{28,20},{1,9},{5... | collective-permute-start | bytes 393224 | tf_op jit(solution)/shard_map/ppermute | solution.py:26
  153.2 6.8 %collective-permute-start.41 = (bf16[32,1024]{1,0:T(8,128)(2,1)S(1)}, bf16[32,1024]{1,0:T(8,128)(2,1)S(1)}, u32[]{:S(2)}, u32[]{:S(2)}) collective-permute-start(bf16[32,1024]{1,0:T(8,128)(2,1)S(1)} %get-tuple-element.267), channel_id=1, source_target_pairs={{0,16},{4,20},{8,24},{12,28},{16,0},{20,4},{24,8},{28,12},{1,17},{... | collective-permute-start | bytes 196616 | tf_op jit(solution)/shard_map/ppermute | solution.py:26
  (49 other events, 245.5 us)

commit v6 on v5

--- a/solution.py
+++ b/solution.py
@@ -701,7 +701,7 @@
             (whole((rows, width)), out((rows, width), BF16)),
             stat_out,
         ],
-        vmem=62, name="mix",
+        vmem=40, name="mix",
     )(*parts, lat, w_out, gains, biases)
     bit = peers // 2
     ffs = {0: ff_low, bit: swap(ff_low, "patch", bit)}

time: 165 us -> 163 us (0.988)
  Pallas kernels: 75.9 us -> 73.7 us
    pallas_call x1, Pallas kernels: 3.85 us -> 1.52 us  [on_device(): call(functools.partial(mix_kernel, peers), (1,), [whole((part_rows, inner...]
    unnamed x74 -> x84, local copies, waits for them, and re-layouts: 5.23 us -> 6.46 us
  transfers between devices with their start and end apart: 44 -> 44, of which waited for: 18 -> 19; matrix products, arithmetic and copies ran while one was open for 0% -> 0% of each run, Pallas kernels for 41% -> 40%
where the time goes in v6:
time: 163 us
  Pallas kernels  73.7 us (45%)
  starting transfers between devices  44 us (27%)
  waiting for transfers between devices  36.2 us (22%)
  local copies, waits for them, and re-layouts  7.12 us (4%)
    ppermute x43, starting transfers between devices, swap(): return lax.ppermute(values, axis, [(k, k ^ bit) for k in range(n)])  40.6 us
    ppermute x43, waiting for transfers between devices, swap(): return lax.ppermute(values, axis, [(k, k ^ bit) for k in range(n)])  36.2 us
    pallas_call x16, Pallas kernels, fold(): call(functools.partial(fold_kernel, nxt, end, len(kept), extra is not Non...  14 us
    pallas_call x1, Pallas kernels, on_device(): call(functools.partial(feed_end_kernel, per_slot, count, here), (here, ha...  12.1 us
    pallas_call x3, Pallas kernels, outer(): call(functools.partial(outer_kernel, count, [(order[0], plan[0]) for orde...  10.7 us
    pallas_call x1, Pallas kernels, on_device(): call(functools.partial(feed_kernel, count, here), (here, halves), [whole(...  9.53 us
    unnamed x84, local copies, waits for them, and re-layouts  6.46 us
    pallas_call x1, Pallas kernels, attend_back(): call(functools.partial(attend_back_kernel, peers, per_slot, scale), (slot...  5.63 us
  transfers between devices with their start and end apart: 44, of which 19 were waited for; matrix products, arithmetic and copies ran while one was open for 0% of the time, Pallas kernels for 40%

profile of v6, /device:TPU:0, one launch (start us, length us, event | category | flops | bytes accessed | tf_op | source)
XLA Modules:
  0.0 162.8 jit_solution(6098941246398830490)
XLA Ops:
  0.6 2.8 %latent.1 = (bf16[160,1024]{1,0:T(8,128)(2,1)}, bf16[160,512]{1,0:T(8,128)(2,1)}, bf16[160,1024]{1,0:T(8,128)(2,1)}) custom-call(s32[2]{0:T(128)} %counts.3, bf16[160,1024]{1,0:T(8,128)(2,1)} %bitcast.13, bf16[160,1024]{1,0:T(8,128)(2,1)} %bitcast.18, f32[3,1024]{1,0:T(4,128)} %refs_6_.7, f32[3,1024]{1,0:T(4,128)} %refs_7_.3, bf16[1024,512]{1,0:T(8,128)(2,1)} %refs_5_.7), custom_call_target="tpu_custom_call" | custom-call | flops 5800000000 | bytes 100000 | tf_op jit(solution)/shard_map/latent/pallas_call | solution.py:640
  3.5 3.0 %collective-permute-start.1 = (bf16[160,512]{1,0:T(8,128)(2,1)}, bf16[160,512]{1,0:T(8,128)(2,1)S(1)}, u32[]{:S(2)}, u32[]{:S(2)}) collective-permute-start(bf16[160,512]{1,0:T(8,128)(2,1)} %get-tuple-element.142.refs_0_), channel_id=1, source_target_pairs={{0,2},{1,3},{2,0},{3,1},{4,6},{5,7},{6,4},{7,5},{8,10},{9,11},{10,... | collective-permute-start | bytes 491528 | tf_op jit(solution)/shard_map/ppermute | solution.py:26
  6.5 5.5 %media.3 = (bf16[10,80,1024]{2,1,0:T(8,128)(2,1)}, bf16[10,80,1024]{2,1,0:T(8,128)(2,1)}) custom-call(bf16[10,64,1024]{2,1,0:T(8,128)(2,1)} %media.5, bf16[160,1024]{1,0:T(8,128)(2,1)} %get-tuple-element.143.lat_low, f32[3,1024]{1,0:T(4,128)} %refs_6_.7, f32[3,1024]{1,0:T(4,128)} %refs_7_.3, bf16[1024,1024]{1,0:T(8,128)(2,1)} %w_keyval.3), custom_call_target="tpu_custom_call" | custom-call | flops 5400000000 | bytes 100000 | tf_op jit(solution)/shard_map/media/pallas_call | solution.py:656
  15.1 2.9 %attend.1 = (bf16[176,512]{1,0:T(8,128)(2,1)S(1)}, bf16[176,512]{1,0:T(8,128)(2,1)S(1)}, bf16[176,512]{1,0:T(8,128)(2,1)S(1)}, bf16[176,512]{1,0:T(8,128)(2,1)S(1)}) custom-call(bf16[160,512]{1,0:T(8,128)(2,1)S(1)} %copy-done.14, bf16[160,512]{1,0:T(8,128)(2,1)S(1)} %collective-permute-done.refs_1_, bf16[160,512]{1,0:T(8,128)(2,1)S(1)} %collective-permute-done.1.refs_2_, ...), custom_call_target="tpu_custom_call" | custom-call | flops 6200000000 | bytes 100000 | tf_op jit(solution)/shard_map/attend/pallas_call | solution.py:681
  20.0 5.9 %collective-permute-done.4.refs_2_ = bf16[176,512]{1,0:T(8,128)(2,1)S(1)} collective-permute-done((bf16[176,512]{1,0:T(8,128)(2,1)S(1)}, bf16[176,512]{1,0:T(8,128)(2,1)S(1)}, u32[]{:S(2)}, u32[]{:S(2)}) %collective-permute-start.4) | collective-permute-done | bytes 180256 | tf_op jit(solution)/shard_map/ppermute | solution.py:26
  25.9 2.2 %collective-permute-done.5.refs_3_ = bf16[176,512]{1,0:T(8,128)(2,1)S(1)} collective-permute-done((bf16[176,512]{1,0:T(8,128)(2,1)S(1)}, bf16[176,512]{1,0:T(8,128)(2,1)S(1)}, u32[]{:S(2)}, u32[]{:S(2)}) %collective-permute-start.5) | collective-permute-done | bytes 180256 | tf_op jit(solution)/shard_map/ppermute | solution.py:26
  28.8 1.5 mix.1
  35.6 9.5 %feed.1 = (bf16[2,160,512]{2,1,0:T(8,128)(2,1)}, bf16[2,160,512]{2,1,0:T(8,128)(2,1)}, bf16[2,160,512]{2,1,0:T(8,128)(2,1)}, bf16[2,160,512]{2,1,0:T(8,128)(2,1)...) custom-call(s32[2]{0:T(128)} %pad_add_fusion.own, bf16[160,1024]{1,0:T(8,128)(2,1)} %copy-done, ...), custom_call_target="tpu_custom_call" | custom-call | flops 200000000 | bytes 100000 | tf_op jit(solution)/shard_map/feed/pallas_call | solution.py:737
  48.2 12.1 %feed_end.1 = (bf16[2,160,512]{2,1,0:T(8,128)(2,1)}, bf16[2,160,512]{2,1,0:T(8,128)(2,1)}, bf16[2,160,512]{2,1,0:T(8,128)(2,1)}, bf16[2,160,512]{2,1,0:T(8,128)(...) custom-call(s32[2]{0:T(128)} %pad_add_fusion.own, ...), custom_call_target="tpu_custom_call" | custom-call | flops 71999995904 | bytes 100000 | tf_op jit(solution)/shard_map/feed_end/pallas_call | solution.py:752
  63.7 4.1 %down_grad.1 = (bf16[512,512]{1,0:T(8,128)(2,1)S(1)}, bf16[512,512]{1,0:T(8,128)(2,1)S(1)}, bf16[512,512]{1,0:T(8,128)(2,1)S(1)}, bf16[512,512]{1,0:T(8,128)(2,1)S(1)}) custom-call(s32[2]{0:T(128)S(1)} %copy-done.4, bf16[160,1024]{1,0:T(8,128)(2,1)S(1)} %copy-done.3, bf16[160,1024]{1,0:T(8,128)(2,1)} %collective-permute-done.10.refs_1_, ...), custom_call_target="tpu_custom_call" | custom-call | flops 8000000000 | bytes 100000 | tf_op jit(solution)/shard_map/down_grad/pallas_call | solution.py:536
  68.6 1.4 collective-permute-start.24
  70.1 1.5 collective-permute-start.18
  71.6 1.6 collective-permute-start.19
  73.7 5.6 %attend_back.1 = (bf16[10,80,1024]{2,1,0:T(8,128)(2,1)S(1)}, bf16[2,160,512]{2,1,0:T(8,128)(2,1)S(1)}, bf16[2,160,512]{2,1,0:T(8,128)(2,1)S(1)}) custom-call(bf16[160,512]{1,0:T(8,128)(2,1)S(1)} %copy-done.15, bf16[160,512]{1,0:T(8,128)(2,1)S(1)} %copy-done.19, bf16[160,512]{1,0:T(8,128)(2,1)S(1)} %copy-done.17, bf16[160,512]{1,0:T(8,128)(2,1)S(1)} %copy-done.21, ...), custom_call_target="tpu_custom_call" | custom-call | flops 3400000000 | bytes 100000 | tf_op jit(solution)/shard_map/attend_back/pallas_call | solution.py:816
  79.4 4.2 %keyval_back.1 = (bf16[10,64,1024]{2,1,0:T(8,128)(2,1)}, f32[160,1024]{1,0:T(8,128)S(1)}, f32[2,1024]{1,0:T(2,128)S(1)}) custom-call(bf16[10,64,1024]{2,1,0:T(8,128)(2,1)S(1)} %copy-done.6, bf16[10,80,1024]{2,1,0:T(8,128)(2,1)S(1)} %get-tuple-element.189.dkv, bf16[1024,1024]{1,0:T(8,128)(2,1)S(1)} %copy-done.5, f32[3,1024]{1,0:T(4,128)S(1)} %copy-done.24), custom_call_target="tpu_custom_call" | custom-call | flops 8000000000 | bytes 100000 | tf_op jit(solution)/shard_map/keyval_back/pallas_call | solution.py:842
  86.1 3.9 %keyval_grad.1 = (bf16[512,1024]{1,0:T(8,128)(2,1)S(1)}, bf16[512,1024]{1,0:T(8,128)(2,1)S(1)}) custom-call(s32[2]{0:T(128)S(1)} %copy-done.4, bf16[800,1024]{1,0:T(8,128)(2,1)S(1)} %bitcast.17, bf16[800,1024]{1,0:T(8,128)(2,1)S(1)} %bitcast.16), custom_call_target="tpu_custom_call" | custom-call | flops 22799998976 | bytes 100000 | tf_op jit(solution)/shard_map/keyval_grad/pallas_call | solution.py:536
  90.2 1.6 %collective-permute-start.26 = (bf16[256,512]{1,0:T(8,128)(2,1)S(1)}, bf16[256,512]{1,0:T(8,128)(2,1)S(1)}, u32[]{:S(2)}, u32[]{:S(2)}) collective-permute-start(bf16[256,512]{1,0:T(8,128)(2,1)S(1)} %get-tuple-element.213), channel_id=1, source_target_pairs={{0,8},{4,12},{8,0},{12,4},{16,24},{20,28},{24,16},{28,20},{1,9},{5... | collective-permute-start | bytes 786440 | tf_op jit(solution)/shard_map/ppermute | solution.py:26
  92.7 2.7 %up_grad.1 = (bf16[512,512]{1,0:T(8,128)(2,1)S(1)}, bf16[512,512]{1,0:T(8,128)(2,1)S(1)}, bf16[512,512]{1,0:T(8,128)(2,1)S(1)}, bf16[512,512]{1,0:T(8,128)(2,1)S(1)}) custom-call(s32[2]{0:T(128)S(1)} %copy-done.4, bf16[2,160,512]{2,1,0:T(8,128)(2,1)S(1)} %copy-done.35, bf16[2,160,512]{2,1,0:T(8,128)(2,1)S(1)} %collective-permute-done.22.refs_1_, ...), custom_call_target="tpu_custom_call" | custom-call | flops 8000000000 | bytes 100000 | tf_op jit(solution)/shard_map/up_grad/pallas_call | solution.py:536
  99.0 2.0 %collective-permute-done.27.refs_3_ = bf16[256,512]{1,0:T(8,128)(2,1)S(1)} collective-permute-done((bf16[256,512]{1,0:T(8,128)(2,1)S(1)}, bf16[256,512]{1,0:T(8,128)(2,1)S(1)}, u32[]{:S(2)}, u32[]{:S(2)}) %collective-permute-start.27) | collective-permute-done | bytes 262176 | tf_op jit(solution)/shard_map/ppermute | solution.py:26
  102.7 1.5 latent_back.1
  105.7 2.7 %collective-permute-start.30 = (bf16[128,1024]{1,0:T(8,128)(2,1)S(1)}, bf16[128,1024]{1,0:T(8,128)(2,1)S(1)}, u32[]{:S(2)}, u32[]{:S(2)}) collective-permute-start(bf16[128,1024]{1,0:T(8,128)(2,1)S(1)} %get-tuple-element.233), channel_id=1, source_target_pairs={{0,16},{4,20},{8,24},{12,28},{16,0},{20,4},{24,8},{28,12},{1,17},{... | collective-permute-start | bytes 786440 | tf_op jit(solution)/shard_map/ppermute | solution.py:26
  108.9 2.6 %collective-permute-done.28.refs_2_ = bf16[512,512]{1,0:T(8,128)(2,1)S(1)} collective-permute-done((bf16[512,512]{1,0:T(8,128)(2,1)S(1)}, bf16[512,512]{1,0:T(8,128)(2,1)S(1)}, u32[]{:S(2)}, u32[]{:S(2)}) %collective-permute-start.28) | collective-permute-done | bytes 524320 | tf_op jit(solution)/shard_map/ppermute | solution.py:26
  113.8 7.2 %collective-permute-done.30.refs_1_ = bf16[128,1024]{1,0:T(8,128)(2,1)S(1)} collective-permute-done((bf16[128,1024]{1,0:T(8,128)(2,1)S(1)}, bf16[128,1024]{1,0:T(8,128)(2,1)S(1)}, u32[]{:S(2)}, u32[]{:S(2)}) %collective-permute-start.30) | collective-permute-done | bytes 262176 | tf_op jit(solution)/shard_map/ppermute | solution.py:26
  126.0 2.9 %collective-permute-start.37 = (bf16[128,1024]{1,0:T(8,128)(2,1)S(1)}, bf16[128,1024]{1,0:T(8,128)(2,1)S(1)}, u32[]{:S(2)}, u32[]{:S(2)}) collective-permute-start(bf16[128,1024]{1,0:T(8,128)(2,1)S(1)} %get-tuple-element.254), channel_id=1, source_target_pairs={{0,16},{4,20},{8,24},{12,28},{16,0},{20,4},{24,8},{28,12},{1,17},{... | collective-permute-start | bytes 786440 | tf_op jit(solution)/shard_map/ppermute | solution.py:26
  128.9 3.4 %all-to-all-start = ((bf16[4,32,1024]{2,1,0:T(8,128)(2,1)}), bf16[4,32,1024]{2,1,0:T(8,128)(2,1)S(1)}, u32[]{:S(2)}, u32[]{:S(2)}) async-start(bf16[4,32,1024]{2,1,0:T(8,128)(2,1)} %bitcast.11), calls=%async_computation | async-start | bytes 524288 | tf_op jit(solution)/shard_map/all_to_all | solution.py:928
  133.2 7.0 %collective-permute-done.35.refs_1_ = bf16[272,1024]{1,0:T(8,128)(2,1)S(1)} collective-permute-done((bf16[272,1024]{1,0:T(8,128)(2,1)S(1)}, bf16[272,1024]{1,0:T(8,128)(2,1)S(1)}, u32[]{:S(2)}, u32[]{:S(2)}) %collective-permute-start.35) | collective-permute-done | bytes 557088 | tf_op jit(solution)/shard_map/ppermute | solution.py:26
  142.6 1.5 up_fold.5
  144.1 2.1 %collective-permute-start.39 = (bf16[64,1024]{1,0:T(8,128)(2,1)S(1)}, bf16[64,1024]{1,0:T(8,128)(2,1)S(1)}, u32[]{:S(2)}, u32[]{:S(2)}) collective-permute-start(bf16[64,1024]{1,0:T(8,128)(2,1)S(1)} %get-tuple-element.260), channel_id=1, source_target_pairs={{0,8},{4,12},{8,0},{12,4},{16,24},{20,28},{24,16},{28,20},{1,9},{5... | collective-permute-start | bytes 393224 | tf_op jit(solution)/shard_map/ppermute | solution.py:26
  146.2 1.5 collective-permute-done.38.refs_1_
  148.4 2.1 %collective-permute-start.40 = (bf16[80,1024]{1,0:T(8,128)(2,1)S(1)}, bf16[80,1024]{1,0:T(8,128)(2,1)S(1)}, u32[]{:S(2)}, u32[]{:S(2)}) collective-permute-start(bf16[80,1024]{1,0:T(8,128)(2,1)S(1)} %get-tuple-element.263), channel_id=1, source_target_pairs={{0,8},{4,12},{8,0},{12,4},{16,24},{20,28},{24,16},{28,20},{1,9},{5... | collective-permute-start | bytes 491528 | tf_op jit(solution)/shard_map/ppermute | solution.py:26
  152.0 2.8 %collective-permute-start.41 = (bf16[32,1024]{1,0:T(8,128)(2,1)S(1)}, bf16[32,1024]{1,0:T(8,128)(2,1)S(1)}, u32[]{:S(2)}, u32[]{:S(2)}) collective-permute-start(bf16[32,1024]{1,0:T(8,128)(2,1)S(1)} %get-tuple-element.267), channel_id=1, source_target_pairs={{0,16},{4,20},{8,24},{12,28},{16,0},{20,4},{24,8},{28,12},{1,17},{... | collective-permute-start | bytes 196616 | tf_op jit(solution)/shard_map/ppermute | solution.py:26
  155.4 2.4 %collective-permute-start.42 = (bf16[48,1024]{1,0:T(8,128)(2,1)S(1)}, bf16[48,1024]{1,0:T(8,128)(2,1)S(1)}, u32[]{:S(2)}, u32[]{:S(2)}) collective-permute-start(bf16[48,1024]{1,0:T(8,128)(2,1)S(1)} %get-tuple-element.269), channel_id=1, source_target_pairs={{0,16},{4,20},{8,24},{12,28},{16,0},{20,4},{24,8},{28,12},{1,17},{... | collective-permute-start | bytes 294920 | tf_op jit(solution)/shard_map/ppermute | solution.py:26
  (175 shorter events, 47.5 us)
Async XLA Ops:
  3.5 8.5 %collective-permute-start.1 = (bf16[160,512]{1,0:T(8,128)(2,1)}, bf16[160,512]{1,0:T(8,128)(2,1)S(1)}, u32[]{:S(2)}, u32[]{:S(2)}) collective-permute-start(bf16[160,512]{1,0:T(8,128)(2,1)} %get-tuple-element.142.refs_0_), channel_id=1, source_target_pairs={{0,2},{1,3},{2,0},{3,1},{4,6},{5,7},{6,4},{7,5},{8,10},{9,11},{10,... | collective-permute-start | bytes 491528 | tf_op jit(solution)/shard_map/ppermute | solution.py:26
  18.5 7.4 %collective-permute-start.4 = (bf16[176,512]{1,0:T(8,128)(2,1)S(1)}, bf16[176,512]{1,0:T(8,128)(2,1)S(1)}, u32[]{:S(2)}, u32[]{:S(2)}) collective-permute-start(bf16[176,512]{1,0:T(8,128)(2,1)S(1)} %get-tuple-element.148), channel_id=1, source_target_pairs={{0,2},{1,3},{2,0},{3,1},{4,6},{5,7},{6,4},{7,5},{8,10},{9,11},{10,... | collective-permute-start | bytes 540680 | tf_op jit(solution)/shard_map/ppermute | solution.py:26
  18.7 9.4 %collective-permute-start.5 = (bf16[176,512]{1,0:T(8,128)(2,1)S(1)}, bf16[176,512]{1,0:T(8,128)(2,1)S(1)}, u32[]{:S(2)}, u32[]{:S(2)}) collective-permute-start(bf16[176,512]{1,0:T(8,128)(2,1)S(1)} %get-tuple-element.149), channel_id=1, source_target_pairs={{0,3},{1,2},{2,1},{3,0},{4,7},{5,6},{6,5},{7,4},{8,11},{9,10},{10,... | collective-permute-start | bytes 540680 | tf_op jit(solution)/shard_map/ppermute | solution.py:26
  28.1 17.0 %collective-permute-start.8 = (bf16[160,1024]{1,0:T(8,128)(2,1)S(1)}, bf16[160,1024]{1,0:T(8,128)(2,1)S(1)}, u32[]{:S(2)}, u32[]{:S(2)}) collective-permute-start(bf16[160,1024]{1,0:T(8,128)(2,1)S(1)} %copy-done.2), channel_id=1, source_target_pairs={{0,2},{1,3},{2,0},{3,1},{4,6},{5,7},{6,4},{7,5},{8,10},{9,11},{10,... | collective-permute-start | bytes 983048 | tf_op jit(solution)/shard_map/ppermute | solution.py:26
  33.2 12.2 %collective-permute-start.7 = (bf16[160,1024]{1,0:T(8,128)(2,1)S(1)}, bf16[160,1024]{1,0:T(8,128)(2,1)S(1)}, u32[]{:S(2)}, u32[]{:S(2)}) collective-permute-start(bf16[160,1024]{1,0:T(8,128)(2,1)S(1)} %get-tuple-element.157.ff_low.refs_4_), channel_id=1, source_target_pairs={{0,2},{1,3},{2,0},{3,1},{4,6},{5,7},{6,4},{7,5},{8,10},{9,11},{10,... | collective-permute-start | bytes 983048 | tf_op jit(solution)/shard_map/ppermute | solution.py:26
  35.1 12.2 %collective-permute-start.6 = (bf16[160,1024]{1,0:T(8,128)(2,1)S(1)}, bf16[160,1024]{1,0:T(8,128)(2,1)S(1)}, u32[]{:S(2)}, u32[]{:S(2)}) collective-permute-start(bf16[160,1024]{1,0:T(8,128)(2,1)S(1)} %get-tuple-element.157.ff_low.refs_4_), channel_id=1, source_target_pairs={{0,1},{1,0},{2,3},{3,2},{4,5},{5,4},{6,7},{7,6},{8,9},{9,8},{10,11... | collective-permute-start | bytes 983048 | tf_op jit(solution)/shard_map/ppermute | solution.py:26
  35.2 11.2 %collective-permute-start.10 = (bf16[160,1024]{1,0:T(8,128)(2,1)S(1)}, bf16[160,1024]{1,0:T(8,128)(2,1)}, u32[]{:S(2)}, u32[]{:S(2)}) collective-permute-start(bf16[160,1024]{1,0:T(8,128)(2,1)S(1)} %copy-done.2), channel_id=1, source_target_pairs={{0,1},{1,0},{2,3},{3,2},{4,5},{5,4},{6,7},{7,6},{8,9},{9,8},{10,11... | collective-permute-start | bytes 983048 | tf_op jit(solution)/shard_map/ppermute | solution.py:26
  45.9 17.3 %collective-permute-start.15 = (bf16[2,160,512]{2,1,0:T(8,128)(2,1)}, bf16[2,160,512]{2,1,0:T(8,128)(2,1)}, u32[]{:S(2)}, u32[]{:S(2)}) collective-permute-start(bf16[2,160,512]{2,1,0:T(8,128)(2,1)} %get-tuple-element.172), channel_id=1, source_target_pairs={{0,2},{1,3},{2,0},{3,1},{4,6},{5,7},{6,4},{7,5},{8,10},{9,11},{10,... | collective-permute-start | bytes 983048 | tf_op jit(solution)/shard_map/ppermute | solution.py:26
  46.4 16.8 %collective-permute-start.16 = (bf16[2,160,512]{2,1,0:T(8,128)(2,1)}, bf16[2,160,512]{2,1,0:T(8,128)(2,1)S(1)}, u32[]{:S(2)}, u32[]{:S(2)}) collective-permute-start(bf16[2,160,512]{2,1,0:T(8,128)(2,1)} %get-tuple-element.173), channel_id=1, source_target_pairs={{0,3},{1,2},{2,1},{3,0},{4,7},{5,6},{6,5},{7,4},{8,11},{9,10},{10,... | collective-permute-start | bytes 983048 | tf_op jit(solution)/shard_map/ppermute | solution.py:26
  61.0 7.1 %collective-permute-start.13 = (bf16[192,512]{1,0:T(8,128)(2,1)}, bf16[192,512]{1,0:T(8,128)(2,1)S(1)}, u32[]{:S(2)}, u32[]{:S(2)}) collective-permute-start(bf16[192,512]{1,0:T(8,128)(2,1)} %get-tuple-element.163.refs_4_), channel_id=1, source_target_pairs={{0,2},{1,3},{2,0},{3,1},{4,6},{5,7},{6,4},{7,5},{8,10},{9,11},{10,... | collective-permute-start | bytes 589832 | tf_op jit(solution)/shard_map/ppermute | solution.py:26
  61.5 10.1 %collective-permute-start.12 = (bf16[192,512]{1,0:T(8,128)(2,1)}, bf16[192,512]{1,0:T(8,128)(2,1)S(1)}, u32[]{:S(2)}, u32[]{:S(2)}) collective-permute-start(bf16[192,512]{1,0:T(8,128)(2,1)} %get-tuple-element.163.refs_4_), channel_id=1, source_target_pairs={{0,1},{1,0},{2,3},{3,2},{4,5},{5,4},{6,7},{7,6},{8,9},{9,8},{10,11... | collective-permute-start | bytes 589832 | tf_op jit(solution)/shard_map/ppermute | solution.py:26
  68.4 24.3 %collective-permute-start.22 = (bf16[2,160,512]{2,1,0:T(8,128)(2,1)S(1)}, bf16[2,160,512]{2,1,0:T(8,128)(2,1)S(1)}, u32[]{:S(2)}, u32[]{:S(2)}) collective-permute-start(bf16[2,160,512]{2,1,0:T(8,128)(2,1)S(1)} %copy-done.41), channel_id=1, source_target_pairs={{0,1},{1,0},{2,3},{3,2},{4,5},{5,4},{6,7},{7,6},{8,9},{9,8},{10,11... | collective-permute-start | bytes 983048 | tf_op jit(solution)/shard_map/ppermute | solution.py:26
  68.6 21.6 %collective-permute-start.24 = (bf16[2,160,512]{2,1,0:T(8,128)(2,1)S(1)}, bf16[2,160,512]{2,1,0:T(8,128)(2,1)S(1)}, u32[]{:S(2)}, u32[]{:S(2)}) collective-permute-start(bf16[2,160,512]{2,1,0:T(8,128)(2,1)S(1)} %copy-done.40), channel_id=1, source_target_pairs={{0,3},{1,2},{2,1},{3,0},{4,7},{5,6},{6,5},{7,4},{8,11},{9,10},{10,... | collective-permute-start | bytes 983048 | tf_op jit(solution)/shard_map/ppermute | solution.py:26
  70.1 13.9 %collective-permute-start.18 = (bf16[512,512]{1,0:T(8,128)(2,1)S(1)}, bf16[512,512]{1,0:T(8,128)(2,1)S(1)}, u32[]{:S(2)}, u32[]{:S(2)}) collective-permute-start(bf16[512,512]{1,0:T(8,128)(2,1)S(1)} %get-tuple-element.186), channel_id=1, source_target_pairs={{0,4},{4,0},{8,12},{12,8},{16,20},{20,16},{24,28},{28,24},{1,5},{5... | collective-permute-start | bytes 1572872 | tf_op jit(solution)/shard_map/ppermute | solution.py:26
  71.6 13.6 %collective-permute-start.19 = (bf16[512,512]{1,0:T(8,128)(2,1)S(1)}, bf16[512,512]{1,0:T(8,128)(2,1)S(1)}, u32[]{:S(2)}, u32[]{:S(2)}) collective-permute-start(bf16[512,512]{1,0:T(8,128)(2,1)S(1)} %get-tuple-element.187), channel_id=1, source_target_pairs={{0,8},{4,12},{8,0},{12,4},{16,24},{20,28},{24,16},{28,20},{1,9},{5... | collective-permute-start | bytes 1572872 | tf_op jit(solution)/shard_map/ppermute | solution.py:26
  73.2 19.5 %collective-permute-start.23 = (bf16[2,160,512]{2,1,0:T(8,128)(2,1)S(1)}, bf16[2,160,512]{2,1,0:T(8,128)(2,1)S(1)}, u32[]{:S(2)}, u32[]{:S(2)}) collective-permute-start(bf16[2,160,512]{2,1,0:T(8,128)(2,1)S(1)} %copy-done.39), channel_id=1, source_target_pairs={{0,2},{1,3},{2,0},{3,1},{4,6},{5,7},{6,4},{7,5},{8,10},{9,11},{10,... | collective-permute-start | bytes 983048 | tf_op jit(solution)/shard_map/ppermute | solution.py:26
  90.0 7.2 %collective-permute-start.25 = (bf16[512,1024]{1,0:T(8,128)(2,1)S(1)}, bf16[512,1024]{1,0:T(8,128)(2,1)S(1)}, u32[]{:S(2)}, u32[]{:S(2)}) collective-permute-start(bf16[512,1024]{1,0:T(8,128)(2,1)S(1)} %get-tuple-element.207), channel_id=1, source_target_pairs={{0,1},{1,0},{2,3},{3,2},{4,5},{5,4},{6,7},{7,6},{8,9},{9,8},{10,11... | collective-permute-start | bytes 3145736 | tf_op jit(solution)/shard_map/ppermute | solution.py:26
  90.2 8.8 %collective-permute-start.26 = (bf16[256,512]{1,0:T(8,128)(2,1)S(1)}, bf16[256,512]{1,0:T(8,128)(2,1)S(1)}, u32[]{:S(2)}, u32[]{:S(2)}) collective-permute-start(bf16[256,512]{1,0:T(8,128)(2,1)S(1)} %get-tuple-element.213), channel_id=1, source_target_pairs={{0,8},{4,12},{8,0},{12,4},{16,24},{20,28},{24,16},{28,20},{1,9},{5... | collective-permute-start | bytes 786440 | tf_op jit(solution)/shard_map/ppermute | solution.py:26
  91.9 9.2 %collective-permute-start.27 = (bf16[256,512]{1,0:T(8,128)(2,1)S(1)}, bf16[256,512]{1,0:T(8,128)(2,1)S(1)}, u32[]{:S(2)}, u32[]{:S(2)}) collective-permute-start(bf16[256,512]{1,0:T(8,128)(2,1)S(1)} %get-tuple-element.214), channel_id=1, source_target_pairs={{0,4},{4,0},{8,12},{12,8},{16,20},{20,16},{24,28},{28,24},{1,5},{5... | collective-permute-start | bytes 786440 | tf_op jit(solution)/shard_map/ppermute | solution.py:26
  95.4 16.1 %collective-permute-start.28 = (bf16[512,512]{1,0:T(8,128)(2,1)S(1)}, bf16[512,512]{1,0:T(8,128)(2,1)S(1)}, u32[]{:S(2)}, u32[]{:S(2)}) collective-permute-start(bf16[512,512]{1,0:T(8,128)(2,1)S(1)} %get-tuple-element.228), channel_id=1, source_target_pairs={{0,4},{4,0},{8,12},{12,8},{16,20},{20,16},{24,28},{28,24},{1,5},{5... | collective-permute-start | bytes 1572872 | tf_op jit(solution)/shard_map/ppermute | solution.py:26
  96.7 15.3 %collective-permute-start.29 = (bf16[512,512]{1,0:T(8,128)(2,1)S(1)}, bf16[512,512]{1,0:T(8,128)(2,1)S(1)}, u32[]{:S(2)}, u32[]{:S(2)}) collective-permute-start(bf16[512,512]{1,0:T(8,128)(2,1)S(1)} %get-tuple-element.229), channel_id=1, source_target_pairs={{0,8},{4,12},{8,0},{12,4},{16,24},{20,28},{24,16},{28,20},{1,9},{5... | collective-permute-start | bytes 1572872 | tf_op jit(solution)/shard_map/ppermute | solution.py:26
  105.6 18.8 %collective-permute-start.34 = (bf16[528,1024]{1,0:T(8,128)(2,1)S(1)}, bf16[528,1024]{1,0:T(8,128)(2,1)S(1)}, u32[]{:S(2)}, u32[]{:S(2)}) collective-permute-start(bf16[528,1024]{1,0:T(8,128)(2,1)S(1)} %get-tuple-element.245), channel_id=1, source_target_pairs={{0,1},{1,0},{2,3},{3,2},{4,5},{5,4},{6,7},{7,6},{8,9},{9,8},{10,11... | collective-permute-start | bytes 3244040 | tf_op jit(solution)/shard_map/ppermute | solution.py:26
  105.7 15.4 %collective-permute-start.30 = (bf16[128,1024]{1,0:T(8,128)(2,1)S(1)}, bf16[128,1024]{1,0:T(8,128)(2,1)S(1)}, u32[]{:S(2)}, u32[]{:S(2)}) collective-permute-start(bf16[128,1024]{1,0:T(8,128)(2,1)S(1)} %get-tuple-element.233), channel_id=1, source_target_pairs={{0,16},{4,20},{8,24},{12,28},{16,0},{20,4},{24,8},{28,12},{1,17},{... | collective-permute-start | bytes 786440 | tf_op jit(solution)/shard_map/ppermute | solution.py:26
  108.3 15.4 %collective-permute-start.33 = (bf16[256,1024]{1,0:T(8,128)(2,1)S(1)}, bf16[256,1024]{1,0:T(8,128)(2,1)S(1)}, u32[]{:S(2)}, u32[]{:S(2)}) collective-permute-start(bf16[256,1024]{1,0:T(8,128)(2,1)S(1)} %get-tuple-element.242), channel_id=1, source_target_pairs={{0,2},{1,3},{2,0},{3,1},{4,6},{5,7},{6,4},{7,5},{8,10},{9,11},{10,... | collective-permute-start | bytes 1572872 | tf_op jit(solution)/shard_map/ppermute | solution.py:26
  112.9 10.1 %collective-permute-start.31 = (bf16[256,512]{1,0:T(8,128)(2,1)S(1)}, bf16[256,512]{1,0:T(8,128)(2,1)S(1)}, u32[]{:S(2)}, u32[]{:S(2)}) collective-permute-start(bf16[256,512]{1,0:T(8,128)(2,1)S(1)} %get-tuple-element.238), channel_id=1, source_target_pairs={{0,8},{4,12},{8,0},{12,4},{16,24},{20,28},{24,16},{28,20},{1,9},{5... | collective-permute-start | bytes 786440 | tf_op jit(solution)/shard_map/ppermute | solution.py:26
  113.2 9.8 %collective-permute-start.32 = (bf16[256,512]{1,0:T(8,128)(2,1)S(1)}, bf16[256,512]{1,0:T(8,128)(2,1)S(1)}, u32[]{:S(2)}, u32[]{:S(2)}) collective-permute-start(bf16[256,512]{1,0:T(8,128)(2,1)S(1)} %get-tuple-element.239), channel_id=1, source_target_pairs={{0,4},{4,0},{8,12},{12,8},{16,20},{20,16},{24,28},{28,24},{1,5},{5... | collective-permute-start | bytes 786440 | tf_op jit(solution)/shard_map/ppermute | solution.py:26
  125.3 14.9 %collective-permute-start.35 = (bf16[272,1024]{1,0:T(8,128)(2,1)S(1)}, bf16[272,1024]{1,0:T(8,128)(2,1)S(1)}, u32[]{:S(2)}, u32[]{:S(2)}) collective-permute-start(bf16[272,1024]{1,0:T(8,128)(2,1)S(1)} %get-tuple-element.247), channel_id=1, source_target_pairs={{0,2},{1,3},{2,0},{3,1},{4,6},{5,7},{6,4},{7,5},{8,10},{9,11},{10,... | collective-permute-start | bytes 1671176 | tf_op jit(solution)/shard_map/ppermute | solution.py:26
  126.0 16.6 %collective-permute-start.37 = (bf16[128,1024]{1,0:T(8,128)(2,1)S(1)}, bf16[128,1024]{1,0:T(8,128)(2,1)S(1)}, u32[]{:S(2)}, u32[]{:S(2)}) collective-permute-start(bf16[128,1024]{1,0:T(8,128)(2,1)S(1)} %get-tuple-element.254), channel_id=1, source_target_pairs={{0,16},{4,20},{8,24},{12,28},{16,0},{20,4},{24,8},{28,12},{1,17},{... | collective-permute-start | bytes 786440 | tf_op jit(solution)/shard_map/ppermute | solution.py:26
  128.9 21.6 %all-to-all-start = ((bf16[4,32,1024]{2,1,0:T(8,128)(2,1)}), bf16[4,32,1024]{2,1,0:T(8,128)(2,1)S(1)}, u32[]{:S(2)}, u32[]{:S(2)}) async-start(bf16[4,32,1024]{2,1,0:T(8,128)(2,1)} %bitcast.11), calls=%async_computation | async-start | bytes 524288 | tf_op jit(solution)/shard_map/all_to_all | solution.py:928
  132.3 9.7 %collective-permute-start.36 = (bf16[128,1024]{1,0:T(8,128)(2,1)S(1)}, bf16[128,1024]{1,0:T(8,128)(2,1)S(1)}, u32[]{:S(2)}, u32[]{:S(2)}) collective-permute-start(bf16[128,1024]{1,0:T(8,128)(2,1)S(1)} %get-tuple-element.251), channel_id=1, source_target_pairs={{0,4},{4,0},{8,12},{12,8},{16,20},{20,16},{24,28},{28,24},{1,5},{5... | collective-permute-start | bytes 786440 | tf_op jit(solution)/shard_map/ppermute | solution.py:26
  144.1 7.2 %collective-permute-start.39 = (bf16[64,1024]{1,0:T(8,128)(2,1)S(1)}, bf16[64,1024]{1,0:T(8,128)(2,1)S(1)}, u32[]{:S(2)}, u32[]{:S(2)}) collective-permute-start(bf16[64,1024]{1,0:T(8,128)(2,1)S(1)} %get-tuple-element.260), channel_id=1, source_target_pairs={{0,8},{4,12},{8,0},{12,4},{16,24},{20,28},{24,16},{28,20},{1,9},{5... | collective-permute-start | bytes 393224 | tf_op jit(solution)/shard_map/ppermute | solution.py:26
  152.0 6.8 %collective-permute-start.41 = (bf16[32,1024]{1,0:T(8,128)(2,1)S(1)}, bf16[32,1024]{1,0:T(8,128)(2,1)S(1)}, u32[]{:S(2)}, u32[]{:S(2)}) collective-permute-start(bf16[32,1024]{1,0:T(8,128)(2,1)S(1)} %get-tuple-element.267), channel_id=1, source_target_pairs={{0,16},{4,20},{8,24},{12,28},{16,0},{20,4},{24,8},{28,12},{1,17},{... | collective-permute-start | bytes 196616 | tf_op jit(solution)/shard_map/ppermute | solution.py:26
  (54 other events, 314.9 us)

commit v7 on v6

--- a/solution.py
+++ b/solution.py
@@ -758,7 +758,7 @@
         + [wide_low, wide, wide_low]
         + [(whole((rows + 4 * HEADS, inner)), out((rows + 4 * HEADS, inner), BF16)), (whole((2, width)), out((2, width), F32))],
         scratch=[pltpu.VMEM((rows, width), F32), pltpu.VMEM((rows, width), F32)],
-        vmem=62, prefetch=1, name="feed_end",
+        vmem=52, prefetch=1, name="feed_end",
     )(own, counts, after(ff_low, *ffs[1:], *dys[1:]), dy, *([w_up] * count), *([w_down] * count),
       far[2 * here], far[2 * here + 1], hidden, attended, lse, w_out, gains)
     result, dhidden, dhid_low, datt_low, sums_ff = near[2 * here :]

time: 163 us -> 162 us (level)
  local copies, waits for them, and re-layouts: 7.12 us -> 4.46 us
  starting transfers between devices: 44 us -> 45.9 us
    unnamed x84 -> x64, local copies, waits for them, and re-layouts: 6.46 us -> 3.8 us
    ppermute x43, starting transfers between devices: 40.6 us -> 42.5 us  [swap(): return lax.ppermute(values, axis, [(k, k ^ bit) for k in range(n)])]
  transfers between devices with their start and end apart: 44 -> 44, of which waited for: 19 -> 20; matrix products, arithmetic and copies ran while one was open for 0% -> 0% of each run, Pallas kernels for 40% -> 40%
where the time goes in v7:
time: 162 us; the launch traced here: 161 us
  Pallas kernels  72.6 us (45%)
  starting transfers between devices  45.9 us (28%)
  waiting for transfers between devices  36.8 us (23%)
  local copies, waits for them, and re-layouts  4.46 us (3%)
    ppermute x43, starting transfers between devices, swap(): return lax.ppermute(values, axis, [(k, k ^ bit) for k in range(n)])  42.5 us
    ppermute x43, waiting for transfers between devices, swap(): return lax.ppermute(values, axis, [(k, k ^ bit) for k in range(n)])  36.8 us
    pallas_call x16, Pallas kernels, fold(): call(functools.partial(fold_kernel, nxt, end, len(kept), extra is not Non...  14.1 us
    pallas_call x1, Pallas kernels, on_device(): call(functools.partial(feed_end_kernel, per_slot, count, here), (here, ha...  11.3 us
    pallas_call x3, Pallas kernels, outer(): call(functools.partial(outer_kernel, count, [(order[0], plan[0]) for orde...  10.5 us
    pallas_call x1, Pallas kernels, on_device(): call(functools.partial(feed_kernel, count, here), (here, halves), [whole(...  9.54 us
    pallas_call x1, Pallas kernels, attend_back(): call(functools.partial(attend_back_kernel, peers, per_slot, scale), (slot...  5.67 us
    pallas_call x1, Pallas kernels, on_device(): call(media_kernel, (slots // group,), [leading((group, patch_rows, width)...  5.53 us
  transfers between devices with their start and end apart: 44, of which 20 were waited for; matrix products, arithmetic and copies ran while one was open for 0% of the time, Pallas kernels for 40%

profile of v7, /device:TPU:0, one launch (start us, length us, event | category | flops | bytes accessed | tf_op | source)
XLA Modules:
  0.0 161.5 jit_solution(9268995853279156002)
XLA Ops:
  0.6 2.8 %latent.1 = (bf16[160,1024]{1,0:T(8,128)(2,1)}, bf16[160,512]{1,0:T(8,128)(2,1)}, bf16[160,1024]{1,0:T(8,128)(2,1)}) custom-call(s32[2]{0:T(128)} %counts.3, bf16[160,1024]{1,0:T(8,128)(2,1)} %bitcast.13, bf16[160,1024]{1,0:T(8,128)(2,1)} %bitcast.18, f32[3,1024]{1,0:T(4,128)} %refs_6_.7, f32[3,1024]{1,0:T(4,128)} %refs_7_.3, bf16[1024,512]{1,0:T(8,128)(2,1)} %refs_5_.7), custom_call_target="tpu_custom_call" | custom-call | flops 5800000000 | bytes 100000 | tf_op jit(solution)/shard_map/latent/pallas_call | solution.py:640
  3.5 3.0 %collective-permute-start.1 = (bf16[160,512]{1,0:T(8,128)(2,1)}, bf16[160,512]{1,0:T(8,128)(2,1)S(1)}, u32[]{:S(2)}, u32[]{:S(2)}) collective-permute-start(bf16[160,512]{1,0:T(8,128)(2,1)} %get-tuple-element.142.refs_0_), channel_id=1, source_target_pairs={{0,2},{1,3},{2,0},{3,1},{4,6},{5,7},{6,4},{7,5},{8,10},{9,11},{10,... | collective-permute-start | bytes 491528 | tf_op jit(solution)/shard_map/ppermute | solution.py:26
  6.5 5.5 %media.3 = (bf16[10,80,1024]{2,1,0:T(8,128)(2,1)}, bf16[10,80,1024]{2,1,0:T(8,128)(2,1)}) custom-call(bf16[10,64,1024]{2,1,0:T(8,128)(2,1)} %media.5, bf16[160,1024]{1,0:T(8,128)(2,1)} %get-tuple-element.143.lat_low, f32[3,1024]{1,0:T(4,128)} %refs_6_.7, f32[3,1024]{1,0:T(4,128)} %refs_7_.3, bf16[1024,1024]{1,0:T(8,128)(2,1)} %w_keyval.3), custom_call_target="tpu_custom_call" | custom-call | flops 5400000000 | bytes 100000 | tf_op jit(solution)/shard_map/media/pallas_call | solution.py:656
  15.1 2.9 %attend.1 = (bf16[176,512]{1,0:T(8,128)(2,1)S(1)}, bf16[176,512]{1,0:T(8,128)(2,1)S(1)}, bf16[176,512]{1,0:T(8,128)(2,1)S(1)}, bf16[176,512]{1,0:T(8,128)(2,1)S(1)}) custom-call(bf16[160,512]{1,0:T(8,128)(2,1)S(1)} %copy-done.11, bf16[160,512]{1,0:T(8,128)(2,1)S(1)} %collective-permute-done.refs_1_, bf16[160,512]{1,0:T(8,128)(2,1)S(1)} %collective-permute-done.1.refs_2_, ...), custom_call_target="tpu_custom_call" | custom-call | flops 6200000000 | bytes 100000 | tf_op jit(solution)/shard_map/attend/pallas_call | solution.py:681
  20.0 5.9 %collective-permute-done.4.refs_2_ = bf16[176,512]{1,0:T(8,128)(2,1)S(1)} collective-permute-done((bf16[176,512]{1,0:T(8,128)(2,1)S(1)}, bf16[176,512]{1,0:T(8,128)(2,1)S(1)}, u32[]{:S(2)}, u32[]{:S(2)}) %collective-permute-start.4) | collective-permute-done | bytes 180256 | tf_op jit(solution)/shard_map/ppermute | solution.py:26
  25.9 2.2 %collective-permute-done.5.refs_3_ = bf16[176,512]{1,0:T(8,128)(2,1)S(1)} collective-permute-done((bf16[176,512]{1,0:T(8,128)(2,1)S(1)}, bf16[176,512]{1,0:T(8,128)(2,1)S(1)}, u32[]{:S(2)}, u32[]{:S(2)}) %collective-permute-start.5) | collective-permute-done | bytes 180256 | tf_op jit(solution)/shard_map/ppermute | solution.py:26
  28.8 1.5 mix.1
  35.1 9.5 %feed.1 = (bf16[2,160,512]{2,1,0:T(8,128)(2,1)}, bf16[2,160,512]{2,1,0:T(8,128)(2,1)}, bf16[2,160,512]{2,1,0:T(8,128)(2,1)}, bf16[2,160,512]{2,1,0:T(8,128)(2,1)...) custom-call(s32[2]{0:T(128)} %pad_add_fusion.own, bf16[160,1024]{1,0:T(8,128)(2,1)} %copy-done, ...), custom_call_target="tpu_custom_call" | custom-call | flops 200000000 | bytes 100000 | tf_op jit(solution)/shard_map/feed/pallas_call | solution.py:737
  47.5 11.3 %feed_end.1 = (bf16[2,160,512]{2,1,0:T(8,128)(2,1)S(1)}, bf16[2,160,512]{2,1,0:T(8,128)(2,1)S(1)}, bf16[2,160,512]{2,1,0:T(8,128)(2,1)S(1)}, bf16[2,160,512]{2,1...) custom-call(s32[2]{0:T(128)S(1)} %copy-done.4, ...), custom_call_target="tpu_custom_call" | custom-call | flops 71999995904 | bytes 100000 | tf_op jit(solution)/shard_map/feed_end/pallas_call | solution.py:752
  61.9 3.9 %down_grad.1 = (bf16[512,512]{1,0:T(8,128)(2,1)S(1)}, bf16[512,512]{1,0:T(8,128)(2,1)S(1)}, bf16[512,512]{1,0:T(8,128)(2,1)S(1)}, bf16[512,512]{1,0:T(8,128)(2,1)S(1)}) custom-call(s32[2]{0:T(128)S(1)} %copy-done.4, bf16[160,1024]{1,0:T(8,128)(2,1)S(1)} %copy-done.3, bf16[160,1024]{1,0:T(8,128)(2,1)S(1)} %collective-permute-done.10.refs_1_, ...), custom_call_target="tpu_custom_call" | custom-call | flops 8000000000 | bytes 100000 | tf_op jit(solution)/shard_map/down_grad/pallas_call | solution.py:536
  67.8 1.6 %collective-permute-start.18 = (bf16[512,512]{1,0:T(8,128)(2,1)S(1)}, bf16[512,512]{1,0:T(8,128)(2,1)S(1)}, u32[]{:S(2)}, u32[]{:S(2)}) collective-permute-start(bf16[512,512]{1,0:T(8,128)(2,1)S(1)} %get-tuple-element.186), channel_id=1, source_target_pairs={{0,4},{4,0},{8,12},{12,8},{16,20},{20,16},{24,28},{28,24},{1,5},{5... | collective-permute-start | bytes 1572872 | tf_op jit(solution)/shard_map/ppermute | solution.py:26
  69.5 1.6 collective-permute-start.19
  72.5 5.7 %attend_back.1 = (bf16[10,80,1024]{2,1,0:T(8,128)(2,1)S(1)}, bf16[2,160,512]{2,1,0:T(8,128)(2,1)S(1)}, bf16[2,160,512]{2,1,0:T(8,128)(2,1)S(1)}) custom-call(bf16[160,512]{1,0:T(8,128)(2,1)S(1)} %copy-done.11, bf16[160,512]{1,0:T(8,128)(2,1)S(1)} %copy-done.15, bf16[160,512]{1,0:T(8,128)(2,1)S(1)} %copy-done.13, bf16[160,512]{1,0:T(8,128)(2,1)S(1)} %copy-done.17, ...), custom_call_target="tpu_custom_call" | custom-call | flops 3400000000 | bytes 100000 | tf_op jit(solution)/shard_map/attend_back/pallas_call | solution.py:816
  78.2 4.2 %keyval_back.1 = (bf16[10,64,1024]{2,1,0:T(8,128)(2,1)}, f32[160,1024]{1,0:T(8,128)S(1)}, f32[2,1024]{1,0:T(2,128)S(1)}) custom-call(bf16[10,64,1024]{2,1,0:T(8,128)(2,1)S(1)} %copy-done.6, bf16[10,80,1024]{2,1,0:T(8,128)(2,1)S(1)} %get-tuple-element.189.dkv, bf16[1024,1024]{1,0:T(8,128)(2,1)S(1)} %copy-done.5, f32[3,1024]{1,0:T(4,128)S(1)} %copy-done.19), custom_call_target="tpu_custom_call" | custom-call | flops 8000000000 | bytes 100000 | tf_op jit(solution)/shard_map/keyval_back/pallas_call | solution.py:842
  84.2 3.9 %keyval_grad.1 = (bf16[512,1024]{1,0:T(8,128)(2,1)S(1)}, bf16[512,1024]{1,0:T(8,128)(2,1)S(1)}) custom-call(s32[2]{0:T(128)S(1)} %copy-done.4, bf16[800,1024]{1,0:T(8,128)(2,1)S(1)} %bitcast.17, bf16[800,1024]{1,0:T(8,128)(2,1)S(1)} %bitcast.16), custom_call_target="tpu_custom_call" | custom-call | flops 22799998976 | bytes 100000 | tf_op jit(solution)/shard_map/keyval_grad/pallas_call | solution.py:536
  88.3 1.6 %collective-permute-start.26 = (bf16[256,512]{1,0:T(8,128)(2,1)S(1)}, bf16[256,512]{1,0:T(8,128)(2,1)S(1)}, u32[]{:S(2)}, u32[]{:S(2)}) collective-permute-start(bf16[256,512]{1,0:T(8,128)(2,1)S(1)} %get-tuple-element.213), channel_id=1, source_target_pairs={{0,8},{4,12},{8,0},{12,4},{16,24},{20,28},{24,16},{28,20},{1,9},{5... | collective-permute-start | bytes 786440 | tf_op jit(solution)/shard_map/ppermute | solution.py:26
  90.7 2.7 %up_grad.1 = (bf16[512,512]{1,0:T(8,128)(2,1)S(1)}, bf16[512,512]{1,0:T(8,128)(2,1)S(1)}, bf16[512,512]{1,0:T(8,128)(2,1)S(1)}, bf16[512,512]{1,0:T(8,128)(2,1)S(1)}) custom-call(s32[2]{0:T(128)S(1)} %copy-done.4, bf16[2,160,512]{2,1,0:T(8,128)(2,1)S(1)} %get-tuple-element.198.refs_0_, bf16[2,160,512]{2,1,0:T(8,128)(2,1)S(1)} %collective-permute-done.22.refs_1_, ...), custom_call_target="tpu_custom_call" | custom-call | flops 8000000000 | bytes 100000 | tf_op jit(solution)/shard_map/up_grad/pallas_call | solution.py:536
  97.6 1.5 collective-permute-done.27.refs_3_
  103.7 2.6 %collective-permute-start.30 = (bf16[128,1024]{1,0:T(8,128)(2,1)S(1)}, bf16[128,1024]{1,0:T(8,128)(2,1)S(1)}, u32[]{:S(2)}, u32[]{:S(2)}) collective-permute-start(bf16[128,1024]{1,0:T(8,128)(2,1)S(1)} %get-tuple-element.233), channel_id=1, source_target_pairs={{0,16},{4,20},{8,24},{12,28},{16,0},{20,4},{24,8},{28,12},{1,17},{... | collective-permute-start | bytes 786440 | tf_op jit(solution)/shard_map/ppermute | solution.py:26
  106.3 1.5 collective-permute-start.33
  107.8 1.8 %collective-permute-done.28.refs_2_ = bf16[512,512]{1,0:T(8,128)(2,1)S(1)} collective-permute-done((bf16[512,512]{1,0:T(8,128)(2,1)S(1)}, bf16[512,512]{1,0:T(8,128)(2,1)S(1)}, u32[]{:S(2)}, u32[]{:S(2)}) %collective-permute-start.28) | collective-permute-done | bytes 524320 | tf_op jit(solution)/shard_map/ppermute | solution.py:26
  111.9 7.1 %collective-permute-done.30.refs_1_ = bf16[128,1024]{1,0:T(8,128)(2,1)S(1)} collective-permute-done((bf16[128,1024]{1,0:T(8,128)(2,1)S(1)}, bf16[128,1024]{1,0:T(8,128)(2,1)S(1)}, u32[]{:S(2)}, u32[]{:S(2)}) %collective-permute-start.30) | collective-permute-done | bytes 262176 | tf_op jit(solution)/shard_map/ppermute | solution.py:26
  123.3 1.5 collective-permute-start.35
  124.8 3.0 %collective-permute-start.37 = (bf16[128,1024]{1,0:T(8,128)(2,1)S(1)}, bf16[128,1024]{1,0:T(8,128)(2,1)S(1)}, u32[]{:S(2)}, u32[]{:S(2)}) collective-permute-start(bf16[128,1024]{1,0:T(8,128)(2,1)S(1)} %get-tuple-element.254), channel_id=1, source_target_pairs={{0,16},{4,20},{8,24},{12,28},{16,0},{20,4},{24,8},{28,12},{1,17},{... | collective-permute-start | bytes 786440 | tf_op jit(solution)/shard_map/ppermute | solution.py:26
  127.8 3.4 %all-to-all-start = ((bf16[4,32,1024]{2,1,0:T(8,128)(2,1)}), bf16[4,32,1024]{2,1,0:T(8,128)(2,1)S(1)}, u32[]{:S(2)}, u32[]{:S(2)}) async-start(bf16[4,32,1024]{2,1,0:T(8,128)(2,1)} %bitcast.11), calls=%async_computation | async-start | bytes 524288 | tf_op jit(solution)/shard_map/all_to_all | solution.py:928
  132.2 6.1 %collective-permute-done.35.refs_1_ = bf16[272,1024]{1,0:T(8,128)(2,1)S(1)} collective-permute-done((bf16[272,1024]{1,0:T(8,128)(2,1)S(1)}, bf16[272,1024]{1,0:T(8,128)(2,1)S(1)}, u32[]{:S(2)}, u32[]{:S(2)}) %collective-permute-start.35) | collective-permute-done | bytes 557088 | tf_op jit(solution)/shard_map/ppermute | solution.py:26
  141.1 1.5 up_fold.5
  142.7 2.5 %collective-permute-start.39 = (bf16[64,1024]{1,0:T(8,128)(2,1)S(1)}, bf16[64,1024]{1,0:T(8,128)(2,1)S(1)}, u32[]{:S(2)}, u32[]{:S(2)}) collective-permute-start(bf16[64,1024]{1,0:T(8,128)(2,1)S(1)} %get-tuple-element.260), channel_id=1, source_target_pairs={{0,8},{4,12},{8,0},{12,4},{16,24},{20,28},{24,16},{28,20},{1,9},{5... | collective-permute-start | bytes 393224 | tf_op jit(solution)/shard_map/ppermute | solution.py:26
  146.9 2.5 %collective-permute-start.40 = (bf16[80,1024]{1,0:T(8,128)(2,1)S(1)}, bf16[80,1024]{1,0:T(8,128)(2,1)S(1)}, u32[]{:S(2)}, u32[]{:S(2)}) collective-permute-start(bf16[80,1024]{1,0:T(8,128)(2,1)S(1)} %get-tuple-element.263), channel_id=1, source_target_pairs={{0,8},{4,12},{8,0},{12,4},{16,24},{20,28},{24,16},{28,20},{1,9},{5... | collective-permute-start | bytes 491528 | tf_op jit(solution)/shard_map/ppermute | solution.py:26
  150.9 1.9 %collective-permute-start.41 = (bf16[32,1024]{1,0:T(8,128)(2,1)S(1)}, bf16[32,1024]{1,0:T(8,128)(2,1)S(1)}, u32[]{:S(2)}, u32[]{:S(2)}) collective-permute-start(bf16[32,1024]{1,0:T(8,128)(2,1)S(1)} %get-tuple-element.267), channel_id=1, source_target_pairs={{0,16},{4,20},{8,24},{12,28},{16,0},{20,4},{24,8},{28,12},{1,17},{... | collective-permute-start | bytes 196616 | tf_op jit(solution)/shard_map/ppermute | solution.py:26
  153.9 1.9 %collective-permute-start.42 = (bf16[48,1024]{1,0:T(8,128)(2,1)S(1)}, bf16[48,1024]{1,0:T(8,128)(2,1)S(1)}, u32[]{:S(2)}, u32[]{:S(2)}) collective-permute-start(bf16[48,1024]{1,0:T(8,128)(2,1)S(1)} %get-tuple-element.269), channel_id=1, source_target_pairs={{0,16},{4,20},{8,24},{12,28},{16,0},{20,4},{24,8},{28,12},{1,17},{... | collective-permute-start | bytes 294920 | tf_op jit(solution)/shard_map/ppermute | solution.py:26
  157.6 2.0 %collective-permute-done.42.refs_1_ = bf16[48,1024]{1,0:T(8,128)(2,1)S(1)} collective-permute-done((bf16[48,1024]{1,0:T(8,128)(2,1)S(1)}, bf16[48,1024]{1,0:T(8,128)(2,1)S(1)}, u32[]{:S(2)}, u32[]{:S(2)}) %collective-permute-start.42) | collective-permute-done | bytes 98336 | tf_op jit(solution)/shard_map/ppermute | solution.py:26
  (155 shorter events, 49.6 us)
Async XLA Ops:
  3.5 8.5 %collective-permute-start.1 = (bf16[160,512]{1,0:T(8,128)(2,1)}, bf16[160,512]{1,0:T(8,128)(2,1)S(1)}, u32[]{:S(2)}, u32[]{:S(2)}) collective-permute-start(bf16[160,512]{1,0:T(8,128)(2,1)} %get-tuple-element.142.refs_0_), channel_id=1, source_target_pairs={{0,2},{1,3},{2,0},{3,1},{4,6},{5,7},{6,4},{7,5},{8,10},{9,11},{10,... | collective-permute-start | bytes 491528 | tf_op jit(solution)/shard_map/ppermute | solution.py:26
  18.5 7.4 %collective-permute-start.4 = (bf16[176,512]{1,0:T(8,128)(2,1)S(1)}, bf16[176,512]{1,0:T(8,128)(2,1)S(1)}, u32[]{:S(2)}, u32[]{:S(2)}) collective-permute-start(bf16[176,512]{1,0:T(8,128)(2,1)S(1)} %get-tuple-element.148), channel_id=1, source_target_pairs={{0,2},{1,3},{2,0},{3,1},{4,6},{5,7},{6,4},{7,5},{8,10},{9,11},{10,... | collective-permute-start | bytes 540680 | tf_op jit(solution)/shard_map/ppermute | solution.py:26
  18.7 9.4 %collective-permute-start.5 = (bf16[176,512]{1,0:T(8,128)(2,1)S(1)}, bf16[176,512]{1,0:T(8,128)(2,1)S(1)}, u32[]{:S(2)}, u32[]{:S(2)}) collective-permute-start(bf16[176,512]{1,0:T(8,128)(2,1)S(1)} %get-tuple-element.149), channel_id=1, source_target_pairs={{0,3},{1,2},{2,1},{3,0},{4,7},{5,6},{6,5},{7,4},{8,11},{9,10},{10,... | collective-permute-start | bytes 540680 | tf_op jit(solution)/shard_map/ppermute | solution.py:26
  28.1 16.5 %collective-permute-start.8 = (bf16[160,1024]{1,0:T(8,128)(2,1)S(1)}, bf16[160,1024]{1,0:T(8,128)(2,1)}, u32[]{:S(2)}, u32[]{:S(2)}) collective-permute-start(bf16[160,1024]{1,0:T(8,128)(2,1)S(1)} %copy-done.2), channel_id=1, source_target_pairs={{0,2},{1,3},{2,0},{3,1},{4,6},{5,7},{6,4},{7,5},{8,10},{9,11},{10,... | collective-permute-start | bytes 983048 | tf_op jit(solution)/shard_map/ppermute | solution.py:26
  32.6 12.8 %collective-permute-start.7 = (bf16[160,1024]{1,0:T(8,128)(2,1)S(1)}, bf16[160,1024]{1,0:T(8,128)(2,1)S(1)}, u32[]{:S(2)}, u32[]{:S(2)}) collective-permute-start(bf16[160,1024]{1,0:T(8,128)(2,1)S(1)} %get-tuple-element.157.ff_low.refs_4_), channel_id=1, source_target_pairs={{0,2},{1,3},{2,0},{3,1},{4,6},{5,7},{6,4},{7,5},{8,10},{9,11},{10,... | collective-permute-start | bytes 983048 | tf_op jit(solution)/shard_map/ppermute | solution.py:26
  34.6 12.7 %collective-permute-start.6 = (bf16[160,1024]{1,0:T(8,128)(2,1)S(1)}, bf16[160,1024]{1,0:T(8,128)(2,1)S(1)}, u32[]{:S(2)}, u32[]{:S(2)}) collective-permute-start(bf16[160,1024]{1,0:T(8,128)(2,1)S(1)} %get-tuple-element.157.ff_low.refs_4_), channel_id=1, source_target_pairs={{0,1},{1,0},{2,3},{3,2},{4,5},{5,4},{6,7},{7,6},{8,9},{9,8},{10,11... | collective-permute-start | bytes 983048 | tf_op jit(solution)/shard_map/ppermute | solution.py:26
  34.7 11.7 %collective-permute-start.10 = (bf16[160,1024]{1,0:T(8,128)(2,1)S(1)}, bf16[160,1024]{1,0:T(8,128)(2,1)S(1)}, u32[]{:S(2)}, u32[]{:S(2)}) collective-permute-start(bf16[160,1024]{1,0:T(8,128)(2,1)S(1)} %copy-done.2), channel_id=1, source_target_pairs={{0,1},{1,0},{2,3},{3,2},{4,5},{5,4},{6,7},{7,6},{8,9},{9,8},{10,11... | collective-permute-start | bytes 983048 | tf_op jit(solution)/shard_map/ppermute | solution.py:26
  45.9 14.7 %collective-permute-start.15 = (bf16[2,160,512]{2,1,0:T(8,128)(2,1)}, bf16[2,160,512]{2,1,0:T(8,128)(2,1)S(1)}, u32[]{:S(2)}, u32[]{:S(2)}) collective-permute-start(bf16[2,160,512]{2,1,0:T(8,128)(2,1)} %get-tuple-element.172), channel_id=1, source_target_pairs={{0,2},{1,3},{2,0},{3,1},{4,6},{5,7},{6,4},{7,5},{8,10},{9,11},{10,... | collective-permute-start | bytes 983048 | tf_op jit(solution)/shard_map/ppermute | solution.py:26
  46.4 15.4 %collective-permute-start.16 = (bf16[2,160,512]{2,1,0:T(8,128)(2,1)}, bf16[2,160,512]{2,1,0:T(8,128)(2,1)S(1)}, u32[]{:S(2)}, u32[]{:S(2)}) collective-permute-start(bf16[2,160,512]{2,1,0:T(8,128)(2,1)} %get-tuple-element.173), channel_id=1, source_target_pairs={{0,3},{1,2},{2,1},{3,0},{4,7},{5,6},{6,5},{7,4},{8,11},{9,10},{10,... | collective-permute-start | bytes 983048 | tf_op jit(solution)/shard_map/ppermute | solution.py:26
  59.5 7.5 %collective-permute-start.13 = (bf16[192,512]{1,0:T(8,128)(2,1)S(1)}, bf16[192,512]{1,0:T(8,128)(2,1)S(1)}, u32[]{:S(2)}, u32[]{:S(2)}) collective-permute-start(bf16[192,512]{1,0:T(8,128)(2,1)S(1)} %get-tuple-element.163.refs_4_), channel_id=1, source_target_pairs={{0,2},{1,3},{2,0},{3,1},{4,6},{5,7},{6,4},{7,5},{8,10},{9,11},{10,... | collective-permute-start | bytes 589832 | tf_op jit(solution)/shard_map/ppermute | solution.py:26
  59.9 9.6 %collective-permute-start.12 = (bf16[192,512]{1,0:T(8,128)(2,1)S(1)}, bf16[192,512]{1,0:T(8,128)(2,1)S(1)}, u32[]{:S(2)}, u32[]{:S(2)}) collective-permute-start(bf16[192,512]{1,0:T(8,128)(2,1)S(1)} %get-tuple-element.163.refs_4_), channel_id=1, source_target_pairs={{0,1},{1,0},{2,3},{3,2},{4,5},{5,4},{6,7},{7,6},{8,9},{9,8},{10,11... | collective-permute-start | bytes 589832 | tf_op jit(solution)/shard_map/ppermute | solution.py:26
  67.3 23.4 %collective-permute-start.22 = (bf16[2,160,512]{2,1,0:T(8,128)(2,1)S(1)}, bf16[2,160,512]{2,1,0:T(8,128)(2,1)S(1)}, u32[]{:S(2)}, u32[]{:S(2)}) collective-permute-start(bf16[2,160,512]{2,1,0:T(8,128)(2,1)S(1)} %get-tuple-element.199), channel_id=1, source_target_pairs={{0,1},{1,0},{2,3},{3,2},{4,5},{5,4},{6,7},{7,6},{8,9},{9,8},{10,11... | collective-permute-start | bytes 983048 | tf_op jit(solution)/shard_map/ppermute | solution.py:26
  67.5 20.8 %collective-permute-start.24 = (bf16[2,160,512]{2,1,0:T(8,128)(2,1)S(1)}, bf16[2,160,512]{2,1,0:T(8,128)(2,1)S(1)}, u32[]{:S(2)}, u32[]{:S(2)}) collective-permute-start(bf16[2,160,512]{2,1,0:T(8,128)(2,1)S(1)} %copy-done.31), channel_id=1, source_target_pairs={{0,3},{1,2},{2,1},{3,0},{4,7},{5,6},{6,5},{7,4},{8,11},{9,10},{10,... | collective-permute-start | bytes 983048 | tf_op jit(solution)/shard_map/ppermute | solution.py:26
  67.8 14.6 %collective-permute-start.18 = (bf16[512,512]{1,0:T(8,128)(2,1)S(1)}, bf16[512,512]{1,0:T(8,128)(2,1)S(1)}, u32[]{:S(2)}, u32[]{:S(2)}) collective-permute-start(bf16[512,512]{1,0:T(8,128)(2,1)S(1)} %get-tuple-element.186), channel_id=1, source_target_pairs={{0,4},{4,0},{8,12},{12,8},{16,20},{20,16},{24,28},{28,24},{1,5},{5... | collective-permute-start | bytes 1572872 | tf_op jit(solution)/shard_map/ppermute | solution.py:26
  69.5 13.8 %collective-permute-start.19 = (bf16[512,512]{1,0:T(8,128)(2,1)S(1)}, bf16[512,512]{1,0:T(8,128)(2,1)S(1)}, u32[]{:S(2)}, u32[]{:S(2)}) collective-permute-start(bf16[512,512]{1,0:T(8,128)(2,1)S(1)} %get-tuple-element.187), channel_id=1, source_target_pairs={{0,8},{4,12},{8,0},{12,4},{16,24},{20,28},{24,16},{28,20},{1,9},{5... | collective-permute-start | bytes 1572872 | tf_op jit(solution)/shard_map/ppermute | solution.py:26
  71.0 19.7 %collective-permute-start.23 = (bf16[2,160,512]{2,1,0:T(8,128)(2,1)S(1)}, bf16[2,160,512]{2,1,0:T(8,128)(2,1)S(1)}, u32[]{:S(2)}, u32[]{:S(2)}) collective-permute-start(bf16[2,160,512]{2,1,0:T(8,128)(2,1)S(1)} %copy-done.30), channel_id=1, source_target_pairs={{0,2},{1,3},{2,0},{3,1},{4,6},{5,7},{6,4},{7,5},{8,10},{9,11},{10,... | collective-permute-start | bytes 983048 | tf_op jit(solution)/shard_map/ppermute | solution.py:26
  88.1 7.1 %collective-permute-start.25 = (bf16[512,1024]{1,0:T(8,128)(2,1)S(1)}, bf16[512,1024]{1,0:T(8,128)(2,1)S(1)}, u32[]{:S(2)}, u32[]{:S(2)}) collective-permute-start(bf16[512,1024]{1,0:T(8,128)(2,1)S(1)} %get-tuple-element.207), channel_id=1, source_target_pairs={{0,1},{1,0},{2,3},{3,2},{4,5},{5,4},{6,7},{7,6},{8,9},{9,8},{10,11... | collective-permute-start | bytes 3145736 | tf_op jit(solution)/shard_map/ppermute | solution.py:26
  88.3 9.3 %collective-permute-start.26 = (bf16[256,512]{1,0:T(8,128)(2,1)S(1)}, bf16[256,512]{1,0:T(8,128)(2,1)S(1)}, u32[]{:S(2)}, u32[]{:S(2)}) collective-permute-start(bf16[256,512]{1,0:T(8,128)(2,1)S(1)} %get-tuple-element.213), channel_id=1, source_target_pairs={{0,8},{4,12},{8,0},{12,4},{16,24},{20,28},{24,16},{28,20},{1,9},{5... | collective-permute-start | bytes 786440 | tf_op jit(solution)/shard_map/ppermute | solution.py:26
  89.9 9.2 %collective-permute-start.27 = (bf16[256,512]{1,0:T(8,128)(2,1)S(1)}, bf16[256,512]{1,0:T(8,128)(2,1)S(1)}, u32[]{:S(2)}, u32[]{:S(2)}) collective-permute-start(bf16[256,512]{1,0:T(8,128)(2,1)S(1)} %get-tuple-element.214), channel_id=1, source_target_pairs={{0,4},{4,0},{8,12},{12,8},{16,20},{20,16},{24,28},{28,24},{1,5},{5... | collective-permute-start | bytes 786440 | tf_op jit(solution)/shard_map/ppermute | solution.py:26
  93.4 16.1 %collective-permute-start.28 = (bf16[512,512]{1,0:T(8,128)(2,1)S(1)}, bf16[512,512]{1,0:T(8,128)(2,1)S(1)}, u32[]{:S(2)}, u32[]{:S(2)}) collective-permute-start(bf16[512,512]{1,0:T(8,128)(2,1)S(1)} %get-tuple-element.228), channel_id=1, source_target_pairs={{0,4},{4,0},{8,12},{12,8},{16,20},{20,16},{24,28},{28,24},{1,5},{5... | collective-permute-start | bytes 1572872 | tf_op jit(solution)/shard_map/ppermute | solution.py:26
  94.7 15.4 %collective-permute-start.29 = (bf16[512,512]{1,0:T(8,128)(2,1)S(1)}, bf16[512,512]{1,0:T(8,128)(2,1)S(1)}, u32[]{:S(2)}, u32[]{:S(2)}) collective-permute-start(bf16[512,512]{1,0:T(8,128)(2,1)S(1)} %get-tuple-element.229), channel_id=1, source_target_pairs={{0,8},{4,12},{8,0},{12,4},{16,24},{20,28},{24,16},{28,20},{1,9},{5... | collective-permute-start | bytes 1572872 | tf_op jit(solution)/shard_map/ppermute | solution.py:26
  103.6 18.9 %collective-permute-start.34 = (bf16[528,1024]{1,0:T(8,128)(2,1)S(1)}, bf16[528,1024]{1,0:T(8,128)(2,1)S(1)}, u32[]{:S(2)}, u32[]{:S(2)}) collective-permute-start(bf16[528,1024]{1,0:T(8,128)(2,1)S(1)} %get-tuple-element.245), channel_id=1, source_target_pairs={{0,1},{1,0},{2,3},{3,2},{4,5},{5,4},{6,7},{7,6},{8,9},{9,8},{10,11... | collective-permute-start | bytes 3244040 | tf_op jit(solution)/shard_map/ppermute | solution.py:26
  103.7 15.4 %collective-permute-start.30 = (bf16[128,1024]{1,0:T(8,128)(2,1)S(1)}, bf16[128,1024]{1,0:T(8,128)(2,1)S(1)}, u32[]{:S(2)}, u32[]{:S(2)}) collective-permute-start(bf16[128,1024]{1,0:T(8,128)(2,1)S(1)} %get-tuple-element.233), channel_id=1, source_target_pairs={{0,16},{4,20},{8,24},{12,28},{16,0},{20,4},{24,8},{28,12},{1,17},{... | collective-permute-start | bytes 786440 | tf_op jit(solution)/shard_map/ppermute | solution.py:26
  106.3 15.4 %collective-permute-start.33 = (bf16[256,1024]{1,0:T(8,128)(2,1)S(1)}, bf16[256,1024]{1,0:T(8,128)(2,1)S(1)}, u32[]{:S(2)}, u32[]{:S(2)}) collective-permute-start(bf16[256,1024]{1,0:T(8,128)(2,1)S(1)} %get-tuple-element.242), channel_id=1, source_target_pairs={{0,2},{1,3},{2,0},{3,1},{4,6},{5,7},{6,4},{7,5},{8,10},{9,11},{10,... | collective-permute-start | bytes 1572872 | tf_op jit(solution)/shard_map/ppermute | solution.py:26
  111.0 10.0 %collective-permute-start.31 = (bf16[256,512]{1,0:T(8,128)(2,1)S(1)}, bf16[256,512]{1,0:T(8,128)(2,1)S(1)}, u32[]{:S(2)}, u32[]{:S(2)}) collective-permute-start(bf16[256,512]{1,0:T(8,128)(2,1)S(1)} %get-tuple-element.238), channel_id=1, source_target_pairs={{0,8},{4,12},{8,0},{12,4},{16,24},{20,28},{24,16},{28,20},{1,9},{5... | collective-permute-start | bytes 786440 | tf_op jit(solution)/shard_map/ppermute | solution.py:26
  111.3 9.7 %collective-permute-start.32 = (bf16[256,512]{1,0:T(8,128)(2,1)S(1)}, bf16[256,512]{1,0:T(8,128)(2,1)S(1)}, u32[]{:S(2)}, u32[]{:S(2)}) collective-permute-start(bf16[256,512]{1,0:T(8,128)(2,1)S(1)} %get-tuple-element.239), channel_id=1, source_target_pairs={{0,4},{4,0},{8,12},{12,8},{16,20},{20,16},{24,28},{28,24},{1,5},{5... | collective-permute-start | bytes 786440 | tf_op jit(solution)/shard_map/ppermute | solution.py:26
  123.3 14.9 %collective-permute-start.35 = (bf16[272,1024]{1,0:T(8,128)(2,1)S(1)}, bf16[272,1024]{1,0:T(8,128)(2,1)S(1)}, u32[]{:S(2)}, u32[]{:S(2)}) collective-permute-start(bf16[272,1024]{1,0:T(8,128)(2,1)S(1)} %get-tuple-element.247), channel_id=1, source_target_pairs={{0,2},{1,3},{2,0},{3,1},{4,6},{5,7},{6,4},{7,5},{8,10},{9,11},{10,... | collective-permute-start | bytes 1671176 | tf_op jit(solution)/shard_map/ppermute | solution.py:26
  124.8 16.3 %collective-permute-start.37 = (bf16[128,1024]{1,0:T(8,128)(2,1)S(1)}, bf16[128,1024]{1,0:T(8,128)(2,1)S(1)}, u32[]{:S(2)}, u32[]{:S(2)}) collective-permute-start(bf16[128,1024]{1,0:T(8,128)(2,1)S(1)} %get-tuple-element.254), channel_id=1, source_target_pairs={{0,16},{4,20},{8,24},{12,28},{16,0},{20,4},{24,8},{28,12},{1,17},{... | collective-permute-start | bytes 786440 | tf_op jit(solution)/shard_map/ppermute | solution.py:26
  127.8 21.6 %all-to-all-start = ((bf16[4,32,1024]{2,1,0:T(8,128)(2,1)}), bf16[4,32,1024]{2,1,0:T(8,128)(2,1)S(1)}, u32[]{:S(2)}, u32[]{:S(2)}) async-start(bf16[4,32,1024]{2,1,0:T(8,128)(2,1)} %bitcast.11), calls=%async_computation | async-start | bytes 524288 | tf_op jit(solution)/shard_map/all_to_all | solution.py:928
  131.2 9.2 %collective-permute-start.36 = (bf16[128,1024]{1,0:T(8,128)(2,1)S(1)}, bf16[128,1024]{1,0:T(8,128)(2,1)S(1)}, u32[]{:S(2)}, u32[]{:S(2)}) collective-permute-start(bf16[128,1024]{1,0:T(8,128)(2,1)S(1)} %get-tuple-element.251), channel_id=1, source_target_pairs={{0,4},{4,0},{8,12},{12,8},{16,20},{20,16},{24,28},{28,24},{1,5},{5... | collective-permute-start | bytes 786440 | tf_op jit(solution)/shard_map/ppermute | solution.py:26
  138.9 7.3 %collective-permute-start.38 = (bf16[144,1024]{1,0:T(8,128)(2,1)S(1)}, bf16[144,1024]{1,0:T(8,128)(2,1)S(1)}, u32[]{:S(2)}, u32[]{:S(2)}) collective-permute-start(bf16[144,1024]{1,0:T(8,128)(2,1)S(1)} %get-tuple-element.256), channel_id=1, source_target_pairs={{0,4},{4,0},{8,12},{12,8},{16,20},{20,16},{24,28},{28,24},{1,5},{5... | collective-permute-start | bytes 884744 | tf_op jit(solution)/shard_map/ppermute | solution.py:26
  142.7 7.6 %collective-permute-start.39 = (bf16[64,1024]{1,0:T(8,128)(2,1)S(1)}, bf16[64,1024]{1,0:T(8,128)(2,1)S(1)}, u32[]{:S(2)}, u32[]{:S(2)}) collective-permute-start(bf16[64,1024]{1,0:T(8,128)(2,1)S(1)} %get-tuple-element.260), channel_id=1, source_target_pairs={{0,8},{4,12},{8,0},{12,4},{16,24},{20,28},{24,16},{28,20},{1,9},{5... | collective-permute-start | bytes 393224 | tf_op jit(solution)/shard_map/ppermute | solution.py:26
  (44 other events, 294.3 us)
